TPU v7x, 32 devices: a whole 2x2x4 slice. The times are simulated.
32 devices in a mesh: dp: 8 (over y, x, core), tensor: 4 (over z).
Axes of the slice: x: 2, y: 2, z: 4, core: 2. Of those that a mesh axis runs over, the one named last changes fastest.
Arguments:
- hidden: bfloat16 [16384, 768], P('dp'), may hold values from -6 to 6
- teacher: float32 [16384, 768], P('dp'), may hold values from -6 to 6
- valid: int32 [8, 2048], P('dp'), may hold values from 0 to 1, as said below
- w_qkv: bfloat16 [3, 768, 768], P(None, None, 'tensor'), may hold values from -0.21875 to 0.21875
- b_qv: float32 [2, 768], P(None, 'tensor'), may hold values from -1 to 1
- w_attn_out: bfloat16 [768, 768], P('tensor'), may hold values from -1.25 to 1.25
- b_attn_out: float32 [768], replicated, may hold values from -1.5 to 1.5
- gain_one: float32 [768], replicated, may hold values from 0.5 to 1.5
- bias_one: float32 [768], replicated, may hold values from -1.5 to 1.5
- w_up: bfloat16 [768, 3072], P(None, 'tensor'), may hold values from -0.21875 to 0.21875
- b_up: float32 [3072], P('tensor'), may hold values from -2.5 to 2.5
- w_down: bfloat16 [3072, 768], P('tensor'), may hold values from -0.109375 to 0.109375
- b_down: float32 [768], replicated, may hold values from -1.5 to 1.5
- gain_two: float32 [768], replicated, may hold values from 0.5 to 1.5
- bias_two: float32 [768], replicated, may hold values from -1.5 to 1.5
- pairwise_gate_odds_table: float32 [12, 512, 512], P('tensor'), may hold values from -5 to 5
- gate_random_perturbation: float32 [12, 512, 512], P('tensor'), may hold values from -2 to 2
Outputs:
- out_states: float32 [16384, 768], P('dp')
- loss: float32 [], replicated
- grad_hidden: float32 [16384, 768], P('dp')
- grad_w_qkv: float32 [3, 768, 768], P(None, None, 'tensor')
- grad_b_qv: float32 [2, 768], P(None, 'tensor')
- grad_w_attn_out: float32 [768, 768], P('tensor')
- grad_b_attn_out: float32 [768], replicated
- grad_gain_one: float32 [768], replicated
- derivative_first_offset: float32 [768], replicated
- grad_w_up: float32 [768, 3072], P(None, 'tensor')
- grad_b_up: float32 [3072], P('tensor')
- grad_w_down: float32 [3072, 768], P('tensor')
- grad_b_down: float32 [768], replicated
- grad_gain_two: float32 [768], replicated
- grad_bias_two: float32 [768], replicated
- grad_mask_logits: float32 [12, 512, 512], P('tensor')
Inputs may be any that keep to these rules, and one draw needn't show every extreme that they name: The first token of every sequence is valid.
All inputs are finite; a program needn't handle non-finite values.
Results may differ from a plain program's by a relative error of at most 0.019.
Values may be sent and summed in bfloat16 or wider, within the bound.
No kernel may reach another device: no remote copies, remote signals or barrier semaphores. Data moves between devices by JAX's collectives and lax.ppermute only.
A program may use at most 256 MiB of HBM per device.

v0:
```python
import math

import jax
import jax.numpy as jnp
from jax import lax
from jax.sharding import PartitionSpec as P

BLOCK = 256


epsilon = 1e-06
gumbel_softening_factor = 0.5


def normed(resid, gain, shift):
    average = jnp.mean(resid, axis=-1, keepdims=True)
    centred = resid - average
    variance = jnp.mean(centred * centred, axis=-1, keepdims=True)
    return centred * lax.rsqrt(variance + epsilon) * gain + shift


def exact_gelu(inputs):
    return jax.nn.gelu(inputs, approximate=False)


def block_scores(queries, key_vectors, gate_natural_log, block_index, score_scale):
    period = gate_natural_log.shape[1]
    head_count = gate_natural_log.shape[0]
    head_width = queries.shape[1] // head_count
    key_span = (block_index + 1) * period
    query_rows = queries[block_index * period : key_span].reshape(period, head_count, head_width)
    key_row_block = key_vectors[:key_span].reshape(key_span, head_count, head_width)
    scores = (
        jnp.einsum("qhd,khd->hqk", query_rows, key_row_block, preferred_element_type=jnp.float32)
        * score_scale
    )
    scores = scores + jnp.tile(gate_natural_log, (1, 1, block_index + 1))
    row_pos = lax.broadcasted_iota(jnp.int32, (period, key_span), 0) + block_index * period
    col_pos = lax.broadcasted_iota(jnp.int32, (period, key_span), 1)
    allowed = col_pos // BLOCK <= row_pos // BLOCK
    return jnp.where(allowed[None], scores, -1e30)


def body(
    hidden,
    teacher,
    valid,
    w_qkv,
    b_qv,
    w_attn_out,
    b_attn_out,
    gain_one,
    bias_one,
    w_up,
    b_up,
    w_down,
    b_down,
    gain_two,
    bias_two,
    pairwise_gate_odds_table,
    gate_random_perturbation,
):
    seq_tokens = hidden.shape[0]
    model_width = hidden.shape[1]
    period = pairwise_gate_odds_table.shape[1]
    head_count = pairwise_gate_odds_table.shape[0]
    local_width = w_qkv.shape[2]
    head_width = local_width // head_count
    score_scale = 1.0 / math.sqrt(head_width)
    num_blocks = seq_tokens // period
    projected = jnp.einsum("td,kde->kte", hidden, w_qkv, preferred_element_type=jnp.float32)
    queries = (projected[0] + b_qv[0]).astype(jnp.bfloat16)
    key_vectors = projected[1].astype(jnp.bfloat16)
    values = (projected[2] + b_qv[1]).astype(jnp.bfloat16)

    def soft_mask(affinity_preactivations):
        return jax.nn.log_sigmoid(
            (affinity_preactivations + gate_random_perturbation) / gumbel_softening_factor
        )

    gate_natural_log, mask_pull = jax.vjp(soft_mask, pairwise_gate_odds_table)
    contexts = []
    logarithm_sums = []
    for block_index in range(num_blocks):
        scores = block_scores(queries, key_vectors, gate_natural_log, block_index, score_scale)
        highest = jnp.max(scores, axis=-1, keepdims=True)
        exponent = jnp.exp(scores - highest)
        totals = jnp.sum(exponent, axis=-1, keepdims=True)
        soft_weights = (exponent / totals).astype(jnp.bfloat16)
        logarithm_sums.append(highest + jnp.log(totals))
        key_span = (block_index + 1) * period
        value_rows = values[:key_span].reshape(key_span, head_count, head_width)
        contexts.append(
            jnp.einsum("hqk,khd->qhd", soft_weights, value_rows, preferred_element_type=jnp.float32)
        )
    context = (
        jnp.concatenate(contexts, axis=0).reshape(seq_tokens, local_width).astype(jnp.bfloat16)
    )
    hidden_wide = hidden.astype(jnp.float32)
    attn_part = jnp.dot(context, w_attn_out, preferred_element_type=jnp.float32)
    attention = lax.psum(attn_part.astype(jnp.bfloat16), "tensor").astype(jnp.float32) + b_attn_out
    first, first_pull = jax.vjp(normed, hidden_wide + attention, gain_one, bias_one)
    first_low = first.astype(jnp.bfloat16)
    before = jnp.dot(first_low, w_up, preferred_element_type=jnp.float32) + b_up
    activated, gelu_pull = jax.vjp(exact_gelu, before)
    act_low = activated.astype(jnp.bfloat16)
    ffn_part = jnp.dot(act_low, w_down, preferred_element_type=jnp.float32)
    feedforward = lax.psum(ffn_part.astype(jnp.bfloat16), "tensor").astype(jnp.float32) + b_down
    out_states, second_pull = jax.vjp(normed, first + feedforward, gain_two, bias_two)
    valid_rows = valid[0].astype(jnp.float32)[:, None]
    residue = out_states - teacher
    local_error = jnp.sum(valid_rows * residue * residue)
    local_count = jnp.sum(valid_rows)
    total_valid, total_error = lax.psum((local_count, local_error), "dp")
    loss_value = total_error / (total_valid * model_width)
    factor = seq_tokens / total_valid
    upstream_derivative = 2.0 * factor * valid_rows * residue
    grad_second, grad_gain_two, grad_bias_two = second_pull(upstream_derivative)
    grad_ffn = grad_second.astype(jnp.bfloat16)
    grad_b_down = jnp.sum(grad_ffn, axis=0, dtype=jnp.float32)
    grad_w_down = jnp.einsum("tf,td->fd", act_low, grad_ffn, preferred_element_type=jnp.float32)
    grad_act = jnp.einsum("td,fd->tf", grad_ffn, w_down, preferred_element_type=jnp.float32)
    grad_before = gelu_pull(grad_act)[0].astype(jnp.bfloat16)
    grad_b_up = jnp.sum(grad_before, axis=0, dtype=jnp.float32)
    grad_w_up = jnp.einsum("td,tf->df", first_low, grad_before, preferred_element_type=jnp.float32)
    back_first = jnp.einsum("tf,df->td", grad_before, w_up, preferred_element_type=jnp.float32)
    grad_first = grad_second + lax.psum(back_first.astype(jnp.bfloat16), "tensor").astype(
        jnp.float32
    )
    grad_resid, grad_gain_one, derivative_first_offset = first_pull(grad_first)
    grad_attn = grad_resid.astype(jnp.bfloat16)
    grad_b_attn_out = jnp.sum(grad_attn, axis=0, dtype=jnp.float32)
    grad_w_attn_out = jnp.einsum(
        "tc,td->cd", context, grad_attn, preferred_element_type=jnp.float32
    )
    grad_context = jnp.einsum(
        "td,cd->tc", grad_attn, w_attn_out, preferred_element_type=jnp.float32
    ).astype(jnp.bfloat16)
    grad_queries = []
    grad_keys = jnp.zeros((seq_tokens, head_count, head_width), jnp.float32)
    grad_values = jnp.zeros((seq_tokens, head_count, head_width), jnp.float32)
    grad_log_mask = jnp.zeros(gate_natural_log.shape, jnp.float32)
    for block_index in range(num_blocks):
        scores = block_scores(queries, key_vectors, gate_natural_log, block_index, score_scale)
        soft = jnp.exp(scores - logarithm_sums[block_index])
        start_row = block_index * period
        key_span = start_row + period
        grad_rows = grad_context[start_row:key_span].reshape(period, head_count, head_width)
        query_rows = queries[start_row:key_span].reshape(period, head_count, head_width)
        key_row_block = key_vectors[:key_span].reshape(key_span, head_count, head_width)
        value_rows = values[:key_span].reshape(key_span, head_count, head_width)
        grad_soft = jnp.einsum(
            "qhd,khd->hqk", grad_rows, value_rows, preferred_element_type=jnp.float32
        )
        inner = jnp.sum(soft * grad_soft, axis=-1, keepdims=True)
        grad_scores = (soft * (grad_soft - inner)).astype(jnp.bfloat16)
        grad_log_mask = grad_log_mask + jnp.sum(
            grad_scores.reshape(head_count, period, block_index + 1, period),
            axis=2,
            dtype=jnp.float32,
        )
        grad_queries.append(
            jnp.einsum(
                "hqk,khd->qhd", grad_scores, key_row_block, preferred_element_type=jnp.float32
            )
            * score_scale
        )
        grad_keys = grad_keys.at[:key_span].add(
            jnp.einsum("hqk,qhd->khd", grad_scores, query_rows, preferred_element_type=jnp.float32)
            * score_scale
        )
        grad_values = grad_values.at[:key_span].add(
            jnp.einsum(
                "hqk,qhd->khd",
                soft.astype(jnp.bfloat16),
                grad_rows,
                preferred_element_type=jnp.float32,
            )
        )
    grad_qkv = jnp.stack(
        [
            jnp.concatenate(grad_queries, axis=0).reshape(seq_tokens, local_width),
            grad_keys.reshape(seq_tokens, local_width),
            grad_values.reshape(seq_tokens, local_width),
        ]
    ).astype(jnp.bfloat16)
    grad_w_qkv = jnp.einsum("td,kte->kde", hidden, grad_qkv, preferred_element_type=jnp.float32)
    grad_b_qv = jnp.sum(grad_qkv[0::2], axis=1, dtype=jnp.float32)
    back_hidden = jnp.einsum("kte,kde->td", grad_qkv, w_qkv, preferred_element_type=jnp.float32)
    grad_hidden = grad_resid + lax.psum(back_hidden.astype(jnp.bfloat16), "tensor").astype(
        jnp.float32
    )
    mask_gradient = mask_pull(grad_log_mask)[0]
    summed = lax.psum(
        (
            grad_w_qkv,
            grad_b_qv,
            grad_w_attn_out,
            grad_b_attn_out,
            grad_gain_one,
            derivative_first_offset,
            grad_w_up,
            grad_b_up,
            grad_w_down,
            grad_b_down,
            grad_gain_two,
            grad_bias_two,
            mask_gradient,
        ),
        "dp",
    )
    return (
        out_states,
        loss_value,
        grad_hidden,
        summed[0],
        summed[1],
        summed[2],
        summed[3],
        summed[4],
        summed[5],
        summed[6],
        summed[7],
        summed[8],
        summed[9],
        summed[10],
        summed[11],
        summed[12],
    )


def solution(mesh):
    placed = (
        P("dp", None),
        P("dp", None),
        P("dp", None),
        P(None, None, "tensor"),
        P(None, "tensor"),
        P("tensor", None),
        P(),
        P(),
        P(),
        P(None, "tensor"),
        P("tensor"),
        P("tensor", None),
        P(),
        P(),
        P(),
        P("tensor", None, None),
        P("tensor", None, None),
    )
    return jax.shard_map(
        body,
        mesh=mesh,
        in_specs=placed,
        out_specs=(
            P("dp", None),
            P(),
            P("dp", None),
            P(None, None, "tensor"),
            P(None, "tensor"),
            P("tensor", None),
            P(),
            P(),
            P(),
            P(None, "tensor"),
            P("tensor"),
            P("tensor", None),
            P(),
            P(),
            P(),
            P("tensor", None, None),
        ),
        check_vma=False,
    )
```

profile of v0, /device:TPU:0, one launch (start us, length us, event | category | flops | bytes accessed | tf_op | source)
XLA Modules:
  0.0 1031.9 jit_solution(5200982813277051562)
XLA Ops:
  15.1 4.2 convolution_bitcast_fusion
  26.7 3.5 copy.54
  30.2 3.6 copy.55
  33.8 6.4 fusion.35
  40.2 3.6 copy.57
  46.0 7.0 tile.14
  53.0 9.6 copy.58
  62.6 6.6 tile.12
  69.1 9.2 tile.13
  78.3 7.7 tile.16
  86.1 15.9 %tile.17 = f32[3,512,2048]{2,1,0:T(8,128)} reshape(f32[3,512,4,512]{3,2,1,0:T(4,128)} %tile.16) | data formatting | bytes 25165824 | tf_op jit(solution)/shard_map/tile | solution.py:37
  126.1 6.7 fusion.143
  137.5 3.2 fusion.97
  144.6 123.8 %all-reduce.10.cloned.1.call-done = bf16[2048,768]{1,0:T(8,128)(2,1)} async-done(((bf16[2048,768]{1,0:T(8,128)(2,1)}), bf16[2048,768]{1,0:T(8,128)(2,1)}) %all-reduce.10.cloned.1.call-update) | async-done | bytes 3145744 | tf_op jit(solution)/shard_map/psum | solution.py:101
  268.4 4.1 fusion.17
  274.9 18.6 %multiply_convert_fusion.3 = (bf16[2048,768]{1,0:T(8,128)(2,1)S(1)}, f32[2048,768]{1,0:T(8,128)}, f32[2048,768]{1,0:T(8,128)}) fusion(f32[768]{0:T(1024)S(1)} %copy-done.118, bf16[768,768]{1,0:T(8,128)(2,1)S(1)} %copy-done, f32[768]{0:T(1024)S(1)} %copy-done.107, f32[768]{0:T(1024)S(1)} %copy-done.75, f32[2048]{0:T(1024)S(1)} %fusion.112, ...), kind=kOutput, calls=%fused_computation.44 | convolution fusion | flops 2533883904 | bytes 23228416 | tf_op jit(solution)/shard_map/dot_general | solution.py:104
  295.3 4.0 convolution_convert_fusion.1
  300.0 14.6 %psum.136 = f32[]{:T(128)} all-reduce(f32[]{:T(128)} %convert_reduce_fusion.4), channel_id=1, replica_groups=mesh['dp'=8,'tensor'=4] {'dp'}, use_global_device_ids=true, to_apply=%region_17.18 | all-reduce | flops 1 | bytes 8 | tf_op jit(solution)/shard_map/psum | solution.py:114
  315.3 104.2 %all-reduce.12.cloned.1.call-done = bf16[2048,768]{1,0:T(8,128)(2,1)} async-done(((bf16[2048,768]{1,0:T(8,128)(2,1)}), bf16[2048,768]{1,0:T(8,128)(2,1)}) %all-reduce.12.cloned.1.call-update) | async-done | bytes 3145744 | tf_op jit(solution)/shard_map/psum | solution.py:108
  419.5 5.2 fusion.138
  425.7 8.2 multiply_reduce_fusion.2
  433.9 3.4 fusion.137
  439.4 8.4 convert_reduce_fusion.1
  449.6 4.0 convolution_convert_fusion
  454.4 119.4 %all-reduce.14.cloned.1.call-done = bf16[2048,768]{1,0:T(8,128)(2,1)} async-done(((bf16[2048,768]{1,0:T(8,128)(2,1)}), bf16[2048,768]{1,0:T(8,128)(2,1)}) %all-reduce.14.cloned.1.call-update) | async-done | bytes 3145744 | tf_op jit(solution)/shard_map/psum | solution.py:127
  573.8 10.1 multiply_reduce_fusion.3
  583.9 6.0 fusion.136
  606.3 9.1 reshape.827
  615.5 5.2 multiply_reduce_fusion.1
  627.5 7.4 copy.64
  634.9 10.8 %multiply_reduce_fusion = (f32[3,512]{1,0:T(4,128)S(1)}, f32[3,512,2048]{2,1,0:T(8,128)}) fusion(f32[3,512,2048]{2,1,0:T(8,128)} %copy-done.2, f32[3,512]{1,0:T(4,128)S(1)} %log_add_fusion, bf16[512,3,64]{0,2,1:T(8,128)(2,1)S(1)} %bitcast.203, f32[2048,3,64]{0,2,1:T(8,128)S(1)} %bitcast.187, f32[3,64]{1,0:T(4,128)S(1)} %copy-done.74), kind=kOutput, calls=%fused_computation.1 | convolution fusion | flops 412875264 | bytes 26948352 | tf_op jit(solution)/shard_map/qhd,khd->hqk/dot_general | solution.py:152
  647.6 6.3 multiply_convert_fusion
  659.3 15.4 %reshape.829 = f32[3,512,4,512]{3,2,1,0:T(4,128)} reshape(bf16[3,512,2048]{2,1,0:T(8,128)(2,1)} %copy-done.5) | data formatting | bytes 18874368 | tf_op jit(solution)/shard_map/convert_element_type | solution.py:157
  674.7 11.9 %reduce_sum.323 = f32[3,512,512]{2,1,0:T(8,128)} reduce(f32[3,512,2,512]{3,2,1,0:T(2,128)} %reshape.827, f32[]{:T(128)} %constant.386.clone.1), dimensions={2}, to_apply=%region_48.49 | reduce | flops 786432 | bytes 9437188 | tf_op jit(solution)/shard_map/reduce_sum | solution.py:157
  686.6 3.5 copy.63
  690.1 7.0 reduce_sum.324
  697.1 12.7 %reduce_sum.325 = f32[3,512,512]{2,1,0:T(8,128)} reduce(f32[3,512,4,512]{3,2,1,0:T(4,128)} %reshape.829, f32[]{:T(128)} %constant.386.clone.1), dimensions={2}, to_apply=%region_50.51 | reduce | flops 2359296 | bytes 15728644 | tf_op jit(solution)/shard_map/reduce_sum | solution.py:157
  709.8 3.7 copy.65
  713.5 11.1 %fusion.30 = (f32[3,512,512]{1,2,0:T(8,128)}, bf16[3,512,512]{1,2,0:T(8,128)(2,1)S(1)}) fusion(f32[3,512,512]{1,2,0:T(8,128)} %copy.65, f32[3,512,512]{1,2,0:T(8,128)} %reduce_sum.324, f32[3,512,512]{1,2,0:T(8,128)} %copy.63, f32[3,512,512]{1,2,0:T(8,128)} %copy.54, f32[3,512,512]{1,2,0:T(8,128)} %copy.55, f32[3,512,512]{1,2,0:T(8,128)} %get-tuple-element.244, ...), kind=kLoop, calls=%fused_computation.86 | loop fusion | flops 20447232 | bytes 26750976 | tf_op jit(solution)/shard_map/transpose(jvp())/div | solution.py:78
  737.3 4.1 bitcast_convert_fusion
  741.8 7.1 fusion.148
  748.9 4.8 fusion.129
  755.4 3.2 fusion.70
  760.0 26.0 %all-reduce.2 = (f32[]{:T(128)}, f32[2,192]{1,0:T(2,128)}, f32[768]{0:T(1024)}, f32[768]{0:T(1024)}, f32[768]{0:T(1024)}, /*index=5*/f32[768]{0:T(1024)}, f32[768]{0:T(1024)}, f32[768]{0:T(1024)}, f32[768]{0:T(1024)}) all-reduce(f32[]{:T(128)} %get-tuple-element.182, ...), channel_id=1, replica_groups=mesh['dp'=8,'tensor'=4] {'dp'}, use_global_device_ids=true, to_apply=%region_15.16 | all-reduce | flops 5761 | bytes 46088 | tf_op jit(solution)/shard_map/psum | solution.py:114
  786.6 75.0 %all-reduce.16.cloned.1.call-done = bf16[2048,768]{1,0:T(8,128)(2,1)} async-done(((bf16[2048,768]{1,0:T(8,128)(2,1)}), bf16[2048,768]{1,0:T(8,128)(2,1)}) %all-reduce.16.cloned.1.call-update) | async-done | bytes 3145744 | tf_op jit(solution)/shard_map/psum | solution.py:190
  861.6 7.1 convert_add_fusion
  868.7 143.7 %all-reduce.18.cloned.1.call-done = (f32[3,768,192]{1,2,0:T(8,128)}, f32[192,768]{1,0:T(8,128)}, f32[768,768]{1,0:T(8,128)}, f32[768,768]{1,0:T(8,128)}, f32[3,512,512]{1,2,0:T(8,128)}) async-done(((f32[3,768,192]{1,2,0:T(8,128)}, f32[192,768]{1,0:T(8,128)}, f32[768,768]{1,0:T(8,128)}, f32[768,768]{1,0:T(8,128)}, f32[3,512,512]{1,2,0:T(8,128)}), (f32[3,768,192]{1,2,0:T(8,128)}, f32[192,768]{1,0:T(8,128)}, ...) | async-done | bytes 10223632 | tf_op jit(solution)/shard_map/psum | solution.py:194
  1012.4 3.7 copy.66
  (408 shorter events, 112.9 us)
Async XLA Ops:
  7.2 267.7 %copy-start = (bf16[768,768]{1,0:T(8,128)(2,1)S(1)}, bf16[768,768]{1,0:T(8,128)(2,1)}, u32[]{:S(2)}) copy-start(bf16[768,768]{1,0:T(8,128)(2,1)} %param.46) | copy-start | bytes 3538948
  7.2 261.2 %all-reduce.10.cloned.1.call-start = ((), (), s32[]{:S(2)}) async-start(), calls=%async_computation | async-start | bytes 6291456 | tf_op jit(solution)/shard_map/psum | solution.py:101
  19.4 106.7 %copy-start.19 = (bf16[1,2048,192]{1,2,0:T(8,128)(2,1)}, bf16[1,2048,192]{1,2,0:T(8,128)(2,1)S(1)}, u32[]{:S(2)}) copy-start(bf16[1,2048,192]{1,2,0:T(8,128)(2,1)S(1)} %slice.312) | copy-start | bytes 2359300
  26.7 108.1 %copy-start.73 = (f32[3,64]{1,0:T(4,128)}, f32[3,64]{1,0:T(4,128)S(1)}, u32[]{:S(2)}) copy-start(f32[3,64]{1,0:T(4,128)S(1)} %add.308) | copy-start | bytes 2308
  140.8 127.7 %copy-start.61 = (f32[768]{0:T(1024)S(1)}, f32[768]{0:T(1024)}, u32[]{:S(2)}) copy-start(f32[768]{0:T(1024)} %param.43) | copy-start | bytes 9220
  144.5 130.4 %copy-start.75 = (f32[768]{0:T(1024)S(1)}, f32[768]{0:T(1024)}, u32[]{:S(2)}) copy-start(f32[768]{0:T(1024)} %param.44) | copy-start | bytes 9220
  144.5 130.4 %copy-start.107 = (f32[768]{0:T(1024)S(1)}, f32[768]{0:T(1024)}, u32[]{:S(2)}) copy-start(f32[768]{0:T(1024)} %param.45) | copy-start | bytes 9220
  144.5 130.4 %copy-start.118 = (f32[768]{0:T(1024)S(1)}, f32[768]{0:T(1024)}, u32[]{:S(2)}) copy-start(f32[768]{0:T(1024)} %param.47) | copy-start | bytes 9220
  144.5 275.0 %all-reduce.12.cloned.1.call-start = ((), (), s32[]{:S(2)}) async-start(), calls=%async_computation.1 | async-start | bytes 6291456 | tf_op jit(solution)/shard_map/psum | solution.py:108
  274.9 309.0 %copy-start.54 = (f32[2048]{0:T(1024)}, f32[2048]{0:T(1024)S(1)}, u32[]{:S(2)}) copy-start(f32[2048]{0:T(1024)S(1)} %fusion.112) | copy-start | bytes 24580
  274.9 20.4 %copy-start.115 = (bf16[768,768]{1,0:T(8,128)(2,1)S(1)}, bf16[768,768]{1,0:T(8,128)(2,1)}, u32[]{:S(2)}) copy-start(bf16[768,768]{1,0:T(8,128)(2,1)} %param.48) | copy-start | bytes 3538948
  295.3 124.2 %copy-start.105 = (f32[768]{0:T(1024)S(1)}, f32[768]{0:T(1024)}, u32[]{:S(2)}) copy-start(f32[768]{0:T(1024)} %param.49) | copy-start | bytes 9220
  299.3 274.5 %all-reduce.14.cloned.1.call-start = ((), (), s32[]{:S(2)}) async-start(), calls=%async_computation.2 | async-start | bytes 6291456 | tf_op jit(solution)/shard_map/psum | solution.py:127
  437.3 10.6 %copy-start.6 = (f32[2048,768]{1,0:T(8,128)}, f32[2048,768]{1,0:T(8,128)S(1)}, u32[]{:S(2)}) copy-start(f32[2048,768]{1,0:T(8,128)S(1)} %get-tuple-element.208) | copy-start | bytes 18874372
  438.5 9.4 copy-start.30
  453.6 408.0 %all-reduce.16.cloned.1.call-start = ((), (), s32[]{:S(2)}) async-start(), calls=%async_computation.3 | async-start | bytes 6291456 | tf_op jit(solution)/shard_map/psum | solution.py:190
  453.7 142.7 %copy-start.59 = (f32[3,512]{1,0:T(4,128)}, f32[3,512]{1,0:T(4,128)S(1)}, u32[]{:S(2)}) copy-start(f32[3,512]{1,0:T(4,128)S(1)} %log_add_fusion.3) | copy-start | bytes 18436
  454.4 147.1 %copy-start.57 = (f32[3,512]{1,0:T(4,128)}, f32[3,512]{1,0:T(4,128)S(1)}, u32[]{:S(2)}) copy-start(f32[3,512]{1,0:T(4,128)S(1)} %log_add_fusion.2) | copy-start | bytes 18436
  573.8 10.1 copy-start.8
  573.8 10.1 copy-start.11
  573.8 10.1 copy-start.23
  591.6 7.9 copy-start.21
  591.6 7.9 slice-start.12
  604.6 10.9 %copy-start.32 = (bf16[1536,192]{0,1:T(8,128)(2,1)S(1)}, bf16[1536,192]{0,1:T(8,128)(2,1)}, u32[]{:S(2)}) copy-start(bf16[1536,192]{0,1:T(8,128)(2,1)} %slice.289) | copy-start | bytes 1769476
  604.6 10.9 %copy-start.56 = (f32[3,512]{1,0:T(4,128)S(1)}, f32[3,512]{1,0:T(4,128)}, u32[]{:S(2)}) copy-start(f32[3,512]{1,0:T(4,128)} %log_add_fusion.1) | copy-start | bytes 18436
  627.5 7.4 copy-start.74
  634.9 10.8 %slice-start = ((s8[12582912]{0:T(1024)(128)(4,1)}), s8[4194304]{0:T(1024)(128)(4,1)S(1)}, s32[]{:S(2)}) async-start(s8[12582912]{0:T(1024)(128)(4,1)} %bitcast.160), calls=%async_computation.5 | async-start | bytes 8388608
  634.9 10.8 %slice-start.1 = ((s8[12582912]{0:T(1024)(128)(4,1)}), s8[4194304]{0:T(1024)(128)(4,1)S(1)}, s32[]{:S(2)}) async-start(s8[12582912]{0:T(1024)(128)(4,1)} %bitcast.160), calls=%async_computation.6 | async-start | bytes 8388608
  634.9 12.6 %slice-start.2 = ((s8[12582912]{0:T(1024)(128)(4,1)}), s8[4194304]{0:T(1024)(128)(4,1)S(1)}, s32[]{:S(2)}) async-start(s8[12582912]{0:T(1024)(128)(4,1)} %bitcast.160), calls=%async_computation.7 | async-start | bytes 8388608
  647.6 9.0 copy-start.20
  713.5 12.3 %slice-start.14 = ((s8[6291456]{0:T(1024)(128)(4,1)}), s8[4194304]{0:T(1024)(128)(4,1)S(1)}, s32[]{:S(2)}) async-start(s8[6291456]{0:T(1024)(128)(4,1)} %bitcast.170), calls=%async_computation.19 | async-start | bytes 8388608
  713.5 11.1 %copy-start.42 = (bf16[1,512,192]{1,2,0:T(8,128)(2,1)S(1)}, bf16[1,512,192]{1,2,0:T(8,128)(2,1)}, u32[]{:S(2)}) copy-start(bf16[1,512,192]{1,2,0:T(8,128)(2,1)} %slice.285) | copy-start | bytes 589828
  713.5 11.5 %copy-start.41 = (bf16[512,192]{0,1:T(8,128)(2,1)S(1)}, bf16[512,192]{0,1:T(8,128)(2,1)}, u32[]{:S(2)}) copy-start(bf16[512,192]{0,1:T(8,128)(2,1)} %get-tuple-element.221) | copy-start | bytes 589828
  713.5 12.1 %copy-start.45 = (f32[512,3,64]{0,2,1:T(8,128)S(1)}, f32[512,3,64]{0,2,1:T(8,128)}, u32[]{:S(2)}) copy-start(f32[512,3,64]{0,2,1:T(8,128)} %fusion.85) | copy-start | bytes 1179652
  713.5 12.3 %slice-start.15 = ((s8[6291456]{0:T(1024)(128)(4,1)}), s8[2097152]{0:T(1024)(128)(4,1)S(1)}, s32[]{:S(2)}) async-start(s8[6291456]{0:T(1024)(128)(4,1)} %bitcast.170), calls=%async_computation.20 | async-start | bytes 4194304
  713.5 12.3 %copy-start.58 = (f32[3,512]{1,0:T(4,128)S(1)}, f32[3,512]{1,0:T(4,128)}, u32[]{:S(2)}) copy-start(f32[3,512]{1,0:T(4,128)} %copy-done.57) | copy-start | bytes 18436
  713.5 13.6 %slice-start.9 = ((s8[9437184]{0:T(1024)(128)(4,1)}), s8[4194304]{0:T(1024)(128)(4,1)S(1)}, s32[]{:S(2)}) async-start(s8[9437184]{0:T(1024)(128)(4,1)} %bitcast.166), calls=%async_computation.14 | async-start | bytes 8388608
  713.5 13.6 %slice-start.10 = ((s8[9437184]{0:T(1024)(128)(4,1)}), s8[4194304]{0:T(1024)(128)(4,1)S(1)}, s32[]{:S(2)}) async-start(s8[9437184]{0:T(1024)(128)(4,1)} %bitcast.166), calls=%async_computation.15 | async-start | bytes 8388608
  741.4 7.4 copy-start.55
  741.4 7.4 copy-start.62
  741.4 7.4 copy-start.76
  741.4 7.4 copy-start.108
  741.4 271.0 %all-reduce.18.cloned.1.call-start = ((), (), s32[]{:S(2)}) async-start(), calls=%async_computation.4 | async-start | bytes 20447232 | tf_op jit(solution)/shard_map/psum | solution.py:194
  741.7 7.1 copy-start.9
  741.8 7.1 copy-start.12
  758.6 103.0 %copy-start.64 = (f32[2048]{0:T(1024)S(1)}, f32[2048]{0:T(1024)}, u32[]{:S(2)}) copy-start(f32[2048]{0:T(1024)} %copy-done.63) | copy-start | bytes 24580
  1012.4 8.6 copy-start.34
  1016.1 7.7 copy-start.1
  (106 other events, 357.0 us)
Sparse Core Ops, SparseCore 0:
  144.6 123.7 all-reduce.9
  299.4 120.0 all-reduce.11
  453.7 120.0 all-reduce.13
  741.5 120.0 all-reduce.15
  867.0 145.3 all-reduce.17
where the time goes:
time: 1040 us; the launch traced here: 1030 us
  waiting for transfers between devices  566 us (54%)
  local copies, waits for them, and re-layouts  153 us (15%)
  other arithmetic  127 us (12%)
  matrix products  126 us (12%)
  blocking collectives  40.6 us (4%)
  between operations  19.2 us (2%)
    psum x1, waiting for transfers between devices, body(): lax.psum((grad_w_qkv, grad_b_qv, grad_w_attn_out, grad_b_attn_out, grad_g...  144 us
    psum x1, waiting for transfers between devices, body(): lax.psum(attn_part.astype(jnp.bfloat16), 'tensor').astype(jnp.float32)  124 us
    psum x1, waiting for transfers between devices, body(): lax.psum(back_first.astype(jnp.bfloat16), 'tensor').astype(jnp.float32)  119 us
    psum x1, waiting for transfers between devices, body(): lax.psum(ffn_part.astype(jnp.bfloat16), 'tensor').astype(jnp.float32)  104 us
    psum x1, waiting for transfers between devices, body(): lax.psum(back_hidden.astype(jnp.bfloat16), 'tensor').astype(jnp.float32)  75 us
    another operation x6, local copies, waits for them, and re-layouts, block_scores(): scores = scores + jnp.tile(gate_natural_log, (1, 1, block_index + 1))  56 us
    unnamed x305, local copies, waits for them, and re-layouts  45.1 us
    psum x2, blocking collectives, body(): total_valid, total_error = lax.psum((local_count, local_error), 'dp')  40.6 us
  transfers between devices with their start and end apart: 5, of which 5 were waited for; matrix products, arithmetic and copies ran while one was open for 2% of the time, Pallas kernels for 0%

commit v1 on v0

v1 whole, which is shorter than its diff:
```python
import functools
import math

import jax
import jax.numpy as jnp
from jax import lax
from jax.experimental import pallas as pl
from jax.experimental.pallas import tpu as pltpu
from jax.sharding import PartitionSpec as P

BLOCK = 256
LOG2E = math.log2(math.e)
SOFTENING = 0.5
EPS = 1e-6
F32 = jnp.float32
BF16 = jnp.bfloat16


def dot(a, b):
    return jnp.dot(a, b, preferred_element_type=F32)


def dot_nt(a, b):
    return lax.dot_general(a, b, (((1,), (1,)), ((), ())), preferred_element_type=F32)


def dot_tn(a, b):
    return lax.dot_general(a, b, (((0,), (0,)), ((), ())), preferred_element_type=F32)


def dot_tt(a, b):
    return lax.dot_general(a, b, (((0,), (1,)), ((), ())), preferred_element_type=F32)


def attn_fwd_kernel(hid, w, b, bt, table, noise, ctx, ctxt, q3, k3, v3, qt, kt, lse, lmt, vt):
    heads, period = table.shape[0], table.shape[1]
    tokens = hid.shape[0]
    hd = q3.shape[2]
    width = heads * hd
    coef = LOG2E / math.sqrt(hd)
    parts = period // BLOCK
    for h in range(heads):
        x = (table[h] + noise[h]) * (1.0 / SOFTENING)
        ls = jnp.minimum(x, 0.0) - jnp.log1p(jnp.exp(-jnp.abs(x)))
        lmt[h] = jnp.transpose(ls * LOG2E)

    step = 2 * BLOCK

    def project(i, _):
        rows = pl.ds(pl.multiple_of(i * step, step), step)
        x = hid[rows, :]
        for n, (nat, tr) in enumerate(((q3, qt), (k3, kt), (v3, vt))):
            y = dot(x, w[n])
            yt = dot_tt(w[n], x)
            if n != 1:
                y = y + b[n // 2 : n // 2 + 1, :]
                yt = yt + bt[:, n // 2 : n // 2 + 1]
            y = y.astype(BF16)
            for h in range(heads):
                nat[h, rows, :] = y[:, h * hd : (h + 1) * hd]
            tr[:, rows] = yt.astype(BF16)
        return 0

    lax.fori_loop(0, tokens // step, project, 0)
    lse[...] = jnp.zeros(lse.shape, F32)

    def per_q(qb, _):
        qcol = pl.ds(pl.multiple_of(qb * BLOCK, BLOCK), BLOCK)
        mcol = pl.ds(pl.multiple_of(lax.rem(qb, parts) * BLOCK, BLOCK), BLOCK)

        def per_k(kb, carry):
            krow = pl.ds(pl.multiple_of(kb * BLOCK, BLOCK), BLOCK)
            mrow = pl.ds(pl.multiple_of(lax.rem(kb, parts) * BLOCK, BLOCK), BLOCK)
            out = []
            ss = [dot(k3[h, krow, :], qt[h * hd : (h + 1) * hd, qcol]) for h in range(heads)]
            for h in range(heads):
                m, l, acc = carry[h]
                s = ss[h] * coef + lmt[h, mrow, mcol]
                mn = jnp.maximum(m, jnp.max(s, axis=0, keepdims=True))
                al = jnp.exp2(m - mn)
                p = jnp.exp2(s - mn)
                l = l * al + jnp.sum(p, axis=0, keepdims=True)
                acc = acc * al + dot(vt[h * hd : (h + 1) * hd, krow], p.astype(BF16))
                out.append((mn, l, acc))
            return tuple(out)

        init = tuple(
            (
                jnp.full((1, BLOCK), -1e30, F32),
                jnp.zeros((1, BLOCK), F32),
                jnp.zeros((hd, BLOCK), F32),
            )
            for _ in range(heads)
        )
        res = lax.fori_loop(0, qb + 1, per_k, init)
        cols = []
        for h in range(heads):
            m, l, acc = res[h]
            c = acc / l
            ctxt[h * hd : (h + 1) * hd, qcol] = c
            lse[h : h + 1, qcol] = m + jnp.log2(l)
            cols.append(c)
        pad = -width % 128
        if pad:
            cols.append(jnp.zeros((pad, BLOCK), F32))
        full = jnp.transpose(jnp.concatenate(cols, axis=0))
        ctx[qcol, :] = full[:, :width].astype(BF16)
        return 0

    lax.fori_loop(0, tokens // BLOCK, per_q, 0)


def attn_fwd(hidden, w_qkv, b_qv, table, noise):
    tokens = hidden.shape[0]
    heads, period = table.shape[0], table.shape[1]
    width = w_qkv.shape[2]
    hd = width // heads
    sd = jax.ShapeDtypeStruct
    nat = sd((heads, tokens, hd), BF16)
    tr = sd((width, tokens), BF16)
    return pl.pallas_call(
        attn_fwd_kernel,
        out_shape=(
            sd((tokens, width), BF16),
            sd((width, tokens), F32),
            nat, nat, nat, tr, tr,
            sd((8, tokens), F32),
            sd(table.shape, F32),
        ),
        scratch_shapes=[pltpu.VMEM((width, tokens), BF16)],
        compiler_params=pltpu.CompilerParams(vmem_limit_bytes=56 << 20),
        name="attn_fwd",
    )(hidden, w_qkv, b_qv, b_qv.T, table, noise)


def attn_bwd_kernel(gctx, ctxt, q3, k3, v3, qt, kt, lse, lmt, gqkv, glm, gk, gv, g3, glmt):
    heads, tokens, hd = q3.shape
    period = lmt.shape[1]
    width = heads * hd
    coef = LOG2E / math.sqrt(hd)
    scale = 1.0 / math.sqrt(hd)
    parts = period // BLOCK
    pad = -width % 128
    gk[...] = jnp.zeros(gk.shape, F32)
    gv[...] = jnp.zeros(gv.shape, F32)
    glmt[...] = jnp.zeros(glmt.shape, F32)

    def per_q(i, _):
        qb = tokens // BLOCK - 1 - i
        qcol = pl.ds(pl.multiple_of(qb * BLOCK, BLOCK), BLOCK)
        mcol = pl.ds(pl.multiple_of(lax.rem(qb, parts) * BLOCK, BLOCK), BLOCK)
        g = gctx[qcol, :].astype(F32)
        gpad = jnp.concatenate([g, jnp.zeros((BLOCK, pad), F32)], axis=1) if pad else g
        gt = jnp.transpose(gpad)
        delta, gtb = [], []
        for h in range(heads):
            gth = gt[h * hd : (h + 1) * hd, :]
            delta.append(jnp.sum(gth * ctxt[h * hd : (h + 1) * hd, qcol], axis=0, keepdims=True))
            gtb.append(gth.astype(BF16))
            g3[h] = gctx[qcol, h * hd : (h + 1) * hd]

        def per_k(kb, carry):
            krow = pl.ds(pl.multiple_of(kb * BLOCK, BLOCK), BLOCK)
            mrow = pl.ds(pl.multiple_of(lax.rem(kb, parts) * BLOCK, BLOCK), BLOCK)
            out = []
            for h in range(heads):
                hs = slice(h * hd, (h + 1) * hd)
                s = dot(k3[h, krow, :], qt[hs, qcol]) * coef + lmt[h, mrow, mcol]
                p = jnp.exp2(s - lse[h : h + 1, qcol])
                dp = dot(v3[h, krow, :], gtb[h])
                ds = p * (dp - delta[h])
                dsb = ds.astype(BF16)
                glmt[h, mrow, mcol] += ds
                gv[h, krow, :] += dot(p.astype(BF16), g3[h])
                gk[h, krow, :] += dot(dsb, q3[h, qcol, :])
                out.append(carry[h] + dot(kt[hs, krow], dsb))
            return tuple(out)

        init = tuple(jnp.zeros((hd, BLOCK), F32) for _ in range(heads))
        res = lax.fori_loop(0, qb + 1, per_k, init)
        rows = [r * scale for r in res]
        if pad:
            rows.append(jnp.zeros((pad, BLOCK), F32))
        gq = jnp.transpose(jnp.concatenate(rows, axis=0))[:, :width]
        gkb = jnp.concatenate([gk[h, qcol, :] for h in range(heads)], axis=1) * scale
        gvb = jnp.concatenate([gv[h, qcol, :] for h in range(heads)], axis=1)
        gqkv[0, qcol, :] = gq.astype(BF16)
        gqkv[1, qcol, :] = gkb.astype(BF16)
        gqkv[2, qcol, :] = gvb.astype(BF16)
        return 0

    lax.fori_loop(0, tokens // BLOCK, per_q, 0)
    for h in range(heads):
        glm[h] = jnp.transpose(glmt[h])


def attn_bwd(gctx, ctxt, q3, k3, v3, qt, kt, lse, lmt):
    heads, tokens, hd = q3.shape
    width = heads * hd
    sd = jax.ShapeDtypeStruct
    return pl.pallas_call(
        attn_bwd_kernel,
        out_shape=(sd((3, tokens, width), BF16), sd(lmt.shape, F32)),
        scratch_shapes=[
            pltpu.VMEM((heads, tokens, hd), F32),
            pltpu.VMEM((heads, tokens, hd), F32),
            pltpu.VMEM((heads, BLOCK, hd), BF16),
            pltpu.VMEM(lmt.shape, F32),
        ],
        compiler_params=pltpu.CompilerParams(vmem_limit_bytes=56 << 20),
        name="attn_bwd",
    )(gctx, ctxt, q3, k3, v3, qt, kt, lse, lmt)


def shift(x, axis, size, amount):
    return lax.ppermute(x, axis, [(j, (j + amount) % size) for j in range(size)])


def swap(x, axis, size, bit):
    return lax.ppermute(x, axis, [(j, j ^ bit) for j in range(size)])


def small_sum(x, axis, size):
    bit = 1
    while bit < size:
        x = x + swap(x, axis, size, bit)
        bit *= 2
    return x


def rows_of(x, start, count):
    return lax.dynamic_slice_in_dim(x, start, count, axis=0)


def norm_parts(resid):
    centred = resid - jnp.mean(resid, axis=-1, keepdims=True)
    rstd = lax.rsqrt(jnp.mean(centred * centred, axis=-1, keepdims=True) + EPS)
    return centred * rstd, rstd


def norm_back(grad, xhat, rstd, gain):
    gy = grad * gain
    return rstd * (
        gy
        - jnp.mean(gy, axis=-1, keepdims=True)
        - xhat * jnp.mean(gy * xhat, axis=-1, keepdims=True)
    )


def bit_orders(size):
    bits = []
    bit = 2
    while bit < size:
        bits.append(bit)
        bit *= 2
    return bits, bits[::-1]


def gather_dp(x, size, dp_bits, index):
    for bit in dp_bits:
        other = swap(x, "dp", size, bit)
        x = (x, other)
        x = jnp.stack(x)
    return x


def body(
    hidden, teacher, valid, w_qkv, b_qv, w_attn_out, b_attn_out, gain_one, bias_one,
    w_up, b_up, w_down, b_down, gain_two, bias_two, table, noise, *, n_d, n_t,
):
    tokens, width = hidden.shape
    units = w_up.shape[1]
    local = w_qkv.shape[2]
    chunk = tokens // n_t
    ti = lax.axis_index("tensor")
    di = lax.axis_index("dp")
    slab = units // n_d
    low_bits, high_bits = bit_orders(n_d)
    valid_f = valid[0].astype(F32)
    total_valid = small_sum(jnp.sum(valid_f).reshape(1, 1), "dp", n_d)[0, 0]

    def own_slabs(w):
        return [rows_of(w, (di ^ r) * slab, slab) for r in range(n_d)]

    def gather_weight(w, bits):
        mine = rows_of(w, di * slab, slab)
        blocks = [own_slabs(w)]
        for s in range(1, n_t):
            held = {0: shift(mine, "tensor", n_t, s)}
            for bit in bits + [1]:
                keys = sorted(held)
                sent = jnp.concatenate([held[r] for r in keys], axis=0)
                got = swap(sent, "dp", n_d, bit)
                for n, r in enumerate(keys):
                    held[r | bit] = got[n * slab : (n + 1) * slab]
            blocks.append([held[r] for r in range(n_d)])
        return jnp.stack([jnp.concatenate([b[r] for b in blocks for r in range(half, n_d, 2)]) for half in (0, 1)])

    up_t = gather_weight(w_up.T, low_bits)
    down = gather_weight(w_down, high_bits)
    out_w = [w_attn_out] + [shift(w_attn_out, "tensor", n_t, s) for s in range(1, n_t)]
    order = jnp.stack([di ^ r for r in range(n_d)])
    b_all = [b_up] + [shift(b_up, "tensor", n_t, s) for s in range(1, n_t)]
    b_all = jnp.stack(b_all).reshape(n_t, n_d, slab)[:, order]
    b_half = [b_all[:, half::2].reshape(-1) for half in (0, 1)]

    ctx, ctxt, q3, k3, v3, qt, kt, lse, lmt = attn_fwd(hidden, w_qkv, b_qv, table, noise)

    ctx_parts = [rows_of(ctx, ti * chunk, chunk)] + [
        shift(rows_of(ctx, lax.rem(ti + s, n_t) * chunk, chunk), "tensor", n_t, s)
        for s in range(1, n_t)
    ]
    ctx_rel = jnp.concatenate(ctx_parts, axis=1)
    wo_rel = jnp.concatenate(out_w, axis=0)
    hid_own = rows_of(hidden, ti * chunk, chunk).astype(F32)
    teach_own = rows_of(teacher, ti * chunk, chunk)
    valid_own = lax.dynamic_slice_in_dim(valid_f, ti * chunk, chunk)[:, None]

    attention = dot(ctx_rel, wo_rel) + b_attn_out
    xhat1, rstd1 = norm_parts(hid_own + attention)
    first = xhat1 * gain_one + bias_one
    first_low = first.astype(BF16)
    acts, slopes = [], []
    for half in (0, 1):
        before = dot_nt(first_low, up_t[half]) + b_half[half]
        phi = 0.5 * (1.0 + lax.erf(before * math.sqrt(0.5)))
        dens = jnp.exp(-0.5 * before * before) * (1.0 / math.sqrt(2.0 * math.pi))
        a, d = lax.optimization_barrier(
            ((before * phi).astype(BF16), (phi + before * dens).astype(BF16))
        )
        acts.append(a)
        slopes.append(d)
    feed = dot(acts[0], down[0]) + dot(acts[1], down[1]) + b_down
    xhat2, rstd2 = norm_parts(first + feed)
    out_own = xhat2 * gain_two + bias_two
    residue = out_own - teach_own
    error = jnp.sum(valid_own * residue * residue)
    grad_out = (2.0 * tokens / total_valid) * valid_own * residue
    g_gain_two = jnp.sum(grad_out * xhat2, axis=0)
    g_bias_two = jnp.sum(grad_out, axis=0)
    grad_second = norm_back(grad_out, xhat2, rstd2, gain_two)
    grad_ffn = grad_second.astype(BF16)
    g_b_down = jnp.sum(grad_ffn.astype(F32), axis=0)
    out_low = out_own.astype(BF16)
    out_parts = [out_low] + [shift(out_low, "tensor", n_t, s) for s in range(1, n_t)]

    gb = [(dot_nt(grad_ffn, down[half]) * slopes[half].astype(F32)).astype(BF16) for half in (0, 1)]
    g_b_up = [jnp.sum(g.astype(F32), axis=0) for g in gb]
    grad_first = grad_second + dot(gb[0], up_t[0]) + dot(gb[1], up_t[1])
    g_gain_one = jnp.sum(grad_first * xhat1, axis=0)
    g_bias_one = jnp.sum(grad_first, axis=0)
    grad_resid = norm_back(grad_first, xhat1, rstd1, gain_one)
    grad_attn = grad_resid.astype(BF16)
    g_b_ao = jnp.sum(grad_attn.astype(F32), axis=0)
    gctx_rel = dot_nt(grad_attn, wo_rel).astype(BF16)
    gctx = jnp.zeros((tokens, local), BF16)
    gctx = lax.dynamic_update_slice(gctx, gctx_rel[:, :local], (ti * chunk, 0))
    for s in range(1, n_t):
        got = shift(gctx_rel[:, s * local : (s + 1) * local], "tensor", n_t, -s)
        gctx = lax.dynamic_update_slice(gctx, got, (lax.rem(ti + s, n_t) * chunk, 0))

    def reduce_weight(lhs, rhs, bits):
        sent = dot_tn(lhs[1], rhs).astype(BF16)
        got = swap(sent, "dp", n_d, 1)
        g = (dot_tn(lhs[0], rhs) + got.astype(F32)).astype(BF16)
        g = g.reshape((n_t,) + (2,) * len(low_bits) + (slab, width))
        axes = list(low_bits)[::-1]
        for bit in bits:
            ax = 1 + axes.index(bit)
            axes.remove(bit)
            keep = lax.index_in_dim(g, 0, ax, keepdims=False)
            send = lax.index_in_dim(g, 1, ax, keepdims=False)
            got = swap(send, "dp", n_d, bit)
            g = (keep.astype(F32) + got.astype(F32)).astype(BF16)
        total = g[0].astype(F32)
        for s in range(1, n_t):
            total = total + shift(g[s], "tensor", n_t, -s).astype(F32)
        return gather_absolute(total.astype(BF16), bits)

    def gather_absolute(x, bits):
        held = {0: x}
        for bit in bits + [1]:
            keys = sorted(held)
            got = swap(jnp.concatenate([held[r] for r in keys], axis=0), "dp", n_d, bit)
            n = x.shape[0]
            for m, r in enumerate(keys):
                held[r | bit] = got[m * n : (m + 1) * n]
        stack = jnp.stack([held[r] for r in range(n_d)])
        return jnp.concatenate([lax.dynamic_index_in_dim(stack, di ^ a, 0, keepdims=False) for a in range(n_d)], axis=0).astype(F32)

    g_down = reduce_weight(acts, grad_ffn, high_bits)
    g_up = reduce_weight(gb, first_low, low_bits).T

    g_ao_rel = dot_tn(ctx_rel, grad_attn).astype(BF16).reshape(n_t, local, width)

    def halve(x, bits):
        for bit in bits:
            half = x.shape[0] // 2
            up = (di // bit) % 2
            send = rows_of(x, (1 - up) * half, half)
            keep = rows_of(x, up * half, half)
            x = (keep.astype(F32) + swap(send, "dp", n_d, bit).astype(F32)).astype(BF16)
        return x

    def unhalve(x, bits):
        for bit in bits[::-1]:
            up = (di // bit) % 2
            other = swap(x, "dp", n_d, bit)
            pair = jnp.stack([x, other])
            x = jnp.concatenate([lax.dynamic_index_in_dim(pair, up, 0, keepdims=False), lax.dynamic_index_in_dim(pair, 1 - up, 0, keepdims=False)], axis=0)
        return x

    bits = [1] + low_bits
    g_ao = g_ao_rel.reshape(n_t, n_d, local // n_d, width).transpose(1, 0, 2, 3).reshape(n_d, -1, width)
    g_ao = halve(g_ao, bits)[0].reshape(n_t, local // n_d, width)
    total = g_ao[0].astype(F32)
    for s in range(1, n_t):
        total = total + shift(g_ao[s], "tensor", n_t, -s).astype(F32)
    g_ao = unhalve(total.astype(BF16)[None], bits).reshape(local, width).astype(F32)

    gbu = jnp.stack(g_b_up).reshape(2, n_t, n_d // 2, slab).transpose(1, 2, 0, 3).reshape(n_t, n_d, slab)
    gbu = gbu[:, order].reshape(n_t, units)
    gbu = gbu[jnp.stack([lax.rem(ti - z + n_t, n_t) for z in range(n_t)])]
    pack = jnp.concatenate(
        [
            jnp.stack([g_b_ao, g_gain_one, g_bias_one, g_b_down, g_gain_two, g_bias_two]).reshape(-1),
            gbu.reshape(-1),
            jnp.full((width,), error),
        ]
    ).reshape(-1, 128)
    pack = small_sum(small_sum(pack, "dp", n_d), "tensor", n_t).reshape(-1)
    vecs = [pack[n * width : (n + 1) * width] for n in range(6)]
    gbu = lax.dynamic_slice_in_dim(pack, 6 * width + ti * units, units)
    loss = pack[6 * width + n_t * units] / (total_valid * width)

    gqkv, glm = attn_bwd(gctx, ctxt, q3, k3, v3, qt, kt, lse, lmt)
    back = jnp.einsum("kte,kde->td", gqkv, w_qkv, preferred_element_type=F32).astype(BF16)
    mine = grad_resid + rows_of(back, ti * chunk, chunk).astype(F32)
    for s in range(1, n_t):
        mine = mine + shift(rows_of(back, lax.rem(ti + s, n_t) * chunk, chunk), "tensor", n_t, s).astype(F32)
    gh_low = mine.astype(BF16)
    gh_parts = [gh_low] + [shift(gh_low, "tensor", n_t, s) for s in range(1, n_t)]

    def whole(own, parts):
        out = jnp.zeros((tokens, width), F32)
        out = lax.dynamic_update_slice(out, own, (ti * chunk, 0))
        for s in range(1, n_t):
            out = lax.dynamic_update_slice(out, parts[s].astype(F32), (lax.rem(ti - s + n_t, n_t) * chunk, 0))
        return out

    grad_hidden = whole(mine, gh_parts)
    out_states = whole(out_own, out_parts)

    g_qkv_w = jnp.einsum("td,kte->kde", hidden, gqkv, preferred_element_type=F32).astype(BF16)
    slope = jax.nn.sigmoid((table + noise) * (-1.0 / SOFTENING)) * (1.0 / SOFTENING)
    g_mask = (glm * slope).astype(BF16)
    g_qkv_w = unhalve(halve(g_qkv_w.reshape(-1, local), [1] + low_bits), [1] + low_bits)
    g_mask = unhalve(halve(g_mask.reshape(-1, table.shape[2]), [1] + high_bits), [1] + high_bits)
    g_b_qv = small_sum(jnp.sum(gqkv[0::2].astype(F32), axis=1), "dp", n_d)
    return (
        out_states, loss, grad_hidden,
        g_qkv_w.reshape(w_qkv.shape).astype(F32), g_b_qv, g_ao, vecs[0], vecs[1], vecs[2],
        g_up, gbu, g_down, vecs[3], vecs[4], vecs[5],
        g_mask.reshape(table.shape).astype(F32),
    )


def solution(mesh):
    row, col = P("tensor", None), P(None, "tensor")
    heads = P("tensor", None, None)
    dp = P("dp", None)
    qkv = P(None, None, "tensor")
    sizes = dict(mesh.shape)
    return jax.shard_map(
        functools.partial(body, n_d=sizes["dp"], n_t=sizes["tensor"]),
        mesh=mesh,
        in_specs=(dp, dp, dp, qkv, col, row, P(), P(), P(), col, P("tensor"), row, P(), P(), P(), heads, heads),
        out_specs=(dp, P(), dp, qkv, col, row, P(), P(), P(), col, P("tensor"), row, P(), P(), P(), heads),
        check_vma=False,
    )
```

time: 1040 us -> 653 us (0.63)
  waiting for transfers between devices: 566 us -> 268 us
  starting transfers between devices: 0.46 us -> 136 us
  other arithmetic: 127 us -> 39.7 us
  matrix products: 126 us -> 45.1 us
  local copies, waits for them, and re-layouts: 153 us -> 73 us
  Pallas kernels: 0 us -> 76.8 us
  blocking collectives: 40.6 us -> 0 us
  between operations: 19.2 us -> 7.19 us
    psum x5 -> x0, waiting for transfers between devices: 566 us -> none  [the longest x1 144 us: body(): lax.psum((grad_w_qkv, grad_b_qv, grad_w_attn_out, grad_b_attn_out, grad_g...]
    ppermute x0 -> x95, waiting for transfers between devices: none -> 268 us  [the longest x59 147 us: swap(): return lax.ppermute(x, axis, [(j, j ^ bit) for j in range(size)])]
    ppermute x0 -> x95, starting transfers between devices: none -> 136 us  [the longest x36 82 us: shift(): lax.ppermute(x, axis, [(j, (j + amount) % size) for j in range(size)])]
    dot_general x36 -> x17, matrix products: 126 us -> 45.1 us  [the longest x5 15.6 us: dot_nt(): lax.dot_general(a, b, (((1,), (1,)), ((), ())), preferred_element_type=F32)]
    pallas_call x0 -> x2, Pallas kernels: none -> 76.8 us  [the longest x1 40.5 us: attn_bwd(): pl.pallas_call(attn_bwd_kernel, out_shape=(sd((3, tokens, width), BF16),...]
    reduce_sum x19 -> x7, other arithmetic: 80 us -> 8.83 us  [the longest x1 4.18 us: body(): g_gain_two = jnp.sum(grad_out * xhat2, axis=0)]
    another operation x6 -> x19, local copies, waits for them, and re-layouts: 56 us -> 4.97 us  [block_scores(): scores = scores + jnp.tile(gate_natural_log, (1, 1, block_index + 1))]
    psum x2 -> x0, blocking collectives: 40.6 us -> none  [body(): total_valid, total_error = lax.psum((local_count, local_error), 'dp')]
  transfers between devices with their start and end apart: 5 -> 95, of which waited for: 5 -> 42; matrix products, arithmetic and copies ran while one was open for 2% -> 18% of each run, Pallas kernels for 0% -> 12%
where the time goes in v1:
time: 653 us; the launch traced here: 646 us
  waiting for transfers between devices  268 us (41%)
  starting transfers between devices  136 us (21%)
  Pallas kernels  76.8 us (12%)
  local copies, waits for them, and re-layouts  73 us (11%)
  matrix products  45.1 us (7%)
  other arithmetic  39.7 us (6%)
  between operations  7.19 us (1%)
    ppermute x59, waiting for transfers between devices, swap(): return lax.ppermute(x, axis, [(j, j ^ bit) for j in range(size)])  147 us
    ppermute x36, waiting for transfers between devices, shift(): lax.ppermute(x, axis, [(j, (j + amount) % size) for j in range(size)])  121 us
    ppermute x36, starting transfers between devices, shift(): lax.ppermute(x, axis, [(j, (j + amount) % size) for j in range(size)])  82 us
    ppermute x59, starting transfers between devices, swap(): return lax.ppermute(x, axis, [(j, j ^ bit) for j in range(size)])  54.2 us
    pallas_call x1, Pallas kernels, attn_bwd(): pl.pallas_call(attn_bwd_kernel, out_shape=(sd((3, tokens, width), BF16),...  40.5 us
    pallas_call x1, Pallas kernels, attn_fwd(): pl.pallas_call(attn_fwd_kernel, out_shape=(sd((tokens, width), BF16), sd(...  36.3 us
    unnamed x173, local copies, waits for them, and re-layouts  31.8 us
    dot_general x5, matrix products, dot_nt(): lax.dot_general(a, b, (((1,), (1,)), ((), ())), preferred_element_type=F32)  15.6 us
  transfers between devices with their start and end apart: 95, of which 42 were waited for; matrix products, arithmetic and copies ran while one was open for 18% of the time, Pallas kernels for 12%

profile of v1, /device:TPU:0, one launch (start us, length us, event | category | flops | bytes accessed | tf_op | source)
XLA Modules:
  0.0 646.2 jit_solution(8259176066273819525)
XLA Ops:
  0.7 3.1 collective-permute-start.3
  21.8 36.3 %attn_fwd.1 = (bf16[2048,192]{1,0:T(8,128)(2,1)}, f32[192,2048]{1,0:T(8,128)}, bf16[3,2048,64]{2,1,0:T(8,128)(2,1)}, bf16[3,2048,64]{2,1,0:T(8,128)(2,1)}, bf16[...) custom-call(bf16[2048,768]{1,0:T(8,128)(2,1)} %hid.1, ...), custom_call_target="tpu_custom_call" | custom-call | tf_op jit(solution)/shard_map/attn_fwd/pallas_call | solution.py:121
  78.0 9.7 %collective-permute-done.18 = bf16[96,768]{1,0:T(8,128)(2,1)} collective-permute-done((bf16[96,768]{1,0:T(8,128)(2,1)S(1)}, bf16[96,768]{1,0:T(8,128)(2,1)}, u32[]{:S(2)}, u32[]{:S(2)}) %collective-permute-start.18) | collective-permute-done | bytes 147488 | tf_op jit(solution)/shard_map/ppermute | solution.py:216
  89.3 6.5 %collective-permute-start = (bf16[512,192]{1,0:T(8,128)(2,1)S(1)}, bf16[512,192]{1,0:T(8,128)(2,1)S(1)}, u32[]{:S(2)}, u32[]{:S(2)}) collective-permute-start(bf16[512,192]{1,0:T(8,128)(2,1)S(1)} %get-tuple-element.135), channel_id=1, source_target_pairs={{0,1},{1,2},{2,3},{3,0},{4,5},{5,6},{6,7},{7,4},{8,9},{9,10},{10,1... | collective-permute-start | bytes 589832 | tf_op jit(solution)/shard_map/ppermute | solution.py:216
  96.5 4.0 collective-permute-start.1
  104.1 5.0 collective-permute-done
  109.7 9.4 %collective-permute-done.1 = bf16[512,192]{1,0:T(8,128)(2,1)S(1)} collective-permute-done((bf16[512,192]{1,0:T(8,128)(2,1)S(1)}, bf16[512,192]{1,0:T(8,128)(2,1)S(1)}, u32[]{:S(2)}, u32[]{:S(2)}) %collective-permute-start.1) | collective-permute-done | bytes 196640 | tf_op jit(solution)/shard_map/ppermute | solution.py:216
  126.4 8.5 %collective-permute-done.21 = bf16[96,768]{1,0:T(8,128)(2,1)S(1)} collective-permute-done((bf16[96,768]{1,0:T(8,128)(2,1)S(1)}, bf16[96,768]{1,0:T(8,128)(2,1)S(1)}, u32[]{:S(2)}, u32[]{:S(2)}) %collective-permute-start.21) | collective-permute-done | bytes 147488 | tf_op jit(solution)/shard_map/ppermute | solution.py:216
  149.7 5.2 collective-permute-done.11
  155.2 8.0 %collective-permute-done.14 = bf16[192,768]{0,1:T(8,128)(2,1)S(1)} collective-permute-done((bf16[192,768]{0,1:T(8,128)(2,1)S(1)}, bf16[192,768]{0,1:T(8,128)(2,1)S(1)}, u32[]{:S(2)}, u32[]{:S(2)}) %collective-permute-start.14) | collective-permute-done | bytes 294944 | tf_op jit(solution)/shard_map/ppermute | solution.py:220
  163.3 6.3 collective-permute-done.8
  169.6 5.2 concatenate.154
  174.8 5.9 fusion.4
  202.2 5.1 concatenate.162
  207.3 4.2 fusion.9
  217.3 3.2 fusion.102
  223.0 4.2 multiply_reduce_fusion
  227.1 3.1 broadcast.147.clone
  234.9 3.2 convert_reduce_fusion.1
  247.6 4.8 convolution_convert_fusion.1
  252.4 4.0 collective-permute-start.33
  270.7 31.9 %collective-permute-done.42 = f32[66,128]{1,0:T(8,128)S(1)} collective-permute-done((f32[66,128]{1,0:T(8,128)S(1)}, f32[66,128]{1,0:T(8,128)S(1)}, u32[]{:S(2)}, u32[]{:S(2)}) %collective-permute-start.42) | collective-permute-done | bytes 33824 | tf_op jit(solution)/shard_map/ppermute | solution.py:220
  304.5 21.7 %collective-permute-done.43 = f32[66,128]{1,0:T(8,128)S(1)} collective-permute-done((f32[66,128]{1,0:T(8,128)S(1)}, f32[66,128]{1,0:T(8,128)S(1)}, u32[]{:S(2)}, u32[]{:S(2)}) %collective-permute-start.43) | collective-permute-done | bytes 33824 | tf_op jit(solution)/shard_map/ppermute | solution.py:220
  332.2 4.4 collective-permute-done.46
  338.3 40.5 %attn_bwd.1 = (bf16[3,2048,192]{2,1,0:T(8,128)(2,1)}, f32[3,512,512]{2,1,0:T(8,128)}) custom-call(bf16[2048,192]{1,0:T(8,128)(2,1)} %constant_dynamic-update-slice_fusion.21.gctx, f32[192,2048]{1,0:T(8,128)} %get-tuple-element.36.ctxt, bf16[3,2048,64]{2,1,0:T(8,128)(2,1)} %get-tuple-element.37.q3, bf16[3,2048,64]{2,1,0:T(8,128)(2,1)} %get-tuple-element.38.k3, ...), custom_call_target="tpu_custom_call" | custom-call | tf_op jit(solution)/shard_map/attn_bwd/pallas_call | solution.py:201
  378.8 4.2 fusion.21
  383.0 2.9 bitcast_convert_fusion
  406.5 29.8 %collective-permute-done.35 = bf16[512,768]{1,0:T(8,128)(2,1)S(1)} collective-permute-done((bf16[512,768]{1,0:T(8,128)(2,1)}, bf16[512,768]{1,0:T(8,128)(2,1)S(1)}, u32[]{:S(2)}, u32[]{:S(2)}) %collective-permute-start.35) | collective-permute-done | bytes 786464 | tf_op jit(solution)/shard_map/ppermute | solution.py:216
  438.5 4.1 collective-permute-done.54
  443.7 5.6 collective-permute-done.63
  451.0 3.4 collective-permute-done.55
  455.1 10.8 %collective-permute-done.48 = bf16[512,768]{1,0:T(8,128)(2,1)S(1)} collective-permute-done((bf16[512,768]{1,0:T(8,128)(2,1)S(1)}, bf16[512,768]{1,0:T(8,128)(2,1)S(1)}, u32[]{:S(2)}, u32[]{:S(2)}) %collective-permute-start.48) | collective-permute-done | bytes 786464 | tf_op jit(solution)/shard_map/ppermute | solution.py:216
  471.1 19.1 %collective-permute-start.65 = (bf16[24,768]{1,0:T(8,128)(2,1)S(1)}, bf16[24,768]{1,0:T(8,128)(2,1)S(1)}, u32[]{:S(2)}, u32[]{:S(2)}) collective-permute-start(bf16[24,768]{1,0:T(8,128)(2,1)S(1)} %get-tuple-element.177), channel_id=1, source_target_pairs={{0,3},{1,0},{2,1},{3,2},{4,7},{5,4},{6,5},{7,6},{8,11},{9,8},{10,9... | collective-permute-start | bytes 110600 | tf_op jit(solution)/shard_map/ppermute | solution.py:216
  500.4 5.8 collective-permute-done.68
  507.2 3.5 collective-permute-done.69
  511.5 5.4 collective-permute-done.57
  520.4 5.6 collective-permute-done.91
  529.8 3.5 collective-permute-done.92
  533.2 2.9 collective-permute-start.52
  543.9 20.0 %collective-permute-done.51 = bf16[512,768]{1,0:T(8,128)(2,1)S(1)} collective-permute-done((bf16[512,768]{1,0:T(8,128)(2,1)S(1)}, bf16[512,768]{1,0:T(8,128)(2,1)S(1)}, u32[]{:S(2)}, u32[]{:S(2)}) %collective-permute-start.51) | collective-permute-done | bytes 786464 | tf_op jit(solution)/shard_map/ppermute | solution.py:216
  564.3 6.5 %collective-permute-done.81 = bf16[4,2,96,768]{3,2,1,0:T(8,128)(2,1)S(1)} collective-permute-done((bf16[4,2,96,768]{3,2,1,0:T(8,128)(2,1)S(1)}, bf16[4,2,96,768]{3,2,1,0:T(8,128)(2,1)S(1)}, u32[]{:S(2)}, u32[]{:S(2)}) %collective-permute-start.81) | collective-permute-done | bytes 1179680 | tf_op jit(solution)/shard_map/ppermute | solution.py:220
  574.3 9.4 %collective-permute-done.82 = bf16[4,96,768]{2,1,0:T(8,128)(2,1)S(1)} collective-permute-done((bf16[4,96,768]{2,1,0:T(8,128)(2,1)S(1)}, bf16[4,96,768]{2,1,0:T(8,128)(2,1)S(1)}, u32[]{:S(2)}, u32[]{:S(2)}) %collective-permute-start.82) | collective-permute-done | bytes 589856 | tf_op jit(solution)/shard_map/ppermute | solution.py:220
  583.9 14.0 %collective-permute-start.83 = (bf16[96,768]{1,0:T(8,128)(2,1)S(1)}, bf16[96,768]{1,0:T(8,128)(2,1)S(1)}, u32[]{:S(2)}, u32[]{:S(2)}) collective-permute-start(bf16[96,768]{1,0:T(8,128)(2,1)S(1)} %get-tuple-element.146), channel_id=1, source_target_pairs={{0,3},{1,0},{2,1},{3,2},{4,7},{5,4},{6,5},{7,6},{8,11},{9,8},{10,9... | collective-permute-start | bytes 442376 | tf_op jit(solution)/shard_map/ppermute | solution.py:216
  598.8 3.3 collective-permute-done.83
  602.1 7.2 %collective-permute-done.84 = bf16[96,768]{1,0:T(8,128)(2,1)S(1)} collective-permute-done((bf16[96,768]{1,0:T(8,128)(2,1)S(1)}, bf16[96,768]{1,0:T(8,128)(2,1)S(1)}, u32[]{:S(2)}, u32[]{:S(2)}) %collective-permute-start.84) | collective-permute-done | bytes 147488 | tf_op jit(solution)/shard_map/ppermute | solution.py:216
  617.3 9.3 %collective-permute-done.75 = bf16[96,768]{1,0:T(8,128)(2,1)S(1)} collective-permute-done((bf16[96,768]{1,0:T(8,128)(2,1)S(1)}, bf16[96,768]{1,0:T(8,128)(2,1)S(1)}, u32[]{:S(2)}, u32[]{:S(2)}) %collective-permute-start.75) | collective-permute-done | bytes 147488 | tf_op jit(solution)/shard_map/ppermute | solution.py:216
  627.7 4.2 collective-permute-done.77
  635.2 3.5 collective-permute-done.78
  (510 shorter events, 211.5 us)
Async XLA Ops:
  0.7 88.6 %collective-permute-start.3 = (bf16[192,768]{1,0:T(8,128)(2,1)}, bf16[192,768]{1,0:T(8,128)(2,1)S(1)}, u32[]{:S(2)}, u32[]{:S(2)}) collective-permute-start(bf16[192,768]{1,0:T(8,128)(2,1)} %param.22), channel_id=1, source_target_pairs={{0,1},{1,2},{2,3},{3,0},{4,5},{5,6},{6,7},{7,4},{8,9},{9,10},{10,1... | collective-permute-start | bytes 884744 | tf_op jit(solution)/shard_map/ppermute | solution.py:216
  3.8 92.7 %collective-permute-start.4 = (bf16[192,768]{1,0:T(8,128)(2,1)}, bf16[192,768]{1,0:T(8,128)(2,1)S(1)}, u32[]{:S(2)}, u32[]{:S(2)}) collective-permute-start(bf16[192,768]{1,0:T(8,128)(2,1)} %param.22), channel_id=1, source_target_pairs={{0,2},{1,3},{2,0},{3,1},{4,6},{5,7},{6,4},{7,5},{8,10},{9,11},{10,... | collective-permute-start | bytes 884744 | tf_op jit(solution)/shard_map/ppermute | solution.py:216
  6.4 65.1 %collective-permute-start.15 = (f32[768]{0:T(1024)}, f32[768]{0:T(1024)S(1)}, u32[]{:S(2)}, u32[]{:S(2)}) collective-permute-start(f32[768]{0:T(1024)} %param.27), channel_id=1, source_target_pairs={{0,1},{1,2},{2,3},{3,0},{4,5},{5,6},{6,7},{7,4},{8,9},{9,10},{10,1... | collective-permute-start | bytes 9224 | tf_op jit(solution)/shard_map/ppermute | solution.py:216
  6.4 65.8 %collective-permute-start.16 = (f32[768]{0:T(1024)}, f32[768]{0:T(1024)S(1)}, u32[]{:S(2)}, u32[]{:S(2)}) collective-permute-start(f32[768]{0:T(1024)} %param.27), channel_id=1, source_target_pairs={{0,2},{1,3},{2,0},{3,1},{4,6},{5,7},{6,4},{7,5},{8,10},{9,11},{10,... | collective-permute-start | bytes 9224 | tf_op jit(solution)/shard_map/ppermute | solution.py:216
  9.6 49.9 %collective-permute-start.36 = (f32[1,1]{1,0:T(1,128)}, f32[1,1]{1,0:T(1,128)}, u32[]{:S(2)}, u32[]{:S(2)}) collective-permute-start(f32[1,1]{1,0:T(1,128)} %bitcast.19), channel_id=1, source_target_pairs={{0,4},{4,0},{8,12},{12,8},{16,20},{20,16},{24,28},{28,24},{1,5},{5... | collective-permute-start | bytes 20 | tf_op jit(solution)/shard_map/ppermute | solution.py:220
  71.5 29.1 %collective-permute-start.5 = (bf16[192,768]{1,0:T(8,128)(2,1)S(1)}, bf16[192,768]{1,0:T(8,128)(2,1)S(1)}, u32[]{:S(2)}, u32[]{:S(2)}) collective-permute-start(bf16[192,768]{1,0:T(8,128)(2,1)S(1)} %copy-done.34), channel_id=1, source_target_pairs={{0,3},{1,0},{2,1},{3,2},{4,7},{5,4},{6,5},{7,6},{8,11},{9,8},{10,9... | collective-permute-start | bytes 884744 | tf_op jit(solution)/shard_map/ppermute | solution.py:216
  72.3 30.7 %collective-permute-start.9 = (bf16[96,768]{0,1:T(8,128)(2,1)S(1)}, bf16[96,768]{0,1:T(8,128)(2,1)S(1)}, u32[]{:S(2)}, u32[]{:S(2)}) collective-permute-start(bf16[96,768]{0,1:T(8,128)(2,1)S(1)} %get-tuple-element.129), channel_id=1, source_target_pairs={{0,2},{1,3},{2,0},{3,1},{4,6},{5,7},{6,4},{7,5},{8,10},{9,11},{10,... | collective-permute-start | bytes 442376 | tf_op jit(solution)/shard_map/ppermute | solution.py:216
  89.3 19.9 %collective-permute-start = (bf16[512,192]{1,0:T(8,128)(2,1)S(1)}, bf16[512,192]{1,0:T(8,128)(2,1)S(1)}, u32[]{:S(2)}, u32[]{:S(2)}) collective-permute-start(bf16[512,192]{1,0:T(8,128)(2,1)S(1)} %get-tuple-element.135), channel_id=1, source_target_pairs={{0,1},{1,2},{2,3},{3,0},{4,5},{5,6},{6,7},{7,4},{8,9},{9,10},{10,1... | collective-permute-start | bytes 589832 | tf_op jit(solution)/shard_map/ppermute | solution.py:216
  96.5 22.5 %collective-permute-start.1 = (bf16[512,192]{1,0:T(8,128)(2,1)S(1)}, bf16[512,192]{1,0:T(8,128)(2,1)S(1)}, u32[]{:S(2)}, u32[]{:S(2)}) collective-permute-start(bf16[512,192]{1,0:T(8,128)(2,1)S(1)} %get-tuple-element.134), channel_id=1, source_target_pairs={{0,2},{1,3},{2,0},{3,1},{4,6},{5,7},{6,4},{7,5},{8,10},{9,11},{10,... | collective-permute-start | bytes 589832 | tf_op jit(solution)/shard_map/ppermute | solution.py:216
  100.6 20.1 %collective-permute-start.2 = (bf16[512,192]{1,0:T(8,128)(2,1)S(1)}, bf16[512,192]{1,0:T(8,128)(2,1)S(1)}, u32[]{:S(2)}, u32[]{:S(2)}) collective-permute-start(bf16[512,192]{1,0:T(8,128)(2,1)S(1)} %get-tuple-element.133), channel_id=1, source_target_pairs={{0,3},{1,0},{2,1},{3,2},{4,7},{5,4},{6,5},{7,6},{8,11},{9,8},{10,9... | collective-permute-start | bytes 589832 | tf_op jit(solution)/shard_map/ppermute | solution.py:216
  103.0 21.7 %collective-permute-start.6 = (bf16[96,768]{0,1:T(8,128)(2,1)S(1)}, bf16[96,768]{0,1:T(8,128)(2,1)S(1)}, u32[]{:S(2)}, u32[]{:S(2)}) collective-permute-start(bf16[96,768]{0,1:T(8,128)(2,1)S(1)} %get-tuple-element.129), channel_id=1, source_target_pairs={{0,1},{1,2},{2,3},{3,0},{4,5},{5,6},{6,7},{7,4},{8,9},{9,10},{10,1... | collective-permute-start | bytes 442376 | tf_op jit(solution)/shard_map/ppermute | solution.py:216
  104.1 30.8 %collective-permute-start.21 = (bf16[96,768]{1,0:T(8,128)(2,1)S(1)}, bf16[96,768]{1,0:T(8,128)(2,1)S(1)}, u32[]{:S(2)}, u32[]{:S(2)}) collective-permute-start(bf16[96,768]{1,0:T(8,128)(2,1)S(1)} %get-tuple-element.98), channel_id=1, source_target_pairs={{0,2},{1,3},{2,0},{3,1},{4,6},{5,7},{6,4},{7,5},{8,10},{9,11},{10,... | collective-permute-start | bytes 442376 | tf_op jit(solution)/shard_map/ppermute | solution.py:216
  109.2 27.4 %collective-permute-start.24 = (bf16[96,768]{1,0:T(8,128)(2,1)S(1)}, bf16[96,768]{1,0:T(8,128)(2,1)S(1)}, u32[]{:S(2)}, u32[]{:S(2)}) collective-permute-start(bf16[96,768]{1,0:T(8,128)(2,1)S(1)} %get-tuple-element.98), channel_id=1, source_target_pairs={{0,3},{1,0},{2,1},{3,2},{4,7},{5,4},{6,5},{7,6},{8,11},{9,8},{10,9... | collective-permute-start | bytes 442376 | tf_op jit(solution)/shard_map/ppermute | solution.py:216
  119.0 19.0 %collective-permute-start.10 = (bf16[96,768]{0,1:T(8,128)(2,1)S(1)}, bf16[96,768]{0,1:T(8,128)(2,1)S(1)}, u32[]{:S(2)}, u32[]{:S(2)}) collective-permute-start(bf16[96,768]{0,1:T(8,128)(2,1)S(1)} %collective-permute-done.9), channel_id=1, source_target_pairs={{0,8},{4,12},{8,0},{12,4},{16,24},{20,28},{24,16},{28,20},{1,9},{5... | collective-permute-start | bytes 442376 | tf_op jit(solution)/shard_map/ppermute | solution.py:220
  120.7 18.1 %collective-permute-start.13 = (bf16[96,768]{0,1:T(8,128)(2,1)S(1)}, bf16[96,768]{0,1:T(8,128)(2,1)S(1)}, u32[]{:S(2)}, u32[]{:S(2)}) collective-permute-start(bf16[96,768]{0,1:T(8,128)(2,1)S(1)} %collective-permute-done.12), channel_id=1, source_target_pairs={{0,8},{4,12},{8,0},{12,4},{16,24},{20,28},{24,16},{28,20},{1,9},{5... | collective-permute-start | bytes 442376 | tf_op jit(solution)/shard_map/ppermute | solution.py:220
  124.7 18.0 %collective-permute-start.19 = (bf16[96,768]{1,0:T(8,128)(2,1)}, bf16[96,768]{1,0:T(8,128)(2,1)S(1)}, u32[]{:S(2)}, u32[]{:S(2)}) collective-permute-start(bf16[96,768]{1,0:T(8,128)(2,1)} %collective-permute-done.18), channel_id=1, source_target_pairs={{0,16},{4,20},{8,24},{12,28},{16,0},{20,4},{24,8},{28,12},{1,17},{... | collective-permute-start | bytes 442376 | tf_op jit(solution)/shard_map/ppermute | solution.py:220
  140.8 22.5 %collective-permute-start.14 = (bf16[192,768]{0,1:T(8,128)(2,1)S(1)}, bf16[192,768]{0,1:T(8,128)(2,1)S(1)}, u32[]{:S(2)}, u32[]{:S(2)}) collective-permute-start(bf16[192,768]{0,1:T(8,128)(2,1)S(1)} %pad_maximum_fusion.14), channel_id=1, source_target_pairs={{0,16},{4,20},{8,24},{12,28},{16,0},{20,4},{24,8},{28,12},{1,17},{... | collective-permute-start | bytes 884744 | tf_op jit(solution)/shard_map/ppermute | solution.py:220
  142.7 26.9 %collective-permute-start.8 = (bf16[192,768]{0,1:T(8,128)(2,1)S(1)}, bf16[192,768]{0,1:T(8,128)(2,1)}, u32[]{:S(2)}, u32[]{:S(2)}) collective-permute-start(bf16[192,768]{0,1:T(8,128)(2,1)S(1)} %pad_maximum_fusion.12), channel_id=1, source_target_pairs={{0,16},{4,20},{8,24},{12,28},{16,0},{20,4},{24,8},{28,12},{1,17},{... | collective-permute-start | bytes 884744 | tf_op jit(solution)/shard_map/ppermute | solution.py:220
  144.7 38.7 %collective-permute-start.20 = (bf16[192,768]{1,0:T(8,128)(2,1)}, bf16[192,768]{1,0:T(8,128)(2,1)}, u32[]{:S(2)}, u32[]{:S(2)}) collective-permute-start(bf16[192,768]{1,0:T(8,128)(2,1)} %pad_maximum_fusion.16), channel_id=1, source_target_pairs={{0,8},{4,12},{8,0},{12,4},{16,24},{20,28},{24,16},{28,20},{1,9},{5... | collective-permute-start | bytes 884744 | tf_op jit(solution)/shard_map/ppermute | solution.py:220
  147.1 41.0 %collective-permute-start.23 = (bf16[192,768]{1,0:T(8,128)(2,1)}, bf16[192,768]{1,0:T(8,128)(2,1)}, u32[]{:S(2)}, u32[]{:S(2)}) collective-permute-start(bf16[192,768]{1,0:T(8,128)(2,1)} %pad_maximum_fusion.17), channel_id=1, source_target_pairs={{0,8},{4,12},{8,0},{12,4},{16,24},{20,28},{24,16},{28,20},{1,9},{5... | collective-permute-start | bytes 884744 | tf_op jit(solution)/shard_map/ppermute | solution.py:220
  154.8 37.8 %collective-permute-start.26 = (bf16[192,768]{1,0:T(8,128)(2,1)}, bf16[192,768]{1,0:T(8,128)(2,1)}, u32[]{:S(2)}, u32[]{:S(2)}) collective-permute-start(bf16[192,768]{1,0:T(8,128)(2,1)} %pad_maximum_fusion.18), channel_id=1, source_target_pairs={{0,8},{4,12},{8,0},{12,4},{16,24},{20,28},{24,16},{28,20},{1,9},{5... | collective-permute-start | bytes 884744 | tf_op jit(solution)/shard_map/ppermute | solution.py:220
  182.0 18.6 %collective-permute-start.27 = (bf16[384,768]{0,1:T(8,128)(2,1)S(1)}, bf16[384,768]{0,1:T(8,128)(2,1)S(1)}, u32[]{:S(2)}, u32[]{:S(2)}) collective-permute-start(bf16[384,768]{0,1:T(8,128)(2,1)S(1)} %pad_maximum_fusion.3), channel_id=1, source_target_pairs={{0,4},{4,0},{8,12},{12,8},{16,20},{20,16},{24,28},{28,24},{1,5},{5... | collective-permute-start | bytes 1769480 | tf_op jit(solution)/shard_map/ppermute | solution.py:220
  182.4 18.7 %collective-permute-start.28 = (bf16[384,768]{0,1:T(8,128)(2,1)S(1)}, bf16[384,768]{0,1:T(8,128)(2,1)S(1)}, u32[]{:S(2)}, u32[]{:S(2)}) collective-permute-start(bf16[384,768]{0,1:T(8,128)(2,1)S(1)} %pad_maximum_fusion.4), channel_id=1, source_target_pairs={{0,4},{4,0},{8,12},{12,8},{16,20},{20,16},{24,28},{28,24},{1,5},{5... | collective-permute-start | bytes 1769480 | tf_op jit(solution)/shard_map/ppermute | solution.py:220
  252.4 148.0 %collective-permute-start.33 = (bf16[512,768]{1,0:T(8,128)(2,1)}, bf16[512,768]{1,0:T(8,128)(2,1)}, u32[]{:S(2)}, u32[]{:S(2)}) collective-permute-start(bf16[512,768]{1,0:T(8,128)(2,1)} %get-tuple-element.108), channel_id=1, source_target_pairs={{0,1},{1,2},{2,3},{3,0},{4,5},{5,6},{6,7},{7,4},{8,9},{9,10},{10,1... | collective-permute-start | bytes 2359304 | tf_op jit(solution)/shard_map/ppermute | solution.py:216
  256.3 146.5 %collective-permute-start.34 = (bf16[512,768]{1,0:T(8,128)(2,1)}, bf16[512,768]{1,0:T(8,128)(2,1)S(1)}, u32[]{:S(2)}, u32[]{:S(2)}) collective-permute-start(bf16[512,768]{1,0:T(8,128)(2,1)} %get-tuple-element.108), channel_id=1, source_target_pairs={{0,2},{1,3},{2,0},{3,1},{4,6},{5,7},{6,4},{7,5},{8,10},{9,11},{10,... | collective-permute-start | bytes 2359304 | tf_op jit(solution)/shard_map/ppermute | solution.py:216
  264.5 64.2 %collective-permute-start.44 = (bf16[512,192]{1,0:T(8,128)(2,1)}, bf16[512,192]{1,0:T(8,128)(2,1)}, u32[]{:S(2)}, u32[]{:S(2)}) collective-permute-start(bf16[512,192]{1,0:T(8,128)(2,1)} %get-tuple-element.144), channel_id=1, source_target_pairs={{0,3},{1,0},{2,1},{3,2},{4,7},{5,4},{6,5},{7,6},{8,11},{9,8},{10,9... | collective-permute-start | bytes 589832 | tf_op jit(solution)/shard_map/ppermute | solution.py:216
  266.9 63.7 %collective-permute-start.45 = (bf16[512,192]{1,0:T(8,128)(2,1)}, bf16[512,192]{1,0:T(8,128)(2,1)}, u32[]{:S(2)}, u32[]{:S(2)}) collective-permute-start(bf16[512,192]{1,0:T(8,128)(2,1)} %get-tuple-element.143), channel_id=1, source_target_pairs={{0,2},{1,3},{2,0},{3,1},{4,6},{5,7},{6,4},{7,5},{8,10},{9,11},{10,... | collective-permute-start | bytes 589832 | tf_op jit(solution)/shard_map/ppermute | solution.py:216
  267.4 35.2 %collective-permute-start.42 = (f32[66,128]{1,0:T(8,128)S(1)}, f32[66,128]{1,0:T(8,128)S(1)}, u32[]{:S(2)}, u32[]{:S(2)}) collective-permute-start(f32[66,128]{1,0:T(8,128)S(1)} %add.546), channel_id=1, source_target_pairs={{0,1},{1,0},{2,3},{3,2},{4,5},{5,4},{6,7},{7,6},{8,9},{9,8},{10,11... | collective-permute-start | bytes 101384 | tf_op jit(solution)/shard_map/ppermute | solution.py:220
  302.7 23.6 %collective-permute-start.43 = (f32[66,128]{1,0:T(8,128)S(1)}, f32[66,128]{1,0:T(8,128)S(1)}, u32[]{:S(2)}, u32[]{:S(2)}) collective-permute-start(f32[66,128]{1,0:T(8,128)S(1)} %add.547), channel_id=1, source_target_pairs={{0,2},{1,3},{2,0},{3,1},{4,6},{5,7},{6,4},{7,5},{8,10},{9,11},{10,... | collective-permute-start | bytes 101384 | tf_op jit(solution)/shard_map/ppermute | solution.py:220
  328.7 69.3 %collective-permute-start.62 = (bf16[4,96,768]{2,1,0:T(8,128)(2,1)}, bf16[4,96,768]{2,1,0:T(8,128)(2,1)S(1)}, u32[]{:S(2)}, u32[]{:S(2)}) collective-permute-start(bf16[4,96,768]{2,1,0:T(8,128)(2,1)} %constant_dynamic-slice_fusion.13), channel_id=1, source_target_pairs={{0,4},{4,0},{8,12},{12,8},{16,20},{20,16},{24,28},{28,24},{1,5},{5... | collective-permute-start | bytes 1769480 | tf_op jit(solution)/shard_map/ppermute | solution.py:220
  396.8 39.6 %collective-permute-start.35 = (bf16[512,768]{1,0:T(8,128)(2,1)}, bf16[512,768]{1,0:T(8,128)(2,1)S(1)}, u32[]{:S(2)}, u32[]{:S(2)}) collective-permute-start(bf16[512,768]{1,0:T(8,128)(2,1)} %get-tuple-element.108), channel_id=1, source_target_pairs={{0,3},{1,0},{2,1},{3,2},{4,7},{5,4},{6,5},{7,6},{8,11},{9,8},{10,9... | collective-permute-start | bytes 2359304 | tf_op jit(solution)/shard_map/ppermute | solution.py:216
  398.0 70.5 %collective-permute-start.89 = (bf16[768,512]{1,0:T(8,128)(2,1)S(1)}, bf16[768,512]{1,0:T(8,128)(2,1)S(1)}, u32[]{:S(2)}, u32[]{:S(2)}) collective-permute-start(bf16[768,512]{1,0:T(8,128)(2,1)S(1)} %constant_dynamic-slice_fusion.2), channel_id=1, source_target_pairs={{0,4},{4,0},{8,12},{12,8},{16,20},{20,16},{24,28},{28,24},{1,5},{5... | collective-permute-start | bytes 2359304 | tf_op jit(solution)/shard_map/ppermute | solution.py:220
  398.2 56.3 %collective-permute-start.47 = (bf16[512,768]{1,0:T(8,128)(2,1)S(1)}, bf16[512,768]{1,0:T(8,128)(2,1)S(1)}, u32[]{:S(2)}, u32[]{:S(2)}) collective-permute-start(bf16[512,768]{1,0:T(8,128)(2,1)S(1)} %get-tuple-element.101), channel_id=1, source_target_pairs={{0,1},{1,2},{2,3},{3,0},{4,5},{5,6},{6,7},{7,4},{8,9},{9,10},{10,1... | collective-permute-start | bytes 2359304 | tf_op jit(solution)/shard_map/ppermute | solution.py:216
  400.4 65.6 %collective-permute-start.48 = (bf16[512,768]{1,0:T(8,128)(2,1)S(1)}, bf16[512,768]{1,0:T(8,128)(2,1)S(1)}, u32[]{:S(2)}, u32[]{:S(2)}) collective-permute-start(bf16[512,768]{1,0:T(8,128)(2,1)S(1)} %get-tuple-element.103), channel_id=1, source_target_pairs={{0,2},{1,3},{2,0},{3,1},{4,6},{5,7},{6,4},{7,5},{8,10},{9,11},{10,... | collective-permute-start | bytes 2359304 | tf_op jit(solution)/shard_map/ppermute | solution.py:216
  402.8 64.7 %collective-permute-start.49 = (bf16[512,768]{1,0:T(8,128)(2,1)S(1)}, bf16[512,768]{1,0:T(8,128)(2,1)S(1)}, u32[]{:S(2)}, u32[]{:S(2)}) collective-permute-start(bf16[512,768]{1,0:T(8,128)(2,1)S(1)} %get-tuple-element.102), channel_id=1, source_target_pairs={{0,3},{1,0},{2,1},{3,2},{4,7},{5,4},{6,5},{7,6},{8,11},{9,8},{10,9... | collective-permute-start | bytes 2359304 | tf_op jit(solution)/shard_map/ppermute | solution.py:216
  454.4 81.9 %collective-permute-start.80 = (bf16[1536,768]{1,0:T(8,128)(2,1)S(1)}, bf16[1536,768]{1,0:T(8,128)(2,1)S(1)}, u32[]{:S(2)}, u32[]{:S(2)}) collective-permute-start(bf16[1536,768]{1,0:T(8,128)(2,1)S(1)} %copy-done.49), channel_id=1, source_target_pairs={{0,4},{4,0},{8,12},{12,8},{16,20},{20,16},{24,28},{28,24},{1,5},{5... | collective-permute-start | bytes 7077896 | tf_op jit(solution)/shard_map/ppermute | solution.py:220
  454.6 85.1 %collective-permute-start.71 = (bf16[1536,768]{1,0:T(8,128)(2,1)S(1)}, bf16[1536,768]{1,0:T(8,128)(2,1)S(1)}, u32[]{:S(2)}, u32[]{:S(2)}) collective-permute-start(bf16[1536,768]{1,0:T(8,128)(2,1)S(1)} %copy-done.50), channel_id=1, source_target_pairs={{0,4},{4,0},{8,12},{12,8},{16,20},{20,16},{24,28},{28,24},{1,5},{5... | collective-permute-start | bytes 7077896 | tf_op jit(solution)/shard_map/ppermute | solution.py:220
  471.1 20.7 %collective-permute-start.65 = (bf16[24,768]{1,0:T(8,128)(2,1)S(1)}, bf16[24,768]{1,0:T(8,128)(2,1)S(1)}, u32[]{:S(2)}, u32[]{:S(2)}) collective-permute-start(bf16[24,768]{1,0:T(8,128)(2,1)S(1)} %get-tuple-element.177), channel_id=1, source_target_pairs={{0,3},{1,0},{2,1},{3,2},{4,7},{5,4},{6,5},{7,6},{8,11},{9,8},{10,9... | collective-permute-start | bytes 110600 | tf_op jit(solution)/shard_map/ppermute | solution.py:216
  495.1 23.5 %collective-permute-start.90 = (bf16[384,512]{1,0:T(8,128)(2,1)S(1)}, bf16[384,512]{1,0:T(8,128)(2,1)S(1)}, u32[]{:S(2)}, u32[]{:S(2)}) collective-permute-start(bf16[384,512]{1,0:T(8,128)(2,1)S(1)} %constant_dynamic-slice_fusion.1), channel_id=1, source_target_pairs={{0,16},{4,20},{8,24},{12,28},{16,0},{20,4},{24,8},{28,12},{1,17},{... | collective-permute-start | bytes 1179656 | tf_op jit(solution)/shard_map/ppermute | solution.py:220
  496.7 46.2 %collective-permute-start.50 = (bf16[512,768]{1,0:T(8,128)(2,1)S(1)}, bf16[512,768]{1,0:T(8,128)(2,1)S(1)}, u32[]{:S(2)}, u32[]{:S(2)}) collective-permute-start(bf16[512,768]{1,0:T(8,128)(2,1)S(1)} %get-tuple-element.99), channel_id=1, source_target_pairs={{0,1},{1,2},{2,3},{3,0},{4,5},{5,6},{6,7},{7,4},{8,9},{9,10},{10,1... | collective-permute-start | bytes 2359304 | tf_op jit(solution)/shard_map/ppermute | solution.py:216
  525.9 38.0 %collective-permute-start.51 = (bf16[512,768]{1,0:T(8,128)(2,1)S(1)}, bf16[512,768]{1,0:T(8,128)(2,1)S(1)}, u32[]{:S(2)}, u32[]{:S(2)}) collective-permute-start(bf16[512,768]{1,0:T(8,128)(2,1)S(1)} %get-tuple-element.99), channel_id=1, source_target_pairs={{0,2},{1,3},{2,0},{3,1},{4,6},{5,7},{6,4},{7,5},{8,10},{9,11},{10,... | collective-permute-start | bytes 2359304 | tf_op jit(solution)/shard_map/ppermute | solution.py:216
  533.2 83.0 %collective-permute-start.52 = (bf16[512,768]{1,0:T(8,128)(2,1)S(1)}, bf16[512,768]{1,0:T(8,128)(2,1)S(1)}, u32[]{:S(2)}, u32[]{:S(2)}) collective-permute-start(bf16[512,768]{1,0:T(8,128)(2,1)S(1)} %get-tuple-element.99), channel_id=1, source_target_pairs={{0,3},{1,0},{2,1},{3,2},{4,7},{5,4},{6,5},{7,6},{8,11},{9,8},{10,9... | collective-permute-start | bytes 2359304 | tf_op jit(solution)/shard_map/ppermute | solution.py:216
  536.4 27.6 %collective-permute-start.93 = (bf16[384,512]{1,0:T(8,128)(2,1)S(1)}, bf16[384,512]{1,0:T(8,128)(2,1)S(1)}, u32[]{:S(2)}, u32[]{:S(2)}) collective-permute-start(bf16[384,512]{1,0:T(8,128)(2,1)S(1)} %get-tuple-element.154), channel_id=1, source_target_pairs={{0,16},{4,20},{8,24},{12,28},{16,0},{20,4},{24,8},{28,12},{1,17},{... | collective-permute-start | bytes 1179656 | tf_op jit(solution)/shard_map/ppermute | solution.py:220
  539.7 31.1 %collective-permute-start.81 = (bf16[4,2,96,768]{3,2,1,0:T(8,128)(2,1)S(1)}, bf16[4,2,96,768]{3,2,1,0:T(8,128)(2,1)S(1)}, u32[]{:S(2)}, u32[]{:S(2)}) collective-permute-start(bf16[4,2,96,768]{3,2,1,0:T(8,128)(2,1)S(1)} %slice_bitcast_fusion), channel_id=1, source_target_pairs={{0,16},{4,20},{8,24},{12,28},{16,0},{20,4},{24,8},{28,12},{1,17},{... | collective-permute-start | bytes 3538952 | tf_op jit(solution)/shard_map/ppermute | solution.py:220
  542.9 29.1 %collective-permute-start.72 = (bf16[4,2,96,768]{3,2,1,0:T(8,128)(2,1)S(1)}, bf16[4,2,96,768]{3,2,1,0:T(8,128)(2,1)S(1)}, u32[]{:S(2)}, u32[]{:S(2)}) collective-permute-start(bf16[4,2,96,768]{3,2,1,0:T(8,128)(2,1)S(1)} %slice_bitcast_fusion.2), channel_id=1, source_target_pairs={{0,8},{4,12},{8,0},{12,4},{16,24},{20,28},{24,16},{28,20},{1,9},{5... | collective-permute-start | bytes 3538952 | tf_op jit(solution)/shard_map/ppermute | solution.py:220
  572.3 25.6 %collective-permute-start.73 = (bf16[4,96,768]{2,1,0:T(8,128)(2,1)S(1)}, bf16[4,96,768]{2,1,0:T(8,128)(2,1)S(1)}, u32[]{:S(2)}, u32[]{:S(2)}) collective-permute-start(bf16[4,96,768]{2,1,0:T(8,128)(2,1)S(1)} %slice_bitcast_fusion.6), channel_id=1, source_target_pairs={{0,16},{4,20},{8,24},{12,28},{16,0},{20,4},{24,8},{28,12},{1,17},{... | collective-permute-start | bytes 1769480 | tf_op jit(solution)/shard_map/ppermute | solution.py:220
  574.2 58.2 %collective-permute-start.94 = (bf16[768,512]{1,0:T(8,128)(2,1)S(1)}, bf16[768,512]{1,0:T(8,128)(2,1)S(1)}, u32[]{:S(2)}, u32[]{:S(2)}) collective-permute-start(bf16[768,512]{1,0:T(8,128)(2,1)S(1)} %get-tuple-element.138), channel_id=1, source_target_pairs={{0,4},{4,0},{8,12},{12,8},{16,20},{20,16},{24,28},{28,24},{1,5},{5... | collective-permute-start | bytes 2359304 | tf_op jit(solution)/shard_map/ppermute | solution.py:220
  583.9 18.2 %collective-permute-start.83 = (bf16[96,768]{1,0:T(8,128)(2,1)S(1)}, bf16[96,768]{1,0:T(8,128)(2,1)S(1)}, u32[]{:S(2)}, u32[]{:S(2)}) collective-permute-start(bf16[96,768]{1,0:T(8,128)(2,1)S(1)} %get-tuple-element.146), channel_id=1, source_target_pairs={{0,3},{1,0},{2,1},{3,2},{4,7},{5,4},{6,5},{7,6},{8,11},{9,8},{10,9... | collective-permute-start | bytes 442376 | tf_op jit(solution)/shard_map/ppermute | solution.py:216
  (112 other events, 1063.9 us)

commit v2 on v1

v2 whole, which is shorter than its diff:
```python
import functools
import math

import jax
import jax.numpy as jnp
from jax import lax
from jax.experimental import pallas as pl
from jax.experimental.pallas import tpu as pltpu
from jax.sharding import PartitionSpec as P

BLOCK = 256
LOG2E = math.log2(math.e)
SOFTENING = 0.5
EPS = 1e-6
F32 = jnp.float32
BF16 = jnp.bfloat16


def dot(a, b):
    return jnp.dot(a, b, preferred_element_type=F32)


def dot_nt(a, b):
    return lax.dot_general(a, b, (((1,), (1,)), ((), ())), preferred_element_type=F32)


def dot_tn(a, b):
    return lax.dot_general(a, b, (((0,), (0,)), ((), ())), preferred_element_type=F32)


def dot_tt(a, b):
    return lax.dot_general(a, b, (((0,), (1,)), ((), ())), preferred_element_type=F32)


def prep_kernel(hid, w, b, bt, table, noise, q3, k3, v3, qt, kt, vt, lmt):
    heads = table.shape[0]
    tokens = hid.shape[0]
    hd = q3.shape[2]
    for h in range(heads):
        x = (table[h] + noise[h]) * (1.0 / SOFTENING)
        ls = jnp.minimum(x, 0.0) - jnp.log1p(jnp.exp(-jnp.abs(x)))
        lmt[h] = jnp.transpose(ls * LOG2E)

    step = 2 * BLOCK

    def project(i, _):
        rows = pl.ds(pl.multiple_of(i * step, step), step)
        x = hid[rows, :]
        for n, (nat, tr) in enumerate(((q3, qt), (k3, kt), (v3, vt))):
            y = dot(x, w[n])
            yt = dot_tt(w[n], x)
            if n != 1:
                y = y + b[n // 2 : n // 2 + 1, :]
                yt = yt + bt[:, n // 2 : n // 2 + 1]
            y = y.astype(BF16)
            for h in range(heads):
                nat[h, rows, :] = y[:, h * hd : (h + 1) * hd]
            tr[:, rows] = yt.astype(BF16)
        return 0

    lax.fori_loop(0, tokens // step, project, 0)


def attn_prep(hidden, w_qkv, b_qv, table, noise):
    tokens = hidden.shape[0]
    heads = table.shape[0]
    width = w_qkv.shape[2]
    sd = jax.ShapeDtypeStruct
    nat = sd((heads, tokens, width // heads), BF16)
    tr = sd((width, tokens), BF16)
    return pl.pallas_call(
        prep_kernel,
        out_shape=(nat, nat, nat, tr, tr, tr, sd(table.shape, F32)),
        compiler_params=pltpu.CompilerParams(vmem_limit_bytes=56 << 20),
        name="attn_prep",
    )(hidden, w_qkv, b_qv, b_qv.T, table, noise)


def attn_fwd_kernel(lo, n_prev, qt, k3, vt, lmt, *refs):
    ctx, ctxt, lse = refs[n_prev:]
    heads, tokens, hd = k3.shape
    period = lmt.shape[1]
    width = heads * hd
    coef = LOG2E / math.sqrt(hd)
    parts = period // BLOCK
    lse[...] = jnp.zeros(lse.shape, F32)
    first = (pl.program_id(0) + lo) * parts

    def per_q(j, _):
        qb = first + j
        qcol = pl.ds(pl.multiple_of(qb * BLOCK, BLOCK), BLOCK)
        ocol = pl.ds(pl.multiple_of(j * BLOCK, BLOCK), BLOCK)
        mcol = ocol

        def per_k(kb, carry):
            krow = pl.ds(pl.multiple_of(kb * BLOCK, BLOCK), BLOCK)
            mrow = pl.ds(pl.multiple_of(lax.rem(kb, parts) * BLOCK, BLOCK), BLOCK)
            out = []
            ss = [dot(k3[h, krow, :], qt[h * hd : (h + 1) * hd, qcol]) for h in range(heads)]
            for h in range(heads):
                m, l, acc = carry[h]
                s = ss[h] * coef + lmt[h, mrow, mcol]
                mn = jnp.maximum(m, jnp.max(s, axis=0, keepdims=True))
                al = jnp.exp2(m - mn)
                p = jnp.exp2(s - mn)
                l = l * al + jnp.sum(p, axis=0, keepdims=True)
                acc = acc * al + dot(vt[h * hd : (h + 1) * hd, krow], p.astype(BF16))
                out.append((mn, l, acc))
            return tuple(out)

        init = tuple(
            (
                jnp.full((1, BLOCK), -1e30, F32),
                jnp.zeros((1, BLOCK), F32),
                jnp.zeros((hd, BLOCK), F32),
            )
            for _ in range(heads)
        )
        res = lax.fori_loop(0, qb + 1, per_k, init)
        cols = []
        for h in range(heads):
            m, l, acc = res[h]
            c = acc / l
            ctxt[h * hd : (h + 1) * hd, ocol] = c
            lse[h : h + 1, ocol] = m + jnp.log2(l)
            cols.append(c)
        pad = -width % 128
        if pad:
            cols.append(jnp.zeros((pad, BLOCK), F32))
        full = jnp.transpose(jnp.concatenate(cols, axis=0))
        ctx[ocol, :] = full[:, :width].astype(BF16)
        return 0

    lax.fori_loop(0, parts, per_q, 0)


def attn_fwd(qt, k3, vt, lmt, lo, hi, prev=()):
    heads, tokens, hd = k3.shape
    width = heads * hd
    period = lmt.shape[1]
    sd = jax.ShapeDtypeStruct
    whole = lambda x: pl.BlockSpec(x.shape, lambda i, n=len(x.shape): (0,) * n)
    return pl.pallas_call(
        functools.partial(attn_fwd_kernel, lo, len(prev)),
        grid=(hi - lo,),
        in_specs=[whole(x) for x in (qt, k3, vt, lmt)] + [pl.BlockSpec(memory_space=pl.ANY)] * len(prev),
        out_specs=(
            pl.BlockSpec((period, width), lambda i: (i + lo, 0)),
            pl.BlockSpec((width, period), lambda i: (0, i + lo)),
            pl.BlockSpec((8, period), lambda i: (0, i + lo)),
        ),
        out_shape=(sd((tokens, width), BF16), sd((width, tokens), F32), sd((8, tokens), F32)),
        input_output_aliases={4 + n: n for n in range(len(prev))},
        compiler_params=pltpu.CompilerParams(vmem_limit_bytes=56 << 20),
        name="attn_fwd",
    )(qt, k3, vt, lmt, *prev)


def attn_bwd_kernel(gctx, ctxt, q3, k3, v3, qt, kt, lse, lmt, gqkv, glm, gk, gv, g3, glmt):
    heads, tokens, hd = q3.shape
    period = lmt.shape[1]
    width = heads * hd
    coef = LOG2E / math.sqrt(hd)
    scale = 1.0 / math.sqrt(hd)
    parts = period // BLOCK
    pad = -width % 128
    gk[...] = jnp.zeros(gk.shape, F32)
    gv[...] = jnp.zeros(gv.shape, F32)
    glmt[...] = jnp.zeros(glmt.shape, F32)

    def per_q(i, _):
        qb = tokens // BLOCK - 1 - i
        qcol = pl.ds(pl.multiple_of(qb * BLOCK, BLOCK), BLOCK)
        mcol = pl.ds(pl.multiple_of(lax.rem(qb, parts) * BLOCK, BLOCK), BLOCK)
        g = gctx[qcol, :].astype(F32)
        gpad = jnp.concatenate([g, jnp.zeros((BLOCK, pad), F32)], axis=1) if pad else g
        gt = jnp.transpose(gpad)
        delta, gtb = [], []
        for h in range(heads):
            gth = gt[h * hd : (h + 1) * hd, :]
            delta.append(jnp.sum(gth * ctxt[h * hd : (h + 1) * hd, qcol], axis=0, keepdims=True))
            gtb.append(gth.astype(BF16))
            g3[h] = gctx[qcol, h * hd : (h + 1) * hd]

        def per_k(kb, carry):
            krow = pl.ds(pl.multiple_of(kb * BLOCK, BLOCK), BLOCK)
            mrow = pl.ds(pl.multiple_of(lax.rem(kb, parts) * BLOCK, BLOCK), BLOCK)
            out = []
            for h in range(heads):
                hs = slice(h * hd, (h + 1) * hd)
                s = dot(k3[h, krow, :], qt[hs, qcol]) * coef + lmt[h, mrow, mcol]
                p = jnp.exp2(s - lse[h : h + 1, qcol])
                dp = dot(v3[h, krow, :], gtb[h])
                ds = p * (dp - delta[h])
                dsb = ds.astype(BF16)
                glmt[h, mrow, mcol] += ds
                gv[h, krow, :] += dot(p.astype(BF16), g3[h])
                gk[h, krow, :] += dot(dsb, q3[h, qcol, :])
                out.append(carry[h] + dot(kt[hs, krow], dsb))
            return tuple(out)

        init = tuple(jnp.zeros((hd, BLOCK), F32) for _ in range(heads))
        res = lax.fori_loop(0, qb + 1, per_k, init)
        rows = [r * scale for r in res]
        if pad:
            rows.append(jnp.zeros((pad, BLOCK), F32))
        gq = jnp.transpose(jnp.concatenate(rows, axis=0))[:, :width]
        gkb = jnp.concatenate([gk[h, qcol, :] for h in range(heads)], axis=1) * scale
        gvb = jnp.concatenate([gv[h, qcol, :] for h in range(heads)], axis=1)
        gqkv[0, qcol, :] = gq.astype(BF16)
        gqkv[1, qcol, :] = gkb.astype(BF16)
        gqkv[2, qcol, :] = gvb.astype(BF16)
        return 0

    lax.fori_loop(0, tokens // BLOCK, per_q, 0)
    for h in range(heads):
        glm[h] = jnp.transpose(glmt[h])


def attn_bwd(gctx, ctxt, q3, k3, v3, qt, kt, lse, lmt):
    heads, tokens, hd = q3.shape
    width = heads * hd
    sd = jax.ShapeDtypeStruct
    return pl.pallas_call(
        attn_bwd_kernel,
        out_shape=(sd((3, tokens, width), BF16), sd(lmt.shape, F32)),
        scratch_shapes=[
            pltpu.VMEM((heads, tokens, hd), F32),
            pltpu.VMEM((heads, tokens, hd), F32),
            pltpu.VMEM((heads, BLOCK, hd), BF16),
            pltpu.VMEM(lmt.shape, F32),
        ],
        compiler_params=pltpu.CompilerParams(vmem_limit_bytes=56 << 20),
        name="attn_bwd",
    )(gctx, ctxt, q3, k3, v3, qt, kt, lse, lmt)


def norm_parts(resid):
    centred = resid - jnp.mean(resid, axis=-1, keepdims=True)
    rstd = lax.rsqrt(jnp.mean(centred * centred, axis=-1, keepdims=True) + EPS)
    return centred * rstd, rstd


def norm_back(grad, xhat, rstd, gain):
    gy = grad * gain
    return rstd * (
        gy
        - jnp.mean(gy, axis=-1, keepdims=True)
        - xhat * jnp.mean(gy * xhat, axis=-1, keepdims=True)
    )


def ffn_kernel(
    n_t, slab, core, coef, *refs
):
    ctx = refs[:n_t]
    (wao, hid, teach, valid, vec, bup, up_o, up_m, up_t, dn_o, dn_m, dn_t,
     out, out_low, act, gb, first_low, grad_ffn, grad_attn, grad_resid, gctx, vecs, gbup,
     up_s, dn_s, slope, xhat_s, sems) = refs[n_t:]
    units, width = up_s.shape
    half = units // 2
    spots = half // (n_t * slab)
    c = core[0]
    copies = []
    for n, (o, m, t, dst) in enumerate(((up_o, up_m, up_t, up_s), (dn_o, dn_m, dn_t, dn_s))):
        for side, f in enumerate((m, t)):
            base = (c if side == 0 else 1 - c) * (spots * slab)
            for p in range(spots):
                to = side * half + p * n_t * slab
                copies.append((n, o.at[pl.ds(pl.multiple_of(base + p * slab, slab), slab)], dst.at[pl.ds(to, slab)]))
                rest = (n_t - 1) * slab
                copies.append((n, f.at[pl.ds(p * rest, rest)], dst.at[pl.ds(to + slab, rest)]))
    copies = [pltpu.make_async_copy(a, b, sems.at[i]) for i, (n, a, b) in enumerate(copies)]
    for cp in copies:
        cp.start()
    b_ao, g1, b1, b_dn, g2, b2 = (vec[n : n + 1, :] for n in range(6))
    attention = sum(dot(ctx[s][...], wao[s]) for s in range(n_t)) + b_ao
    xhat1, rstd1 = norm_parts(hid[...].astype(F32) + attention)
    first = xhat1 * g1 + b1
    first_low[...] = first.astype(BF16)
    xhat_s[...] = xhat1
    for cp in copies:
        cp.wait()
    blocks, _, size = bup.shape

    def forward(i, feed):
        rows = pl.ds(pl.multiple_of(i * size, size), size)
        before = dot_nt(first_low[...], up_s[rows, :]) + bup[i]
        phi = 0.5 * (1.0 + lax.erf(before * math.sqrt(0.5)))
        dens = jnp.exp(-0.5 * before * before) * (1.0 / math.sqrt(2.0 * math.pi))
        low = (before * phi).astype(BF16)
        act[:, rows] = low
        slope[:, rows] = (phi + before * dens).astype(BF16)
        return feed + dot(low, dn_s[rows, :])

    feed = lax.fori_loop(0, blocks, forward, jnp.zeros(out.shape, F32))
    xhat2, rstd2 = norm_parts(first + feed + b_dn)
    own = xhat2 * g2 + b2
    out[...] = own
    out_low[...] = own.astype(BF16)
    residue = own - teach[...]
    weighed = valid[...] * residue
    grad_out = coef[0] * weighed
    total = lambda x: jnp.sum(x, axis=0, keepdims=True)
    vecs[...] = jnp.zeros(vecs.shape, F32)
    vecs[4:5, :] = total(grad_out * xhat2)
    vecs[5:6, :] = total(grad_out)
    vecs[6:7, :] = total(weighed * residue)
    grad_second = norm_back(grad_out, xhat2, rstd2, g2)
    grad_resid[...] = grad_second
    low = grad_second.astype(BF16)
    grad_ffn[...] = low
    vecs[3:4, :] = total(low.astype(F32))

    def backward(i, acc):
        rows = pl.ds(pl.multiple_of(i * size, size), size)
        g = dot_nt(grad_ffn[...], dn_s[rows, :]) * slope[:, rows].astype(F32)
        low = g.astype(BF16)
        gb[:, rows] = low
        gbup[i] = total(low.astype(F32))
        return acc + dot(low, up_s[rows, :])

    grad_first = lax.fori_loop(0, blocks, backward, jnp.zeros(out.shape, F32)) + grad_resid[...]
    xhat1 = xhat_s[...]
    vecs[1:2, :] = total(grad_first * xhat1)
    vecs[2:3, :] = total(grad_first)
    back = norm_back(grad_first, xhat1, rstd1, g1)
    grad_resid[...] = back
    low = back.astype(BF16)
    grad_attn[...] = low
    vecs[0:1, :] = total(low.astype(F32))
    local = ctx[0].shape[1]
    for s in range(n_t):
        gctx[s] = dot_nt(low, wao[s]).astype(BF16)


def ffn(core, coef, ctx, wao, hid, teach, valid, vec, bup, ups, downs, slab):
    n_t = len(ctx)
    chunk, width = hid.shape
    local = ctx[0].shape[1]
    blocks, _, size = bup.shape
    units = blocks * size
    spots = units // (2 * n_t * slab)
    sd = jax.ShapeDtypeStruct
    vm = pl.BlockSpec(memory_space=pltpu.VMEM)
    sm = pl.BlockSpec(memory_space=pltpu.SMEM)
    hbm = pl.BlockSpec(memory_space=pl.ANY)
    return pl.pallas_call(
        functools.partial(ffn_kernel, n_t, slab),
        in_specs=[sm, sm] + [vm] * (n_t + 6) + [hbm] * 6,
        out_shape=(
            sd((chunk, width), F32),
            sd((chunk, width), BF16),
            sd((chunk, units), BF16),
            sd((chunk, units), BF16),
            sd((chunk, width), BF16),
            sd((chunk, width), BF16),
            sd((chunk, width), BF16),
            sd((chunk, width), F32),
            sd((n_t, chunk, local), BF16),
            sd((8, width), F32),
            sd((blocks, 1, size), F32),
        ),
        scratch_shapes=[
            pltpu.VMEM((units, width), BF16),
            pltpu.VMEM((units, width), BF16),
            pltpu.VMEM((chunk, units), BF16),
            pltpu.VMEM((chunk, width), F32),
            pltpu.SemaphoreType.DMA((8 * spots,)),
        ],
        compiler_params=pltpu.CompilerParams(vmem_limit_bytes=56 << 20),
        name="ffn",
    )(core, coef, *ctx, wao, hid, teach, valid, vec, bup, *ups, *downs)


def shift(x, size, amount):
    return lax.ppermute(x, "tensor", [(j, (j + amount) % size) for j in range(size)])


def swap(x, axis, size, bit):
    return lax.ppermute(x, axis, [(j, j ^ bit) for j in range(size)])


def rows_of(x, start, count):
    return lax.dynamic_slice_in_dim(x, start, count, axis=0)


def body(
    hidden, teacher, valid, w_qkv, b_qv, w_attn_out, b_attn_out, gain_one, bias_one,
    w_up, b_up, w_down, b_down, gain_two, bias_two, table, noise, *, n_d, n_t,
):
    tokens, width = hidden.shape
    units = w_up.shape[1]
    local = w_qkv.shape[2]
    chunk = tokens // n_t
    ti = lax.axis_index("tensor")
    di = lax.axis_index("dp")
    group = min(n_d, 8)
    low_bits = [b for b in (2, 4) if b < group]
    high_bits = low_bits[::-1]
    extra = [b for b in (8, 16, 32, 64, 128, 256, 512) if b < n_d]
    spots = group // 2
    slab = units // group
    piece = local // spots
    core = di % 2
    spot = (di // 2) % spots

    def bit_of(bit):
        return (di // bit) % 2

    def dp_swap(x, bit):
        return swap(x, "dp", n_d, bit)

    def everyone(x):
        bit = 1
        while bit < n_d:
            x = x + dp_swap(x, bit)
            bit *= 2
        return x

    def spread(x, bits):
        done = []
        for bit in bits:
            other = dp_swap(x, bit)
            up = bit_of(bit) == 1
            pos = sum(1 for b in done if b > bit)
            x = jnp.stack([jnp.where(up, other, x), jnp.where(up, x, other)], axis=pos)
            done.append(bit)
        return x.reshape((-1,) + x.shape[len(done) :])

    def narrow(x, bits):
        left = sorted(bits, reverse=True)
        for bit in bits:
            ax = left.index(bit)
            left.remove(bit)
            up = bit_of(bit)
            send = lax.dynamic_index_in_dim(x, 1 - up, ax, keepdims=False)
            keep = lax.dynamic_index_in_dim(x, up, ax, keepdims=False)
            x = (keep.astype(F32) + dp_swap(send, bit).astype(F32)).astype(BF16)
        return x

    def finish(x):
        for bit in extra:
            x = (x.astype(F32) + dp_swap(x, bit).astype(F32)).astype(BF16)
        return x

    valid_f = valid[0].astype(F32)
    total_valid = everyone(jnp.sum(valid_f).reshape(1, 1))[0, 0]

    up_own = w_up.T
    b_hi = b_up.astype(BF16)
    b_lo = (b_up - b_hi.astype(F32)).astype(BF16)
    start = core * (spots * slab) + spot * slab
    sent = jnp.concatenate(
        [
            rows_of(up_own, start, slab),
            rows_of(w_attn_out, spot * piece, piece),
            rows_of(w_down, start, slab),
            b_hi[None],
            b_lo[None],
            jnp.zeros((14, width), BF16),
        ]
    )
    came = [shift(sent, n_t, s) for s in range(1, n_t)]

    q3, k3, v3, qt, kt, vt, lmt = attn_prep(hidden, w_qkv, b_qv, table, noise)
    n_sup = tokens // lmt.shape[1]
    part = attn_fwd(qt, k3, vt, lmt, 0, n_sup - 1)
    part, came = lax.optimization_barrier((part, came))

    cut = slab + piece
    wide_a = jnp.stack([x[:cut] for x in came])
    wide_b = jnp.stack([x[cut : cut + slab] for x in came])
    wide_a = spread(wide_a, low_bits)
    wide_b = spread(wide_b, high_bits)
    up_m = wide_a[:, :, :slab].reshape(-1, width)
    down_m = wide_b.reshape(-1, width)
    wao = wide_a[:, :, slab:].transpose(1, 0, 2, 3).reshape(n_t - 1, local, width)
    wao = jnp.concatenate([w_attn_out[None], wao])
    up_t = dp_swap(up_m, 1)
    down_t = dp_swap(down_m, 1)
    b_all = jnp.stack(
        [b_up]
        + [x[cut + slab].astype(F32) + x[cut + slab + 1].astype(F32) for x in came]
    ).reshape(n_t, 2, spots, slab)
    b_mine = lax.dynamic_index_in_dim(b_all, core, 1, keepdims=False)
    b_theirs = lax.dynamic_index_in_dim(b_all, 1 - core, 1, keepdims=False)
    bup = jnp.stack([b_mine, b_theirs]).transpose(0, 2, 1, 3).reshape(2 * spots, 1, n_t * slab)

    ctx, ctxt, lse = attn_fwd(qt, k3, vt, lmt, n_sup - 1, n_sup, part)

    ctx_parts = [rows_of(ctx, ti * chunk, chunk)] + [
        shift(rows_of(ctx, lax.rem(ti + s, n_t) * chunk, chunk), n_t, s) for s in range(1, n_t)
    ]
    vec = jnp.stack([b_attn_out, gain_one, bias_one, b_down, gain_two, bias_two, b_down, b_down])
    coef = (2.0 * tokens / total_valid).reshape(1)
    (out_own, out_low, act, gb, first_low, grad_ffn, grad_attn, grad_resid, gctx_rel, vecs, gbup) = ffn(
        core.reshape(1),
        coef,
        ctx_parts,
        wao,
        rows_of(hidden, ti * chunk, chunk),
        rows_of(teacher, ti * chunk, chunk),
        lax.dynamic_slice_in_dim(valid_f, ti * chunk, chunk)[:, None],
        vec,
        bup,
        (up_own, up_m, up_t),
        (w_down, down_m, down_t),
        slab,
    )
    out_all = lax.all_gather(out_low, "tensor", axis=0, tiled=True)

    gctx = jnp.zeros((tokens, local), BF16)
    gctx = lax.dynamic_update_slice(gctx, gctx_rel[0], (ti * chunk, 0))
    for s in range(1, n_t):
        got = shift(gctx_rel[s], n_t, -s)
        gctx = lax.dynamic_update_slice(gctx, got, (lax.rem(ti + s, n_t) * chunk, 0))

    half = n_t * units // 2
    lead = (2,) * len(low_bits)
    send_up = dot_tn(gb[:, half:], first_low).astype(BF16).reshape(spots, n_t, slab, width)
    g_ao = jnp.stack([dot_tn(c, grad_attn) for c in ctx_parts]).astype(BF16)
    g_ao = g_ao.reshape(n_t, spots, piece, width).transpose(1, 0, 2, 3)
    send_a = jnp.concatenate([send_up, g_ao], axis=2)
    send_b = dot_tn(act[:, half:], grad_ffn).astype(BF16)
    got_a = dp_swap(send_a, 1)
    got_b = dp_swap(send_b, 1)
    keep_up = dot_tn(gb[:, :half], first_low).reshape(spots, n_t, slab, width)
    keep_a = jnp.concatenate([keep_up.astype(BF16), g_ao], axis=2)
    g_a = (keep_a.astype(F32) + got_a.astype(F32)).astype(BF16)
    g_b = (dot_tn(act[:, :half], grad_ffn) + got_b.astype(F32)).astype(BF16)
    gctx, g_a, g_b = lax.optimization_barrier((gctx, g_a, g_b))
    g_a = finish(narrow(g_a.reshape(lead + (n_t, cut, width)), low_bits))
    g_b = finish(narrow(g_b.reshape(lead + (n_t, slab, width)), high_bits))

    gqkv, glm = attn_bwd(gctx, ctxt, q3, k3, v3, qt, kt, lse, lmt)
    back = jnp.einsum("kte,kde->td", gqkv, w_qkv, preferred_element_type=F32)
    mine = (jnp.arange(n_t) == ti)[:, None, None]
    back = back.reshape(n_t, chunk, width) + jnp.where(mine, grad_resid[None], 0.0)
    grad_hidden = lax.psum(back.reshape(tokens, width).astype(BF16), "tensor").astype(F32)
    out_states = out_all.astype(F32)

    g_qkv_w = jnp.einsum("td,kte->kde", hidden, gqkv, preferred_element_type=F32).astype(BF16)
    slope = jax.nn.sigmoid((table + noise) * (-1.0 / SOFTENING)) * (1.0 / SOFTENING)
    g_mask = (glm * slope).astype(BF16)
    g_qkv_w = finish(narrow(g_qkv_w.reshape(lead + (2, -1, local)), [1] + low_bits))
    g_mask = finish(narrow(g_mask.reshape(lead + (2, -1, table.shape[2])), [1] + high_bits))
    g_qkv_w = spread(g_qkv_w, low_bits + [1])
    g_mask = spread(g_mask, high_bits + [1])

    total = jnp.concatenate([g_a, g_b], axis=1)
    summed = total[0].astype(F32)
    for s in range(1, n_t):
        summed = summed + shift(total[s], n_t, -s).astype(F32)
    summed = summed.astype(BF16)
    all_a = spread(summed[:cut], low_bits)
    all_b = spread(summed[cut:], high_bits)
    g_ao = all_a[:, slab:].reshape(local, width).astype(F32)
    pair = jnp.stack([all_a[:, :slab].reshape(-1, width), all_b.reshape(-1, width)])
    other = dp_swap(pair, 1)
    up = core == 1
    pair = jnp.concatenate([jnp.where(up, other, pair), jnp.where(up, pair, other)], axis=1)
    g_up = pair[0].T.astype(F32)
    g_down = pair[1].astype(F32)

    gbu = gbup.reshape(2, spots, n_t, slab)
    gbu = jnp.where(up, gbu[::-1], gbu).transpose(2, 0, 1, 3).reshape(n_t, units)
    gbu = gbu[jnp.stack([lax.rem(ti - z + n_t, n_t) for z in range(n_t)])]
    g_b_qv = jnp.sum(gqkv[0::2].astype(F32), axis=1)
    g_b_qv = jnp.where(mine, g_b_qv[None], 0.0)
    pack = jnp.concatenate([vecs[:7].reshape(-1), gbu.reshape(-1), g_b_qv.reshape(-1)]).reshape(-1, 128)
    pack = everyone(pack)
    bit = 1
    while bit < n_t:
        pack = pack + swap(pack, "tensor", n_t, bit)
        bit *= 2
    pack = pack.reshape(-1)
    rows = [pack[n * width : (n + 1) * width] for n in range(7)]
    gbu = lax.dynamic_slice_in_dim(pack, 7 * width + ti * units, units)
    g_b_qv = lax.dynamic_slice_in_dim(pack, 7 * width + n_t * units + ti * 2 * local, 2 * local)
    loss = jnp.sum(rows[6]) / (total_valid * width)
    return (
        out_states, loss, grad_hidden,
        g_qkv_w.reshape(w_qkv.shape).astype(F32), g_b_qv.reshape(2, local), g_ao, rows[0], rows[1], rows[2],
        g_up, gbu, g_down, rows[3], rows[4], rows[5],
        g_mask.reshape(table.shape).astype(F32),
    )


def solution(mesh):
    row, col = P("tensor", None), P(None, "tensor")
    heads = P("tensor", None, None)
    dp = P("dp", None)
    qkv = P(None, None, "tensor")
    sizes = dict(mesh.shape)
    return jax.shard_map(
        functools.partial(body, n_d=sizes["dp"], n_t=sizes["tensor"]),
        mesh=mesh,
        in_specs=(dp, dp, dp, qkv, col, row, P(), P(), P(), col, P("tensor"), row, P(), P(), P(), heads, heads),
        out_specs=(dp, P(), dp, qkv, col, row, P(), P(), P(), col, P("tensor"), row, P(), P(), P(), heads),
        check_vma=False,
    )
```

time: 653 us -> 524 us (0.80)
  waiting for transfers between devices: 268 us -> 185 us
  starting transfers between devices: 136 us -> 67.5 us
  Pallas kernels: 76.8 us -> 117 us
  local copies, waits for them, and re-layouts: 73 us -> 43.9 us
  matrix products: 45.1 us -> 30.2 us
  between operations: 7.19 us -> 19.7 us
  other arithmetic: 39.7 us -> 51.4 us
    ppermute x36 -> x12, starting transfers between devices: 82 us -> 21.6 us  [shift(): lax.ppermute(x, 'tensor', [(j, (j + amount) % size) for j in range(size)])]
    ppermute x59 -> x37, waiting for transfers between devices: 147 us -> 94.9 us  [swap(): return lax.ppermute(x, axis, [(j, j ^ bit) for j in range(size)])]
    pallas_call x1 -> x4, Pallas kernels: 36.3 us -> 76.6 us  [the longest x1 34.4 us: ffn(): pl.pallas_call(functools.partial(ffn_kernel, n_t, slab), in_specs=[sm, sm...]
    ppermute x36 -> x12, waiting for transfers between devices: 121 us -> 90.3 us  [shift(): lax.ppermute(x, 'tensor', [(j, (j + amount) % size) for j in range(size)])]
    dot_general x11 -> x1, matrix products: 29.1 us -> 6.95 us  [body(): back = jnp.einsum('kte,kde->td', gqkv, w_qkv, preferred_element_type=F32)]
    ppermute x59 -> x37, starting transfers between devices: 54.2 us -> 33.3 us  [swap(): return lax.ppermute(x, axis, [(j, j ^ bit) for j in range(size)])]
    unnamed x173 -> x94, local copies, waits for them, and re-layouts: 31.8 us -> 12.6 us
    convert_element_type x18 -> x17, other arithmetic: 6.26 us -> 22.4 us  [the longest x10 6.98 us: narrow(): x = (keep.astype(F32) + dp_swap(send, bit).astype(F32)).astype(BF16)]
  transfers between devices with their start and end apart: 95 -> 51, of which waited for: 42 -> 23; matrix products, arithmetic and copies ran while one was open for 18% -> 20% of each run, Pallas kernels for 12% -> 16%
where the time goes in v2:
time: 524 us; the launch traced here: 515 us
  waiting for transfers between devices  185 us (35%)
  Pallas kernels  117 us (22%)
  starting transfers between devices  67.5 us (13%)
  other arithmetic  51.4 us (10%)
  local copies, waits for them, and re-layouts  43.9 us (8%)
  matrix products  30.2 us (6%)
  between operations  19.7 us (4%)
    ppermute x37, waiting for transfers between devices, swap(): return lax.ppermute(x, axis, [(j, j ^ bit) for j in range(size)])  94.9 us
    ppermute x12, waiting for transfers between devices, shift(): lax.ppermute(x, 'tensor', [(j, (j + amount) % size) for j in range(size)])  90.3 us
    pallas_call x1, Pallas kernels, attn_bwd(): pl.pallas_call(attn_bwd_kernel, out_shape=(sd((3, tokens, width), BF16),...  40.6 us
    pallas_call x1, Pallas kernels, ffn(): pl.pallas_call(functools.partial(ffn_kernel, n_t, slab), in_specs=[sm, sm...  34.4 us
    ppermute x37, starting transfers between devices, swap(): return lax.ppermute(x, axis, [(j, j ^ bit) for j in range(size)])  33.3 us
    pallas_call x2, Pallas kernels, attn_fwd(): pl.pallas_call(functools.partial(attn_fwd_kernel, lo, len(prev)), grid=(h...  27.2 us
    ppermute x12, starting transfers between devices, shift(): lax.ppermute(x, 'tensor', [(j, (j + amount) % size) for j in range(size)])  21.6 us
    dot_general x8, matrix products, dot_tn(): lax.dot_general(a, b, (((0,), (0,)), ((), ())), preferred_element_type=F32)  18.3 us
  transfers between devices with their start and end apart: 51, of which 23 were waited for; matrix products, arithmetic and copies ran while one was open for 20% of the time, Pallas kernels for 16%

profile of v2, /device:TPU:0, one launch (start us, length us, event | category | flops | bytes accessed | tf_op | source)
XLA Modules:
  0.0 515.2 jit_solution(605528451640857251)
XLA Ops:
  11.4 3.1 collective-permute-start.3
  14.5 2.6 collective-permute-start.4
  20.7 15.0 %attn_prep.1 = (bf16[3,2048,64]{2,1,0:T(8,128)(2,1)}, bf16[3,2048,64]{2,1,0:T(8,128)(2,1)}, bf16[3,2048,64]{2,1,0:T(8,128)(2,1)}, bf16[192,2048]{1,0:T(8,128)(2,...) custom-call(bf16[2048,768]{1,0:T(8,128)(2,1)} %hid.1, ...), custom_call_target="tpu_custom_call" | custom-call | tf_op jit(solution)/shard_map/attn_prep/pallas_call | solution.py:71
  35.7 15.6 %attn_fwd.2 = (bf16[2048,192]{1,0:T(8,128)(2,1)}, f32[192,2048]{1,0:T(8,128)}, f32[8,2048]{1,0:T(8,128)}) custom-call(bf16[192,2048]{1,0:T(8,128)(2,1)} %get-tuple-element.50.qt, bf16[3,2048,64]{2,1,0:T(8,128)(2,1)} %get-tuple-element.51.k3, bf16[192,2048]{1,0:T(8,128)(2,1)} %get-tuple-element.52.vt, f32[3,512,512]{2,1,0:T(8,128)} %get-tuple-element.53.lmt), custom_call_target="tpu_custom_call" | custom-call | tf_op jit(solution)/shard_map/attn_fwd/pallas_call | solution.py:143
  56.7 7.1 %collective-permute-done.12 = bf16[3,96,768]{2,1,0:T(8,128)(2,1)} collective-permute-done((bf16[3,96,768]{2,1,0:T(8,128)(2,1)S(1)}, bf16[3,96,768]{2,1,0:T(8,128)(2,1)}, u32[]{:S(2)}, u32[]{:S(2)}) %collective-permute-start.12) | collective-permute-done | bytes 442400 | tf_op jit(solution)/shard_map/ppermute | solution.py:381
  67.4 5.7 %collective-permute-done.9 = bf16[3,144,768]{2,1,0:T(8,128)(2,1)S(1)} collective-permute-done((bf16[3,144,768]{2,1,0:T(8,128)(2,1)S(1)}, bf16[3,144,768]{2,1,0:T(8,128)(2,1)S(1)}, u32[]{:S(2)}, u32[]{:S(2)}) %collective-permute-start.9) | collective-permute-done | bytes 663584 | tf_op jit(solution)/shard_map/ppermute | solution.py:381
  74.5 15.3 %collective-permute-done.13 = bf16[2,3,96,768]{3,2,1,0:T(8,128)(2,1)} collective-permute-done((bf16[2,3,96,768]{3,2,1,0:T(8,128)(2,1)}, bf16[2,3,96,768]{3,2,1,0:T(8,128)(2,1)}, u32[]{:S(2)}, u32[]{:S(2)}) %collective-permute-start.13) | collective-permute-done | bytes 884768 | tf_op jit(solution)/shard_map/ppermute | solution.py:381
  92.6 7.5 %collective-permute-done.10 = bf16[2,3,144,768]{3,2,1,0:T(8,128)(2,1)} collective-permute-done((bf16[2,3,144,768]{3,2,1,0:T(8,128)(2,1)S(1)}, bf16[2,3,144,768]{3,2,1,0:T(8,128)(2,1)}, u32[]{:S(2)}, u32[]{:S(2)}) %collective-permute-start.10) | collective-permute-done | bytes 1327136 | tf_op jit(solution)/shard_map/ppermute | solution.py:381
  105.0 2.1 constant_dynamic-slice_fusion.4.refs_5_
  107.1 2.7 constant_dynamic-slice_fusion.3.refs_6_
  111.0 2.9 collective-permute-start.1
  122.2 11.7 %attn_fwd.3 = (bf16[2048,192]{1,0:T(8,128)(2,1)}, f32[192,2048]{1,0:T(8,128)}, f32[8,2048]{1,0:T(8,128)}) custom-call(bf16[192,2048]{1,0:T(8,128)(2,1)} %get-tuple-element.50.qt, bf16[3,2048,64]{2,1,0:T(8,128)(2,1)} %get-tuple-element.51.k3, bf16[192,2048]{1,0:T(8,128)(2,1)} %get-tuple-element.52.vt, ...), custom_call_target="tpu_custom_call", output_to_operand_aliasing={{0}: (4, {}), {1}: (5, {}), {2}: (6, {})} | custom-call | tf_op jit(solution)/shard_map/attn_fwd/pallas_call | solution.py:143
  137.7 2.2 collective-permute-start.8
  141.2 5.7 %collective-permute-done.6.refs_1_ = bf16[512,192]{1,0:T(8,128)(2,1)S(1)} collective-permute-done((bf16[512,192]{1,0:T(8,128)(2,1)S(1)}, bf16[512,192]{1,0:T(8,128)(2,1)S(1)}, u32[]{:S(2)}, u32[]{:S(2)}) %collective-permute-start.6) | collective-permute-done | bytes 196640 | tf_op jit(solution)/shard_map/ppermute | solution.py:377
  146.8 8.3 %collective-permute-done.7.refs_2_ = bf16[512,192]{1,0:T(8,128)(2,1)S(1)} collective-permute-done((bf16[512,192]{1,0:T(8,128)(2,1)S(1)}, bf16[512,192]{1,0:T(8,128)(2,1)S(1)}, u32[]{:S(2)}, u32[]{:S(2)}) %collective-permute-start.7) | collective-permute-done | bytes 196640 | tf_op jit(solution)/shard_map/ppermute | solution.py:377
  156.0 34.4 %ffn.1 = (f32[512,768]{1,0:T(8,128)}, bf16[512,768]{1,0:T(8,128)(2,1)}, bf16[512,3072]{1,0:T(8,128)(2,1)}, bf16[512,3072]{1,0:T(8,128)(2,1)}, bf16[512,768]{1,0:...) custom-call(s32[1]{0:T(128)} %bitcast.core, ...), custom_call_target="tpu_custom_call" | custom-call | tf_op jit(solution)/shard_map/ffn/pallas_call | solution.py:348
  191.9 3.1 convolution_convert_fusion.1
  196.6 2.0 pad_maximum_fusion
  200.3 2.9 convolution_convert_fusion
  204.1 6.0 %collective-permute-start.15 = (bf16[512,192]{1,0:T(8,128)(2,1)}, bf16[512,192]{1,0:T(8,128)(2,1)S(1)}, u32[]{:S(2)}, u32[]{:S(2)}) collective-permute-start(bf16[512,192]{1,0:T(8,128)(2,1)} %get-tuple-element.153), channel_id=1, source_target_pairs={{0,3},{1,0},{2,1},{3,2},{4,7},{5,4},{6,5},{7,6},{8,11},{9,8},{10,9... | collective-permute-start | bytes 589832 | tf_op jit(solution)/shard_map/ppermute | solution.py:377
  211.7 4.4 convolution_convert_fusion.2
  217.5 12.5 %all-reduce.2.cloned.1.call-start = ((), (), s32[]{:S(2)}) async-start(), calls=%async_computation.1 | async-start | bytes 6291456 | tf_op jit(solution)/shard_map/psum | solution.py:540
  230.1 21.4 %collective-permute-done.16 = bf16[512,192]{1,0:T(8,128)(2,1)S(1)} collective-permute-done((bf16[512,192]{1,0:T(8,128)(2,1)S(1)}, bf16[512,192]{1,0:T(8,128)(2,1)S(1)}, u32[]{:S(2)}, u32[]{:S(2)}) %collective-permute-start.16) | collective-permute-done | bytes 196640 | tf_op jit(solution)/shard_map/ppermute | solution.py:377
  251.6 5.4 %add_convert_fusion.1 = bf16[1536,768]{1,0:T(8,128)(2,1)} fusion(bf16[1536,768]{1,0:T(8,128)(2,1)} %collective-permute-done.19, bf16[512,768]{1,0:T(8,128)(2,1)S(1)} %copy-done.41, bf16[512,3072]{1,0:T(8,128)(2,1)} %get-tuple-element.71), kind=kOutput, calls=%fused_computation.5 | convolution fusion | flops 1211498496 | bytes 7077888 | tf_op jit(solution)/shard_map/dot_general | solution.py:28
  257.0 2.5 add_convert_fusion
  259.5 40.6 %attn_bwd.1 = (bf16[3,2048,192]{2,1,0:T(8,128)(2,1)}, f32[3,512,512]{2,1,0:T(8,128)}) custom-call(bf16[2048,192]{1,0:T(8,128)(2,1)} %copy-done.6, f32[192,2048]{1,0:T(8,128)} %get-tuple-element.74.ctxt, bf16[3,2048,64]{2,1,0:T(8,128)(2,1)} %get-tuple-element.75.q3, bf16[3,2048,64]{2,1,0:T(8,128)(2,1)} %get-tuple-element.51.k3, ...), custom_call_target="tpu_custom_call" | custom-call | tf_op jit(solution)/shard_map/attn_bwd/pallas_call | solution.py:224
  300.0 4.9 fusion.15
  304.9 2.3 copy.94
  312.1 5.1 multiply_convert_fusion
  319.5 2.4 collective-permute-done.21
  324.8 2.0 collective-permute-start.33
  337.1 6.9 %fusion.1 = bf16[2048,768]{1,0:T(8,128)(2,1)} fusion(f32[512,768]{1,0:T(8,128)} %get-tuple-element.80, pred[2048]{0:T(1024)(128)(4,1)S(1)} %bitcast.302, bf16[3,2048,192]{2,1,0:T(8,128)(2,1)} %get-tuple-element.79, bf16[3,768,192]{1,2,0:T(8,128)(2,1)} %param.20), kind=kOutput, calls=%fused_computation.4 | convolution fusion | flops 1816657920 | bytes 7964672 | tf_op jit(solution)/shard_map/kte,kde->td/dot_general | solution.py:537
  344.9 12.2 %collective-permute-done.27 = bf16[288,192]{1,0:T(8,128)(2,1)} collective-permute-done((bf16[288,192]{1,0:T(8,128)(2,1)}, bf16[288,192]{1,0:T(8,128)(2,1)}, u32[]{:S(2)}, u32[]{:S(2)}) %collective-permute-start.27) | collective-permute-done | bytes 110624 | tf_op jit(solution)/shard_map/ppermute | solution.py:381
  358.8 4.4 collective-permute-done.44
  368.6 8.7 %collective-permute-done.45 = bf16[192,512]{1,0:T(8,128)(2,1)S(1)} collective-permute-done((bf16[192,512]{1,0:T(8,128)(2,1)S(1)}, bf16[192,512]{1,0:T(8,128)(2,1)S(1)}, u32[]{:S(2)}, u32[]{:S(2)}) %collective-permute-start.45) | collective-permute-done | bytes 196640 | tf_op jit(solution)/shard_map/ppermute | solution.py:381
  377.4 2.1 collective-permute-start.46
  381.7 2.1 collective-permute-start.29
  386.9 3.0 collective-permute-done.34
  390.1 13.5 %collective-permute-done.32 = bf16[4,144,768]{2,1,0:T(8,128)(2,1)S(1)} collective-permute-done((bf16[4,144,768]{2,1,0:T(8,128)(2,1)S(1)}, bf16[4,144,768]{2,1,0:T(8,128)(2,1)S(1)}, u32[]{:S(2)}, u32[]{:S(2)}) %collective-permute-start.32) | collective-permute-done | bytes 884768 | tf_op jit(solution)/shard_map/ppermute | solution.py:381
  407.3 5.7 %collective-permute-done.35 = bf16[240,768]{1,0:T(8,128)(2,1)S(1)} collective-permute-done((bf16[240,768]{1,0:T(8,128)(2,1)S(1)}, bf16[240,768]{1,0:T(8,128)(2,1)S(1)}, u32[]{:S(2)}, u32[]{:S(2)}) %collective-permute-start.35) | collective-permute-done | bytes 368672 | tf_op jit(solution)/shard_map/ppermute | solution.py:377
  413.0 49.3 %collective-permute-done.36 = bf16[240,768]{1,0:T(8,128)(2,1)S(1)} collective-permute-done((bf16[240,768]{1,0:T(8,128)(2,1)S(1)}, bf16[240,768]{1,0:T(8,128)(2,1)S(1)}, u32[]{:S(2)}, u32[]{:S(2)}) %collective-permute-start.36) | collective-permute-done | bytes 368672 | tf_op jit(solution)/shard_map/ppermute | solution.py:377
  464.9 2.8 collective-permute-done.40
  471.8 2.7 collective-permute-done.41
  474.6 3.3 collective-permute-done.39
  483.5 5.1 convert_element_type.268
  489.2 2.0 copy.99
  492.9 2.0 copy.98
  494.9 5.1 convert_element_type.280
  (307 shorter events, 105.4 us)
Async XLA Ops:
  7.2 476.3 %all-gather.2.cloned.1.call-start = ((), (), s32[]{:S(2)}) async-start(), calls=%async_computation | async-start | bytes 3932160 | tf_op jit(solution)/shard_map/all_gather | solution.py:511
  11.4 39.8 %collective-permute-start.3 = (bf16[256,768]{1,0:T(8,128)(2,1)S(1)}, bf16[256,768]{1,0:T(8,128)(2,1)}, u32[]{:S(2)}, u32[]{:S(2)}) collective-permute-start(bf16[256,768]{1,0:T(8,128)(2,1)S(1)} %concatenate.43), channel_id=1, source_target_pairs={{0,1},{1,2},{2,3},{3,0},{4,5},{5,6},{6,7},{7,4},{8,9},{9,10},{10,1... | collective-permute-start | bytes 1179656 | tf_op jit(solution)/shard_map/ppermute | solution.py:377
  14.5 36.7 %collective-permute-start.4 = (bf16[256,768]{1,0:T(8,128)(2,1)S(1)}, bf16[256,768]{1,0:T(8,128)(2,1)S(1)}, u32[]{:S(2)}, u32[]{:S(2)}) collective-permute-start(bf16[256,768]{1,0:T(8,128)(2,1)S(1)} %concatenate.43), channel_id=1, source_target_pairs={{0,2},{1,3},{2,0},{3,1},{4,6},{5,7},{6,4},{7,5},{8,10},{9,11},{10,... | collective-permute-start | bytes 1179656 | tf_op jit(solution)/shard_map/ppermute | solution.py:377
  17.1 34.2 %collective-permute-start.5 = (bf16[256,768]{1,0:T(8,128)(2,1)S(1)}, bf16[256,768]{1,0:T(8,128)(2,1)S(1)}, u32[]{:S(2)}, u32[]{:S(2)}) collective-permute-start(bf16[256,768]{1,0:T(8,128)(2,1)S(1)} %concatenate.43), channel_id=1, source_target_pairs={{0,3},{1,0},{2,1},{3,2},{4,7},{5,4},{6,5},{7,6},{8,11},{9,8},{10,9... | collective-permute-start | bytes 1179656 | tf_op jit(solution)/shard_map/ppermute | solution.py:377
  52.5 11.2 %collective-permute-start.12 = (bf16[3,96,768]{2,1,0:T(8,128)(2,1)S(1)}, bf16[3,96,768]{2,1,0:T(8,128)(2,1)}, u32[]{:S(2)}, u32[]{:S(2)}) collective-permute-start(bf16[3,96,768]{2,1,0:T(8,128)(2,1)S(1)} %pad_maximum_fusion.14), channel_id=1, source_target_pairs={{0,16},{4,20},{8,24},{12,28},{16,0},{20,4},{24,8},{28,12},{1,17},{... | collective-permute-start | bytes 1327112 | tf_op jit(solution)/shard_map/ppermute | solution.py:381
  55.2 17.8 %collective-permute-start.9 = (bf16[3,144,768]{2,1,0:T(8,128)(2,1)S(1)}, bf16[3,144,768]{2,1,0:T(8,128)(2,1)S(1)}, u32[]{:S(2)}, u32[]{:S(2)}) collective-permute-start(bf16[3,144,768]{2,1,0:T(8,128)(2,1)S(1)} %pad_maximum_fusion.11), channel_id=1, source_target_pairs={{0,8},{4,12},{8,0},{12,4},{16,24},{20,28},{24,16},{28,20},{1,9},{5... | collective-permute-start | bytes 1990664 | tf_op jit(solution)/shard_map/ppermute | solution.py:381
  65.9 24.0 %collective-permute-start.13 = (bf16[2,3,96,768]{3,2,1,0:T(8,128)(2,1)}, bf16[2,3,96,768]{3,2,1,0:T(8,128)(2,1)}, u32[]{:S(2)}, u32[]{:S(2)}) collective-permute-start(bf16[2,3,96,768]{3,2,1,0:T(8,128)(2,1)} %pad_maximum_fusion.8), channel_id=1, source_target_pairs={{0,8},{4,12},{8,0},{12,4},{16,24},{20,28},{24,16},{28,20},{1,9},{5... | collective-permute-start | bytes 2654216 | tf_op jit(solution)/shard_map/ppermute | solution.py:381
  73.3 26.8 %collective-permute-start.10 = (bf16[2,3,144,768]{3,2,1,0:T(8,128)(2,1)S(1)}, bf16[2,3,144,768]{3,2,1,0:T(8,128)(2,1)}, u32[]{:S(2)}, u32[]{:S(2)}) collective-permute-start(bf16[2,3,144,768]{3,2,1,0:T(8,128)(2,1)S(1)} %pad_maximum_fusion.4), channel_id=1, source_target_pairs={{0,16},{4,20},{8,24},{12,28},{16,0},{20,4},{24,8},{28,12},{1,17},{... | collective-permute-start | bytes 3981320 | tf_op jit(solution)/shard_map/ppermute | solution.py:381
  74.5 35.3 %collective-permute-start = (f32[1,1]{1,0:T(1,128)}, f32[1,1]{1,0:T(1,128)}, u32[]{:S(2)}, u32[]{:S(2)}) collective-permute-start(f32[1,1]{1,0:T(1,128)} %bitcast.1), channel_id=1, source_target_pairs={{0,4},{4,0},{8,12},{12,8},{16,20},{20,16},{24,28},{28,24},{1,5},{5... | collective-permute-start | bytes 20 | tf_op jit(solution)/shard_map/ppermute | solution.py:381
  92.6 62.5 %collective-permute-start.14 = (bf16[1152,768]{1,0:T(8,128)(2,1)}, bf16[1152,768]{1,0:T(8,128)(2,1)}, u32[]{:S(2)}, u32[]{:S(2)}) collective-permute-start(bf16[1152,768]{1,0:T(8,128)(2,1)} %bitcast.29.refs_14_), channel_id=1, source_target_pairs={{0,4},{4,0},{8,12},{12,8},{16,20},{20,16},{24,28},{28,24},{1,5},{5... | collective-permute-start | bytes 5308424 | tf_op jit(solution)/shard_map/ppermute | solution.py:381
  103.3 51.9 %collective-permute-start.11 = (bf16[1152,768]{1,0:T(8,128)(2,1)}, bf16[1152,768]{1,0:T(8,128)(2,1)}, u32[]{:S(2)}, u32[]{:S(2)}) collective-permute-start(bf16[1152,768]{1,0:T(8,128)(2,1)} %bitcast.21.refs_11_), channel_id=1, source_target_pairs={{0,4},{4,0},{8,12},{12,8},{16,20},{20,16},{24,28},{28,24},{1,5},{5... | collective-permute-start | bytes 5308424 | tf_op jit(solution)/shard_map/ppermute | solution.py:381
  135.9 11.0 %collective-permute-start.6 = (bf16[512,192]{1,0:T(8,128)(2,1)S(1)}, bf16[512,192]{1,0:T(8,128)(2,1)S(1)}, u32[]{:S(2)}, u32[]{:S(2)}) collective-permute-start(bf16[512,192]{1,0:T(8,128)(2,1)S(1)} %get-tuple-element.156), channel_id=1, source_target_pairs={{0,1},{1,2},{2,3},{3,0},{4,5},{5,6},{6,7},{7,4},{8,9},{9,10},{10,1... | collective-permute-start | bytes 589832 | tf_op jit(solution)/shard_map/ppermute | solution.py:377
  137.6 17.6 %collective-permute-start.7 = (bf16[512,192]{1,0:T(8,128)(2,1)S(1)}, bf16[512,192]{1,0:T(8,128)(2,1)S(1)}, u32[]{:S(2)}, u32[]{:S(2)}) collective-permute-start(bf16[512,192]{1,0:T(8,128)(2,1)S(1)} %get-tuple-element.155), channel_id=1, source_target_pairs={{0,2},{1,3},{2,0},{3,1},{4,6},{5,7},{6,4},{7,5},{8,10},{9,11},{10,... | collective-permute-start | bytes 589832 | tf_op jit(solution)/shard_map/ppermute | solution.py:377
  137.7 17.5 %collective-permute-start.8 = (bf16[512,192]{1,0:T(8,128)(2,1)S(1)}, bf16[512,192]{1,0:T(8,128)(2,1)S(1)}, u32[]{:S(2)}, u32[]{:S(2)}) collective-permute-start(bf16[512,192]{1,0:T(8,128)(2,1)S(1)} %get-tuple-element.154), channel_id=1, source_target_pairs={{0,3},{1,0},{2,1},{3,2},{4,7},{5,4},{6,5},{7,6},{8,11},{9,8},{10,9... | collective-permute-start | bytes 589832 | tf_op jit(solution)/shard_map/ppermute | solution.py:377
  198.9 58.0 %collective-permute-start.18 = (bf16[4,4,144,768]{3,2,1,0:T(8,128)(2,1)}, bf16[4,4,144,768]{3,2,1,0:T(8,128)(2,1)}, u32[]{:S(2)}, u32[]{:S(2)}) collective-permute-start(bf16[4,4,144,768]{3,2,1,0:T(8,128)(2,1)} %pad_maximum_fusion), channel_id=1, source_target_pairs={{0,4},{4,0},{8,12},{12,8},{16,20},{20,16},{24,28},{28,24},{1,5},{5... | collective-permute-start | bytes 10616840 | tf_op jit(solution)/shard_map/ppermute | solution.py:381
  203.2 48.4 %collective-permute-start.19 = (bf16[1536,768]{1,0:T(8,128)(2,1)}, bf16[1536,768]{1,0:T(8,128)(2,1)}, u32[]{:S(2)}, u32[]{:S(2)}) collective-permute-start(bf16[1536,768]{1,0:T(8,128)(2,1)} %convolution_convert_fusion), channel_id=1, source_target_pairs={{0,4},{4,0},{8,12},{12,8},{16,20},{20,16},{24,28},{28,24},{1,5},{5... | collective-permute-start | bytes 7077896 | tf_op jit(solution)/shard_map/ppermute | solution.py:381
  204.1 26.0 %collective-permute-start.15 = (bf16[512,192]{1,0:T(8,128)(2,1)}, bf16[512,192]{1,0:T(8,128)(2,1)S(1)}, u32[]{:S(2)}, u32[]{:S(2)}) collective-permute-start(bf16[512,192]{1,0:T(8,128)(2,1)} %get-tuple-element.153), channel_id=1, source_target_pairs={{0,3},{1,0},{2,1},{3,2},{4,7},{5,4},{6,5},{7,6},{8,11},{9,8},{10,9... | collective-permute-start | bytes 589832 | tf_op jit(solution)/shard_map/ppermute | solution.py:377
  210.1 41.4 %collective-permute-start.16 = (bf16[512,192]{1,0:T(8,128)(2,1)S(1)}, bf16[512,192]{1,0:T(8,128)(2,1)S(1)}, u32[]{:S(2)}, u32[]{:S(2)}) collective-permute-start(bf16[512,192]{1,0:T(8,128)(2,1)S(1)} %get-tuple-element.152), channel_id=1, source_target_pairs={{0,2},{1,3},{2,0},{3,1},{4,6},{5,7},{6,4},{7,5},{8,10},{9,11},{10,... | collective-permute-start | bytes 589832 | tf_op jit(solution)/shard_map/ppermute | solution.py:377
  211.5 40.0 %collective-permute-start.17 = (bf16[512,192]{1,0:T(8,128)(2,1)S(1)}, bf16[512,192]{1,0:T(8,128)(2,1)S(1)}, u32[]{:S(2)}, u32[]{:S(2)}) collective-permute-start(bf16[512,192]{1,0:T(8,128)(2,1)S(1)} %get-tuple-element.151), channel_id=1, source_target_pairs={{0,1},{1,2},{2,3},{3,0},{4,5},{5,6},{6,7},{7,4},{8,9},{9,10},{10,1... | collective-permute-start | bytes 589832 | tf_op jit(solution)/shard_map/ppermute | solution.py:377
  217.5 277.4 %all-reduce.2.cloned.1.call-start = ((), (), s32[]{:S(2)}) async-start(), calls=%async_computation.1 | async-start | bytes 6291456 | tf_op jit(solution)/shard_map/psum | solution.py:540
  312.0 5.7 %collective-permute-start.20 = (f32[78,128]{1,0:T(8,128)S(1)}, f32[78,128]{1,0:T(8,128)S(1)}, u32[]{:S(2)}, u32[]{:S(2)}) collective-permute-start(f32[78,128]{1,0:T(8,128)S(1)} %maximum_bitcast_fusion.1), channel_id=1, source_target_pairs={{0,4},{4,0},{8,12},{12,8},{16,20},{20,16},{24,28},{28,24},{1,5},{5... | collective-permute-start | bytes 119816 | tf_op jit(solution)/shard_map/ppermute | solution.py:381
  317.2 4.7 collective-permute-start.25
  317.8 4.1 collective-permute-start.21
  319.4 15.5 %collective-permute-start.43 = (bf16[2,2,192,512]{3,2,1,0:T(8,128)(2,1)S(1)}, bf16[2,2,192,512]{3,2,1,0:T(8,128)(2,1)S(1)}, u32[]{:S(2)}, u32[]{:S(2)}) collective-permute-start(bf16[2,2,192,512]{3,2,1,0:T(8,128)(2,1)S(1)} %dynamic-slice_bitcast_fusion.3), channel_id=1, source_target_pairs={{0,4},{4,0},{8,12},{12,8},{16,20},{20,16},{24,28},{28,24},{1,5},{5... | collective-permute-start | bytes 2359304 | tf_op jit(solution)/shard_map/ppermute | solution.py:381
  321.9 5.0 collective-permute-start.22
  322.2 10.1 %collective-permute-start.26 = (bf16[2,288,192]{2,1,0:T(8,128)(2,1)S(1)}, bf16[2,288,192]{2,1,0:T(8,128)(2,1)S(1)}, u32[]{:S(2)}, u32[]{:S(2)}) collective-permute-start(bf16[2,288,192]{2,1,0:T(8,128)(2,1)S(1)} %dynamic-slice_bitcast_fusion.7), channel_id=1, source_target_pairs={{0,8},{4,12},{8,0},{12,4},{16,24},{20,28},{24,16},{28,20},{1,9},{5... | collective-permute-start | bytes 663560 | tf_op jit(solution)/shard_map/ppermute | solution.py:381
  324.8 40.7 %collective-permute-start.33 = (bf16[2,4,96,768]{3,2,1,0:T(8,128)(2,1)}, bf16[2,4,96,768]{3,2,1,0:T(8,128)(2,1)}, u32[]{:S(2)}, u32[]{:S(2)}) collective-permute-start(bf16[2,4,96,768]{3,2,1,0:T(8,128)(2,1)} %dynamic-slice_bitcast_fusion.1), channel_id=1, source_target_pairs={{0,16},{4,20},{8,24},{12,28},{16,0},{20,4},{24,8},{28,12},{1,17},{... | collective-permute-start | bytes 3538952 | tf_op jit(solution)/shard_map/ppermute | solution.py:381
  328.2 51.3 %collective-permute-start.31 = (bf16[2,4,144,768]{3,2,1,0:T(8,128)(2,1)}, bf16[2,4,144,768]{3,2,1,0:T(8,128)(2,1)}, u32[]{:S(2)}, u32[]{:S(2)}) collective-permute-start(bf16[2,4,144,768]{3,2,1,0:T(8,128)(2,1)} %dynamic-slice_bitcast_fusion), channel_id=1, source_target_pairs={{0,8},{4,12},{8,0},{12,4},{16,24},{20,28},{24,16},{28,20},{1,9},{5... | collective-permute-start | bytes 5308424 | tf_op jit(solution)/shard_map/ppermute | solution.py:381
  331.5 12.6 %collective-permute-start.24 = (f32[78,128]{1,0:T(8,128)}, f32[78,128]{1,0:T(8,128)}, u32[]{:S(2)}, u32[]{:S(2)}) collective-permute-start(f32[78,128]{1,0:T(8,128)} %add.285), channel_id=1, source_target_pairs={{0,2},{1,3},{2,0},{3,1},{4,6},{5,7},{6,4},{7,5},{8,10},{9,11},{10,... | collective-permute-start | bytes 119816 | tf_op jit(solution)/shard_map/ppermute | solution.py:381
  333.1 24.0 %collective-permute-start.27 = (bf16[288,192]{1,0:T(8,128)(2,1)}, bf16[288,192]{1,0:T(8,128)(2,1)}, u32[]{:S(2)}, u32[]{:S(2)}) collective-permute-start(bf16[288,192]{1,0:T(8,128)(2,1)} %dynamic-slice_bitcast_fusion.9), channel_id=1, source_target_pairs={{0,16},{4,20},{8,24},{12,28},{16,0},{20,4},{24,8},{28,12},{1,17},{... | collective-permute-start | bytes 331784 | tf_op jit(solution)/shard_map/ppermute | solution.py:381
  336.8 26.4 %collective-permute-start.44 = (bf16[2,192,512]{2,1,0:T(8,128)(2,1)}, bf16[2,192,512]{2,1,0:T(8,128)(2,1)}, u32[]{:S(2)}, u32[]{:S(2)}) collective-permute-start(bf16[2,192,512]{2,1,0:T(8,128)(2,1)} %dynamic-slice_bitcast_fusion.6), channel_id=1, source_target_pairs={{0,16},{4,20},{8,24},{12,28},{16,0},{20,4},{24,8},{28,12},{1,17},{... | collective-permute-start | bytes 1179656 | tf_op jit(solution)/shard_map/ppermute | solution.py:381
  358.2 23.4 %collective-permute-start.28 = (bf16[288,192]{1,0:T(8,128)(2,1)S(1)}, bf16[288,192]{1,0:T(8,128)(2,1)S(1)}, u32[]{:S(2)}, u32[]{:S(2)}) collective-permute-start(bf16[288,192]{1,0:T(8,128)(2,1)S(1)} %fusion.37), channel_id=1, source_target_pairs={{0,8},{4,12},{8,0},{12,4},{16,24},{20,28},{24,16},{28,20},{1,9},{5... | collective-permute-start | bytes 331784 | tf_op jit(solution)/shard_map/ppermute | solution.py:381
  364.4 12.9 %collective-permute-start.45 = (bf16[192,512]{1,0:T(8,128)(2,1)S(1)}, bf16[192,512]{1,0:T(8,128)(2,1)S(1)}, u32[]{:S(2)}, u32[]{:S(2)}) collective-permute-start(bf16[192,512]{1,0:T(8,128)(2,1)S(1)} %dynamic-slice_bitcast_fusion.8), channel_id=1, source_target_pairs={{0,8},{4,12},{8,0},{12,4},{16,24},{20,28},{24,16},{28,20},{1,9},{5... | collective-permute-start | bytes 589832 | tf_op jit(solution)/shard_map/ppermute | solution.py:381
  367.5 22.5 %collective-permute-start.34 = (bf16[4,96,768]{2,1,0:T(8,128)(2,1)S(1)}, bf16[4,96,768]{2,1,0:T(8,128)(2,1)S(1)}, u32[]{:S(2)}, u32[]{:S(2)}) collective-permute-start(bf16[4,96,768]{2,1,0:T(8,128)(2,1)S(1)} %dynamic-slice_bitcast_fusion.4), channel_id=1, source_target_pairs={{0,8},{4,12},{8,0},{12,4},{16,24},{20,28},{24,16},{28,20},{1,9},{5... | collective-permute-start | bytes 1769480 | tf_op jit(solution)/shard_map/ppermute | solution.py:381
  377.4 7.9 %collective-permute-start.46 = (bf16[192,512]{1,0:T(8,128)(2,1)S(1)}, bf16[192,512]{1,0:T(8,128)(2,1)S(1)}, u32[]{:S(2)}, u32[]{:S(2)}) collective-permute-start(bf16[192,512]{1,0:T(8,128)(2,1)S(1)} %fusion.29), channel_id=1, source_target_pairs={{0,16},{4,20},{8,24},{12,28},{16,0},{20,4},{24,8},{28,12},{1,17},{... | collective-permute-start | bytes 589832 | tf_op jit(solution)/shard_map/ppermute | solution.py:381
  381.5 22.1 %collective-permute-start.32 = (bf16[4,144,768]{2,1,0:T(8,128)(2,1)S(1)}, bf16[4,144,768]{2,1,0:T(8,128)(2,1)S(1)}, u32[]{:S(2)}, u32[]{:S(2)}) collective-permute-start(bf16[4,144,768]{2,1,0:T(8,128)(2,1)S(1)} %dynamic-slice_bitcast_fusion.2), channel_id=1, source_target_pairs={{0,16},{4,20},{8,24},{12,28},{16,0},{20,4},{24,8},{28,12},{1,17},{... | collective-permute-start | bytes 2654216 | tf_op jit(solution)/shard_map/ppermute | solution.py:381
  381.7 25.3 %collective-permute-start.29 = (bf16[2,288,192]{2,1,0:T(8,128)(2,1)S(1)}, bf16[2,288,192]{2,1,0:T(8,128)(2,1)S(1)}, u32[]{:S(2)}, u32[]{:S(2)}) collective-permute-start(bf16[2,288,192]{2,1,0:T(8,128)(2,1)S(1)} %pad_maximum_fusion.18), channel_id=1, source_target_pairs={{0,16},{4,20},{8,24},{12,28},{16,0},{20,4},{24,8},{28,12},{1,17},{... | collective-permute-start | bytes 663560 | tf_op jit(solution)/shard_map/ppermute | solution.py:381
  385.4 78.0 %collective-permute-start.47 = (bf16[2,192,512]{2,1,0:T(8,128)(2,1)S(1)}, bf16[2,192,512]{2,1,0:T(8,128)(2,1)S(1)}, u32[]{:S(2)}, u32[]{:S(2)}) collective-permute-start(bf16[2,192,512]{2,1,0:T(8,128)(2,1)S(1)} %pad_maximum_fusion.16), channel_id=1, source_target_pairs={{0,8},{4,12},{8,0},{12,4},{16,24},{20,28},{24,16},{28,20},{1,9},{5... | collective-permute-start | bytes 1179656 | tf_op jit(solution)/shard_map/ppermute | solution.py:381
  403.9 9.0 %collective-permute-start.35 = (bf16[240,768]{1,0:T(8,128)(2,1)S(1)}, bf16[240,768]{1,0:T(8,128)(2,1)S(1)}, u32[]{:S(2)}, u32[]{:S(2)}) collective-permute-start(bf16[240,768]{1,0:T(8,128)(2,1)S(1)} %get-tuple-element.144), channel_id=1, source_target_pairs={{0,3},{1,0},{2,1},{3,2},{4,7},{5,4},{6,5},{7,6},{8,11},{9,8},{10,9... | collective-permute-start | bytes 1105928 | tf_op jit(solution)/shard_map/ppermute | solution.py:377
  404.0 58.2 %collective-permute-start.36 = (bf16[240,768]{1,0:T(8,128)(2,1)S(1)}, bf16[240,768]{1,0:T(8,128)(2,1)S(1)}, u32[]{:S(2)}, u32[]{:S(2)}) collective-permute-start(bf16[240,768]{1,0:T(8,128)(2,1)S(1)} %get-tuple-element.146), channel_id=1, source_target_pairs={{0,2},{1,3},{2,0},{3,1},{4,6},{5,7},{6,4},{7,5},{8,10},{9,11},{10,... | collective-permute-start | bytes 1105928 | tf_op jit(solution)/shard_map/ppermute | solution.py:377
  405.0 57.2 %collective-permute-start.37 = (bf16[240,768]{1,0:T(8,128)(2,1)S(1)}, bf16[240,768]{1,0:T(8,128)(2,1)S(1)}, u32[]{:S(2)}, u32[]{:S(2)}) collective-permute-start(bf16[240,768]{1,0:T(8,128)(2,1)S(1)} %get-tuple-element.145), channel_id=1, source_target_pairs={{0,1},{1,2},{2,3},{3,0},{4,5},{5,6},{6,7},{7,4},{8,9},{9,10},{10,1... | collective-permute-start | bytes 1105928 | tf_op jit(solution)/shard_map/ppermute | solution.py:377
  407.2 81.4 %collective-permute-start.30 = (bf16[2,2,288,192]{3,2,1,0:T(8,128)(2,1)S(1)}, bf16[2,2,288,192]{3,2,1,0:T(8,128)(2,1)S(1)}, u32[]{:S(2)}, u32[]{:S(2)}) collective-permute-start(bf16[2,2,288,192]{3,2,1,0:T(8,128)(2,1)S(1)} %pad_maximum_fusion.12), channel_id=1, source_target_pairs={{0,4},{4,0},{8,12},{12,8},{16,20},{20,16},{24,28},{28,24},{1,5},{5... | collective-permute-start | bytes 1327112 | tf_op jit(solution)/shard_map/ppermute | solution.py:381
  462.5 5.2 %collective-permute-start.40 = (bf16[96,768]{1,0:T(8,128)(2,1)S(1)}, bf16[96,768]{1,0:T(8,128)(2,1)S(1)}, u32[]{:S(2)}, u32[]{:S(2)}) collective-permute-start(bf16[96,768]{1,0:T(8,128)(2,1)S(1)} %slice.206), channel_id=1, source_target_pairs={{0,16},{4,20},{8,24},{12,28},{16,0},{20,4},{24,8},{28,12},{1,17},{... | collective-permute-start | bytes 442376 | tf_op jit(solution)/shard_map/ppermute | solution.py:381
  463.5 6.0 %collective-permute-start.38 = (bf16[144,768]{1,0:T(8,128)(2,1)S(1)}, bf16[144,768]{1,0:T(8,128)(2,1)S(1)}, u32[]{:S(2)}, u32[]{:S(2)}) collective-permute-start(bf16[144,768]{1,0:T(8,128)(2,1)S(1)} %slice.200), channel_id=1, source_target_pairs={{0,8},{4,12},{8,0},{12,4},{16,24},{20,28},{24,16},{28,20},{1,9},{5... | collective-permute-start | bytes 663560 | tf_op jit(solution)/shard_map/ppermute | solution.py:381
  467.7 6.8 %collective-permute-start.41 = (bf16[2,96,768]{2,1,0:T(8,128)(2,1)S(1)}, bf16[2,96,768]{2,1,0:T(8,128)(2,1)S(1)}, u32[]{:S(2)}, u32[]{:S(2)}) collective-permute-start(bf16[2,96,768]{2,1,0:T(8,128)(2,1)S(1)} %pad_maximum_fusion.19), channel_id=1, source_target_pairs={{0,8},{4,12},{8,0},{12,4},{16,24},{20,28},{24,16},{28,20},{1,9},{5... | collective-permute-start | bytes 884744 | tf_op jit(solution)/shard_map/ppermute | solution.py:381
  469.6 8.4 %collective-permute-start.39 = (bf16[2,144,768]{2,1,0:T(8,128)(2,1)S(1)}, bf16[2,144,768]{2,1,0:T(8,128)(2,1)S(1)}, u32[]{:S(2)}, u32[]{:S(2)}) collective-permute-start(bf16[2,144,768]{2,1,0:T(8,128)(2,1)S(1)} %pad_maximum_fusion.15), channel_id=1, source_target_pairs={{0,16},{4,20},{8,24},{12,28},{16,0},{20,4},{24,8},{28,12},{1,17},{... | collective-permute-start | bytes 1327112 | tf_op jit(solution)/shard_map/ppermute | solution.py:381
  471.8 19.4 %collective-permute-start.48 = (bf16[2,2,192,512]{3,2,0,1:T(8,128)(2,1)}, bf16[2,2,192,512]{3,2,0,1:T(8,128)(2,1)}, u32[]{:S(2)}, u32[]{:S(2)}) collective-permute-start(bf16[2,2,192,512]{3,2,0,1:T(8,128)(2,1)} %pad_maximum_fusion.10), channel_id=1, source_target_pairs={{0,4},{4,0},{8,12},{12,8},{16,20},{20,16},{24,28},{28,24},{1,5},{5... | collective-permute-start | bytes 2359304 | tf_op jit(solution)/shard_map/ppermute | solution.py:381
  480.2 21.6 %collective-permute-start.42 = (bf16[2,384,768]{2,1,0:T(8,128)(2,1)}, bf16[2,384,768]{2,1,0:T(8,128)(2,1)}, u32[]{:S(2)}, u32[]{:S(2)}) collective-permute-start(bf16[2,384,768]{2,1,0:T(8,128)(2,1)} %pad_maximum_fusion.7), channel_id=1, source_target_pairs={{0,4},{4,0},{8,12},{12,8},{16,20},{20,16},{24,28},{28,24},{1,5},{5... | collective-permute-start | bytes 3538952 | tf_op jit(solution)/shard_map/ppermute | solution.py:381
  (45 other events, 288.4 us)
Sparse Core Ops, SparseCore 0:
  217.6 68.9 all-gather.1
  344.2 140.9 all-reduce.1

commit v3 on v2

--- a/solution.py
+++ b/solution.py
@@ -30,6 +30,10 @@
 
 def dot_tt(a, b):
     return lax.dot_general(a, b, (((0,), (1,)), ((), ())), preferred_element_type=F32)
+
+
+def cost(micros, moved):
+    return pl.CostEstimate(flops=int(micros * 1e9), transcendentals=0, bytes_accessed=moved)
 
 
 def prep_kernel(hid, w, b, bt, table, noise, q3, k3, v3, qt, kt, vt, lmt):
@@ -72,6 +76,7 @@
         prep_kernel,
         out_shape=(nat, nat, nat, tr, tr, tr, sd(table.shape, F32)),
         compiler_params=pltpu.CompilerParams(vmem_limit_bytes=56 << 20),
+        cost_estimate=cost(15, 20 << 20),
         name="attn_prep",
     )(hidden, w_qkv, b_qv, b_qv.T, table, noise)
 
@@ -152,12 +157,23 @@
         out_shape=(sd((tokens, width), BF16), sd((width, tokens), F32), sd((8, tokens), F32)),
         input_output_aliases={4 + n: n for n in range(len(prev))},
         compiler_params=pltpu.CompilerParams(vmem_limit_bytes=56 << 20),
+        cost_estimate=cost(1.5 * (hi * hi - lo * lo) / 2, 8 << 20),
         name="attn_fwd",
     )(qt, k3, vt, lmt, *prev)
 
 
-def attn_bwd_kernel(gctx, ctxt, q3, k3, v3, qt, kt, lse, lmt, gqkv, glm, gk, gv, g3, glmt):
+def attn_bwd_kernel(n_t, place, *refs):
+    pieces = refs[:n_t]
+    (ctxt, q3, k3, v3, qt, kt, lse, lmt, gqkv, glm, gk, gv, g3, glmt, gctx, sems) = refs[n_t:]
     heads, tokens, hd = q3.shape
+    chunk = tokens // n_t
+    copies = []
+    for s in range(n_t):
+        at = lax.rem(place[0] + s, n_t) * chunk
+        to = gctx.at[pl.ds(pl.multiple_of(at, chunk), chunk), :]
+        copies.append(pltpu.make_async_copy(pieces[s], to, sems.at[s]))
+    for cp in copies:
+        cp.start()
     period = lmt.shape[1]
     width = heads * hd
     coef = LOG2E / math.sqrt(hd)
@@ -167,6 +183,8 @@
     gk[...] = jnp.zeros(gk.shape, F32)
     gv[...] = jnp.zeros(gv.shape, F32)
     glmt[...] = jnp.zeros(glmt.shape, F32)
+    for cp in copies:
+        cp.wait()
 
     def per_q(i, _):
         qb = tokens // BLOCK - 1 - i
@@ -217,22 +235,28 @@
         glm[h] = jnp.transpose(glmt[h])
 
 
-def attn_bwd(gctx, ctxt, q3, k3, v3, qt, kt, lse, lmt):
+def attn_bwd(place, parts, ctxt, q3, k3, v3, qt, kt, lse, lmt):
     heads, tokens, hd = q3.shape
     width = heads * hd
+    n_t = len(parts)
     sd = jax.ShapeDtypeStruct
+    vm = pl.BlockSpec(memory_space=pltpu.VMEM)
     return pl.pallas_call(
-        attn_bwd_kernel,
+        functools.partial(attn_bwd_kernel, n_t),
+        in_specs=[pl.BlockSpec(memory_space=pltpu.SMEM)] + [pl.BlockSpec(memory_space=pl.ANY)] * n_t + [vm] * 8,
         out_shape=(sd((3, tokens, width), BF16), sd(lmt.shape, F32)),
         scratch_shapes=[
             pltpu.VMEM((heads, tokens, hd), F32),
             pltpu.VMEM((heads, tokens, hd), F32),
             pltpu.VMEM((heads, BLOCK, hd), BF16),
             pltpu.VMEM(lmt.shape, F32),
+            pltpu.VMEM((tokens, width), BF16),
+            pltpu.SemaphoreType.DMA((n_t,)),
         ],
         compiler_params=pltpu.CompilerParams(vmem_limit_bytes=56 << 20),
+        cost_estimate=cost(40, 20 << 20),
         name="attn_bwd",
-    )(gctx, ctxt, q3, k3, v3, qt, kt, lse, lmt)
+    )(place, *parts, ctxt, q3, k3, v3, qt, kt, lse, lmt)
 
 
 def norm_parts(resid):
@@ -251,7 +275,7 @@
 
 
 def ffn_kernel(
-    n_t, slab, core, coef, *refs
+    n_t, slab, core, *refs
 ):
     ctx = refs[:n_t]
     (wao, hid, teach, valid, vec, bup, up_o, up_m, up_t, dn_o, dn_m, dn_t,
@@ -300,12 +324,12 @@
     out_low[...] = own.astype(BF16)
     residue = own - teach[...]
     weighed = valid[...] * residue
-    grad_out = coef[0] * weighed
+    grad_out = weighed
     total = lambda x: jnp.sum(x, axis=0, keepdims=True)
-    vecs[...] = jnp.zeros(vecs.shape, F32)
     vecs[4:5, :] = total(grad_out * xhat2)
     vecs[5:6, :] = total(grad_out)
     vecs[6:7, :] = total(weighed * residue)
+    vecs[7:8, :] = jnp.broadcast_to(jnp.sum(valid[...], axis=0, keepdims=True), (1, width))
     grad_second = norm_back(grad_out, xhat2, rstd2, g2)
     grad_resid[...] = grad_second
     low = grad_second.astype(BF16)
@@ -334,7 +358,7 @@
         gctx[s] = dot_nt(low, wao[s]).astype(BF16)
 
 
-def ffn(core, coef, ctx, wao, hid, teach, valid, vec, bup, ups, downs, slab):
+def ffn(core, ctx, wao, hid, teach, valid, vec, bup, ups, downs, slab):
     n_t = len(ctx)
     chunk, width = hid.shape
     local = ctx[0].shape[1]
@@ -347,7 +371,7 @@
     hbm = pl.BlockSpec(memory_space=pl.ANY)
     return pl.pallas_call(
         functools.partial(ffn_kernel, n_t, slab),
-        in_specs=[sm, sm] + [vm] * (n_t + 6) + [hbm] * 6,
+        in_specs=[sm] + [vm] * (n_t + 6) + [hbm] * 6,
         out_shape=(
             sd((chunk, width), F32),
             sd((chunk, width), BF16),
@@ -369,8 +393,9 @@
             pltpu.SemaphoreType.DMA((8 * spots,)),
         ],
         compiler_params=pltpu.CompilerParams(vmem_limit_bytes=56 << 20),
+        cost_estimate=cost(34, 25 << 20),
         name="ffn",
-    )(core, coef, *ctx, wao, hid, teach, valid, vec, bup, *ups, *downs)
+    )(core, *ctx, wao, hid, teach, valid, vec, bup, *ups, *downs)
 
 
 def shift(x, size, amount):
@@ -418,15 +443,23 @@
             bit *= 2
         return x
 
-    def spread(x, bits):
+    def spread(x, bits, other=None):
         done = []
         for bit in bits:
-            other = dp_swap(x, bit)
+            if done or other is None:
+                other = dp_swap(x, bit)
             up = bit_of(bit) == 1
             pos = sum(1 for b in done if b > bit)
             x = jnp.stack([jnp.where(up, other, x), jnp.where(up, x, other)], axis=pos)
             done.append(bit)
         return x.reshape((-1,) + x.shape[len(done) :])
+
+    def narrow_start(x, bits):
+        ax = sorted(bits, reverse=True).index(bits[0])
+        up = bit_of(bits[0])
+        send = lax.dynamic_index_in_dim(x, 1 - up, ax, keepdims=False)
+        keep = lax.dynamic_index_in_dim(x, up, ax, keepdims=False)
+        return keep, dp_swap(send, bits[0])
 
     def narrow(x, bits):
         left = sorted(bits, reverse=True)
@@ -439,13 +472,31 @@
             x = (keep.astype(F32) + dp_swap(send, bit).astype(F32)).astype(BF16)
         return x
 
+    def quad_parts(x):
+        return [lax.dynamic_index_in_dim(x, spot ^ r, 0, keepdims=False) for r in range(spots)]
+
+    def quad_sum(x):
+        pieces = quad_parts(x)
+        total = pieces[0].astype(F32)
+        for r in range(1, spots):
+            total = total + dp_swap(pieces[r], 2 * r).astype(F32)
+        return total.astype(BF16)
+
+    def quad_gather(x):
+        held = [x] + [dp_swap(x, 2 * r) for r in range(1, spots)]
+        step = 1
+        while step < spots:
+            flip = bit_of(2 * step) == 1
+            held = [jnp.where(flip, held[r ^ step], held[r]) for r in range(spots)]
+            step *= 2
+        return held
+
     def finish(x):
         for bit in extra:
             x = (x.astype(F32) + dp_swap(x, bit).astype(F32)).astype(BF16)
         return x
 
     valid_f = valid[0].astype(F32)
-    total_valid = everyone(jnp.sum(valid_f).reshape(1, 1))[0, 0]
 
     up_own = w_up.T
     b_hi = b_up.astype(BF16)
@@ -465,14 +516,24 @@
 
     q3, k3, v3, qt, kt, vt, lmt = attn_prep(hidden, w_qkv, b_qv, table, noise)
     n_sup = tokens // lmt.shape[1]
-    part = attn_fwd(qt, k3, vt, lmt, 0, n_sup - 1)
+    cuts = [max(n_sup - 2, 1), max(n_sup - 1, 2)]
+    part = attn_fwd(qt, k3, vt, lmt, 0, cuts[0])
     part, came = lax.optimization_barrier((part, came))
 
     cut = slab + piece
     wide_a = jnp.stack([x[:cut] for x in came])
     wide_b = jnp.stack([x[cut : cut + slab] for x in came])
-    wide_a = spread(wide_a, low_bits)
-    wide_b = spread(wide_b, high_bits)
+    first_a = dp_swap(wide_a, low_bits[0])
+    first_b = dp_swap(wide_b, high_bits[0])
+    part = attn_fwd(qt, k3, vt, lmt, cuts[0], cuts[1], part)
+    part, first_a, first_b = lax.optimization_barrier((part, first_a, first_b))
+    ctx, ctxt, lse = attn_fwd(qt, k3, vt, lmt, cuts[1], n_sup, part)
+    wide_a = spread(wide_a, low_bits, first_a)
+    wide_b = spread(wide_b, high_bits, first_b)
+    ctx_parts = [rows_of(ctx, ti * chunk, chunk)] + [
+        shift(rows_of(ctx, lax.rem(ti + s, n_t) * chunk, chunk), n_t, s) for s in range(1, n_t)
+    ]
+    *ctx_parts, wide_a, wide_b = lax.optimization_barrier((*ctx_parts, wide_a, wide_b))
     up_m = wide_a[:, :, :slab].reshape(-1, width)
     down_m = wide_b.reshape(-1, width)
     wao = wide_a[:, :, slab:].transpose(1, 0, 2, 3).reshape(n_t - 1, local, width)
@@ -487,16 +548,9 @@
     b_theirs = lax.dynamic_index_in_dim(b_all, 1 - core, 1, keepdims=False)
     bup = jnp.stack([b_mine, b_theirs]).transpose(0, 2, 1, 3).reshape(2 * spots, 1, n_t * slab)
 
-    ctx, ctxt, lse = attn_fwd(qt, k3, vt, lmt, n_sup - 1, n_sup, part)
-
-    ctx_parts = [rows_of(ctx, ti * chunk, chunk)] + [
-        shift(rows_of(ctx, lax.rem(ti + s, n_t) * chunk, chunk), n_t, s) for s in range(1, n_t)
-    ]
     vec = jnp.stack([b_attn_out, gain_one, bias_one, b_down, gain_two, bias_two, b_down, b_down])
-    coef = (2.0 * tokens / total_valid).reshape(1)
     (out_own, out_low, act, gb, first_low, grad_ffn, grad_attn, grad_resid, gctx_rel, vecs, gbup) = ffn(
         core.reshape(1),
-        coef,
         ctx_parts,
         wao,
         rows_of(hidden, ti * chunk, chunk),
@@ -510,11 +564,21 @@
     )
     out_all = lax.all_gather(out_low, "tensor", axis=0, tiled=True)
 
-    gctx = jnp.zeros((tokens, local), BF16)
-    gctx = lax.dynamic_update_slice(gctx, gctx_rel[0], (ti * chunk, 0))
-    for s in range(1, n_t):
-        got = shift(gctx_rel[s], n_t, -s)
-        gctx = lax.dynamic_update_slice(gctx, got, (lax.rem(ti + s, n_t) * chunk, 0))
+    parts = [gctx_rel[0]] + [shift(gctx_rel[s], n_t, -s) for s in range(1, n_t)]
+    parts[1], gb, act, first_low, grad_ffn, grad_attn = lax.optimization_barrier(
+        (parts[1], gb, act, first_low, grad_ffn, grad_attn)
+    )
+
+    up = core == 1
+    gbu = gbup.reshape(2, spots, n_t, slab)
+    gbu = jnp.where(up, gbu[::-1], gbu).transpose(2, 0, 1, 3).reshape(n_t, units)
+    gbu = gbu[jnp.stack([lax.rem(ti - z + n_t, n_t) for z in range(n_t)])]
+    pack = jnp.concatenate([vecs.reshape(-1), gbu.reshape(-1)]).reshape(-1, 128)
+    pack = everyone(pack)
+    bit = 1
+    while bit < n_t:
+        pack = pack + swap(pack, "tensor", n_t, bit)
+        bit *= 2
 
     half = n_t * units // 2
     lead = (2,) * len(low_bits)
@@ -525,66 +589,69 @@
     send_b = dot_tn(act[:, half:], grad_ffn).astype(BF16)
     got_a = dp_swap(send_a, 1)
     got_b = dp_swap(send_b, 1)
+    parts[3], gb, act = lax.optimization_barrier((parts[3], gb, act))
     keep_up = dot_tn(gb[:, :half], first_low).reshape(spots, n_t, slab, width)
     keep_a = jnp.concatenate([keep_up.astype(BF16), g_ao], axis=2)
     g_a = (keep_a.astype(F32) + got_a.astype(F32)).astype(BF16)
     g_b = (dot_tn(act[:, :half], grad_ffn) + got_b.astype(F32)).astype(BF16)
-    gctx, g_a, g_b = lax.optimization_barrier((gctx, g_a, g_b))
-    g_a = finish(narrow(g_a.reshape(lead + (n_t, cut, width)), low_bits))
-    g_b = finish(narrow(g_b.reshape(lead + (n_t, slab, width)), high_bits))
-
-    gqkv, glm = attn_bwd(gctx, ctxt, q3, k3, v3, qt, kt, lse, lmt)
+    parts[2], g_a, g_b, pack = lax.optimization_barrier((parts[2], g_a, g_b, pack))
+    a_keep, a_came = narrow_start(g_a.reshape(lead + (n_t, cut, width)), low_bits)
+    b_keep, b_came = narrow_start(g_b.reshape(lead + (n_t, slab, width)), high_bits)
+
+    gqkv, glm = attn_bwd(ti.reshape(1), parts, ctxt, q3, k3, v3, qt, kt, lse, lmt)
     back = jnp.einsum("kte,kde->td", gqkv, w_qkv, preferred_element_type=F32)
     mine = (jnp.arange(n_t) == ti)[:, None, None]
     back = back.reshape(n_t, chunk, width) + jnp.where(mine, grad_resid[None], 0.0)
-    grad_hidden = lax.psum(back.reshape(tokens, width).astype(BF16), "tensor").astype(F32)
+    back = back.reshape(tokens, width).astype(BF16)
+    grad_hidden = lax.psum(back, "tensor")
+    gqkv, glm, a_keep, a_came, b_keep, b_came, _ = lax.optimization_barrier(
+        (gqkv, glm, a_keep, a_came, b_keep, b_came, back)
+    )
+    g_a = finish(narrow((a_keep.astype(F32) + a_came.astype(F32)).astype(BF16), low_bits[1:]))
+    g_b = finish(narrow((b_keep.astype(F32) + b_came.astype(F32)).astype(BF16), high_bits[1:]))
+
+    g_qkv_w = [dot_tn(hidden, gqkv[n]).astype(BF16) for n in range(3)]
+    slope = jax.nn.sigmoid((table + noise) * (-1.0 / SOFTENING)) * (1.0 / SOFTENING)
+    g_mask = (glm * slope).astype(BF16).reshape(2, -1, table.shape[2])
+    tail = jnp.concatenate([g_mask[0], g_mask[1]] + g_qkv_w, axis=1)
+    tail = tail.reshape(2, spots, -1, tail.shape[1])
+    send = lax.dynamic_index_in_dim(tail, 1 - core, 0, keepdims=False)
+    keep = lax.dynamic_index_in_dim(tail, core, 0, keepdims=False)
+    tail = (keep.astype(F32) + dp_swap(send, 1).astype(F32)).astype(BF16)
+    tail = jnp.concatenate(quad_gather(finish(quad_sum(tail))))
+    other = dp_swap(tail, 1)
+    tail = jnp.concatenate([jnp.where(up, other, tail), jnp.where(up, tail, other)])
+    cols = table.shape[2]
+    g_mask = jnp.stack([tail[:, :cols], tail[:, cols : 2 * cols]])
+    g_qkv_w = jnp.stack([tail[:, 2 * cols + n * local : 2 * cols + (n + 1) * local] for n in range(3)])
+    g_b_qv = everyone(jnp.sum(gqkv[0::2].astype(F32), axis=1))
+
+    g_a, g_b, out_all = lax.optimization_barrier((g_a, g_b, out_all))
     out_states = out_all.astype(F32)
-
-    g_qkv_w = jnp.einsum("td,kte->kde", hidden, gqkv, preferred_element_type=F32).astype(BF16)
-    slope = jax.nn.sigmoid((table + noise) * (-1.0 / SOFTENING)) * (1.0 / SOFTENING)
-    g_mask = (glm * slope).astype(BF16)
-    g_qkv_w = finish(narrow(g_qkv_w.reshape(lead + (2, -1, local)), [1] + low_bits))
-    g_mask = finish(narrow(g_mask.reshape(lead + (2, -1, table.shape[2])), [1] + high_bits))
-    g_qkv_w = spread(g_qkv_w, low_bits + [1])
-    g_mask = spread(g_mask, high_bits + [1])
-
     total = jnp.concatenate([g_a, g_b], axis=1)
     summed = total[0].astype(F32)
     for s in range(1, n_t):
         summed = summed + shift(total[s], n_t, -s).astype(F32)
     summed = summed.astype(BF16)
-    all_a = spread(summed[:cut], low_bits)
-    all_b = spread(summed[cut:], high_bits)
-    g_ao = all_a[:, slab:].reshape(local, width).astype(F32)
-    pair = jnp.stack([all_a[:, :slab].reshape(-1, width), all_b.reshape(-1, width)])
+    held = quad_gather(summed)
+    g_ao = jnp.concatenate([x[slab:cut] for x in held])
+    pair = jnp.stack([jnp.concatenate([x[:slab] for x in held]), jnp.concatenate([x[cut:] for x in held])])
     other = dp_swap(pair, 1)
-    up = core == 1
     pair = jnp.concatenate([jnp.where(up, other, pair), jnp.where(up, pair, other)], axis=1)
-    g_up = pair[0].T.astype(F32)
-    g_down = pair[1].astype(F32)
-
-    gbu = gbup.reshape(2, spots, n_t, slab)
-    gbu = jnp.where(up, gbu[::-1], gbu).transpose(2, 0, 1, 3).reshape(n_t, units)
-    gbu = gbu[jnp.stack([lax.rem(ti - z + n_t, n_t) for z in range(n_t)])]
-    g_b_qv = jnp.sum(gqkv[0::2].astype(F32), axis=1)
-    g_b_qv = jnp.where(mine, g_b_qv[None], 0.0)
-    pack = jnp.concatenate([vecs[:7].reshape(-1), gbu.reshape(-1), g_b_qv.reshape(-1)]).reshape(-1, 128)
-    pack = everyone(pack)
-    bit = 1
-    while bit < n_t:
-        pack = pack + swap(pack, "tensor", n_t, bit)
-        bit *= 2
+    g_up = pair[0].T
+    g_down = pair[1]
+
     pack = pack.reshape(-1)
-    rows = [pack[n * width : (n + 1) * width] for n in range(7)]
-    gbu = lax.dynamic_slice_in_dim(pack, 7 * width + ti * units, units)
-    g_b_qv = lax.dynamic_slice_in_dim(pack, 7 * width + n_t * units + ti * 2 * local, 2 * local)
+    rows = [pack[n * width : (n + 1) * width] for n in range(8)]
+    gbu = lax.dynamic_slice_in_dim(pack, 8 * width + ti * units, units)
+    total_valid = rows[7][0]
     loss = jnp.sum(rows[6]) / (total_valid * width)
-    return (
-        out_states, loss, grad_hidden,
-        g_qkv_w.reshape(w_qkv.shape).astype(F32), g_b_qv.reshape(2, local), g_ao, rows[0], rows[1], rows[2],
-        g_up, gbu, g_down, rows[3], rows[4], rows[5],
-        g_mask.reshape(table.shape).astype(F32),
-    )
+    coef = 2.0 * tokens / total_valid
+    grads = [
+        grad_hidden, g_qkv_w.reshape(w_qkv.shape), g_b_qv.reshape(2, local), g_ao, rows[0], rows[1], rows[2],
+        g_up, gbu, g_down, rows[3], rows[4], rows[5], g_mask.reshape(table.shape),
+    ]
+    return (out_states, loss, *[g.astype(F32) * coef for g in grads])
 
 
 def solution(mesh):

time: 524 us -> 485 us (0.926)
  waiting for transfers between devices: 185 us -> 136 us
  local copies, waits for them, and re-layouts: 43.9 us -> 59.5 us
  matrix products: 30.2 us -> 20.6 us
    ppermute x37 -> x32, waiting for transfers between devices: 94.9 us -> 41.2 us  [swap(): return lax.ppermute(x, axis, [(j, j ^ bit) for j in range(size)])]
    psum x1, waiting for transfers between devices: 0.01 us -> 38.8 us  [body(): grad_hidden = lax.psum(back, 'tensor')]
    ppermute x12, waiting for transfers between devices: 90.3 us -> 56 us  [shift(): lax.ppermute(x, 'tensor', [(j, (j + amount) % size) for j in range(size)])]
    ppermute x12, starting transfers between devices: 21.6 us -> 43.4 us  [shift(): lax.ppermute(x, 'tensor', [(j, (j + amount) % size) for j in range(size)])]
    mul x0 -> x8, other arithmetic: none -> 14 us  [body(): return (out_states, loss, *[g.astype(F32) * coef for g in grads])]
    psum x1, starting transfers between devices: 12.5 us -> 0.04 us  [body(): grad_hidden = lax.psum(back, 'tensor')]
    ppermute x37 -> x32, starting transfers between devices: 33.3 us -> 25.2 us  [swap(): return lax.ppermute(x, axis, [(j, j ^ bit) for j in range(size)])]
    concatenate x0 -> x6, local copies, waits for them, and re-layouts: none -> 8.1 us  [the longest x4 6.52 us: body(): tail = jnp.concatenate([g_mask[0], g_mask[1]] + g_qkv_w, axis=1)]
  transfers between devices with their start and end apart: 51 -> 46, of which waited for: 23 -> 18; matrix products, arithmetic and copies ran while one was open for 20% -> 22% of each run, Pallas kernels for 16% -> 18%
where the time goes in v3:
time: 485 us; the launch traced here: 478 us
  waiting for transfers between devices  136 us (28%)
  Pallas kernels  121 us (25%)
  starting transfers between devices  68.7 us (14%)
  local copies, waits for them, and re-layouts  59.5 us (12%)
  other arithmetic  54.1 us (11%)
  matrix products  20.6 us (4%)
  between operations  18.6 us (4%)
    ppermute x12, waiting for transfers between devices, shift(): lax.ppermute(x, 'tensor', [(j, (j + amount) % size) for j in range(size)])  56 us
    ppermute x12, starting transfers between devices, shift(): lax.ppermute(x, 'tensor', [(j, (j + amount) % size) for j in range(size)])  43.4 us
    ppermute x32, waiting for transfers between devices, swap(): return lax.ppermute(x, axis, [(j, j ^ bit) for j in range(size)])  41.2 us
    pallas_call x1, Pallas kernels, attn_bwd(): pl.pallas_call(functools.partial(attn_bwd_kernel, n_t), in_specs=[pl.Bloc...  40.8 us
    psum x1, waiting for transfers between devices, body(): grad_hidden = lax.psum(back, 'tensor')  38.8 us
    pallas_call x1, Pallas kernels, ffn(): pl.pallas_call(functools.partial(ffn_kernel, n_t, slab), in_specs=[sm] +...  34 us
    pallas_call x3, Pallas kernels, attn_fwd(): pl.pallas_call(functools.partial(attn_fwd_kernel, lo, len(prev)), grid=(h...  30.8 us
    ppermute x32, starting transfers between devices, swap(): return lax.ppermute(x, axis, [(j, j ^ bit) for j in range(size)])  25.2 us
  transfers between devices with their start and end apart: 46, of which 18 were waited for; matrix products, arithmetic and copies ran while one was open for 22% of the time, Pallas kernels for 18%

profile of v3, /device:TPU:0, one launch (start us, length us, event | category | flops | bytes accessed | tf_op | source)
XLA Modules:
  0.0 478.2 jit_solution(6118820493844407976)
XLA Ops:
  11.4 3.1 collective-permute-start
  14.5 2.6 collective-permute-start.1
  20.7 15.0 %attn_prep.1 = (bf16[3,2048,64]{2,1,0:T(8,128)(2,1)}, bf16[3,2048,64]{2,1,0:T(8,128)(2,1)}, bf16[3,2048,64]{2,1,0:T(8,128)(2,1)}, bf16[192,2048]{1,0:T(8,128)(2,...) custom-call(bf16[2048,768]{1,0:T(8,128)(2,1)} %hid.1, ...), custom_call_target="tpu_custom_call" | custom-call | flops 15000000512 | bytes 20971520 | tf_op jit(solution)/shard_map/attn_prep/pallas_call | solution.py:75
  35.7 9.5 %attn_fwd.3 = (bf16[2048,192]{1,0:T(8,128)(2,1)}, f32[192,2048]{1,0:T(8,128)}, f32[8,2048]{1,0:T(8,128)}) custom-call(bf16[192,2048]{1,0:T(8,128)(2,1)} %get-tuple-element.83.qt.refs_8_, bf16[3,2048,64]{2,1,0:T(8,128)(2,1)} %get-tuple-element.84.k3.refs_6_, bf16[192,2048]{1,0:T(8,128)(2,1)} %get-tuple-element.85.vt, ...), custom_call_target="tpu_custom_call" | custom-call | flops 3000000000 | bytes 8388608 | tf_op jit(solution)/shard_map/attn_fwd/pallas_call | solution.py:148
  51.2 9.6 %attn_fwd.4 = (bf16[2048,192]{1,0:T(8,128)(2,1)}, f32[192,2048]{1,0:T(8,128)}, f32[8,2048]{1,0:T(8,128)}) custom-call(bf16[192,2048]{1,0:T(8,128)(2,1)} %get-tuple-element.83.qt.refs_8_, bf16[3,2048,64]{2,1,0:T(8,128)(2,1)} %get-tuple-element.84.k3.refs_6_, ...), custom_call_target="tpu_custom_call", output_to_operand_aliasing={{0}: (4, {}), {1}: (5, {}), {2}: (6, {})} | custom-call | flops 3750000128 | bytes 8388608 | tf_op jit(solution)/shard_map/attn_fwd/pallas_call | solution.py:148
  60.8 2.1 collective-permute-done.3
  68.4 11.7 %attn_fwd.5 = (bf16[2048,192]{1,0:T(8,128)(2,1)}, f32[192,2048]{1,0:T(8,128)}, f32[8,2048]{1,0:T(8,128)}) custom-call(bf16[192,2048]{1,0:T(8,128)(2,1)} %get-tuple-element.83.qt.refs_8_, bf16[3,2048,64]{2,1,0:T(8,128)(2,1)} %get-tuple-element.84.k3.refs_6_, ...), custom_call_target="tpu_custom_call", output_to_operand_aliasing={{0}: (4, {}), {1}: (5, {}), {2}: (6, {})} | custom-call | flops 5249999872 | bytes 8388608 | tf_op jit(solution)/shard_map/attn_fwd/pallas_call | solution.py:148
  82.0 6.7 %collective-permute-start.5 = (bf16[512,192]{1,0:T(8,128)(2,1)S(1)}, bf16[512,192]{1,0:T(8,128)(2,1)S(1)}, u32[]{:S(2)}, u32[]{:S(2)}) collective-permute-start(bf16[512,192]{1,0:T(8,128)(2,1)S(1)} %get-tuple-element.259), channel_id=1, source_target_pairs={{0,1},{1,2},{2,3},{3,0},{4,5},{5,6},{6,7},{7,4},{8,9},{9,10},{10,1... | collective-permute-start | bytes 589832 | tf_op jit(solution)/shard_map/ppermute | solution.py:402
  97.6 7.0 %collective-permute-done.6.refs_2_ = bf16[512,192]{1,0:T(8,128)(2,1)S(1)} collective-permute-done((bf16[512,192]{1,0:T(8,128)(2,1)S(1)}, bf16[512,192]{1,0:T(8,128)(2,1)S(1)}, u32[]{:S(2)}, u32[]{:S(2)}) %collective-permute-start.6) | collective-permute-done | bytes 196640 | tf_op jit(solution)/shard_map/ppermute | solution.py:402
  109.1 2.1 constant_dynamic-slice_fusion.4.refs_5_
  111.1 2.7 constant_dynamic-slice_fusion.3.refs_6_
  118.5 34.0 %ffn.1 = (f32[512,768]{1,0:T(8,128)}, bf16[512,768]{1,0:T(8,128)(2,1)}, bf16[512,3072]{1,0:T(8,128)(2,1)}, bf16[512,3072]{1,0:T(8,128)(2,1)}, bf16[512,768]{1,0:...) custom-call(s32[1]{0:T(128)} %bitcast.1.core, ...), custom_call_target="tpu_custom_call" | custom-call | flops 33999998976 | bytes 26214400 | tf_op jit(solution)/shard_map/ffn/pallas_call | solution.py:372
  152.6 2.1 slice_bitcast_fusion.5
  154.6 8.8 %collective-permute-start.12 = (bf16[512,192]{1,0:T(8,128)(2,1)S(1)}, bf16[512,192]{1,0:T(8,128)(2,1)S(1)}, u32[]{:S(2)}, u32[]{:S(2)}) collective-permute-start(bf16[512,192]{1,0:T(8,128)(2,1)S(1)} %get-tuple-element.255), channel_id=1, source_target_pairs={{0,3},{1,0},{2,1},{3,2},{4,7},{5,4},{6,5},{7,6},{8,11},{9,8},{10,9... | collective-permute-start | bytes 589832 | tf_op jit(solution)/shard_map/ppermute | solution.py:402
  163.5 5.8 %collective-permute-done.12.refs_1_ = bf16[512,192]{1,0:T(8,128)(2,1)S(1)} collective-permute-done((bf16[512,192]{1,0:T(8,128)(2,1)S(1)}, bf16[512,192]{1,0:T(8,128)(2,1)S(1)}, u32[]{:S(2)}, u32[]{:S(2)}) %collective-permute-start.12) | collective-permute-done | bytes 196640 | tf_op jit(solution)/shard_map/ppermute | solution.py:402
  173.3 2.0 pad_maximum_fusion
  176.7 2.9 convolution_convert_fusion
  181.1 4.3 collective-permute-done.17
  185.9 3.4 collective-permute-done.18
  189.9 3.4 collective-permute-done.19
  195.4 5.2 %collective-permute-done.20 = f32[72,128]{1,0:T(8,128)S(1)} collective-permute-done((f32[72,128]{1,0:T(8,128)S(1)}, f32[72,128]{1,0:T(8,128)S(1)}, u32[]{:S(2)}, u32[]{:S(2)}) %collective-permute-start.20) | collective-permute-done | bytes 36896 | tf_op jit(solution)/shard_map/ppermute | solution.py:406
  200.7 2.9 collective-permute-start.13
  203.7 6.2 %collective-permute-done.21 = f32[72,128]{1,0:T(8,128)S(1)} collective-permute-done((f32[72,128]{1,0:T(8,128)S(1)}, f32[72,128]{1,0:T(8,128)S(1)}, u32[]{:S(2)}, u32[]{:S(2)}) %collective-permute-start.21) | collective-permute-done | bytes 36896 | tf_op jit(solution)/shard_map/ppermute | solution.py:406
  209.9 3.2 convolution_convert_fusion.2
  213.2 3.1 add_convert_fusion.1
  216.3 2.6 add_convert_fusion
  218.9 5.6 %collective-permute-done.13.refs_2_ = bf16[512,192]{1,0:T(8,128)(2,1)S(1)} collective-permute-done((bf16[512,192]{1,0:T(8,128)(2,1)S(1)}, bf16[512,192]{1,0:T(8,128)(2,1)S(1)}, u32[]{:S(2)}, u32[]{:S(2)}) %collective-permute-start.13) | collective-permute-done | bytes 196640 | tf_op jit(solution)/shard_map/ppermute | solution.py:402
  227.2 40.8 %attn_bwd.1 = (bf16[3,2048,192]{2,1,0:T(8,128)(2,1)}, f32[3,512,512]{2,1,0:T(8,128)}) custom-call(s32[1]{0:T(128)} %bitcast.place, bf16[512,192]{1,0:T(8,128)(2,1)} %get-tuple-element.256.refs_0_, bf16[512,192]{1,0:T(8,128)(2,1)} %copy-done.43, bf16[512,192]{1,0:T(8,128)(2,1)} %copy-done.45, bf16[512,192]{1,0:T(8,128)(2,1)} %copy-done.44, ...), custom_call_target="tpu_custom_call" | custom-call | flops 40000000000 | bytes 20971520 | tf_op jit(solution)/shard_map/attn_bwd/pallas_call | solution.py:244
  268.0 6.2 %fusion.1 = bf16[2048,768]{1,0:T(8,128)(2,1)} fusion(f32[512,768]{1,0:T(8,128)S(1)} %copy-done.15, pred[2048]{0:T(1024)(128)(4,1)S(1)} %bitcast.252, bf16[3,2048,192]{2,1,0:T(8,128)(2,1)} %get-tuple-element.147, bf16[3,768,192]{1,2,0:T(8,128)(2,1)S(1)} %copy-done.9), kind=kOutput, calls=%fused_computation.4 | convolution fusion | flops 1816657920 | bytes 7964672 | tf_op jit(solution)/shard_map/kte,kde->td/dot_general | solution.py:602
  277.0 2.1 collective-permute-start.25
  279.1 2.0 add_convert_fusion.2
  282.1 2.0 collective-permute-start.24
  294.0 3.7 concatenate.82
  298.9 2.1 convert_reduce_fusion
  307.1 13.0 %collective-permute-start.37 = (bf16[240,768]{1,0:T(8,128)(2,1)S(1)}, bf16[240,768]{1,0:T(8,128)(2,1)S(1)}, u32[]{:S(2)}, u32[]{:S(2)}) collective-permute-start(bf16[240,768]{1,0:T(8,128)(2,1)S(1)} %get-tuple-element.241), channel_id=1, source_target_pairs={{0,3},{1,0},{2,1},{3,2},{4,7},{5,4},{6,5},{7,6},{8,11},{9,8},{10,9... | collective-permute-start | bytes 1105928 | tf_op jit(solution)/shard_map/ppermute | solution.py:402
  324.7 4.4 collective-permute-done.37
  331.0 33.2 %collective-permute-done.38 = bf16[240,768]{1,0:T(8,128)(2,1)S(1)} collective-permute-done((bf16[240,768]{1,0:T(8,128)(2,1)}, bf16[240,768]{1,0:T(8,128)(2,1)S(1)}, u32[]{:S(2)}, u32[]{:S(2)}) %collective-permute-start.38) | collective-permute-done | bytes 368672 | tf_op jit(solution)/shard_map/ppermute | solution.py:402
  365.5 2.7 collective-permute-start.40
  370.2 2.7 collective-permute-start.30
  372.9 5.1 %collective-permute-done.40 = bf16[240,768]{1,0:T(8,128)(2,1)S(1)} collective-permute-done((bf16[240,768]{1,0:T(8,128)(2,1)S(1)}, bf16[240,768]{1,0:T(8,128)(2,1)S(1)}, u32[]{:S(2)}, u32[]{:S(2)}) %collective-permute-start.40) | collective-permute-done | bytes 368672 | tf_op jit(solution)/shard_map/ppermute | solution.py:406
  379.1 6.0 %collective-permute-done.41 = bf16[240,768]{1,0:T(8,128)(2,1)S(1)} collective-permute-done((bf16[240,768]{1,0:T(8,128)(2,1)S(1)}, bf16[240,768]{1,0:T(8,128)(2,1)S(1)}, u32[]{:S(2)}, u32[]{:S(2)}) %collective-permute-start.41) | collective-permute-done | bytes 368672 | tf_op jit(solution)/shard_map/ppermute | solution.py:406
  388.9 3.0 collective-permute-done.31
  400.0 5.1 %convert_element_type.242 = f32[2048,768]{1,0:T(8,128)} convert(bf16[2048,768]{1,0:T(8,128)(2,1)} %all-gather.2.cloned.1.call-done) | non-fusion elementwise | flops 1572864 | bytes 9437184 | tf_op jit(solution)/shard_map/convert_element_type | solution.py:630
  414.8 2.5 copy.127
  421.1 2.9 copy.129
  424.1 2.1 convert_multiply_fusion.1
  426.3 38.8 %all-reduce.2.cloned.1.call-done = bf16[2048,768]{1,0:T(8,128)(2,1)} async-done(((bf16[2048,768]{1,0:T(8,128)(2,1)}), bf16[2048,768]{1,0:T(8,128)(2,1)}) %all-reduce.2.cloned.1.call-update) | async-done | bytes 3145744 | tf_op jit(solution)/shard_map/psum | solution.py:606
  465.0 5.0 %convert_multiply_fusion = f32[2048,768]{1,0:T(8,128)} fusion(bf16[2048,768]{1,0:T(8,128)(2,1)} %all-reduce.2.cloned.1.call-done, f32[]{:T(128)} %bitcast.67), kind=kLoop, calls=%fused_computation.5 | loop fusion | flops 3145728 | bytes 9437188 | tf_op jit(solution)/shard_map/mul | solution.py:654
  (303 shorter events, 106.6 us)
Async XLA Ops:
  7.2 297.8 %all-gather.2.cloned.1.call-start = ((), (), s32[]{:S(2)}) async-start(), calls=%async_computation | async-start | bytes 3932160 | tf_op jit(solution)/shard_map/all_gather | solution.py:565
  11.4 33.8 %collective-permute-start = (bf16[256,768]{1,0:T(8,128)(2,1)S(1)}, bf16[256,768]{1,0:T(8,128)(2,1)}, u32[]{:S(2)}, u32[]{:S(2)}) collective-permute-start(bf16[256,768]{1,0:T(8,128)(2,1)S(1)} %concatenate.72), channel_id=1, source_target_pairs={{0,1},{1,2},{2,3},{3,0},{4,5},{5,6},{6,7},{7,4},{8,9},{9,10},{10,1... | collective-permute-start | bytes 1179656 | tf_op jit(solution)/shard_map/ppermute | solution.py:402
  14.5 30.7 %collective-permute-start.1 = (bf16[256,768]{1,0:T(8,128)(2,1)S(1)}, bf16[256,768]{1,0:T(8,128)(2,1)S(1)}, u32[]{:S(2)}, u32[]{:S(2)}) collective-permute-start(bf16[256,768]{1,0:T(8,128)(2,1)S(1)} %concatenate.72), channel_id=1, source_target_pairs={{0,2},{1,3},{2,0},{3,1},{4,6},{5,7},{6,4},{7,5},{8,10},{9,11},{10,... | collective-permute-start | bytes 1179656 | tf_op jit(solution)/shard_map/ppermute | solution.py:402
  17.1 28.1 %collective-permute-start.2 = (bf16[256,768]{1,0:T(8,128)(2,1)S(1)}, bf16[256,768]{1,0:T(8,128)(2,1)S(1)}, u32[]{:S(2)}, u32[]{:S(2)}) collective-permute-start(bf16[256,768]{1,0:T(8,128)(2,1)S(1)} %concatenate.72), channel_id=1, source_target_pairs={{0,3},{1,0},{2,1},{3,2},{4,7},{5,4},{6,5},{7,6},{8,11},{9,8},{10,9... | collective-permute-start | bytes 1179656 | tf_op jit(solution)/shard_map/ppermute | solution.py:402
  47.1 15.9 %collective-permute-start.3 = (bf16[3,144,768]{2,1,0:T(8,128)(2,1)S(1)}, bf16[3,144,768]{2,1,0:T(8,128)(2,1)S(1)}, u32[]{:S(2)}, u32[]{:S(2)}) collective-permute-start(bf16[3,144,768]{2,1,0:T(8,128)(2,1)S(1)} %pad_maximum_fusion.11), channel_id=1, source_target_pairs={{0,8},{4,12},{8,0},{12,4},{16,24},{20,28},{24,16},{28,20},{1,9},{5... | collective-permute-start | bytes 1990664 | tf_op jit(solution)/shard_map/ppermute | solution.py:406
  49.6 11.2 %collective-permute-start.4 = (bf16[3,96,768]{2,1,0:T(8,128)(2,1)S(1)}, bf16[3,96,768]{2,1,0:T(8,128)(2,1)S(1)}, u32[]{:S(2)}, u32[]{:S(2)}) collective-permute-start(bf16[3,96,768]{2,1,0:T(8,128)(2,1)S(1)} %pad_maximum_fusion.12), channel_id=1, source_target_pairs={{0,16},{4,20},{8,24},{12,28},{16,0},{20,4},{24,8},{28,12},{1,17},{... | collective-permute-start | bytes 1327112 | tf_op jit(solution)/shard_map/ppermute | solution.py:406
  65.1 26.3 %collective-permute-start.9 = (bf16[2,3,96,768]{3,2,1,0:T(8,128)(2,1)}, bf16[2,3,96,768]{3,2,1,0:T(8,128)(2,1)}, u32[]{:S(2)}, u32[]{:S(2)}) collective-permute-start(bf16[2,3,96,768]{3,2,1,0:T(8,128)(2,1)} %pad_maximum_fusion.9), channel_id=1, source_target_pairs={{0,8},{4,12},{8,0},{12,4},{16,24},{20,28},{24,16},{28,20},{1,9},{5... | collective-permute-start | bytes 2654216 | tf_op jit(solution)/shard_map/ppermute | solution.py:406
  66.8 29.1 %collective-permute-start.8 = (bf16[2,3,144,768]{3,2,1,0:T(8,128)(2,1)S(1)}, bf16[2,3,144,768]{3,2,1,0:T(8,128)(2,1)}, u32[]{:S(2)}, u32[]{:S(2)}) collective-permute-start(bf16[2,3,144,768]{3,2,1,0:T(8,128)(2,1)S(1)} %pad_maximum_fusion.4), channel_id=1, source_target_pairs={{0,16},{4,20},{8,24},{12,28},{16,0},{20,4},{24,8},{28,12},{1,17},{... | collective-permute-start | bytes 3981320 | tf_op jit(solution)/shard_map/ppermute | solution.py:406
  82.0 15.6 %collective-permute-start.5 = (bf16[512,192]{1,0:T(8,128)(2,1)S(1)}, bf16[512,192]{1,0:T(8,128)(2,1)S(1)}, u32[]{:S(2)}, u32[]{:S(2)}) collective-permute-start(bf16[512,192]{1,0:T(8,128)(2,1)S(1)} %get-tuple-element.259), channel_id=1, source_target_pairs={{0,1},{1,2},{2,3},{3,0},{4,5},{5,6},{6,7},{7,4},{8,9},{9,10},{10,1... | collective-permute-start | bytes 589832 | tf_op jit(solution)/shard_map/ppermute | solution.py:402
  88.7 16.0 %collective-permute-start.6 = (bf16[512,192]{1,0:T(8,128)(2,1)S(1)}, bf16[512,192]{1,0:T(8,128)(2,1)S(1)}, u32[]{:S(2)}, u32[]{:S(2)}) collective-permute-start(bf16[512,192]{1,0:T(8,128)(2,1)S(1)} %get-tuple-element.258), channel_id=1, source_target_pairs={{0,2},{1,3},{2,0},{3,1},{4,6},{5,7},{6,4},{7,5},{8,10},{9,11},{10,... | collective-permute-start | bytes 589832 | tf_op jit(solution)/shard_map/ppermute | solution.py:402
  89.8 14.8 %collective-permute-start.7 = (bf16[512,192]{1,0:T(8,128)(2,1)S(1)}, bf16[512,192]{1,0:T(8,128)(2,1)S(1)}, u32[]{:S(2)}, u32[]{:S(2)}) collective-permute-start(bf16[512,192]{1,0:T(8,128)(2,1)S(1)} %get-tuple-element.257), channel_id=1, source_target_pairs={{0,3},{1,0},{2,1},{3,2},{4,7},{5,4},{6,5},{7,6},{8,11},{9,8},{10,9... | collective-permute-start | bytes 589832 | tf_op jit(solution)/shard_map/ppermute | solution.py:402
  106.1 12.4 %collective-permute-start.10 = (bf16[1152,768]{1,0:T(8,128)(2,1)}, bf16[1152,768]{1,0:T(8,128)(2,1)}, u32[]{:S(2)}, u32[]{:S(2)}) collective-permute-start(bf16[1152,768]{1,0:T(8,128)(2,1)} %bitcast.29.refs_11_), channel_id=1, source_target_pairs={{0,4},{4,0},{8,12},{12,8},{16,20},{20,16},{24,28},{28,24},{1,5},{5... | collective-permute-start | bytes 5308424 | tf_op jit(solution)/shard_map/ppermute | solution.py:406
  106.2 12.4 %collective-permute-start.11 = (bf16[1152,768]{1,0:T(8,128)(2,1)}, bf16[1152,768]{1,0:T(8,128)(2,1)}, u32[]{:S(2)}, u32[]{:S(2)}) collective-permute-start(bf16[1152,768]{1,0:T(8,128)(2,1)} %bitcast.30.refs_14_), channel_id=1, source_target_pairs={{0,4},{4,0},{8,12},{12,8},{16,20},{20,16},{24,28},{28,24},{1,5},{5... | collective-permute-start | bytes 5308424 | tf_op jit(solution)/shard_map/ppermute | solution.py:406
  154.6 14.6 %collective-permute-start.12 = (bf16[512,192]{1,0:T(8,128)(2,1)S(1)}, bf16[512,192]{1,0:T(8,128)(2,1)S(1)}, u32[]{:S(2)}, u32[]{:S(2)}) collective-permute-start(bf16[512,192]{1,0:T(8,128)(2,1)S(1)} %get-tuple-element.255), channel_id=1, source_target_pairs={{0,3},{1,0},{2,1},{3,2},{4,7},{5,4},{6,5},{7,6},{8,11},{9,8},{10,9... | collective-permute-start | bytes 589832 | tf_op jit(solution)/shard_map/ppermute | solution.py:402
  175.4 40.9 %collective-permute-start.15 = (bf16[4,4,144,768]{3,2,1,0:T(8,128)(2,1)}, bf16[4,4,144,768]{3,2,1,0:T(8,128)(2,1)}, u32[]{:S(2)}, u32[]{:S(2)}) collective-permute-start(bf16[4,4,144,768]{3,2,1,0:T(8,128)(2,1)} %pad_maximum_fusion), channel_id=1, source_target_pairs={{0,4},{4,0},{8,12},{12,8},{16,20},{20,16},{24,28},{28,24},{1,5},{5... | collective-permute-start | bytes 10616840 | tf_op jit(solution)/shard_map/ppermute | solution.py:406
  179.5 33.6 %collective-permute-start.16 = (bf16[1536,768]{1,0:T(8,128)(2,1)}, bf16[1536,768]{1,0:T(8,128)(2,1)}, u32[]{:S(2)}, u32[]{:S(2)}) collective-permute-start(bf16[1536,768]{1,0:T(8,128)(2,1)} %convolution_convert_fusion), channel_id=1, source_target_pairs={{0,4},{4,0},{8,12},{12,8},{16,20},{20,16},{24,28},{28,24},{1,5},{5... | collective-permute-start | bytes 7077896 | tf_op jit(solution)/shard_map/ppermute | solution.py:406
  180.5 4.8 %collective-permute-start.17 = (f32[72,128]{1,0:T(8,128)S(1)}, f32[72,128]{1,0:T(8,128)S(1)}, u32[]{:S(2)}, u32[]{:S(2)}) collective-permute-start(f32[72,128]{1,0:T(8,128)S(1)} %maximum_bitcast_fusion.7), channel_id=1, source_target_pairs={{0,4},{4,0},{8,12},{12,8},{16,20},{20,16},{24,28},{28,24},{1,5},{5... | collective-permute-start | bytes 110600 | tf_op jit(solution)/shard_map/ppermute | solution.py:406
  185.3 4.0 collective-permute-start.18
  189.3 4.0 collective-permute-start.19
  193.3 7.2 %collective-permute-start.20 = (f32[72,128]{1,0:T(8,128)S(1)}, f32[72,128]{1,0:T(8,128)S(1)}, u32[]{:S(2)}, u32[]{:S(2)}) collective-permute-start(f32[72,128]{1,0:T(8,128)S(1)} %add.247), channel_id=1, source_target_pairs={{0,1},{1,0},{2,3},{3,2},{4,5},{5,4},{6,7},{7,6},{8,9},{9,8},{10,11... | collective-permute-start | bytes 110600 | tf_op jit(solution)/shard_map/ppermute | solution.py:406
  193.6 16.3 %collective-permute-start.14 = (bf16[512,192]{1,0:T(8,128)(2,1)S(1)}, bf16[512,192]{1,0:T(8,128)(2,1)S(1)}, u32[]{:S(2)}, u32[]{:S(2)}) collective-permute-start(bf16[512,192]{1,0:T(8,128)(2,1)S(1)} %get-tuple-element.253), channel_id=1, source_target_pairs={{0,1},{1,2},{2,3},{3,0},{4,5},{5,6},{6,7},{7,4},{8,9},{9,10},{10,1... | collective-permute-start | bytes 589832 | tf_op jit(solution)/shard_map/ppermute | solution.py:402
  200.6 9.3 %collective-permute-start.21 = (f32[72,128]{1,0:T(8,128)S(1)}, f32[72,128]{1,0:T(8,128)S(1)}, u32[]{:S(2)}, u32[]{:S(2)}) collective-permute-start(f32[72,128]{1,0:T(8,128)S(1)} %add.248), channel_id=1, source_target_pairs={{0,2},{1,3},{2,0},{3,1},{4,6},{5,7},{6,4},{7,5},{8,10},{9,11},{10,... | collective-permute-start | bytes 110600 | tf_op jit(solution)/shard_map/ppermute | solution.py:406
  200.7 23.8 %collective-permute-start.13 = (bf16[512,192]{1,0:T(8,128)(2,1)S(1)}, bf16[512,192]{1,0:T(8,128)(2,1)S(1)}, u32[]{:S(2)}, u32[]{:S(2)}) collective-permute-start(bf16[512,192]{1,0:T(8,128)(2,1)S(1)} %get-tuple-element.254), channel_id=1, source_target_pairs={{0,2},{1,3},{2,0},{3,1},{4,6},{5,7},{6,4},{7,5},{8,10},{9,11},{10,... | collective-permute-start | bytes 589832 | tf_op jit(solution)/shard_map/ppermute | solution.py:402
  203.7 261.4 %all-reduce.2.cloned.1.call-start = ((), (), s32[]{:S(2)}) async-start(), calls=%async_computation.1 | async-start | bytes 6291456 | tf_op jit(solution)/shard_map/psum | solution.py:606
  225.9 48.3 %collective-permute-start.22 = (bf16[2,4,144,768]{3,2,1,0:T(8,128)(2,1)}, bf16[2,4,144,768]{3,2,1,0:T(8,128)(2,1)}, u32[]{:S(2)}, u32[]{:S(2)}) collective-permute-start(bf16[2,4,144,768]{3,2,1,0:T(8,128)(2,1)} %get-tuple-element.216), channel_id=1, source_target_pairs={{0,8},{4,12},{8,0},{12,4},{16,24},{20,28},{24,16},{28,20},{1,9},{5... | collective-permute-start | bytes 5308424 | tf_op jit(solution)/shard_map/ppermute | solution.py:406
  227.2 47.1 %collective-permute-start.23 = (bf16[2,4,96,768]{3,2,1,0:T(8,128)(2,1)}, bf16[2,4,96,768]{3,2,1,0:T(8,128)(2,1)}, u32[]{:S(2)}, u32[]{:S(2)}) collective-permute-start(bf16[2,4,96,768]{3,2,1,0:T(8,128)(2,1)} %get-tuple-element.231), channel_id=1, source_target_pairs={{0,16},{4,20},{8,24},{12,28},{16,0},{20,4},{24,8},{28,12},{1,17},{... | collective-permute-start | bytes 3538952 | tf_op jit(solution)/shard_map/ppermute | solution.py:406
  227.2 40.9 %copy-start.9 = (bf16[3,768,192]{1,2,0:T(8,128)(2,1)S(1)}, bf16[3,768,192]{1,2,0:T(8,128)(2,1)}, u32[]{:S(2)}) copy-start(bf16[3,768,192]{1,2,0:T(8,128)(2,1)} %param.20) | copy-start | bytes 2654212
  227.2 40.9 %copy-start.15 = (f32[512,768]{1,0:T(8,128)S(1)}, f32[512,768]{1,0:T(8,128)}, u32[]{:S(2)}) copy-start(f32[512,768]{1,0:T(8,128)} %get-tuple-element.138) | copy-start | bytes 4718596
  277.0 24.5 %collective-permute-start.25 = (bf16[4,96,768]{2,1,0:T(8,128)(2,1)}, bf16[4,96,768]{2,1,0:T(8,128)(2,1)}, u32[]{:S(2)}, u32[]{:S(2)}) collective-permute-start(bf16[4,96,768]{2,1,0:T(8,128)(2,1)} %dynamic-slice_bitcast_fusion.6), channel_id=1, source_target_pairs={{0,8},{4,12},{8,0},{12,4},{16,24},{20,28},{24,16},{28,20},{1,9},{5... | collective-permute-start | bytes 1769480 | tf_op jit(solution)/shard_map/ppermute | solution.py:406
  282.1 21.4 %collective-permute-start.24 = (bf16[4,144,768]{2,1,0:T(8,128)(2,1)}, bf16[4,144,768]{2,1,0:T(8,128)(2,1)}, u32[]{:S(2)}, u32[]{:S(2)}) collective-permute-start(bf16[4,144,768]{2,1,0:T(8,128)(2,1)} %dynamic-slice_bitcast_fusion.5), channel_id=1, source_target_pairs={{0,16},{4,20},{8,24},{12,28},{16,0},{20,4},{24,8},{28,12},{1,17},{... | collective-permute-start | bytes 2654216 | tf_op jit(solution)/shard_map/ppermute | solution.py:406
  298.9 21.7 %collective-permute-start.26 = (bf16[4,96,1600]{2,1,0:T(8,128)(2,1)}, bf16[4,96,1600]{2,1,0:T(8,128)(2,1)}, u32[]{:S(2)}, u32[]{:S(2)}) collective-permute-start(bf16[4,96,1600]{2,1,0:T(8,128)(2,1)} %dynamic-slice_bitcast_fusion.2), channel_id=1, source_target_pairs={{0,4},{4,0},{8,12},{12,8},{16,20},{20,16},{24,28},{28,24},{1,5},{5... | collective-permute-start | bytes 3686408 | tf_op jit(solution)/shard_map/ppermute | solution.py:406
  301.0 22.5 %collective-permute-start.34 = (f32[2,192]{1,0:T(2,128)S(1)}, f32[2,192]{1,0:T(2,128)S(1)}, u32[]{:S(2)}, u32[]{:S(2)}) collective-permute-start(f32[2,192]{1,0:T(2,128)S(1)} %convert_reduce_fusion), channel_id=1, source_target_pairs={{0,4},{4,0},{8,12},{12,8},{16,20},{20,16},{24,28},{28,24},{1,5},{5... | collective-permute-start | bytes 4616 | tf_op jit(solution)/shard_map/ppermute | solution.py:406
  307.1 22.0 %collective-permute-start.37 = (bf16[240,768]{1,0:T(8,128)(2,1)S(1)}, bf16[240,768]{1,0:T(8,128)(2,1)S(1)}, u32[]{:S(2)}, u32[]{:S(2)}) collective-permute-start(bf16[240,768]{1,0:T(8,128)(2,1)S(1)} %get-tuple-element.241), channel_id=1, source_target_pairs={{0,3},{1,0},{2,1},{3,2},{4,7},{5,4},{6,5},{7,6},{8,11},{9,8},{10,9... | collective-permute-start | bytes 1105928 | tf_op jit(solution)/shard_map/ppermute | solution.py:402
  320.0 44.1 %collective-permute-start.38 = (bf16[240,768]{1,0:T(8,128)(2,1)}, bf16[240,768]{1,0:T(8,128)(2,1)S(1)}, u32[]{:S(2)}, u32[]{:S(2)}) collective-permute-start(bf16[240,768]{1,0:T(8,128)(2,1)} %get-tuple-element.243), channel_id=1, source_target_pairs={{0,2},{1,3},{2,0},{3,1},{4,6},{5,7},{6,4},{7,5},{8,10},{9,11},{10,... | collective-permute-start | bytes 1105928 | tf_op jit(solution)/shard_map/ppermute | solution.py:402
  320.0 44.1 %collective-permute-start.39 = (bf16[240,768]{1,0:T(8,128)(2,1)}, bf16[240,768]{1,0:T(8,128)(2,1)}, u32[]{:S(2)}, u32[]{:S(2)}) collective-permute-start(bf16[240,768]{1,0:T(8,128)(2,1)} %get-tuple-element.242), channel_id=1, source_target_pairs={{0,1},{1,2},{2,3},{3,0},{4,5},{5,6},{6,7},{7,4},{8,9},{9,10},{10,1... | collective-permute-start | bytes 1105928 | tf_op jit(solution)/shard_map/ppermute | solution.py:402
  323.4 44.8 %collective-permute-start.27 = (bf16[96,1600]{1,0:T(8,128)(2,1)S(1)}, bf16[96,1600]{1,0:T(8,128)(2,1)S(1)}, u32[]{:S(2)}, u32[]{:S(2)}) collective-permute-start(bf16[96,1600]{1,0:T(8,128)(2,1)S(1)} %get-tuple-element.250), channel_id=1, source_target_pairs={{0,8},{4,12},{8,0},{12,4},{16,24},{20,28},{24,16},{28,20},{1,9},{5... | collective-permute-start | bytes 921608 | tf_op jit(solution)/shard_map/ppermute | solution.py:406
  323.5 45.5 %collective-permute-start.28 = (bf16[96,1600]{1,0:T(8,128)(2,1)S(1)}, bf16[96,1600]{1,0:T(8,128)(2,1)S(1)}, u32[]{:S(2)}, u32[]{:S(2)}) collective-permute-start(bf16[96,1600]{1,0:T(8,128)(2,1)S(1)} %get-tuple-element.252), channel_id=1, source_target_pairs={{0,16},{4,20},{8,24},{12,28},{16,0},{20,4},{24,8},{28,12},{1,17},{... | collective-permute-start | bytes 921608 | tf_op jit(solution)/shard_map/ppermute | solution.py:406
  329.1 39.9 %collective-permute-start.29 = (bf16[96,1600]{1,0:T(8,128)(2,1)S(1)}, bf16[96,1600]{1,0:T(8,128)(2,1)S(1)}, u32[]{:S(2)}, u32[]{:S(2)}) collective-permute-start(bf16[96,1600]{1,0:T(8,128)(2,1)S(1)} %get-tuple-element.251), channel_id=1, source_target_pairs={{0,24},{4,28},{8,16},{12,20},{16,8},{20,12},{24,0},{28,4},{1,25},{... | collective-permute-start | bytes 921608 | tf_op jit(solution)/shard_map/ppermute | solution.py:406
  364.2 31.6 %collective-permute-start.35 = (f32[2,192]{1,0:T(2,128)S(1)}, f32[2,192]{1,0:T(2,128)S(1)}, u32[]{:S(2)}, u32[]{:S(2)}) collective-permute-start(f32[2,192]{1,0:T(2,128)S(1)} %add.269), channel_id=1, source_target_pairs={{0,8},{4,12},{8,0},{12,4},{16,24},{20,28},{24,16},{28,20},{1,9},{5... | collective-permute-start | bytes 4616 | tf_op jit(solution)/shard_map/ppermute | solution.py:406
  365.5 12.5 %collective-permute-start.40 = (bf16[240,768]{1,0:T(8,128)(2,1)S(1)}, bf16[240,768]{1,0:T(8,128)(2,1)S(1)}, u32[]{:S(2)}, u32[]{:S(2)}) collective-permute-start(bf16[240,768]{1,0:T(8,128)(2,1)S(1)} %fusion.22), channel_id=1, source_target_pairs={{0,24},{4,28},{8,16},{12,20},{16,8},{20,12},{24,0},{28,4},{1,25},{... | collective-permute-start | bytes 1105928 | tf_op jit(solution)/shard_map/ppermute | solution.py:406
  368.2 16.9 %collective-permute-start.41 = (bf16[240,768]{1,0:T(8,128)(2,1)S(1)}, bf16[240,768]{1,0:T(8,128)(2,1)S(1)}, u32[]{:S(2)}, u32[]{:S(2)}) collective-permute-start(bf16[240,768]{1,0:T(8,128)(2,1)S(1)} %fusion.22), channel_id=1, source_target_pairs={{0,16},{4,20},{8,24},{12,28},{16,0},{20,4},{24,8},{28,12},{1,17},{... | collective-permute-start | bytes 1105928 | tf_op jit(solution)/shard_map/ppermute | solution.py:406
  369.0 17.4 %collective-permute-start.42 = (bf16[240,768]{1,0:T(8,128)(2,1)S(1)}, bf16[240,768]{1,0:T(8,128)(2,1)S(1)}, u32[]{:S(2)}, u32[]{:S(2)}) collective-permute-start(bf16[240,768]{1,0:T(8,128)(2,1)S(1)} %fusion.22), channel_id=1, source_target_pairs={{0,8},{4,12},{8,0},{12,4},{16,24},{20,28},{24,16},{28,20},{1,9},{5... | collective-permute-start | bytes 1105928 | tf_op jit(solution)/shard_map/ppermute | solution.py:406
  370.2 18.6 %collective-permute-start.30 = (bf16[96,1600]{1,0:T(8,128)(2,1)S(1)}, bf16[96,1600]{1,0:T(8,128)(2,1)S(1)}, u32[]{:S(2)}, u32[]{:S(2)}) collective-permute-start(bf16[96,1600]{1,0:T(8,128)(2,1)S(1)} %fusion.25), channel_id=1, source_target_pairs={{0,24},{4,28},{8,16},{12,20},{16,8},{20,12},{24,0},{28,4},{1,25},{... | collective-permute-start | bytes 921608 | tf_op jit(solution)/shard_map/ppermute | solution.py:406
  377.9 13.9 %collective-permute-start.31 = (bf16[96,1600]{1,0:T(8,128)(2,1)S(1)}, bf16[96,1600]{1,0:T(8,128)(2,1)S(1)}, u32[]{:S(2)}, u32[]{:S(2)}) collective-permute-start(bf16[96,1600]{1,0:T(8,128)(2,1)S(1)} %fusion.25), channel_id=1, source_target_pairs={{0,16},{4,20},{8,24},{12,28},{16,0},{20,4},{24,8},{28,12},{1,17},{... | collective-permute-start | bytes 921608 | tf_op jit(solution)/shard_map/ppermute | solution.py:406
  385.0 7.0 %collective-permute-start.32 = (bf16[96,1600]{1,0:T(8,128)(2,1)S(1)}, bf16[96,1600]{1,0:T(8,128)(2,1)S(1)}, u32[]{:S(2)}, u32[]{:S(2)}) collective-permute-start(bf16[96,1600]{1,0:T(8,128)(2,1)S(1)} %fusion.25), channel_id=1, source_target_pairs={{0,8},{4,12},{8,0},{12,4},{16,24},{20,28},{24,16},{28,20},{1,9},{5... | collective-permute-start | bytes 921608 | tf_op jit(solution)/shard_map/ppermute | solution.py:406
  388.9 20.7 %collective-permute-start.43 = (bf16[2,384,768]{2,1,0:T(8,128)(2,1)}, bf16[2,384,768]{2,1,0:T(8,128)(2,1)}, u32[]{:S(2)}, u32[]{:S(2)}) collective-permute-start(bf16[2,384,768]{2,1,0:T(8,128)(2,1)} %pad_maximum_fusion.8), channel_id=1, source_target_pairs={{0,4},{4,0},{8,12},{12,8},{16,20},{20,16},{24,28},{28,24},{1,5},{5... | collective-permute-start | bytes 3538952 | tf_op jit(solution)/shard_map/ppermute | solution.py:406
  394.6 20.2 %collective-permute-start.33 = (bf16[384,1600]{0,1:T(8,128)(2,1)}, bf16[384,1600]{0,1:T(8,128)(2,1)}, u32[]{:S(2)}, u32[]{:S(2)}) collective-permute-start(bf16[384,1600]{0,1:T(8,128)(2,1)} %copy.126), channel_id=1, source_target_pairs={{0,4},{4,0},{8,12},{12,8},{16,20},{20,16},{24,28},{28,24},{1,5},{5... | collective-permute-start | bytes 3686408 | tf_op jit(solution)/shard_map/ppermute | solution.py:406
  395.8 3.6 collective-permute-start.36
  (49 other events, 222.9 us)
Sparse Core Ops, SparseCore 0:
  203.8 62.7 all-gather.1
  331.1 133.8 all-reduce.1

commit v4 on v3

--- a/solution.py
+++ b/solution.py
@@ -225,9 +225,10 @@
         gq = jnp.transpose(jnp.concatenate(rows, axis=0))[:, :width]
         gkb = jnp.concatenate([gk[h, qcol, :] for h in range(heads)], axis=1) * scale
         gvb = jnp.concatenate([gv[h, qcol, :] for h in range(heads)], axis=1)
-        gqkv[0, qcol, :] = gq.astype(BF16)
-        gqkv[1, qcol, :] = gkb.astype(BF16)
-        gqkv[2, qcol, :] = gvb.astype(BF16)
+        rows = [gq, gkb, gvb]
+        if gqkv.shape[1] > 3 * width:
+            rows.append(jnp.zeros((BLOCK, gqkv.shape[1] - 3 * width), F32))
+        gqkv[qcol, :] = jnp.concatenate(rows, axis=1).astype(BF16)
         return 0
 
     lax.fori_loop(0, tokens // BLOCK, per_q, 0)
@@ -244,7 +245,7 @@
     return pl.pallas_call(
         functools.partial(attn_bwd_kernel, n_t),
         in_specs=[pl.BlockSpec(memory_space=pltpu.SMEM)] + [pl.BlockSpec(memory_space=pl.ANY)] * n_t + [vm] * 8,
-        out_shape=(sd((3, tokens, width), BF16), sd(lmt.shape, F32)),
+        out_shape=(sd((tokens, -(-3 * width // 128) * 128), BF16), sd(lmt.shape, F32)),
         scratch_shapes=[
             pltpu.VMEM((heads, tokens, hd), F32),
             pltpu.VMEM((heads, tokens, hd), F32),
@@ -254,9 +255,116 @@
             pltpu.SemaphoreType.DMA((n_t,)),
         ],
         compiler_params=pltpu.CompilerParams(vmem_limit_bytes=56 << 20),
-        cost_estimate=cost(40, 20 << 20),
+        cost_estimate=cost(400, 20 << 20),
         name="attn_bwd",
     )(place, *parts, ctxt, q3, k3, v3, qt, kt, lse, lmt)
+
+
+def wgrad_kernel(slab, gb, first, act, grad_ffn, grad_attn, *refs):
+    ctx, (to, ao) = refs[:-2], refs[-2:]
+    i = pl.program_id(0)
+    n_t = len(ctx)
+    piece = to.shape[2] - 2 * slab
+
+    @pl.when(i == 0)
+    def _():
+        for z in range(n_t):
+            ao[z] = dot_tn(ctx[z][...], grad_attn[...]).astype(BF16)
+
+    up = dot_tn(gb[...], first[...]).astype(BF16)
+    down = dot_tn(act[...], grad_ffn[...]).astype(BF16)
+    rows = pl.ds(pl.multiple_of(i * piece, piece), piece)
+    for z in range(n_t):
+        to[0, z, :slab, :] = up[z * slab : (z + 1) * slab]
+        to[0, z, slab : slab + piece, :] = ao[z, rows, :]
+        to[0, z, slab + piece :, :] = down[z * slab : (z + 1) * slab]
+
+
+def wgrad(slab, spots, gb, first, act, grad_ffn, grad_attn, ctx):
+    chunk, width = first.shape
+    n_t = len(ctx)
+    local = ctx[0].shape[1]
+    wide = n_t * slab
+    tall = 2 * slab + local // spots
+    vm = pl.BlockSpec(memory_space=pltpu.VMEM)
+    cols = pl.BlockSpec((chunk, wide), lambda i: (0, i))
+    return pl.pallas_call(
+        functools.partial(wgrad_kernel, slab),
+        grid=(spots,),
+        in_specs=[cols, vm, cols, vm, vm] + [vm] * n_t,
+        out_specs=pl.BlockSpec((1, n_t, tall, width), lambda i: (i, 0, 0, 0)),
+        out_shape=jax.ShapeDtypeStruct((spots, n_t, tall, width), BF16),
+        scratch_shapes=[pltpu.VMEM((n_t, local, width), BF16)],
+        compiler_params=pltpu.CompilerParams(vmem_limit_bytes=40 << 20),
+        cost_estimate=cost(60, 10 << 20),
+        name="wgrad",
+    )(gb, first, act, grad_ffn, grad_attn, *ctx)
+
+
+def tail_kernel(hid, gqkv, glm, table, noise, tail, acc):
+    heads, period, _ = glm.shape
+    tokens, width = hid.shape
+    wide = acc.shape[1]
+    tall, lanes = tail.shape
+    at = 2 * period + wide
+    extra = lanes - at
+    step = 2 * BLOCK
+    for n in range(heads * period // BLOCK):
+        h, at = n * BLOCK // period, n * BLOCK % period
+        x = (table[h, at : at + BLOCK, :] + noise[h, at : at + BLOCK, :]) * (1.0 / SOFTENING)
+        e = jnp.exp(-jnp.abs(x))
+        slope = jnp.where(x > 0, e, 1.0) / (1.0 + e) * (1.0 / SOFTENING)
+        g = (glm[h, at : at + BLOCK, :] * slope).astype(BF16)
+        row, col = n * BLOCK % tall, n * BLOCK // tall * period
+        tail[row : row + BLOCK, col : col + period] = g
+    acc[...] = jnp.zeros(acc.shape, F32)
+
+    def add(i, total):
+        rows = pl.ds(pl.multiple_of(i * step, step), step)
+        y = gqkv[rows, :wide]
+        acc[...] += dot_tn(hid[rows, :], y)
+        return total + jnp.sum(y.astype(F32), axis=0, keepdims=True)
+
+    total = lax.fori_loop(0, tokens // step, add, jnp.zeros((1, wide), F32))
+    rows = [total[:, n * extra : (n + 1) * extra] for n in range(wide // extra)]
+    rows.append(jnp.zeros((tall - len(rows), extra), F32))
+    tail[:, 2 * period :] = jnp.concatenate([acc[...], jnp.concatenate(rows, axis=0)], axis=1).astype(BF16)
+
+
+def tail_of(hidden, gqkv, glm, table, noise, wide):
+    heads, period, _ = glm.shape
+    width = hidden.shape[1]
+    lanes = 2 * period + wide
+    sd = jax.ShapeDtypeStruct
+    return pl.pallas_call(
+        tail_kernel,
+        out_shape=sd((heads * period // 2, -(-lanes // 128) * 128), BF16),
+        scratch_shapes=[pltpu.VMEM((width, wide), F32)],
+        compiler_params=pltpu.CompilerParams(vmem_limit_bytes=56 << 20),
+        cost_estimate=cost(400, 20 << 20),
+        name="tail",
+    )(hidden, gqkv, glm, table, noise)
+
+
+def back_kernel(place, w, resid, *refs):
+    pieces, out = refs[:-1], refs[-1]
+    n_t, wide, _ = w.shape
+    total = resid[...]
+    for s in range(n_t):
+        total = total + dot(pieces[s][:, :wide], w[lax.rem(place[0] + n_t - s, n_t)])
+    out[...] = total.astype(BF16)
+
+
+def back_of(place, w, resid, pieces):
+    vm = pl.BlockSpec(memory_space=pltpu.VMEM)
+    return pl.pallas_call(
+        back_kernel,
+        in_specs=[pl.BlockSpec(memory_space=pltpu.SMEM)] + [vm] * (2 + len(pieces)),
+        out_shape=jax.ShapeDtypeStruct(resid.shape, BF16),
+        compiler_params=pltpu.CompilerParams(vmem_limit_bytes=40 << 20),
+        cost_estimate=cost(5, 10 << 20),
+        name="back",
+    )(place, w, resid, *pieces)
 
 
 def norm_parts(resid):
@@ -279,8 +387,11 @@
 ):
     ctx = refs[:n_t]
     (wao, hid, teach, valid, vec, bup, up_o, up_m, up_t, dn_o, dn_m, dn_t,
-     out, out_low, act, gb, first_low, grad_ffn, grad_attn, grad_resid, gctx, vecs, gbup,
-     up_s, dn_s, slope, xhat_s, sems) = refs[n_t:]
+     out, out_low, act_k, act_s, gb_k, gb_s, first_low, grad_ffn, grad_attn, grad_resid, vecs, gbup) = (
+        refs[n_t : n_t + 24]
+    )
+    gctx = refs[n_t + 24 : 2 * n_t + 24]
+    up_s, dn_s, slope, xhat_s, sems = refs[2 * n_t + 24 :]
     units, width = up_s.shape
     half = units // 2
     spots = half // (n_t * slab)
@@ -307,13 +418,22 @@
         cp.wait()
     blocks, _, size = bup.shape
 
+    def halves(i, kept, sent, value):
+        @pl.when(i < spots)
+        def _():
+            kept[:, pl.ds(pl.multiple_of(i * size, size), size)] = value
+
+        @pl.when(i >= spots)
+        def _():
+            sent[:, pl.ds(pl.multiple_of((i - spots) * size, size), size)] = value
+
     def forward(i, feed):
         rows = pl.ds(pl.multiple_of(i * size, size), size)
         before = dot_nt(first_low[...], up_s[rows, :]) + bup[i]
         phi = 0.5 * (1.0 + lax.erf(before * math.sqrt(0.5)))
         dens = jnp.exp(-0.5 * before * before) * (1.0 / math.sqrt(2.0 * math.pi))
         low = (before * phi).astype(BF16)
-        act[:, rows] = low
+        halves(i, act_k, act_s, low)
         slope[:, rows] = (phi + before * dens).astype(BF16)
         return feed + dot(low, dn_s[rows, :])
 
@@ -340,7 +460,7 @@
         rows = pl.ds(pl.multiple_of(i * size, size), size)
         g = dot_nt(grad_ffn[...], dn_s[rows, :]) * slope[:, rows].astype(F32)
         low = g.astype(BF16)
-        gb[:, rows] = low
+        halves(i, gb_k, gb_s, low)
         gbup[i] = total(low.astype(F32))
         return acc + dot(low, up_s[rows, :])
 
@@ -355,7 +475,7 @@
     vecs[0:1, :] = total(low.astype(F32))
     local = ctx[0].shape[1]
     for s in range(n_t):
-        gctx[s] = dot_nt(low, wao[s]).astype(BF16)
+        gctx[s][...] = dot_nt(low, wao[s]).astype(BF16)
 
 
 def ffn(core, ctx, wao, hid, teach, valid, vec, bup, ups, downs, slab):
@@ -375,15 +495,14 @@
         out_shape=(
             sd((chunk, width), F32),
             sd((chunk, width), BF16),
-            sd((chunk, units), BF16),
-            sd((chunk, units), BF16),
+            *[sd((chunk, units // 2), BF16)] * 4,
             sd((chunk, width), BF16),
             sd((chunk, width), BF16),
             sd((chunk, width), BF16),
             sd((chunk, width), F32),
-            sd((n_t, chunk, local), BF16),
             sd((8, width), F32),
             sd((blocks, 1, size), F32),
+            *[sd((chunk, local), BF16)] * n_t,
         ),
         scratch_shapes=[
             pltpu.VMEM((units, width), BF16),
@@ -461,6 +580,14 @@
         keep = lax.dynamic_index_in_dim(x, up, ax, keepdims=False)
         return keep, dp_swap(send, bits[0])
 
+    def narrow_pair(x, y, bits):
+        ax = sorted(bits, reverse=True).index(bits[0])
+        up = bit_of(bits[0])
+        part = lambda v, i: lax.dynamic_index_in_dim(v, i, ax, keepdims=False).astype(F32)
+        send = (part(x, 1 - up) + part(y, 1 - up)).astype(BF16)
+        keep = (part(x, up) + part(y, up)).astype(BF16)
+        return keep, send, bits[0]
+
     def narrow(x, bits):
         left = sorted(bits, reverse=True)
         for bit in bits:
@@ -514,11 +641,14 @@
     )
     came = [shift(sent, n_t, s) for s in range(1, n_t)]
 
+    w_t = w_qkv.transpose(0, 2, 1).reshape(3 * local, width)
+    w_t = rows_of(w_t, core * (3 * local // 2), 3 * local // 2)
     q3, k3, v3, qt, kt, vt, lmt = attn_prep(hidden, w_qkv, b_qv, table, noise)
     n_sup = tokens // lmt.shape[1]
     cuts = [max(n_sup - 2, 1), max(n_sup - 1, 2)]
     part = attn_fwd(qt, k3, vt, lmt, 0, cuts[0])
-    part, came = lax.optimization_barrier((part, came))
+    part, came, w_t = lax.optimization_barrier((part, came, w_t))
+    w_side = lax.all_gather(w_t, "tensor", axis=0)
 
     cut = slab + piece
     wide_a = jnp.stack([x[:cut] for x in came])
@@ -533,7 +663,7 @@
     ctx_parts = [rows_of(ctx, ti * chunk, chunk)] + [
         shift(rows_of(ctx, lax.rem(ti + s, n_t) * chunk, chunk), n_t, s) for s in range(1, n_t)
     ]
-    *ctx_parts, wide_a, wide_b = lax.optimization_barrier((*ctx_parts, wide_a, wide_b))
+    *ctx_parts, wide_a, wide_b, w_side = lax.optimization_barrier((*ctx_parts, wide_a, wide_b, w_side))
     up_m = wide_a[:, :, :slab].reshape(-1, width)
     down_m = wide_b.reshape(-1, width)
     wao = wide_a[:, :, slab:].transpose(1, 0, 2, 3).reshape(n_t - 1, local, width)
@@ -548,8 +678,9 @@
     b_theirs = lax.dynamic_index_in_dim(b_all, 1 - core, 1, keepdims=False)
     bup = jnp.stack([b_mine, b_theirs]).transpose(0, 2, 1, 3).reshape(2 * spots, 1, n_t * slab)
 
+    w_other = dp_swap(w_side, 1)
     vec = jnp.stack([b_attn_out, gain_one, bias_one, b_down, gain_two, bias_two, b_down, b_down])
-    (out_own, out_low, act, gb, first_low, grad_ffn, grad_attn, grad_resid, gctx_rel, vecs, gbup) = ffn(
+    (out_own, out_low, act_k, act_s, gb_k, gb_s, first_low, grad_ffn, grad_attn, grad_resid, vecs, gbup, *gctx_rel) = ffn(
         core.reshape(1),
         ctx_parts,
         wao,
@@ -562,82 +693,95 @@
         (w_down, down_m, down_t),
         slab,
     )
-    out_all = lax.all_gather(out_low, "tensor", axis=0, tiled=True)
-
-    parts = [gctx_rel[0]] + [shift(gctx_rel[s], n_t, -s) for s in range(1, n_t)]
-    parts[1], gb, act, first_low, grad_ffn, grad_attn = lax.optimization_barrier(
-        (parts[1], gb, act, first_low, grad_ffn, grad_attn)
-    )
-
+
+    vecs, w_other, w_side = lax.optimization_barrier((vecs, w_other, w_side))
     up = core == 1
     gbu = gbup.reshape(2, spots, n_t, slab)
     gbu = jnp.where(up, gbu[::-1], gbu).transpose(2, 0, 1, 3).reshape(n_t, units)
     gbu = gbu[jnp.stack([lax.rem(ti - z + n_t, n_t) for z in range(n_t)])]
     pack = jnp.concatenate([vecs.reshape(-1), gbu.reshape(-1)]).reshape(-1, 128)
-    pack = everyone(pack)
-    bit = 1
-    while bit < n_t:
-        pack = pack + swap(pack, "tensor", n_t, bit)
-        bit *= 2
-
-    half = n_t * units // 2
+    pack_came = dp_swap(pack, 1)
+
+    parts = [gctx_rel[0]] + [shift(gctx_rel[s], n_t, -s) for s in range(1, n_t)]
+
+    send = wgrad(slab, spots, gb_s, first_low, act_s, grad_ffn, grad_attn, ctx_parts)
+    got = dp_swap(send, 1)
+    first_low, send, pack, pack_came = lax.optimization_barrier((first_low, send, pack, pack_came))
+    keep = wgrad(slab, spots, gb_k, first_low, act_k, grad_ffn, grad_attn, ctx_parts)
+    got, keep, pack, pack_came = lax.optimization_barrier((got, keep, pack, pack_came))
     lead = (2,) * len(low_bits)
-    send_up = dot_tn(gb[:, half:], first_low).astype(BF16).reshape(spots, n_t, slab, width)
-    g_ao = jnp.stack([dot_tn(c, grad_attn) for c in ctx_parts]).astype(BF16)
-    g_ao = g_ao.reshape(n_t, spots, piece, width).transpose(1, 0, 2, 3)
-    send_a = jnp.concatenate([send_up, g_ao], axis=2)
-    send_b = dot_tn(act[:, half:], grad_ffn).astype(BF16)
-    got_a = dp_swap(send_a, 1)
-    got_b = dp_swap(send_b, 1)
-    parts[3], gb, act = lax.optimization_barrier((parts[3], gb, act))
-    keep_up = dot_tn(gb[:, :half], first_low).reshape(spots, n_t, slab, width)
-    keep_a = jnp.concatenate([keep_up.astype(BF16), g_ao], axis=2)
-    g_a = (keep_a.astype(F32) + got_a.astype(F32)).astype(BF16)
-    g_b = (dot_tn(act[:, :half], grad_ffn) + got_b.astype(F32)).astype(BF16)
-    parts[2], g_a, g_b, pack = lax.optimization_barrier((parts[2], g_a, g_b, pack))
-    a_keep, a_came = narrow_start(g_a.reshape(lead + (n_t, cut, width)), low_bits)
-    b_keep, b_came = narrow_start(g_b.reshape(lead + (n_t, slab, width)), high_bits)
+    shape = lambda x, n: x.reshape(lead + (n_t, n, width))
+    a_keep, a_send, _ = narrow_pair(shape(keep[:, :, :cut], cut), shape(got[:, :, :cut], cut), low_bits)
+    b_keep, b_send, _ = narrow_pair(shape(keep[:, :, cut:], slab), shape(got[:, :, cut:], slab), high_bits)
+    *parts, a_send, b_send, a_keep, b_keep, out_low, pack, pack_came = lax.optimization_barrier(
+        (*parts, a_send, b_send, a_keep, b_keep, out_low, pack, pack_came)
+    )
+    a_came = dp_swap(a_send, low_bits[0])
+    b_came = dp_swap(b_send, high_bits[0])
+    pack = pack + pack_came
+    packs = [pack] + [dp_swap(pack, 2 * r) for r in range(1, spots)]
+    out_all = lax.all_gather(out_low, "tensor", axis=0, tiled=True)
 
     gqkv, glm = attn_bwd(ti.reshape(1), parts, ctxt, q3, k3, v3, qt, kt, lse, lmt)
-    back = jnp.einsum("kte,kde->td", gqkv, w_qkv, preferred_element_type=F32)
-    mine = (jnp.arange(n_t) == ti)[:, None, None]
-    back = back.reshape(n_t, chunk, width) + jnp.where(mine, grad_resid[None], 0.0)
-    back = back.reshape(tokens, width).astype(BF16)
-    grad_hidden = lax.psum(back, "tensor")
-    gqkv, glm, a_keep, a_came, b_keep, b_came, _ = lax.optimization_barrier(
-        (gqkv, glm, a_keep, a_came, b_keep, b_came, back)
+    gqkv, glm, a_keep, a_came, b_keep, b_came, *packs = lax.optimization_barrier(
+        (gqkv, glm, a_keep, a_came, b_keep, b_came, *packs)
     )
-    g_a = finish(narrow((a_keep.astype(F32) + a_came.astype(F32)).astype(BF16), low_bits[1:]))
-    g_b = finish(narrow((b_keep.astype(F32) + b_came.astype(F32)).astype(BF16), high_bits[1:]))
-
-    g_qkv_w = [dot_tn(hidden, gqkv[n]).astype(BF16) for n in range(3)]
-    slope = jax.nn.sigmoid((table + noise) * (-1.0 / SOFTENING)) * (1.0 / SOFTENING)
-    g_mask = (glm * slope).astype(BF16).reshape(2, -1, table.shape[2])
-    tail = jnp.concatenate([g_mask[0], g_mask[1]] + g_qkv_w, axis=1)
+    parts = [rows_of(gqkv, ti * chunk, chunk)] + [
+        shift(rows_of(gqkv, lax.rem(ti + s, n_t) * chunk, chunk), n_t, s) for s in range(1, n_t)
+    ]
+    a_keep, a_send, bit = narrow_pair(a_keep, a_came, low_bits[1:])
+    a_came = dp_swap(a_send, bit)
+    b_keep, b_send, bit = narrow_pair(b_keep, b_came, high_bits[1:])
+    b_came = dp_swap(b_send, bit)
+    tail = tail_of(hidden, gqkv, glm, table, noise, 3 * local)
+    w_all = jnp.concatenate([jnp.where(up, w_other, w_side), jnp.where(up, w_side, w_other)], axis=1)
+    held = lax.optimization_barrier((*parts, w_all, tail, a_keep, a_came, b_keep, b_came, *packs))
+    parts, w_all, (tail, a_keep, a_came, b_keep, b_came, *packs) = held[:n_t], held[n_t], held[n_t + 1 :]
+    g_a = (a_keep.astype(F32) + a_came.astype(F32)).astype(BF16)
+    g_b = (b_keep.astype(F32) + b_came.astype(F32)).astype(BF16)
+    g_a = finish(narrow(g_a, low_bits[2:]))
+    g_b = finish(narrow(g_b, high_bits[2:]))
+    pack = packs[0]
+    for p in packs[1:]:
+        pack = pack + p
+    pack_came = swap(pack, "tensor", n_t, 1)
+    total = jnp.concatenate([g_a, g_b], axis=1)
+    pieces = [total[0]] + [shift(total[s], n_t, -s) for s in range(1, n_t)]
     tail = tail.reshape(2, spots, -1, tail.shape[1])
     send = lax.dynamic_index_in_dim(tail, 1 - core, 0, keepdims=False)
     keep = lax.dynamic_index_in_dim(tail, core, 0, keepdims=False)
-    tail = (keep.astype(F32) + dp_swap(send, 1).astype(F32)).astype(BF16)
+    came = dp_swap(send, 1)
+    back = back_of(ti.reshape(1), w_all, grad_resid, parts)
+    back, keep, came, pack, pack_came, *pieces = lax.optimization_barrier(
+        (back, keep, came, pack, pack_came, *pieces)
+    )
+    grad_hidden = lax.all_gather(back, "tensor", axis=0, tiled=True)
+    summed = pieces[0].astype(F32)
+    for p in pieces[1:]:
+        summed = summed + p.astype(F32)
+    held = quad_gather(summed.astype(BF16))
+    tail = (keep.astype(F32) + came.astype(F32)).astype(BF16)
     tail = jnp.concatenate(quad_gather(finish(quad_sum(tail))))
     other = dp_swap(tail, 1)
     tail = jnp.concatenate([jnp.where(up, other, tail), jnp.where(up, tail, other)])
-    cols = table.shape[2]
-    g_mask = jnp.stack([tail[:, :cols], tail[:, cols : 2 * cols]])
-    g_qkv_w = jnp.stack([tail[:, 2 * cols + n * local : 2 * cols + (n + 1) * local] for n in range(3)])
-    g_b_qv = everyone(jnp.sum(gqkv[0::2].astype(F32), axis=1))
-
-    g_a, g_b, out_all = lax.optimization_barrier((g_a, g_b, out_all))
-    out_states = out_all.astype(F32)
-    total = jnp.concatenate([g_a, g_b], axis=1)
-    summed = total[0].astype(F32)
-    for s in range(1, n_t):
-        summed = summed + shift(total[s], n_t, -s).astype(F32)
-    summed = summed.astype(BF16)
-    held = quad_gather(summed)
     g_ao = jnp.concatenate([x[slab:cut] for x in held])
     pair = jnp.stack([jnp.concatenate([x[:slab] for x in held]), jnp.concatenate([x[cut:] for x in held])])
     other = dp_swap(pair, 1)
     pair = jnp.concatenate([jnp.where(up, other, pair), jnp.where(up, pair, other)], axis=1)
+    pack = pack + pack_came
+    for bit in extra:
+        pack = pack + dp_swap(pack, bit)
+    bit = 2
+    while bit < n_t:
+        pack = pack + swap(pack, "tensor", n_t, bit)
+        bit *= 2
+    cols = table.shape[2]
+    at = 2 * cols + 3 * local
+    extra_cols = tail.shape[1] - at
+    g_mask = jnp.stack([tail[:, :cols], tail[:, cols : 2 * cols]])
+    g_qkv_w = jnp.stack([tail[:, 2 * cols + n * local : 2 * cols + (n + 1) * local] for n in range(3)])
+    g_b_qv = tail[: 3 * local // extra_cols, at:].reshape(3, local)[0::2]
+    out_states = out_all.astype(F32)
     g_up = pair[0].T
     g_down = pair[1]
 

time: 485 us -> 481 us (level)
  Pallas kernels: 121 us -> 150 us
  matrix products: 20.6 us -> 0 us
  waiting for transfers between devices: 136 us -> 121 us
  local copies, waits for them, and re-layouts: 59.5 us -> 52.1 us
  other arithmetic: 54.1 us -> 59.7 us
    psum x1 -> x0, waiting for transfers between devices: 38.8 us -> none  [body(): grad_hidden = lax.psum(back, 'tensor')]
    pallas_call x0 -> x4, Pallas kernels: none -> 25.6 us  [the longest x1 11.8 us: tail_of(): pl.pallas_call(tail_kernel, out_shape=sd((heads * period // 2, -(-lanes /...]
    dot_general x12 -> x0, matrix products: 20.6 us -> none  [the longest x11 14.4 us: dot_tn(): lax.dot_general(a, b, (((0,), (0,)), ((), ())), preferred_element_type=F32)]
    ppermute x32 -> x30, waiting for transfers between devices: 41.2 us -> 56.5 us  [swap(): return lax.ppermute(x, axis, [(j, j ^ bit) for j in range(size)])]
    ppermute x12 -> x15, waiting for transfers between devices: 56 us -> 64.3 us  [shift(): lax.ppermute(x, 'tensor', [(j, (j + amount) % size) for j in range(size)])]
    concatenate x6 -> x0, local copies, waits for them, and re-layouts: 8.1 us -> none  [the longest x4 6.52 us: body(): tail = jnp.concatenate([g_mask[0], g_mask[1]] + g_qkv_w, axis=1)]
    squeeze x6 -> x0, local copies, waits for them, and re-layouts: 7.66 us -> none  [the longest x2 2.66 us: narrow_start(): send = lax.dynamic_index_in_dim(x, 1 - up, ax, keepdims=False)]
    ppermute x32 -> x30, starting transfers between devices: 25.2 us -> 29.4 us  [swap(): return lax.ppermute(x, axis, [(j, j ^ bit) for j in range(size)])]
  transfers between devices with their start and end apart: 46 -> 48, of which waited for: 18 -> 14; matrix products, arithmetic and copies ran while one was open for 22% -> 18% of each run, Pallas kernels for 18% -> 32%
where the time goes in v4:
time: 481 us; the launch traced here: 474 us
  Pallas kernels  150 us (31%)
  waiting for transfers between devices  121 us (25%)
  starting transfers between devices  72.3 us (15%)
  other arithmetic  59.7 us (12%)
  local copies, waits for them, and re-layouts  52.1 us (11%)
  between operations  18.4 us (4%)
    ppermute x15, waiting for transfers between devices, shift(): lax.ppermute(x, 'tensor', [(j, (j + amount) % size) for j in range(size)])  64.3 us
    ppermute x30, waiting for transfers between devices, swap(): return lax.ppermute(x, axis, [(j, j ^ bit) for j in range(size)])  56.5 us
    ppermute x15, starting transfers between devices, shift(): lax.ppermute(x, 'tensor', [(j, (j + amount) % size) for j in range(size)])  42.8 us
    pallas_call x1, Pallas kernels, attn_bwd(): pl.pallas_call(functools.partial(attn_bwd_kernel, n_t), in_specs=[pl.Bloc...  41.4 us
    pallas_call x1, Pallas kernels, ffn(): pl.pallas_call(functools.partial(ffn_kernel, n_t, slab), in_specs=[sm] +...  37.5 us
    pallas_call x3, Pallas kernels, attn_fwd(): pl.pallas_call(functools.partial(attn_fwd_kernel, lo, len(prev)), grid=(h...  30.8 us
    ppermute x30, starting transfers between devices, swap(): return lax.ppermute(x, axis, [(j, j ^ bit) for j in range(size)])  29.4 us
    unnamed x118, local copies, waits for them, and re-layouts  21.1 us
  transfers between devices with their start and end apart: 48, of which 14 were waited for; matrix products, arithmetic and copies ran while one was open for 18% of the time, Pallas kernels for 32%

profile of v4, /device:TPU:0, one launch (start us, length us, event | category | flops | bytes accessed | tf_op | source)
XLA Modules:
  0.0 473.8 jit_solution(2368358744134101249)
XLA Ops:
  11.4 3.1 collective-permute-start
  14.5 2.6 collective-permute-start.1
  20.7 15.1 %attn_prep.1 = (bf16[3,2048,64]{2,1,0:T(8,128)(2,1)}, bf16[3,2048,64]{2,1,0:T(8,128)(2,1)}, bf16[3,2048,64]{2,1,0:T(8,128)(2,1)}, bf16[192,2048]{1,0:T(8,128)(2,...) custom-call(bf16[2048,768]{1,0:T(8,128)(2,1)} %hid.3, ...), custom_call_target="tpu_custom_call" | custom-call | flops 15000000512 | bytes 20971520 | tf_op jit(solution)/shard_map/attn_prep/pallas_call | solution.py:75
  36.6 9.5 %attn_fwd.3 = (bf16[2048,192]{1,0:T(8,128)(2,1)}, f32[192,2048]{1,0:T(8,128)}, f32[8,2048]{1,0:T(8,128)}) custom-call(bf16[192,2048]{1,0:T(8,128)(2,1)} %get-tuple-element.122.qt.refs_8_, bf16[3,2048,64]{2,1,0:T(8,128)(2,1)} %get-tuple-element.123.k3.refs_6_, bf16[192,2048]{1,0:T(8,128)(2,1)} %get-tuple-element.124.vt, ...), custom_call_target="tpu_custom_call" | custom-call | flops 3000000000 | bytes 8388608 | tf_op jit(solution)/shard_map/attn_fwd/pallas_call | solution.py:148
  52.1 9.6 %attn_fwd.4 = (bf16[2048,192]{1,0:T(8,128)(2,1)}, f32[192,2048]{1,0:T(8,128)}, f32[8,2048]{1,0:T(8,128)}) custom-call(bf16[192,2048]{1,0:T(8,128)(2,1)} %get-tuple-element.122.qt.refs_8_, bf16[3,2048,64]{2,1,0:T(8,128)(2,1)} %get-tuple-element.123.k3.refs_6_, ...), custom_call_target="tpu_custom_call", output_to_operand_aliasing={{0}: (4, {}), {1}: (5, {}), {2}: (6, {})} | custom-call | flops 3750000128 | bytes 8388608 | tf_op jit(solution)/shard_map/attn_fwd/pallas_call | solution.py:148
  61.7 2.1 collective-permute-done.3
  72.7 11.7 %attn_fwd.5 = (bf16[2048,192]{1,0:T(8,128)(2,1)}, f32[192,2048]{1,0:T(8,128)}, f32[8,2048]{1,0:T(8,128)}) custom-call(bf16[192,2048]{1,0:T(8,128)(2,1)} %get-tuple-element.122.qt.refs_8_, bf16[3,2048,64]{2,1,0:T(8,128)(2,1)} %get-tuple-element.123.k3.refs_6_, ...), custom_call_target="tpu_custom_call", output_to_operand_aliasing={{0}: (4, {}), {1}: (5, {}), {2}: (6, {})} | custom-call | flops 5249999872 | bytes 8388608 | tf_op jit(solution)/shard_map/attn_fwd/pallas_call | solution.py:148
  84.4 2.0 constant_dynamic-slice_fusion.9
  86.4 5.9 %collective-permute-start.5 = (bf16[512,192]{1,0:T(8,128)(2,1)S(1)}, bf16[512,192]{1,0:T(8,128)(2,1)S(1)}, u32[]{:S(2)}, u32[]{:S(2)}) collective-permute-start(bf16[512,192]{1,0:T(8,128)(2,1)S(1)} %get-tuple-element.344), channel_id=1, source_target_pairs={{0,1},{1,2},{2,3},{3,0},{4,5},{5,6},{6,7},{7,4},{8,9},{9,10},{10,1... | collective-permute-start | bytes 589832 | tf_op jit(solution)/shard_map/ppermute | solution.py:521
  99.7 1.9 collective-permute-done.5.refs_1_
  101.7 9.8 %collective-permute-done.6.refs_2_ = bf16[512,192]{1,0:T(8,128)(2,1)S(1)} collective-permute-done((bf16[512,192]{1,0:T(8,128)(2,1)S(1)}, bf16[512,192]{1,0:T(8,128)(2,1)S(1)}, u32[]{:S(2)}, u32[]{:S(2)}) %collective-permute-start.6) | collective-permute-done | bytes 196640 | tf_op jit(solution)/shard_map/ppermute | solution.py:521
  113.6 2.1 constant_dynamic-slice_fusion.8.refs_5_
  115.6 2.7 constant_dynamic-slice_fusion.7.refs_6_
  123.7 37.5 %ffn.1 = (f32[512,768]{1,0:T(8,128)}, bf16[512,768]{1,0:T(8,128)(2,1)}, bf16[512,1536]{1,0:T(8,128)(2,1)}, bf16[512,1536]{1,0:T(8,128)(2,1)}, bf16[512,1536]{1,0...) custom-call(s32[1]{0:T(128)} %bitcast.core, ...), custom_call_target="tpu_custom_call" | custom-call | flops 33999998976 | bytes 26214400 | tf_op jit(solution)/shard_map/ffn/pallas_call | solution.py:492
  170.2 4.4 wgrad.2
  174.8 6.4 %collective-permute-start.12 = (bf16[512,192]{1,0:T(8,128)(2,1)S(1)}, bf16[512,192]{1,0:T(8,128)(2,1)S(1)}, u32[]{:S(2)}, u32[]{:S(2)}) collective-permute-start(bf16[512,192]{1,0:T(8,128)(2,1)S(1)} %copy-done.52), channel_id=1, source_target_pairs={{0,3},{1,0},{2,1},{3,2},{4,7},{5,4},{6,5},{7,6},{8,11},{9,8},{10,9... | collective-permute-start | bytes 589832 | tf_op jit(solution)/shard_map/ppermute | solution.py:521
  185.4 4.4 wgrad.3
  192.1 2.2 slice.181
  194.4 2.2 fusion.3
  196.6 2.6 fusion.1
  199.2 6.4 %collective-permute-done.13.refs_2_ = bf16[512,192]{1,0:T(8,128)(2,1)S(1)} collective-permute-done((bf16[512,192]{1,0:T(8,128)(2,1)S(1)}, bf16[512,192]{1,0:T(8,128)(2,1)S(1)}, u32[]{:S(2)}, u32[]{:S(2)}) %collective-permute-start.13) | collective-permute-done | bytes 196640 | tf_op jit(solution)/shard_map/ppermute | solution.py:521
  214.4 41.4 %attn_bwd.1 = (bf16[2048,640]{1,0:T(8,128)(2,1)}, f32[3,512,512]{2,1,0:T(8,128)}) custom-call(s32[1]{0:T(128)} %bitcast.48.place, bf16[512,192]{1,0:T(8,128)(2,1)} %get-tuple-element.175.refs_0_, bf16[512,192]{1,0:T(8,128)(2,1)} %copy-done.51, bf16[512,192]{1,0:T(8,128)(2,1)} %copy-done.53, bf16[512,192]{1,0:T(8,128)(2,1)} %copy-done.54, ...), custom_call_target="tpu_custom_call" | custom-call | flops 399999991808 | bytes 20971520 | tf_op jit(solution)/shard_map/attn_bwd/pallas_call | solution.py:245
  255.9 2.7 fusion.12
  258.9 3.3 fusion.6
  264.9 3.2 collective-permute-start.25
  268.1 11.8 %tail.1 = bf16[768,1664]{1,0:T(8,128)(2,1)} custom-call(bf16[2048,768]{1,0:T(8,128)(2,1)} %hid.3, bf16[2048,640]{1,0:T(8,128)(2,1)} %get-tuple-element.192.gqkv, f32[3,512,512]{2,1,0:T(8,128)} %get-tuple-element.195.glm, f32[3,512,512]{2,1,0:T(8,128)} %table.3, f32[3,512,512]{2,1,0:T(8,128)} %noise.3), custom_call_target="tpu_custom_call" | custom-call | flops 399999991808 | bytes 20971520 | tf_op jit(solution)/shard_map/tail/pallas_call | solution.py:339
  279.9 10.4 %collective-permute-done.23.refs_1_ = bf16[512,640]{1,0:T(8,128)(2,1)} collective-permute-done((bf16[512,640]{1,0:T(8,128)(2,1)}, bf16[512,640]{1,0:T(8,128)(2,1)}, u32[]{:S(2)}, u32[]{:S(2)}) %collective-permute-start.23) | collective-permute-done | bytes 655392 | tf_op jit(solution)/shard_map/ppermute | solution.py:521
  290.3 26.9 %collective-permute-done.24.refs_2_ = bf16[512,640]{1,0:T(8,128)(2,1)} collective-permute-done((bf16[512,640]{1,0:T(8,128)(2,1)}, bf16[512,640]{1,0:T(8,128)(2,1)}, u32[]{:S(2)}, u32[]{:S(2)}) %collective-permute-start.24) | collective-permute-done | bytes 655392 | tf_op jit(solution)/shard_map/ppermute | solution.py:521
  317.2 3.4 dynamic-slice_bitcast_fusion
  324.5 14.4 %collective-permute-start.30 = (bf16[240,768]{1,0:T(8,128)(2,1)}, bf16[240,768]{1,0:T(8,128)(2,1)}, u32[]{:S(2)}, u32[]{:S(2)}) collective-permute-start(bf16[240,768]{1,0:T(8,128)(2,1)} %get-tuple-element.331), channel_id=1, source_target_pairs={{0,3},{1,0},{2,1},{3,2},{4,7},{5,4},{6,5},{7,6},{8,11},{9,8},{10,9... | collective-permute-start | bytes 1105928 | tf_op jit(solution)/shard_map/ppermute | solution.py:521
  341.6 2.2 collective-permute-start.29
  343.8 5.0 %back.1 = bf16[512,768]{1,0:T(8,128)(2,1)} custom-call(s32[1]{0:T(128)} %bitcast.48.place, bf16[4,576,768]{2,1,0:T(8,128)(2,1)S(1)} %pad_maximum_fusion.w, f32[512,768]{1,0:T(8,128)S(1)} %copy-done.11, bf16[512,640]{1,0:T(8,128)(2,1)S(1)} %get-tuple-element.206.refs_0_, bf16[512,640]{1,0:T(8,128)(2,1)} %collective-permute-done.23.refs_1_, ...), custom_call_target="tpu_custom_call" | custom-call | flops 5000000000 | bytes 10485760 | tf_op jit(solution)/shard_map/back/pallas_call | solution.py:360
  348.8 15.5 %collective-permute-done.29 = f32[72,128]{1,0:T(8,128)} collective-permute-done((f32[72,128]{1,0:T(8,128)}, f32[72,128]{1,0:T(8,128)}, u32[]{:S(2)}, u32[]{:S(2)}) %collective-permute-start.29) | collective-permute-done | bytes 36896 | tf_op jit(solution)/shard_map/ppermute | solution.py:525
  364.3 8.7 %collective-permute-done.31 = bf16[240,768]{1,0:T(8,128)(2,1)} collective-permute-done((bf16[240,768]{1,0:T(8,128)(2,1)}, bf16[240,768]{1,0:T(8,128)(2,1)}, u32[]{:S(2)}, u32[]{:S(2)}) %collective-permute-start.31) | collective-permute-done | bytes 368672 | tf_op jit(solution)/shard_map/ppermute | solution.py:521
  373.0 2.0 add_convert_fusion.2
  380.9 2.4 collective-permute-start.41
  383.9 2.7 collective-permute-done.34
  388.1 14.7 %collective-permute-done.35 = bf16[96,1664]{1,0:T(8,128)(2,1)S(1)} collective-permute-done((bf16[96,1664]{1,0:T(8,128)(2,1)}, bf16[96,1664]{1,0:T(8,128)(2,1)S(1)}, u32[]{:S(2)}, u32[]{:S(2)}) %collective-permute-start.35) | collective-permute-done | bytes 319520 | tf_op jit(solution)/shard_map/ppermute | solution.py:525
  404.7 1.9 collective-permute-start.39
  406.6 11.0 %collective-permute-done.42 = bf16[240,768]{1,0:T(8,128)(2,1)S(1)} collective-permute-done((bf16[240,768]{1,0:T(8,128)(2,1)S(1)}, bf16[240,768]{1,0:T(8,128)(2,1)S(1)}, u32[]{:S(2)}, u32[]{:S(2)}) %collective-permute-start.42) | collective-permute-done | bytes 368672 | tf_op jit(solution)/shard_map/ppermute | solution.py:525
  419.8 2.8 collective-permute-done.38
  425.8 7.0 %collective-permute-done.33 = f32[72,128]{1,0:T(8,128)S(1)} collective-permute-done((f32[72,128]{1,0:T(8,128)S(1)}, f32[72,128]{1,0:T(8,128)S(1)}, u32[]{:S(2)}, u32[]{:S(2)}) %collective-permute-start.33) | collective-permute-done | bytes 36896 | tf_op jit(solution)/shard_map/ppermute | solution.py:525
  440.7 5.1 %convert_element_type.263 = f32[2048,768]{1,0:T(8,128)} convert(bf16[2048,768]{1,0:T(8,128)(2,1)} %all-gather.5.cloned.1.call-done) | non-fusion elementwise | flops 1572864 | bytes 9437184 | tf_op jit(solution)/shard_map/convert_element_type | solution.py:784
  449.0 1.9 copy.106
  453.2 1.8 convert_multiply_fusion.2
  455.0 2.9 copy.105
  458.0 2.1 convert_multiply_fusion.1
  460.7 5.0 %convert_multiply_fusion = f32[2048,768]{1,0:T(8,128)} fusion(bf16[2048,768]{1,0:T(8,128)(2,1)} %all-gather.7.cloned.1.call-done, f32[]{:T(128)} %bitcast.62), kind=kLoop, calls=%fused_computation.1 | loop fusion | flops 3145728 | bytes 9437188 | tf_op jit(solution)/shard_map/mul | solution.py:798
  (296 shorter events, 98.9 us)
Async XLA Ops:
  7.2 104.3 %all-gather.9.cloned.1.call-start = ((), (), s32[]{:S(2)}) async-start(), calls=%async_computation.2 | async-start | bytes 2211840 | tf_op jit(solution)/shard_map/all_gather | solution.py:651
  11.4 34.7 %collective-permute-start = (bf16[256,768]{1,0:T(8,128)(2,1)S(1)}, bf16[256,768]{1,0:T(8,128)(2,1)}, u32[]{:S(2)}, u32[]{:S(2)}) collective-permute-start(bf16[256,768]{1,0:T(8,128)(2,1)S(1)} %concatenate.53), channel_id=1, source_target_pairs={{0,1},{1,2},{2,3},{3,0},{4,5},{5,6},{6,7},{7,4},{8,9},{9,10},{10,1... | collective-permute-start | bytes 1179656 | tf_op jit(solution)/shard_map/ppermute | solution.py:521
  14.5 31.6 %collective-permute-start.1 = (bf16[256,768]{1,0:T(8,128)(2,1)S(1)}, bf16[256,768]{1,0:T(8,128)(2,1)S(1)}, u32[]{:S(2)}, u32[]{:S(2)}) collective-permute-start(bf16[256,768]{1,0:T(8,128)(2,1)S(1)} %concatenate.53), channel_id=1, source_target_pairs={{0,2},{1,3},{2,0},{3,1},{4,6},{5,7},{6,4},{7,5},{8,10},{9,11},{10,... | collective-permute-start | bytes 1179656 | tf_op jit(solution)/shard_map/ppermute | solution.py:521
  17.1 29.0 %collective-permute-start.2 = (bf16[256,768]{1,0:T(8,128)(2,1)S(1)}, bf16[256,768]{1,0:T(8,128)(2,1)S(1)}, u32[]{:S(2)}, u32[]{:S(2)}) collective-permute-start(bf16[256,768]{1,0:T(8,128)(2,1)S(1)} %concatenate.53), channel_id=1, source_target_pairs={{0,3},{1,0},{2,1},{3,2},{4,7},{5,4},{6,5},{7,6},{8,11},{9,8},{10,9... | collective-permute-start | bytes 1179656 | tf_op jit(solution)/shard_map/ppermute | solution.py:521
  47.9 15.9 %collective-permute-start.3 = (bf16[3,144,768]{2,1,0:T(8,128)(2,1)S(1)}, bf16[3,144,768]{2,1,0:T(8,128)(2,1)S(1)}, u32[]{:S(2)}, u32[]{:S(2)}) collective-permute-start(bf16[3,144,768]{2,1,0:T(8,128)(2,1)S(1)} %pad_maximum_fusion.10), channel_id=1, source_target_pairs={{0,8},{4,12},{8,0},{12,4},{16,24},{20,28},{24,16},{28,20},{1,9},{5... | collective-permute-start | bytes 1990664 | tf_op jit(solution)/shard_map/ppermute | solution.py:525
  50.5 11.3 %collective-permute-start.4 = (bf16[3,96,768]{2,1,0:T(8,128)(2,1)S(1)}, bf16[3,96,768]{2,1,0:T(8,128)(2,1)S(1)}, u32[]{:S(2)}, u32[]{:S(2)}) collective-permute-start(bf16[3,96,768]{2,1,0:T(8,128)(2,1)S(1)} %pad_maximum_fusion.11), channel_id=1, source_target_pairs={{0,16},{4,20},{8,24},{12,28},{16,0},{20,4},{24,8},{28,12},{1,17},{... | collective-permute-start | bytes 1327112 | tf_op jit(solution)/shard_map/ppermute | solution.py:525
  52.1 388.7 %all-gather.5.cloned.1.call-start = ((), (), s32[]{:S(2)}) async-start(), calls=%async_computation | async-start | bytes 3932160 | tf_op jit(solution)/shard_map/all_gather | solution.py:723
  65.9 28.8 %collective-permute-start.9 = (bf16[2,3,96,768]{3,2,1,0:T(8,128)(2,1)}, bf16[2,3,96,768]{3,2,1,0:T(8,128)(2,1)}, u32[]{:S(2)}, u32[]{:S(2)}) collective-permute-start(bf16[2,3,96,768]{3,2,1,0:T(8,128)(2,1)} %pad_maximum_fusion.8), channel_id=1, source_target_pairs={{0,8},{4,12},{8,0},{12,4},{16,24},{20,28},{24,16},{28,20},{1,9},{5... | collective-permute-start | bytes 2654216 | tf_op jit(solution)/shard_map/ppermute | solution.py:525
  68.7 29.2 %collective-permute-start.8 = (bf16[2,3,144,768]{3,2,1,0:T(8,128)(2,1)}, bf16[2,3,144,768]{3,2,1,0:T(8,128)(2,1)}, u32[]{:S(2)}, u32[]{:S(2)}) collective-permute-start(bf16[2,3,144,768]{3,2,1,0:T(8,128)(2,1)} %pad_maximum_fusion.3), channel_id=1, source_target_pairs={{0,16},{4,20},{8,24},{12,28},{16,0},{20,4},{24,8},{28,12},{1,17},{... | collective-permute-start | bytes 3981320 | tf_op jit(solution)/shard_map/ppermute | solution.py:525
  86.4 15.3 %collective-permute-start.5 = (bf16[512,192]{1,0:T(8,128)(2,1)S(1)}, bf16[512,192]{1,0:T(8,128)(2,1)S(1)}, u32[]{:S(2)}, u32[]{:S(2)}) collective-permute-start(bf16[512,192]{1,0:T(8,128)(2,1)S(1)} %get-tuple-element.344), channel_id=1, source_target_pairs={{0,1},{1,2},{2,3},{3,0},{4,5},{5,6},{6,7},{7,4},{8,9},{9,10},{10,1... | collective-permute-start | bytes 589832 | tf_op jit(solution)/shard_map/ppermute | solution.py:521
  92.2 19.3 %collective-permute-start.6 = (bf16[512,192]{1,0:T(8,128)(2,1)S(1)}, bf16[512,192]{1,0:T(8,128)(2,1)S(1)}, u32[]{:S(2)}, u32[]{:S(2)}) collective-permute-start(bf16[512,192]{1,0:T(8,128)(2,1)S(1)} %get-tuple-element.343), channel_id=1, source_target_pairs={{0,2},{1,3},{2,0},{3,1},{4,6},{5,7},{6,4},{7,5},{8,10},{9,11},{10,... | collective-permute-start | bytes 589832 | tf_op jit(solution)/shard_map/ppermute | solution.py:521
  93.4 18.1 %collective-permute-start.7 = (bf16[512,192]{1,0:T(8,128)(2,1)S(1)}, bf16[512,192]{1,0:T(8,128)(2,1)S(1)}, u32[]{:S(2)}, u32[]{:S(2)}) collective-permute-start(bf16[512,192]{1,0:T(8,128)(2,1)S(1)} %get-tuple-element.342), channel_id=1, source_target_pairs={{0,3},{1,0},{2,1},{3,2},{4,7},{5,4},{6,5},{7,6},{8,11},{9,8},{10,9... | collective-permute-start | bytes 589832 | tf_op jit(solution)/shard_map/ppermute | solution.py:521
  112.9 10.7 %collective-permute-start.10 = (bf16[1152,768]{1,0:T(8,128)(2,1)}, bf16[1152,768]{1,0:T(8,128)(2,1)}, u32[]{:S(2)}, u32[]{:S(2)}) collective-permute-start(bf16[1152,768]{1,0:T(8,128)(2,1)} %bitcast.31.refs_11_), channel_id=1, source_target_pairs={{0,4},{4,0},{8,12},{12,8},{16,20},{20,16},{24,28},{28,24},{1,5},{5... | collective-permute-start | bytes 5308424 | tf_op jit(solution)/shard_map/ppermute | solution.py:525
  113.0 10.6 %collective-permute-start.11 = (bf16[1152,768]{1,0:T(8,128)(2,1)}, bf16[1152,768]{1,0:T(8,128)(2,1)}, u32[]{:S(2)}, u32[]{:S(2)}) collective-permute-start(bf16[1152,768]{1,0:T(8,128)(2,1)} %bitcast.32.refs_14_), channel_id=1, source_target_pairs={{0,4},{4,0},{8,12},{12,8},{16,20},{20,16},{24,28},{28,24},{1,5},{5... | collective-permute-start | bytes 5308424 | tf_op jit(solution)/shard_map/ppermute | solution.py:525
  122.4 38.8 %collective-permute-start.16 = (bf16[4,288,768]{2,1,0:T(8,128)(2,1)S(1)}, bf16[4,288,768]{2,1,0:T(8,128)(2,1)S(1)}, u32[]{:S(2)}, u32[]{:S(2)}) collective-permute-start(bf16[4,288,768]{2,1,0:T(8,128)(2,1)S(1)} %bitcast.166), channel_id=1, source_target_pairs={{0,4},{4,0},{8,12},{12,8},{16,20},{20,16},{24,28},{28,24},{1,5},{5... | collective-permute-start | bytes 5308424 | tf_op jit(solution)/shard_map/ppermute | solution.py:525
  163.5 19.5 %collective-permute-start.17 = (f32[72,128]{1,0:T(8,128)S(1)}, f32[72,128]{1,0:T(8,128)S(1)}, u32[]{:S(2)}, u32[]{:S(2)}) collective-permute-start(f32[72,128]{1,0:T(8,128)S(1)} %maximum_bitcast_fusion.6), channel_id=1, source_target_pairs={{0,4},{4,0},{8,12},{12,8},{16,20},{20,16},{24,28},{28,24},{1,5},{5... | collective-permute-start | bytes 110600 | tf_op jit(solution)/shard_map/ppermute | solution.py:525
  174.7 15.1 %collective-permute-start.15 = (bf16[4,4,240,768]{3,2,1,0:T(8,128)(2,1)S(1)}, bf16[4,4,240,768]{3,2,1,0:T(8,128)(2,1)}, u32[]{:S(2)}, u32[]{:S(2)}) collective-permute-start(bf16[4,4,240,768]{3,2,1,0:T(8,128)(2,1)S(1)} %wgrad.2), channel_id=1, source_target_pairs={{0,4},{4,0},{8,12},{12,8},{16,20},{20,16},{24,28},{28,24},{1,5},{5... | collective-permute-start | bytes 17694728 | tf_op jit(solution)/shard_map/ppermute | solution.py:525
  174.8 24.4 %collective-permute-start.12 = (bf16[512,192]{1,0:T(8,128)(2,1)S(1)}, bf16[512,192]{1,0:T(8,128)(2,1)S(1)}, u32[]{:S(2)}, u32[]{:S(2)}) collective-permute-start(bf16[512,192]{1,0:T(8,128)(2,1)S(1)} %copy-done.52), channel_id=1, source_target_pairs={{0,3},{1,0},{2,1},{3,2},{4,7},{5,4},{6,5},{7,6},{8,11},{9,8},{10,9... | collective-permute-start | bytes 589832 | tf_op jit(solution)/shard_map/ppermute | solution.py:521
  181.2 24.5 %collective-permute-start.13 = (bf16[512,192]{1,0:T(8,128)(2,1)S(1)}, bf16[512,192]{1,0:T(8,128)(2,1)S(1)}, u32[]{:S(2)}, u32[]{:S(2)}) collective-permute-start(bf16[512,192]{1,0:T(8,128)(2,1)S(1)} %copy-done.50), channel_id=1, source_target_pairs={{0,2},{1,3},{2,0},{3,1},{4,6},{5,7},{6,4},{7,5},{8,10},{9,11},{10,... | collective-permute-start | bytes 589832 | tf_op jit(solution)/shard_map/ppermute | solution.py:521
  182.2 23.4 %collective-permute-start.14 = (bf16[512,192]{1,0:T(8,128)(2,1)S(1)}, bf16[512,192]{1,0:T(8,128)(2,1)S(1)}, u32[]{:S(2)}, u32[]{:S(2)}) collective-permute-start(bf16[512,192]{1,0:T(8,128)(2,1)S(1)} %copy-done.49), channel_id=1, source_target_pairs={{0,1},{1,2},{2,3},{3,0},{4,5},{5,6},{6,7},{7,4},{8,9},{9,10},{10,1... | collective-permute-start | bytes 589832 | tf_op jit(solution)/shard_map/ppermute | solution.py:521
  207.9 47.9 %collective-permute-start.20 = (f32[72,128]{1,0:T(8,128)}, f32[72,128]{1,0:T(8,128)}, u32[]{:S(2)}, u32[]{:S(2)}) collective-permute-start(f32[72,128]{1,0:T(8,128)} %add.272), channel_id=1, source_target_pairs={{0,8},{4,12},{8,0},{12,4},{16,24},{20,28},{24,16},{28,20},{1,9},{5... | collective-permute-start | bytes 110600 | tf_op jit(solution)/shard_map/ppermute | solution.py:525
  209.4 46.5 %collective-permute-start.21 = (f32[72,128]{1,0:T(8,128)}, f32[72,128]{1,0:T(8,128)}, u32[]{:S(2)}, u32[]{:S(2)}) collective-permute-start(f32[72,128]{1,0:T(8,128)} %add.272), channel_id=1, source_target_pairs={{0,16},{4,20},{8,24},{12,28},{16,0},{20,4},{24,8},{28,12},{1,17},{... | collective-permute-start | bytes 110600 | tf_op jit(solution)/shard_map/ppermute | solution.py:525
  210.8 45.0 %collective-permute-start.22 = (f32[72,128]{1,0:T(8,128)}, f32[72,128]{1,0:T(8,128)}, u32[]{:S(2)}, u32[]{:S(2)}) collective-permute-start(f32[72,128]{1,0:T(8,128)} %add.272), channel_id=1, source_target_pairs={{0,24},{4,28},{8,16},{12,20},{16,8},{20,12},{24,0},{28,4},{1,25},{... | collective-permute-start | bytes 110600 | tf_op jit(solution)/shard_map/ppermute | solution.py:525
  211.4 44.5 %collective-permute-start.18 = (bf16[2,4,144,768]{3,2,1,0:T(8,128)(2,1)}, bf16[2,4,144,768]{3,2,1,0:T(8,128)(2,1)}, u32[]{:S(2)}, u32[]{:S(2)}) collective-permute-start(bf16[2,4,144,768]{3,2,1,0:T(8,128)(2,1)} %get-tuple-element.187), channel_id=1, source_target_pairs={{0,8},{4,12},{8,0},{12,4},{16,24},{20,28},{24,16},{28,20},{1,9},{5... | collective-permute-start | bytes 5308424 | tf_op jit(solution)/shard_map/ppermute | solution.py:525
  212.8 43.0 %collective-permute-start.19 = (bf16[2,4,96,768]{3,2,1,0:T(8,128)(2,1)}, bf16[2,4,96,768]{3,2,1,0:T(8,128)(2,1)}, u32[]{:S(2)}, u32[]{:S(2)}) collective-permute-start(bf16[2,4,96,768]{3,2,1,0:T(8,128)(2,1)} %get-tuple-element.189), channel_id=1, source_target_pairs={{0,16},{4,20},{8,24},{12,28},{16,0},{20,4},{24,8},{28,12},{1,17},{... | collective-permute-start | bytes 3538952 | tf_op jit(solution)/shard_map/ppermute | solution.py:525
  214.4 246.4 %all-gather.7.cloned.1.call-start = ((), (), s32[]{:S(2)}) async-start(), calls=%async_computation.1 | async-start | bytes 3932160 | tf_op jit(solution)/shard_map/all_gather | solution.py:758
  258.5 21.4 %collective-permute-start.27 = (bf16[4,96,768]{2,1,0:T(8,128)(2,1)}, bf16[4,96,768]{2,1,0:T(8,128)(2,1)}, u32[]{:S(2)}, u32[]{:S(2)}) collective-permute-start(bf16[4,96,768]{2,1,0:T(8,128)(2,1)} %get-tuple-element.321), channel_id=1, source_target_pairs={{0,8},{4,12},{8,0},{12,4},{16,24},{20,28},{24,16},{28,20},{1,9},{5... | collective-permute-start | bytes 1769480 | tf_op jit(solution)/shard_map/ppermute | solution.py:525
  262.2 55.0 %collective-permute-start.26 = (bf16[4,144,768]{2,1,0:T(8,128)(2,1)}, bf16[4,144,768]{2,1,0:T(8,128)(2,1)}, u32[]{:S(2)}, u32[]{:S(2)}) collective-permute-start(bf16[4,144,768]{2,1,0:T(8,128)(2,1)} %get-tuple-element.298), channel_id=1, source_target_pairs={{0,16},{4,20},{8,24},{12,28},{16,0},{20,4},{24,8},{28,12},{1,17},{... | collective-permute-start | bytes 2654216 | tf_op jit(solution)/shard_map/ppermute | solution.py:525
  263.9 26.3 %collective-permute-start.23 = (bf16[512,640]{1,0:T(8,128)(2,1)}, bf16[512,640]{1,0:T(8,128)(2,1)}, u32[]{:S(2)}, u32[]{:S(2)}) collective-permute-start(bf16[512,640]{1,0:T(8,128)(2,1)} %get-tuple-element.306), channel_id=1, source_target_pairs={{0,1},{1,2},{2,3},{3,0},{4,5},{5,6},{6,7},{7,4},{8,9},{9,10},{10,1... | collective-permute-start | bytes 1966088 | tf_op jit(solution)/shard_map/ppermute | solution.py:521
  263.9 53.3 %collective-permute-start.24 = (bf16[512,640]{1,0:T(8,128)(2,1)}, bf16[512,640]{1,0:T(8,128)(2,1)}, u32[]{:S(2)}, u32[]{:S(2)}) collective-permute-start(bf16[512,640]{1,0:T(8,128)(2,1)} %get-tuple-element.305), channel_id=1, source_target_pairs={{0,2},{1,3},{2,0},{3,1},{4,6},{5,7},{6,4},{7,5},{8,10},{9,11},{10,... | collective-permute-start | bytes 1966088 | tf_op jit(solution)/shard_map/ppermute | solution.py:521
  264.9 52.3 %collective-permute-start.25 = (bf16[512,640]{1,0:T(8,128)(2,1)}, bf16[512,640]{1,0:T(8,128)(2,1)}, u32[]{:S(2)}, u32[]{:S(2)}) collective-permute-start(bf16[512,640]{1,0:T(8,128)(2,1)} %get-tuple-element.304), channel_id=1, source_target_pairs={{0,3},{1,0},{2,1},{3,2},{4,7},{5,4},{6,5},{7,6},{8,11},{9,8},{10,9... | collective-permute-start | bytes 1966088 | tf_op jit(solution)/shard_map/ppermute | solution.py:521
  320.6 52.4 %collective-permute-start.28 = (bf16[4,96,1664]{2,1,0:T(8,128)(2,1)}, bf16[4,96,1664]{2,1,0:T(8,128)(2,1)}, u32[]{:S(2)}, u32[]{:S(2)}) collective-permute-start(bf16[4,96,1664]{2,1,0:T(8,128)(2,1)} %get-tuple-element.315), channel_id=1, source_target_pairs={{0,4},{4,0},{8,12},{12,8},{16,20},{20,16},{24,28},{28,24},{1,5},{5... | collective-permute-start | bytes 3833864 | tf_op jit(solution)/shard_map/ppermute | solution.py:525
  324.5 39.8 %collective-permute-start.30 = (bf16[240,768]{1,0:T(8,128)(2,1)}, bf16[240,768]{1,0:T(8,128)(2,1)}, u32[]{:S(2)}, u32[]{:S(2)}) collective-permute-start(bf16[240,768]{1,0:T(8,128)(2,1)} %get-tuple-element.331), channel_id=1, source_target_pairs={{0,3},{1,0},{2,1},{3,2},{4,7},{5,4},{6,5},{7,6},{8,11},{9,8},{10,9... | collective-permute-start | bytes 1105928 | tf_op jit(solution)/shard_map/ppermute | solution.py:521
  338.9 34.1 %collective-permute-start.31 = (bf16[240,768]{1,0:T(8,128)(2,1)}, bf16[240,768]{1,0:T(8,128)(2,1)}, u32[]{:S(2)}, u32[]{:S(2)}) collective-permute-start(bf16[240,768]{1,0:T(8,128)(2,1)} %get-tuple-element.332), channel_id=1, source_target_pairs={{0,2},{1,3},{2,0},{3,1},{4,6},{5,7},{6,4},{7,5},{8,10},{9,11},{10,... | collective-permute-start | bytes 1105928 | tf_op jit(solution)/shard_map/ppermute | solution.py:521
  340.1 32.9 %collective-permute-start.32 = (bf16[240,768]{1,0:T(8,128)(2,1)}, bf16[240,768]{1,0:T(8,128)(2,1)}, u32[]{:S(2)}, u32[]{:S(2)}) collective-permute-start(bf16[240,768]{1,0:T(8,128)(2,1)} %get-tuple-element.329), channel_id=1, source_target_pairs={{0,1},{1,2},{2,3},{3,0},{4,5},{5,6},{6,7},{7,4},{8,9},{9,10},{10,1... | collective-permute-start | bytes 1105928 | tf_op jit(solution)/shard_map/ppermute | solution.py:521
  341.6 22.7 %collective-permute-start.29 = (f32[72,128]{1,0:T(8,128)}, f32[72,128]{1,0:T(8,128)}, u32[]{:S(2)}, u32[]{:S(2)}) collective-permute-start(f32[72,128]{1,0:T(8,128)} %add_add_fusion), channel_id=1, source_target_pairs={{0,1},{1,0},{2,3},{3,2},{4,5},{5,4},{6,7},{7,6},{8,9},{9,8},{10,11... | collective-permute-start | bytes 110600 | tf_op jit(solution)/shard_map/ppermute | solution.py:525
  376.0 10.6 %collective-permute-start.34 = (bf16[96,1664]{1,0:T(8,128)(2,1)}, bf16[96,1664]{1,0:T(8,128)(2,1)S(1)}, u32[]{:S(2)}, u32[]{:S(2)}) collective-permute-start(bf16[96,1664]{1,0:T(8,128)(2,1)} %get-tuple-element.339), channel_id=1, source_target_pairs={{0,8},{4,12},{8,0},{12,4},{16,24},{20,28},{24,16},{28,20},{1,9},{5... | collective-permute-start | bytes 958472 | tf_op jit(solution)/shard_map/ppermute | solution.py:525
  377.4 25.4 %collective-permute-start.35 = (bf16[96,1664]{1,0:T(8,128)(2,1)}, bf16[96,1664]{1,0:T(8,128)(2,1)S(1)}, u32[]{:S(2)}, u32[]{:S(2)}) collective-permute-start(bf16[96,1664]{1,0:T(8,128)(2,1)} %get-tuple-element.341), channel_id=1, source_target_pairs={{0,16},{4,20},{8,24},{12,28},{16,0},{20,4},{24,8},{28,12},{1,17},{... | collective-permute-start | bytes 958472 | tf_op jit(solution)/shard_map/ppermute | solution.py:525
  378.9 23.9 %collective-permute-start.36 = (bf16[96,1664]{1,0:T(8,128)(2,1)}, bf16[96,1664]{1,0:T(8,128)(2,1)S(1)}, u32[]{:S(2)}, u32[]{:S(2)}) collective-permute-start(bf16[96,1664]{1,0:T(8,128)(2,1)} %get-tuple-element.340), channel_id=1, source_target_pairs={{0,24},{4,28},{8,16},{12,20},{16,8},{20,12},{24,0},{28,4},{1,25},{... | collective-permute-start | bytes 958472 | tf_op jit(solution)/shard_map/ppermute | solution.py:525
  380.9 23.8 %collective-permute-start.41 = (bf16[240,768]{1,0:T(8,128)(2,1)S(1)}, bf16[240,768]{1,0:T(8,128)(2,1)S(1)}, u32[]{:S(2)}, u32[]{:S(2)}) collective-permute-start(bf16[240,768]{1,0:T(8,128)(2,1)S(1)} %add_convert_fusion.11), channel_id=1, source_target_pairs={{0,24},{4,28},{8,16},{12,20},{16,8},{20,12},{24,0},{28,4},{1,25},{... | collective-permute-start | bytes 1105928 | tf_op jit(solution)/shard_map/ppermute | solution.py:525
  383.3 34.3 %collective-permute-start.42 = (bf16[240,768]{1,0:T(8,128)(2,1)S(1)}, bf16[240,768]{1,0:T(8,128)(2,1)S(1)}, u32[]{:S(2)}, u32[]{:S(2)}) collective-permute-start(bf16[240,768]{1,0:T(8,128)(2,1)S(1)} %add_convert_fusion.11), channel_id=1, source_target_pairs={{0,16},{4,20},{8,24},{12,28},{16,0},{20,4},{24,8},{28,12},{1,17},{... | collective-permute-start | bytes 1105928 | tf_op jit(solution)/shard_map/ppermute | solution.py:525
  386.6 31.0 %collective-permute-start.43 = (bf16[240,768]{1,0:T(8,128)(2,1)S(1)}, bf16[240,768]{1,0:T(8,128)(2,1)S(1)}, u32[]{:S(2)}, u32[]{:S(2)}) collective-permute-start(bf16[240,768]{1,0:T(8,128)(2,1)S(1)} %add_convert_fusion.11), channel_id=1, source_target_pairs={{0,8},{4,12},{8,0},{12,4},{16,24},{20,28},{24,16},{28,20},{1,9},{5... | collective-permute-start | bytes 1105928 | tf_op jit(solution)/shard_map/ppermute | solution.py:525
  403.0 16.8 %collective-permute-start.37 = (bf16[96,1664]{1,0:T(8,128)(2,1)S(1)}, bf16[96,1664]{1,0:T(8,128)(2,1)S(1)}, u32[]{:S(2)}, u32[]{:S(2)}) collective-permute-start(bf16[96,1664]{1,0:T(8,128)(2,1)S(1)} %fusion.10), channel_id=1, source_target_pairs={{0,24},{4,28},{8,16},{12,20},{16,8},{20,12},{24,0},{28,4},{1,25},{... | collective-permute-start | bytes 958472 | tf_op jit(solution)/shard_map/ppermute | solution.py:525
  404.5 18.2 %collective-permute-start.38 = (bf16[96,1664]{1,0:T(8,128)(2,1)S(1)}, bf16[96,1664]{1,0:T(8,128)(2,1)S(1)}, u32[]{:S(2)}, u32[]{:S(2)}) collective-permute-start(bf16[96,1664]{1,0:T(8,128)(2,1)S(1)} %fusion.10), channel_id=1, source_target_pairs={{0,16},{4,20},{8,24},{12,28},{16,0},{20,4},{24,8},{28,12},{1,17},{... | collective-permute-start | bytes 958472 | tf_op jit(solution)/shard_map/ppermute | solution.py:525
  404.7 18.0 %collective-permute-start.39 = (bf16[96,1664]{1,0:T(8,128)(2,1)S(1)}, bf16[96,1664]{1,0:T(8,128)(2,1)S(1)}, u32[]{:S(2)}, u32[]{:S(2)}) collective-permute-start(bf16[96,1664]{1,0:T(8,128)(2,1)S(1)} %fusion.10), channel_id=1, source_target_pairs={{0,8},{4,12},{8,0},{12,4},{16,24},{20,28},{24,16},{28,20},{1,9},{5... | collective-permute-start | bytes 958472 | tf_op jit(solution)/shard_map/ppermute | solution.py:525
  419.8 26.0 %collective-permute-start.44 = (bf16[2,384,768]{2,1,0:T(8,128)(2,1)}, bf16[2,384,768]{2,1,0:T(8,128)(2,1)}, u32[]{:S(2)}, u32[]{:S(2)}) collective-permute-start(bf16[2,384,768]{2,1,0:T(8,128)(2,1)} %pad_maximum_fusion.7), channel_id=1, source_target_pairs={{0,4},{4,0},{8,12},{12,8},{16,20},{20,16},{24,28},{28,24},{1,5},{5... | collective-permute-start | bytes 3538952 | tf_op jit(solution)/shard_map/ppermute | solution.py:525
  424.0 27.0 %collective-permute-start.40 = (bf16[384,1664]{1,0:T(8,128)(2,1)}, bf16[384,1664]{1,0:T(8,128)(2,1)}, u32[]{:S(2)}, u32[]{:S(2)}) collective-permute-start(bf16[384,1664]{1,0:T(8,128)(2,1)} %pad_maximum_fusion.4), channel_id=1, source_target_pairs={{0,4},{4,0},{8,12},{12,8},{16,20},{20,16},{24,28},{28,24},{1,5},{5... | collective-permute-start | bytes 3833864 | tf_op jit(solution)/shard_map/ppermute | solution.py:525
  424.8 8.0 %collective-permute-start.33 = (f32[72,128]{1,0:T(8,128)S(1)}, f32[72,128]{1,0:T(8,128)S(1)}, u32[]{:S(2)}, u32[]{:S(2)}) collective-permute-start(f32[72,128]{1,0:T(8,128)S(1)} %add.282), channel_id=1, source_target_pairs={{0,2},{1,3},{2,0},{3,1},{4,6},{5,7},{6,4},{7,5},{8,10},{9,11},{10,... | collective-permute-start | bytes 110600 | tf_op jit(solution)/shard_map/ppermute | solution.py:525
  (55 other events, 420.1 us)
Sparse Core Ops, SparseCore 0:
  52.2 45.4 all-gather.8
  214.5 93.3 all-gather.4
  384.0 62.6 all-gather.6

commit v5 on v4

--- a/solution.py
+++ b/solution.py
@@ -260,24 +260,33 @@
     )(place, *parts, ctxt, q3, k3, v3, qt, kt, lse, lmt)
 
 
-def wgrad_kernel(slab, gb, first, act, grad_ffn, grad_attn, *refs):
-    ctx, (to, ao) = refs[:-2], refs[-2:]
+def wgrad_kernel(slab, spots, gb, first, act, grad_ffn, grad_attn, *refs):
+    ctx, (send, keep, ao) = refs[:-3], refs[-3:]
     i = pl.program_id(0)
     n_t = len(ctx)
-    piece = to.shape[2] - 2 * slab
+    piece = send.shape[2] - 2 * slab
 
     @pl.when(i == 0)
     def _():
         for z in range(n_t):
             ao[z] = dot_tn(ctx[z][...], grad_attn[...]).astype(BF16)
 
-    up = dot_tn(gb[...], first[...]).astype(BF16)
-    down = dot_tn(act[...], grad_ffn[...]).astype(BF16)
-    rows = pl.ds(pl.multiple_of(i * piece, piece), piece)
-    for z in range(n_t):
-        to[0, z, :slab, :] = up[z * slab : (z + 1) * slab]
-        to[0, z, slab : slab + piece, :] = ao[z, rows, :]
-        to[0, z, slab + piece :, :] = down[z * slab : (z + 1) * slab]
+    def write(to):
+        up = dot_tn(gb[...], first[...]).astype(BF16)
+        down = dot_tn(act[...], grad_ffn[...]).astype(BF16)
+        rows = pl.ds(pl.multiple_of(lax.rem(i, spots) * piece, piece), piece)
+        for z in range(n_t):
+            to[0, z, :slab, :] = up[z * slab : (z + 1) * slab]
+            to[0, z, slab : slab + piece, :] = ao[z, rows, :]
+            to[0, z, slab + piece :, :] = down[z * slab : (z + 1) * slab]
+
+    @pl.when(i < spots)
+    def _():
+        write(send)
+
+    @pl.when(i >= spots)
+    def _():
+        write(keep)
 
 
 def wgrad(slab, spots, gb, first, act, grad_ffn, grad_attn, ctx):
@@ -286,17 +295,22 @@
     local = ctx[0].shape[1]
     wide = n_t * slab
     tall = 2 * slab + local // spots
+    sd = jax.ShapeDtypeStruct
     vm = pl.BlockSpec(memory_space=pltpu.VMEM)
-    cols = pl.BlockSpec((chunk, wide), lambda i: (0, i))
+    cols = pl.BlockSpec((chunk, wide), lambda i: (0, jax.lax.rem(i + spots, 2 * spots)))
+    send = lambda i: jnp.minimum(i, spots - 1)
+    keep = lambda i: jnp.maximum(i - spots, 0)
+    outs = [pl.BlockSpec((1, n_t, tall, width), lambda i, at=at: (at(i), 0, 0, 0)) for at in (send, keep)]
+    shape = sd((spots, n_t, tall, width), BF16)
     return pl.pallas_call(
-        functools.partial(wgrad_kernel, slab),
-        grid=(spots,),
+        functools.partial(wgrad_kernel, slab, spots),
+        grid=(2 * spots,),
         in_specs=[cols, vm, cols, vm, vm] + [vm] * n_t,
-        out_specs=pl.BlockSpec((1, n_t, tall, width), lambda i: (i, 0, 0, 0)),
-        out_shape=jax.ShapeDtypeStruct((spots, n_t, tall, width), BF16),
+        out_specs=tuple(outs),
+        out_shape=(shape, shape),
         scratch_shapes=[pltpu.VMEM((n_t, local, width), BF16)],
         compiler_params=pltpu.CompilerParams(vmem_limit_bytes=40 << 20),
-        cost_estimate=cost(60, 10 << 20),
+        cost_estimate=cost(400, 10 << 20),
         name="wgrad",
     )(gb, first, act, grad_ffn, grad_attn, *ctx)
 
@@ -387,11 +401,9 @@
 ):
     ctx = refs[:n_t]
     (wao, hid, teach, valid, vec, bup, up_o, up_m, up_t, dn_o, dn_m, dn_t,
-     out, out_low, act_k, act_s, gb_k, gb_s, first_low, grad_ffn, grad_attn, grad_resid, vecs, gbup) = (
-        refs[n_t : n_t + 24]
-    )
-    gctx = refs[n_t + 24 : 2 * n_t + 24]
-    up_s, dn_s, slope, xhat_s, sems = refs[2 * n_t + 24 :]
+     out, out_low, act, gb, first_low, grad_ffn, grad_attn, grad_resid, vecs, gbup) = refs[n_t : n_t + 22]
+    gctx = refs[n_t + 22 : 2 * n_t + 22]
+    up_s, dn_s, slope, xhat_s, sems = refs[2 * n_t + 22 :]
     units, width = up_s.shape
     half = units // 2
     spots = half // (n_t * slab)
@@ -418,22 +430,13 @@
         cp.wait()
     blocks, _, size = bup.shape
 
-    def halves(i, kept, sent, value):
-        @pl.when(i < spots)
-        def _():
-            kept[:, pl.ds(pl.multiple_of(i * size, size), size)] = value
-
-        @pl.when(i >= spots)
-        def _():
-            sent[:, pl.ds(pl.multiple_of((i - spots) * size, size), size)] = value
-
     def forward(i, feed):
         rows = pl.ds(pl.multiple_of(i * size, size), size)
         before = dot_nt(first_low[...], up_s[rows, :]) + bup[i]
         phi = 0.5 * (1.0 + lax.erf(before * math.sqrt(0.5)))
         dens = jnp.exp(-0.5 * before * before) * (1.0 / math.sqrt(2.0 * math.pi))
         low = (before * phi).astype(BF16)
-        halves(i, act_k, act_s, low)
+        act[:, rows] = low
         slope[:, rows] = (phi + before * dens).astype(BF16)
         return feed + dot(low, dn_s[rows, :])
 
@@ -460,7 +463,7 @@
         rows = pl.ds(pl.multiple_of(i * size, size), size)
         g = dot_nt(grad_ffn[...], dn_s[rows, :]) * slope[:, rows].astype(F32)
         low = g.astype(BF16)
-        halves(i, gb_k, gb_s, low)
+        gb[:, rows] = low
         gbup[i] = total(low.astype(F32))
         return acc + dot(low, up_s[rows, :])
 
@@ -495,7 +498,8 @@
         out_shape=(
             sd((chunk, width), F32),
             sd((chunk, width), BF16),
-            *[sd((chunk, units // 2), BF16)] * 4,
+            sd((chunk, units), BF16),
+            sd((chunk, units), BF16),
             sd((chunk, width), BF16),
             sd((chunk, width), BF16),
             sd((chunk, width), BF16),
@@ -580,13 +584,21 @@
         keep = lax.dynamic_index_in_dim(x, up, ax, keepdims=False)
         return keep, dp_swap(send, bits[0])
 
-    def narrow_pair(x, y, bits):
+    def narrow_pair(x, y, bits, lo=0, count=None):
         ax = sorted(bits, reverse=True).index(bits[0])
         up = bit_of(bits[0])
-        part = lambda v, i: lax.dynamic_index_in_dim(v, i, ax, keepdims=False).astype(F32)
-        send = (part(x, 1 - up) + part(y, 1 - up)).astype(BF16)
-        keep = (part(x, up) + part(y, up)).astype(BF16)
-        return keep, send, bits[0]
+        sizes = list(x.shape)
+        sizes[ax] = 1
+        sizes[-2] = count or sizes[-2]
+
+        def half(i):
+            at = [0] * x.ndim
+            at[ax] = i
+            at[-2] = lo
+            part = lambda v: lax.dynamic_slice(v, at, sizes).astype(F32)
+            return (part(x) + part(y)).astype(BF16).reshape(sizes[:ax] + sizes[ax + 1 :])
+
+        return half(up), half(1 - up), bits[0]
 
     def narrow(x, bits):
         left = sorted(bits, reverse=True)
@@ -680,7 +692,7 @@
 
     w_other = dp_swap(w_side, 1)
     vec = jnp.stack([b_attn_out, gain_one, bias_one, b_down, gain_two, bias_two, b_down, b_down])
-    (out_own, out_low, act_k, act_s, gb_k, gb_s, first_low, grad_ffn, grad_attn, grad_resid, vecs, gbup, *gctx_rel) = ffn(
+    (out_own, out_low, act, gb, first_low, grad_ffn, grad_attn, grad_resid, vecs, gbup, *gctx_rel) = ffn(
         core.reshape(1),
         ctx_parts,
         wao,
@@ -700,68 +712,73 @@
     gbu = jnp.where(up, gbu[::-1], gbu).transpose(2, 0, 1, 3).reshape(n_t, units)
     gbu = gbu[jnp.stack([lax.rem(ti - z + n_t, n_t) for z in range(n_t)])]
     pack = jnp.concatenate([vecs.reshape(-1), gbu.reshape(-1)]).reshape(-1, 128)
+
+    parts = [gctx_rel[0]] + [shift(gctx_rel[s], n_t, -s) for s in range(1, n_t)]
+
+    lead = (2,) * len(low_bits)
+    send, keep = wgrad(slab, spots, gb, first_low, act, grad_ffn, grad_attn, ctx_parts)
+    *parts, send, keep, out_low, pack = lax.optimization_barrier((*parts, send, keep, out_low, pack))
     pack_came = dp_swap(pack, 1)
-
-    parts = [gctx_rel[0]] + [shift(gctx_rel[s], n_t, -s) for s in range(1, n_t)]
-
-    send = wgrad(slab, spots, gb_s, first_low, act_s, grad_ffn, grad_attn, ctx_parts)
     got = dp_swap(send, 1)
-    first_low, send, pack, pack_came = lax.optimization_barrier((first_low, send, pack, pack_came))
-    keep = wgrad(slab, spots, gb_k, first_low, act_k, grad_ffn, grad_attn, ctx_parts)
-    got, keep, pack, pack_came = lax.optimization_barrier((got, keep, pack, pack_came))
-    lead = (2,) * len(low_bits)
-    shape = lambda x, n: x.reshape(lead + (n_t, n, width))
-    a_keep, a_send, _ = narrow_pair(shape(keep[:, :, :cut], cut), shape(got[:, :, :cut], cut), low_bits)
-    b_keep, b_send, _ = narrow_pair(shape(keep[:, :, cut:], slab), shape(got[:, :, cut:], slab), high_bits)
-    *parts, a_send, b_send, a_keep, b_keep, out_low, pack, pack_came = lax.optimization_barrier(
-        (*parts, a_send, b_send, a_keep, b_keep, out_low, pack, pack_came)
-    )
-    a_came = dp_swap(a_send, low_bits[0])
-    b_came = dp_swap(b_send, high_bits[0])
+    out_all = lax.all_gather(out_low, "tensor", axis=0, tiled=True)
+
+    gqkv, glm = attn_bwd(ti.reshape(1), parts, ctxt, q3, k3, v3, qt, kt, lse, lmt)
+    gqkv, glm, keep, got, pack, pack_came = lax.optimization_barrier((gqkv, glm, keep, got, pack, pack_came))
     pack = pack + pack_came
-    packs = [pack] + [dp_swap(pack, 2 * r) for r in range(1, spots)]
-    out_all = lax.all_gather(out_low, "tensor", axis=0, tiled=True)
-
-    gqkv, glm = attn_bwd(ti.reshape(1), parts, ctxt, q3, k3, v3, qt, kt, lse, lmt)
-    gqkv, glm, a_keep, a_came, b_keep, b_came, *packs = lax.optimization_barrier(
-        (gqkv, glm, a_keep, a_came, b_keep, b_came, *packs)
-    )
+    pack_came = dp_swap(pack, low_bits[0])
     parts = [rows_of(gqkv, ti * chunk, chunk)] + [
         shift(rows_of(gqkv, lax.rem(ti + s, n_t) * chunk, chunk), n_t, s) for s in range(1, n_t)
     ]
+    keep = keep.reshape(lead + keep.shape[1:])
+    got = got.reshape(lead + got.shape[1:])
+    a_keep, a_send, bit = narrow_pair(keep, got, low_bits, 0, cut)
+    a_came = dp_swap(a_send, bit)
+    b_keep, b_send, bit = narrow_pair(keep, got, high_bits, cut, slab)
+    b_came = dp_swap(b_send, bit)
+    tail = tail_of(hidden, gqkv, glm, table, noise, 3 * local)
+    w_all = jnp.concatenate([jnp.where(up, w_other, w_side), jnp.where(up, w_side, w_other)], axis=1)
+    near = [s for s in range(n_t) if s in (0, 1, n_t - 1)]
+    far = [s for s in range(n_t) if s not in near]
+    held = lax.optimization_barrier(
+        (w_all, tail, a_keep, a_came, b_keep, b_came, pack, pack_came, *[parts[s] for s in near])
+    )
+    w_all, tail, a_keep, a_came, b_keep, b_came, pack, pack_came = held[:8]
+    for n, s in enumerate(near):
+        parts[s] = held[8 + n]
+    pack = pack + pack_came
+    pack_came = dp_swap(pack, low_bits[1])
     a_keep, a_send, bit = narrow_pair(a_keep, a_came, low_bits[1:])
     a_came = dp_swap(a_send, bit)
     b_keep, b_send, bit = narrow_pair(b_keep, b_came, high_bits[1:])
     b_came = dp_swap(b_send, bit)
-    tail = tail_of(hidden, gqkv, glm, table, noise, 3 * local)
-    w_all = jnp.concatenate([jnp.where(up, w_other, w_side), jnp.where(up, w_side, w_other)], axis=1)
-    held = lax.optimization_barrier((*parts, w_all, tail, a_keep, a_came, b_keep, b_came, *packs))
-    parts, w_all, (tail, a_keep, a_came, b_keep, b_came, *packs) = held[:n_t], held[n_t], held[n_t + 1 :]
+    tail = tail.reshape((2,) + lead + (-1, tail.shape[1]))
+    send = lax.dynamic_index_in_dim(tail, 1 - core, 0, keepdims=False)
+    t_keep = lax.dynamic_index_in_dim(tail, core, 0, keepdims=False)
+    t_keep, t_send, bit = narrow_pair(t_keep, dp_swap(send, 1), low_bits)
+    t_came = dp_swap(t_send, bit)
+    held = lax.optimization_barrier(
+        (a_keep, a_came, b_keep, b_came, pack, pack_came, *[parts[s] for s in far])
+    )
+    a_keep, a_came, b_keep, b_came, pack, pack_came = held[:6]
+    for n, s in enumerate(far):
+        parts[s] = held[6 + n]
     g_a = (a_keep.astype(F32) + a_came.astype(F32)).astype(BF16)
     g_b = (b_keep.astype(F32) + b_came.astype(F32)).astype(BF16)
     g_a = finish(narrow(g_a, low_bits[2:]))
     g_b = finish(narrow(g_b, high_bits[2:]))
-    pack = packs[0]
-    for p in packs[1:]:
-        pack = pack + p
+    pack = pack + pack_came
     pack_came = swap(pack, "tensor", n_t, 1)
     total = jnp.concatenate([g_a, g_b], axis=1)
     pieces = [total[0]] + [shift(total[s], n_t, -s) for s in range(1, n_t)]
-    tail = tail.reshape(2, spots, -1, tail.shape[1])
-    send = lax.dynamic_index_in_dim(tail, 1 - core, 0, keepdims=False)
-    keep = lax.dynamic_index_in_dim(tail, core, 0, keepdims=False)
-    came = dp_swap(send, 1)
     back = back_of(ti.reshape(1), w_all, grad_resid, parts)
-    back, keep, came, pack, pack_came, *pieces = lax.optimization_barrier(
-        (back, keep, came, pack, pack_came, *pieces)
-    )
+    tail = finish(narrow((t_keep.astype(F32) + t_came.astype(F32)).astype(BF16), low_bits[1:]))
+    back, tail, pack, pack_came, *pieces = lax.optimization_barrier((back, tail, pack, pack_came, *pieces))
     grad_hidden = lax.all_gather(back, "tensor", axis=0, tiled=True)
     summed = pieces[0].astype(F32)
     for p in pieces[1:]:
         summed = summed + p.astype(F32)
     held = quad_gather(summed.astype(BF16))
-    tail = (keep.astype(F32) + came.astype(F32)).astype(BF16)
-    tail = jnp.concatenate(quad_gather(finish(quad_sum(tail))))
+    tail = jnp.concatenate(quad_gather(tail))
     other = dp_swap(tail, 1)
     tail = jnp.concatenate([jnp.where(up, other, tail), jnp.where(up, tail, other)])
     g_ao = jnp.concatenate([x[slab:cut] for x in held])
@@ -769,7 +786,7 @@
     other = dp_swap(pair, 1)
     pair = jnp.concatenate([jnp.where(up, other, pair), jnp.where(up, pair, other)], axis=1)
     pack = pack + pack_came
-    for bit in extra:
+    for bit in low_bits[2:] + extra:
         pack = pack + dp_swap(pack, bit)
     bit = 2
     while bit < n_t:

time: 481 us -> 455 us (0.946)
  waiting for transfers between devices: 121 us -> 106 us
  other arithmetic: 59.7 us -> 74.4 us
  starting transfers between devices: 72.3 us -> 60.4 us
  local copies, waits for them, and re-layouts: 52.1 us -> 40.4 us
    reshape x0 -> x6, other arithmetic: none -> 17.9 us  [half(): return (part(x) + part(y)).astype(BF16).reshape(sizes[:ax] + sizes[ax + 1:])]
    ppermute x30 -> x28, waiting for transfers between devices: 56.5 us -> 39.7 us  [swap(): return lax.ppermute(x, axis, [(j, j ^ bit) for j in range(size)])]
    ppermute x15, starting transfers between devices: 42.8 us -> 30.5 us  [shift(): lax.ppermute(x, 'tensor', [(j, (j + amount) % size) for j in range(size)])]
    convert_element_type x6 -> x2, other arithmetic: 13 us -> 2.65 us  [the longest x1 1.51 us: body(): (t_keep.astype(F32) + t_came.astype(F32)).astype(BF16)]
    unnamed x118 -> x92, local copies, waits for them, and re-layouts: 21.1 us -> 17 us
    pallas_call x2 -> x1, Pallas kernels: 8.86 us -> 10.2 us  [wgrad(): pl.pallas_call(functools.partial(wgrad_kernel, slab, spots), grid=(2 * sp...]
    ppermute x30 -> x28, starting transfers between devices: 29.4 us -> 29.8 us  [swap(): return lax.ppermute(x, axis, [(j, j ^ bit) for j in range(size)])]
  transfers between devices with their start and end apart: 48 -> 46, of which waited for: 14 -> 18; matrix products, arithmetic and copies ran while one was open for 18% -> 21% of each run, Pallas kernels for 32% -> 33%
where the time goes in v5:
time: 455 us; the launch traced here: 447 us
  Pallas kernels  148 us (33%)
  waiting for transfers between devices  106 us (23%)
  other arithmetic  74.4 us (16%)
  starting transfers between devices  60.4 us (13%)
  local copies, waits for them, and re-layouts  40.4 us (9%)
  between operations  18.3 us (4%)
    ppermute x15, waiting for transfers between devices, shift(): lax.ppermute(x, 'tensor', [(j, (j + amount) % size) for j in range(size)])  61.4 us
    pallas_call x1, Pallas kernels, attn_bwd(): pl.pallas_call(functools.partial(attn_bwd_kernel, n_t), in_specs=[pl.Bloc...  41.2 us
    ppermute x28, waiting for transfers between devices, swap(): return lax.ppermute(x, axis, [(j, j ^ bit) for j in range(size)])  39.7 us
    pallas_call x1, Pallas kernels, ffn(): pl.pallas_call(functools.partial(ffn_kernel, n_t, slab), in_specs=[sm] +...  34 us
    pallas_call x3, Pallas kernels, attn_fwd(): pl.pallas_call(functools.partial(attn_fwd_kernel, lo, len(prev)), grid=(h...  30.8 us
    ppermute x15, starting transfers between devices, shift(): lax.ppermute(x, 'tensor', [(j, (j + amount) % size) for j in range(size)])  30.5 us
    ppermute x28, starting transfers between devices, swap(): return lax.ppermute(x, axis, [(j, j ^ bit) for j in range(size)])  29.8 us
    reshape x6, other arithmetic, half(): return (part(x) + part(y)).astype(BF16).reshape(sizes[:ax] + sizes[ax + 1:])  17.9 us
  transfers between devices with their start and end apart: 46, of which 18 were waited for; matrix products, arithmetic and copies ran while one was open for 21% of the time, Pallas kernels for 33%

profile of v5, /device:TPU:0, one launch (start us, length us, event | category | flops | bytes accessed | tf_op | source)
XLA Modules:
  0.0 447.1 jit_solution(14207827212168166967)
XLA Ops:
  11.4 3.1 collective-permute-start
  14.5 2.6 collective-permute-start.1
  20.7 15.1 %attn_prep.1 = (bf16[3,2048,64]{2,1,0:T(8,128)(2,1)}, bf16[3,2048,64]{2,1,0:T(8,128)(2,1)}, bf16[3,2048,64]{2,1,0:T(8,128)(2,1)}, bf16[192,2048]{1,0:T(8,128)(2,...) custom-call(bf16[2048,768]{1,0:T(8,128)(2,1)} %hid.3, ...), custom_call_target="tpu_custom_call" | custom-call | flops 15000000512 | bytes 20971520 | tf_op jit(solution)/shard_map/attn_prep/pallas_call | solution.py:75
  36.6 9.5 %attn_fwd.3 = (bf16[2048,192]{1,0:T(8,128)(2,1)}, f32[192,2048]{1,0:T(8,128)}, f32[8,2048]{1,0:T(8,128)}) custom-call(bf16[192,2048]{1,0:T(8,128)(2,1)} %get-tuple-element.111.qt.refs_8_, bf16[3,2048,64]{2,1,0:T(8,128)(2,1)} %get-tuple-element.112.k3.refs_6_, bf16[192,2048]{1,0:T(8,128)(2,1)} %get-tuple-element.113.vt, ...), custom_call_target="tpu_custom_call" | custom-call | flops 3000000000 | bytes 8388608 | tf_op jit(solution)/shard_map/attn_fwd/pallas_call | solution.py:148
  52.1 9.6 %attn_fwd.4 = (bf16[2048,192]{1,0:T(8,128)(2,1)}, f32[192,2048]{1,0:T(8,128)}, f32[8,2048]{1,0:T(8,128)}) custom-call(bf16[192,2048]{1,0:T(8,128)(2,1)} %get-tuple-element.111.qt.refs_8_, bf16[3,2048,64]{2,1,0:T(8,128)(2,1)} %get-tuple-element.112.k3.refs_6_, ...), custom_call_target="tpu_custom_call", output_to_operand_aliasing={{0}: (4, {}), {1}: (5, {}), {2}: (6, {})} | custom-call | flops 3750000128 | bytes 8388608 | tf_op jit(solution)/shard_map/attn_fwd/pallas_call | solution.py:148
  61.7 2.1 collective-permute-done.3
  72.7 11.7 %attn_fwd.5 = (bf16[2048,192]{1,0:T(8,128)(2,1)}, f32[192,2048]{1,0:T(8,128)}, f32[8,2048]{1,0:T(8,128)}) custom-call(bf16[192,2048]{1,0:T(8,128)(2,1)} %get-tuple-element.111.qt.refs_8_, bf16[3,2048,64]{2,1,0:T(8,128)(2,1)} %get-tuple-element.112.k3.refs_6_, ...), custom_call_target="tpu_custom_call", output_to_operand_aliasing={{0}: (4, {}), {1}: (5, {}), {2}: (6, {})} | custom-call | flops 5249999872 | bytes 8388608 | tf_op jit(solution)/shard_map/attn_fwd/pallas_call | solution.py:148
  84.4 2.0 constant_dynamic-slice_fusion.9
  86.4 5.8 %collective-permute-start.5 = (bf16[512,192]{1,0:T(8,128)(2,1)S(1)}, bf16[512,192]{1,0:T(8,128)(2,1)S(1)}, u32[]{:S(2)}, u32[]{:S(2)}) collective-permute-start(bf16[512,192]{1,0:T(8,128)(2,1)S(1)} %get-tuple-element.315), channel_id=1, source_target_pairs={{0,1},{1,2},{2,3},{3,0},{4,5},{5,6},{6,7},{7,4},{8,9},{9,10},{10,1... | collective-permute-start | bytes 589832 | tf_op jit(solution)/shard_map/ppermute | solution.py:525
  99.7 2.0 collective-permute-done.5.refs_1_
  101.7 9.8 %collective-permute-done.6.refs_2_ = bf16[512,192]{1,0:T(8,128)(2,1)S(1)} collective-permute-done((bf16[512,192]{1,0:T(8,128)(2,1)S(1)}, bf16[512,192]{1,0:T(8,128)(2,1)S(1)}, u32[]{:S(2)}, u32[]{:S(2)}) %collective-permute-start.6) | collective-permute-done | bytes 196640 | tf_op jit(solution)/shard_map/ppermute | solution.py:525
  113.6 2.1 constant_dynamic-slice_fusion.8.refs_5_
  115.7 2.7 constant_dynamic-slice_fusion.7.refs_6_
  123.7 34.0 %ffn.1 = (f32[512,768]{1,0:T(8,128)}, bf16[512,768]{1,0:T(8,128)(2,1)}, bf16[512,3072]{1,0:T(8,128)(2,1)}, bf16[512,3072]{1,0:T(8,128)(2,1)}, bf16[512,768]{1,0:...) custom-call(s32[1]{0:T(128)} %bitcast.core, ...), custom_call_target="tpu_custom_call" | custom-call | flops 33999998976 | bytes 26214400 | tf_op jit(solution)/shard_map/ffn/pallas_call | solution.py:495
  161.2 6.4 %collective-permute-start.12 = (bf16[512,192]{1,0:T(8,128)(2,1)}, bf16[512,192]{1,0:T(8,128)(2,1)}, u32[]{:S(2)}, u32[]{:S(2)}) collective-permute-start(bf16[512,192]{1,0:T(8,128)(2,1)} %get-tuple-element.141), channel_id=1, source_target_pairs={{0,3},{1,0},{2,1},{3,2},{4,7},{5,4},{6,5},{7,6},{8,11},{9,8},{10,9... | collective-permute-start | bytes 589832 | tf_op jit(solution)/shard_map/ppermute | solution.py:525
  169.5 4.2 broadcast_select_fusion.1
  177.2 10.2 %wgrad.1 = (bf16[4,4,240,768]{3,2,1,0:T(8,128)(2,1)}, bf16[4,4,240,768]{3,2,1,0:T(8,128)(2,1)}) custom-call(bf16[512,3072]{1,0:T(8,128)(2,1)S(1)} %copy-done.10, bf16[512,768]{1,0:T(8,128)(2,1)S(1)} %copy-done.11, bf16[512,3072]{1,0:T(8,128)(2,1)S(1)} %copy-done.9, bf16[512,768]{1,0:T(8,128)(2,1)S(1)} %copy-done.12, bf16[512,768]{1,0:T(8,128)(2,1)S(1)} %copy-done.13, ...), custom_call_target="tpu_custom_call" | custom-call | flops 399999991808 | bytes 10485760 | tf_op jit(solution)/shard_map/wgrad/pallas_call | solution.py:305
  187.6 4.8 %collective-permute-done.13.refs_2_ = bf16[512,192]{1,0:T(8,128)(2,1)} collective-permute-done((bf16[512,192]{1,0:T(8,128)(2,1)}, bf16[512,192]{1,0:T(8,128)(2,1)}, u32[]{:S(2)}, u32[]{:S(2)}) %collective-permute-start.13) | collective-permute-done | bytes 196640 | tf_op jit(solution)/shard_map/ppermute | solution.py:525
  193.0 41.2 %attn_bwd.1 = (bf16[2048,640]{1,0:T(8,128)(2,1)}, f32[3,512,512]{2,1,0:T(8,128)}) custom-call(s32[1]{0:T(128)} %bitcast.40.place, bf16[512,192]{1,0:T(8,128)(2,1)} %get-tuple-element.159.refs_0_, bf16[512,192]{1,0:T(8,128)(2,1)} %collective-permute-done.12.refs_1_, bf16[512,192]{1,0:T(8,128)(2,1)} %collective-permute-done.13.refs_2_, ...), custom_call_target="tpu_custom_call" | custom-call | flops 399999991808 | bytes 20971520 | tf_op jit(solution)/shard_map/attn_bwd/pallas_call | solution.py:245
  237.1 4.4 fusion.6
  243.0 3.6 fusion.1
  248.7 3.8 collective-permute-start.22
  252.6 11.8 %tail.1 = bf16[768,1664]{1,0:T(8,128)(2,1)} custom-call(bf16[2048,768]{1,0:T(8,128)(2,1)} %hid.3, bf16[2048,640]{1,0:T(8,128)(2,1)} %get-tuple-element.173.gqkv, f32[3,512,512]{2,1,0:T(8,128)} %get-tuple-element.174.glm, f32[3,512,512]{2,1,0:T(8,128)} %table.3, f32[3,512,512]{2,1,0:T(8,128)} %noise.3), custom_call_target="tpu_custom_call" | custom-call | flops 399999991808 | bytes 20971520 | tf_op jit(solution)/shard_map/tail/pallas_call | solution.py:353
  264.3 2.6 fusion
  266.9 3.4 collective-permute-done.21.refs_1_
  270.4 11.1 %collective-permute-done.22.refs_3_ = bf16[512,640]{1,0:T(8,128)(2,1)} collective-permute-done((bf16[512,640]{1,0:T(8,128)(2,1)}, bf16[512,640]{1,0:T(8,128)(2,1)}, u32[]{:S(2)}, u32[]{:S(2)}) %collective-permute-start.22) | collective-permute-done | bytes 655392 | tf_op jit(solution)/shard_map/ppermute | solution.py:525
  281.5 5.4 %collective-permute-done.18 = bf16[2,4,144,768]{3,2,1,0:T(8,128)(2,1)} collective-permute-done((bf16[2,4,144,768]{3,2,1,0:T(8,128)(2,1)}, bf16[2,4,144,768]{3,2,1,0:T(8,128)(2,1)}, u32[]{:S(2)}, u32[]{:S(2)}) %collective-permute-start.18) | collective-permute-done | bytes 1769504 | tf_op jit(solution)/shard_map/ppermute | solution.py:529
  288.0 3.2 fusion.9
  293.3 2.6 fusion.15
  299.1 23.7 %collective-permute-done.26.refs_2_ = bf16[512,640]{1,0:T(8,128)(2,1)} collective-permute-done((bf16[512,640]{1,0:T(8,128)(2,1)}, bf16[512,640]{1,0:T(8,128)(2,1)}, u32[]{:S(2)}, u32[]{:S(2)}) %collective-permute-start.26) | collective-permute-done | bytes 655392 | tf_op jit(solution)/shard_map/ppermute | solution.py:525
  332.2 2.0 collective-permute-start.30
  334.2 6.5 %collective-permute-done.28 = bf16[2,96,1664]{2,1,0:T(8,128)(2,1)S(1)} collective-permute-done((bf16[2,96,1664]{2,1,0:T(8,128)(2,1)S(1)}, bf16[2,96,1664]{2,1,0:T(8,128)(2,1)S(1)}, u32[]{:S(2)}, u32[]{:S(2)}) %collective-permute-start.28) | collective-permute-done | bytes 639008 | tf_op jit(solution)/shard_map/ppermute | solution.py:529
  345.2 5.0 %back.1 = bf16[512,768]{1,0:T(8,128)(2,1)} custom-call(s32[1]{0:T(128)} %bitcast.40.place, bf16[4,576,768]{2,1,0:T(8,128)(2,1)S(1)} %pad_maximum_fusion.w, f32[512,768]{1,0:T(8,128)S(1)} %copy-done.8, bf16[512,640]{1,0:T(8,128)(2,1)S(1)} %copy-done, bf16[512,640]{1,0:T(8,128)(2,1)} %collective-permute-done.21.refs_1_, ...), custom_call_target="tpu_custom_call" | custom-call | flops 5000000000 | bytes 10485760 | tf_op jit(solution)/shard_map/back/pallas_call | solution.py:374
  350.2 2.7 collective-permute-done.29
  354.0 6.6 %collective-permute-done.32 = bf16[240,768]{1,0:T(8,128)(2,1)} collective-permute-done((bf16[240,768]{1,0:T(8,128)(2,1)}, bf16[240,768]{1,0:T(8,128)(2,1)}, u32[]{:S(2)}, u32[]{:S(2)}) %collective-permute-start.32) | collective-permute-done | bytes 368672 | tf_op jit(solution)/shard_map/ppermute | solution.py:525
  362.1 2.5 collective-permute-start.39
  365.7 2.5 collective-permute-start.35
  368.8 5.8 %collective-permute-done.39 = bf16[240,768]{1,0:T(8,128)(2,1)S(1)} collective-permute-done((bf16[240,768]{1,0:T(8,128)(2,1)S(1)}, bf16[240,768]{1,0:T(8,128)(2,1)S(1)}, u32[]{:S(2)}, u32[]{:S(2)}) %collective-permute-start.39) | collective-permute-done | bytes 368672 | tf_op jit(solution)/shard_map/ppermute | solution.py:529
  376.2 6.3 %collective-permute-done.40 = bf16[240,768]{1,0:T(8,128)(2,1)S(1)} collective-permute-done((bf16[240,768]{1,0:T(8,128)(2,1)S(1)}, bf16[240,768]{1,0:T(8,128)(2,1)S(1)}, u32[]{:S(2)}, u32[]{:S(2)}) %collective-permute-start.40) | collective-permute-done | bytes 368672 | tf_op jit(solution)/shard_map/ppermute | solution.py:529
  384.7 4.8 %collective-permute-done.35 = bf16[96,1664]{1,0:T(8,128)(2,1)} collective-permute-done((bf16[96,1664]{1,0:T(8,128)(2,1)S(1)}, bf16[96,1664]{1,0:T(8,128)(2,1)}, u32[]{:S(2)}, u32[]{:S(2)}) %collective-permute-start.35) | collective-permute-done | bytes 319520 | tf_op jit(solution)/shard_map/ppermute | solution.py:529
  389.5 5.0 %collective-permute-done.36 = bf16[96,1664]{1,0:T(8,128)(2,1)} collective-permute-done((bf16[96,1664]{1,0:T(8,128)(2,1)S(1)}, bf16[96,1664]{1,0:T(8,128)(2,1)}, u32[]{:S(2)}, u32[]{:S(2)}) %collective-permute-start.36) | collective-permute-done | bytes 319520 | tf_op jit(solution)/shard_map/ppermute | solution.py:529
  397.7 4.3 collective-permute-start.34
  402.0 5.1 %convert_element_type.244 = f32[2048,768]{1,0:T(8,128)} convert(bf16[2048,768]{1,0:T(8,128)(2,1)} %all-gather.5.cloned.1.call-done) | non-fusion elementwise | flops 1572864 | bytes 9437184 | tf_op jit(solution)/shard_map/convert_element_type | solution.py:801
  417.9 1.9 copy.104
  423.9 2.9 copy.103
  426.9 2.1 convert_multiply_fusion.1
  429.6 4.4 all-gather.7.cloned.1.call-done
  434.0 5.0 %convert_multiply_fusion = f32[2048,768]{1,0:T(8,128)} fusion(bf16[2048,768]{1,0:T(8,128)(2,1)} %all-gather.7.cloned.1.call-done, f32[]{:T(128)} %bitcast.65), kind=kLoop, calls=%fused_computation.1 | loop fusion | flops 3145728 | bytes 9437188 | tf_op jit(solution)/shard_map/mul | solution.py:815
  (264 shorter events, 99.0 us)
Async XLA Ops:
  7.2 104.3 %all-gather.9.cloned.1.call-start = ((), (), s32[]{:S(2)}) async-start(), calls=%async_computation.2 | async-start | bytes 2211840 | tf_op jit(solution)/shard_map/all_gather | solution.py:663
  11.4 34.7 %collective-permute-start = (bf16[256,768]{1,0:T(8,128)(2,1)S(1)}, bf16[256,768]{1,0:T(8,128)(2,1)}, u32[]{:S(2)}, u32[]{:S(2)}) collective-permute-start(bf16[256,768]{1,0:T(8,128)(2,1)S(1)} %concatenate.53), channel_id=1, source_target_pairs={{0,1},{1,2},{2,3},{3,0},{4,5},{5,6},{6,7},{7,4},{8,9},{9,10},{10,1... | collective-permute-start | bytes 1179656 | tf_op jit(solution)/shard_map/ppermute | solution.py:525
  14.5 31.6 %collective-permute-start.1 = (bf16[256,768]{1,0:T(8,128)(2,1)S(1)}, bf16[256,768]{1,0:T(8,128)(2,1)S(1)}, u32[]{:S(2)}, u32[]{:S(2)}) collective-permute-start(bf16[256,768]{1,0:T(8,128)(2,1)S(1)} %concatenate.53), channel_id=1, source_target_pairs={{0,2},{1,3},{2,0},{3,1},{4,6},{5,7},{6,4},{7,5},{8,10},{9,11},{10,... | collective-permute-start | bytes 1179656 | tf_op jit(solution)/shard_map/ppermute | solution.py:525
  17.1 29.0 %collective-permute-start.2 = (bf16[256,768]{1,0:T(8,128)(2,1)S(1)}, bf16[256,768]{1,0:T(8,128)(2,1)S(1)}, u32[]{:S(2)}, u32[]{:S(2)}) collective-permute-start(bf16[256,768]{1,0:T(8,128)(2,1)S(1)} %concatenate.53), channel_id=1, source_target_pairs={{0,3},{1,0},{2,1},{3,2},{4,7},{5,4},{6,5},{7,6},{8,11},{9,8},{10,9... | collective-permute-start | bytes 1179656 | tf_op jit(solution)/shard_map/ppermute | solution.py:525
  47.9 15.9 %collective-permute-start.3 = (bf16[3,144,768]{2,1,0:T(8,128)(2,1)S(1)}, bf16[3,144,768]{2,1,0:T(8,128)(2,1)S(1)}, u32[]{:S(2)}, u32[]{:S(2)}) collective-permute-start(bf16[3,144,768]{2,1,0:T(8,128)(2,1)S(1)} %pad_maximum_fusion.10), channel_id=1, source_target_pairs={{0,8},{4,12},{8,0},{12,4},{16,24},{20,28},{24,16},{28,20},{1,9},{5... | collective-permute-start | bytes 1990664 | tf_op jit(solution)/shard_map/ppermute | solution.py:529
  50.5 11.3 %collective-permute-start.4 = (bf16[3,96,768]{2,1,0:T(8,128)(2,1)S(1)}, bf16[3,96,768]{2,1,0:T(8,128)(2,1)S(1)}, u32[]{:S(2)}, u32[]{:S(2)}) collective-permute-start(bf16[3,96,768]{2,1,0:T(8,128)(2,1)S(1)} %pad_maximum_fusion.11), channel_id=1, source_target_pairs={{0,16},{4,20},{8,24},{12,28},{16,0},{20,4},{24,8},{28,12},{1,17},{... | collective-permute-start | bytes 1327112 | tf_op jit(solution)/shard_map/ppermute | solution.py:529
  52.1 349.9 %all-gather.5.cloned.1.call-start = ((), (), s32[]{:S(2)}) async-start(), calls=%async_computation | async-start | bytes 3932160 | tf_op jit(solution)/shard_map/all_gather | solution.py:723
  65.9 28.8 %collective-permute-start.9 = (bf16[2,3,96,768]{3,2,1,0:T(8,128)(2,1)}, bf16[2,3,96,768]{3,2,1,0:T(8,128)(2,1)}, u32[]{:S(2)}, u32[]{:S(2)}) collective-permute-start(bf16[2,3,96,768]{3,2,1,0:T(8,128)(2,1)} %pad_maximum_fusion.8), channel_id=1, source_target_pairs={{0,8},{4,12},{8,0},{12,4},{16,24},{20,28},{24,16},{28,20},{1,9},{5... | collective-permute-start | bytes 2654216 | tf_op jit(solution)/shard_map/ppermute | solution.py:529
  68.7 29.2 %collective-permute-start.8 = (bf16[2,3,144,768]{3,2,1,0:T(8,128)(2,1)}, bf16[2,3,144,768]{3,2,1,0:T(8,128)(2,1)}, u32[]{:S(2)}, u32[]{:S(2)}) collective-permute-start(bf16[2,3,144,768]{3,2,1,0:T(8,128)(2,1)} %pad_maximum_fusion.3), channel_id=1, source_target_pairs={{0,16},{4,20},{8,24},{12,28},{16,0},{20,4},{24,8},{28,12},{1,17},{... | collective-permute-start | bytes 3981320 | tf_op jit(solution)/shard_map/ppermute | solution.py:529
  86.4 15.3 %collective-permute-start.5 = (bf16[512,192]{1,0:T(8,128)(2,1)S(1)}, bf16[512,192]{1,0:T(8,128)(2,1)S(1)}, u32[]{:S(2)}, u32[]{:S(2)}) collective-permute-start(bf16[512,192]{1,0:T(8,128)(2,1)S(1)} %get-tuple-element.315), channel_id=1, source_target_pairs={{0,1},{1,2},{2,3},{3,0},{4,5},{5,6},{6,7},{7,4},{8,9},{9,10},{10,1... | collective-permute-start | bytes 589832 | tf_op jit(solution)/shard_map/ppermute | solution.py:525
  92.2 19.3 %collective-permute-start.6 = (bf16[512,192]{1,0:T(8,128)(2,1)S(1)}, bf16[512,192]{1,0:T(8,128)(2,1)S(1)}, u32[]{:S(2)}, u32[]{:S(2)}) collective-permute-start(bf16[512,192]{1,0:T(8,128)(2,1)S(1)} %get-tuple-element.314), channel_id=1, source_target_pairs={{0,2},{1,3},{2,0},{3,1},{4,6},{5,7},{6,4},{7,5},{8,10},{9,11},{10,... | collective-permute-start | bytes 589832 | tf_op jit(solution)/shard_map/ppermute | solution.py:525
  93.4 18.1 %collective-permute-start.7 = (bf16[512,192]{1,0:T(8,128)(2,1)S(1)}, bf16[512,192]{1,0:T(8,128)(2,1)S(1)}, u32[]{:S(2)}, u32[]{:S(2)}) collective-permute-start(bf16[512,192]{1,0:T(8,128)(2,1)S(1)} %get-tuple-element.313), channel_id=1, source_target_pairs={{0,3},{1,0},{2,1},{3,2},{4,7},{5,4},{6,5},{7,6},{8,11},{9,8},{10,9... | collective-permute-start | bytes 589832 | tf_op jit(solution)/shard_map/ppermute | solution.py:525
  112.9 10.8 %collective-permute-start.10 = (bf16[1152,768]{1,0:T(8,128)(2,1)}, bf16[1152,768]{1,0:T(8,128)(2,1)}, u32[]{:S(2)}, u32[]{:S(2)}) collective-permute-start(bf16[1152,768]{1,0:T(8,128)(2,1)} %bitcast.31.refs_11_), channel_id=1, source_target_pairs={{0,4},{4,0},{8,12},{12,8},{16,20},{20,16},{24,28},{28,24},{1,5},{5... | collective-permute-start | bytes 5308424 | tf_op jit(solution)/shard_map/ppermute | solution.py:529
  113.0 10.7 %collective-permute-start.11 = (bf16[1152,768]{1,0:T(8,128)(2,1)}, bf16[1152,768]{1,0:T(8,128)(2,1)}, u32[]{:S(2)}, u32[]{:S(2)}) collective-permute-start(bf16[1152,768]{1,0:T(8,128)(2,1)} %bitcast.32.refs_14_), channel_id=1, source_target_pairs={{0,4},{4,0},{8,12},{12,8},{16,20},{20,16},{24,28},{28,24},{1,5},{5... | collective-permute-start | bytes 5308424 | tf_op jit(solution)/shard_map/ppermute | solution.py:529
  122.5 35.3 %collective-permute-start.15 = (bf16[4,288,768]{2,1,0:T(8,128)(2,1)S(1)}, bf16[4,288,768]{2,1,0:T(8,128)(2,1)S(1)}, u32[]{:S(2)}, u32[]{:S(2)}) collective-permute-start(bf16[4,288,768]{2,1,0:T(8,128)(2,1)S(1)} %bitcast.173), channel_id=1, source_target_pairs={{0,4},{4,0},{8,12},{12,8},{16,20},{20,16},{24,28},{28,24},{1,5},{5... | collective-permute-start | bytes 5308424 | tf_op jit(solution)/shard_map/ppermute | solution.py:529
  161.2 26.4 %collective-permute-start.12 = (bf16[512,192]{1,0:T(8,128)(2,1)}, bf16[512,192]{1,0:T(8,128)(2,1)}, u32[]{:S(2)}, u32[]{:S(2)}) collective-permute-start(bf16[512,192]{1,0:T(8,128)(2,1)} %get-tuple-element.141), channel_id=1, source_target_pairs={{0,3},{1,0},{2,1},{3,2},{4,7},{5,4},{6,5},{7,6},{8,11},{9,8},{10,9... | collective-permute-start | bytes 589832 | tf_op jit(solution)/shard_map/ppermute | solution.py:525
  167.6 24.8 %collective-permute-start.13 = (bf16[512,192]{1,0:T(8,128)(2,1)}, bf16[512,192]{1,0:T(8,128)(2,1)}, u32[]{:S(2)}, u32[]{:S(2)}) collective-permute-start(bf16[512,192]{1,0:T(8,128)(2,1)} %get-tuple-element.142), channel_id=1, source_target_pairs={{0,2},{1,3},{2,0},{3,1},{4,6},{5,7},{6,4},{7,5},{8,10},{9,11},{10,... | collective-permute-start | bytes 589832 | tf_op jit(solution)/shard_map/ppermute | solution.py:525
  168.7 23.8 %collective-permute-start.14 = (bf16[512,192]{1,0:T(8,128)(2,1)}, bf16[512,192]{1,0:T(8,128)(2,1)}, u32[]{:S(2)}, u32[]{:S(2)}) collective-permute-start(bf16[512,192]{1,0:T(8,128)(2,1)} %get-tuple-element.143), channel_id=1, source_target_pairs={{0,1},{1,2},{2,3},{3,0},{4,5},{5,6},{6,7},{7,4},{8,9},{9,10},{10,1... | collective-permute-start | bytes 589832 | tf_op jit(solution)/shard_map/ppermute | solution.py:525
  192.4 41.8 %collective-permute-start.16 = (bf16[4,4,240,768]{3,2,1,0:T(8,128)(2,1)}, bf16[4,4,240,768]{3,2,1,0:T(8,128)(2,1)}, u32[]{:S(2)}, u32[]{:S(2)}) collective-permute-start(bf16[4,4,240,768]{3,2,1,0:T(8,128)(2,1)} %get-tuple-element.171), channel_id=1, source_target_pairs={{0,4},{4,0},{8,12},{12,8},{16,20},{20,16},{24,28},{28,24},{1,5},{5... | collective-permute-start | bytes 17694728 | tf_op jit(solution)/shard_map/ppermute | solution.py:529
  192.4 41.8 %collective-permute-start.17 = (f32[72,128]{1,0:T(8,128)}, f32[72,128]{1,0:T(8,128)}, u32[]{:S(2)}, u32[]{:S(2)}) collective-permute-start(f32[72,128]{1,0:T(8,128)} %maximum_bitcast_fusion.6), channel_id=1, source_target_pairs={{0,4},{4,0},{8,12},{12,8},{16,20},{20,16},{24,28},{28,24},{1,5},{5... | collective-permute-start | bytes 110600 | tf_op jit(solution)/shard_map/ppermute | solution.py:529
  193.0 241.0 %all-gather.7.cloned.1.call-start = ((), (), s32[]{:S(2)}) async-start(), calls=%async_computation.1 | async-start | bytes 3932160 | tf_op jit(solution)/shard_map/all_gather | solution.py:776
  193.0 41.2 %copy-start.33 = (f32[72,128]{1,0:T(8,128)S(1)}, f32[72,128]{1,0:T(8,128)}, u32[]{:S(2)}) copy-start(f32[72,128]{1,0:T(8,128)} %maximum_bitcast_fusion.6) | copy-start | bytes 110596
  235.6 31.3 %collective-permute-start.20 = (f32[72,128]{1,0:T(8,128)}, f32[72,128]{1,0:T(8,128)}, u32[]{:S(2)}, u32[]{:S(2)}) collective-permute-start(f32[72,128]{1,0:T(8,128)} %add.263), channel_id=1, source_target_pairs={{0,8},{4,12},{8,0},{12,4},{16,24},{20,28},{24,16},{28,20},{1,9},{5... | collective-permute-start | bytes 110600 | tf_op jit(solution)/shard_map/ppermute | solution.py:529
  241.5 40.0 %collective-permute-start.19 = (bf16[2,4,96,768]{3,2,1,0:T(8,128)(2,1)}, bf16[2,4,96,768]{3,2,1,0:T(8,128)(2,1)}, u32[]{:S(2)}, u32[]{:S(2)}) collective-permute-start(bf16[2,4,96,768]{3,2,1,0:T(8,128)(2,1)} %get-tuple-element.272), channel_id=1, source_target_pairs={{0,16},{4,20},{8,24},{12,28},{16,0},{20,4},{24,8},{28,12},{1,17},{... | collective-permute-start | bytes 3538952 | tf_op jit(solution)/shard_map/ppermute | solution.py:529
  246.6 40.2 %collective-permute-start.18 = (bf16[2,4,144,768]{3,2,1,0:T(8,128)(2,1)}, bf16[2,4,144,768]{3,2,1,0:T(8,128)(2,1)}, u32[]{:S(2)}, u32[]{:S(2)}) collective-permute-start(bf16[2,4,144,768]{3,2,1,0:T(8,128)(2,1)} %fusion.1), channel_id=1, source_target_pairs={{0,8},{4,12},{8,0},{12,4},{16,24},{20,28},{24,16},{28,20},{1,9},{5... | collective-permute-start | bytes 5308424 | tf_op jit(solution)/shard_map/ppermute | solution.py:529
  248.7 21.6 %collective-permute-start.21 = (bf16[512,640]{1,0:T(8,128)(2,1)}, bf16[512,640]{1,0:T(8,128)(2,1)}, u32[]{:S(2)}, u32[]{:S(2)}) collective-permute-start(bf16[512,640]{1,0:T(8,128)(2,1)} %get-tuple-element.282), channel_id=1, source_target_pairs={{0,1},{1,2},{2,3},{3,0},{4,5},{5,6},{6,7},{7,4},{8,9},{9,10},{10,1... | collective-permute-start | bytes 1966088 | tf_op jit(solution)/shard_map/ppermute | solution.py:525
  248.7 32.7 %collective-permute-start.22 = (bf16[512,640]{1,0:T(8,128)(2,1)}, bf16[512,640]{1,0:T(8,128)(2,1)}, u32[]{:S(2)}, u32[]{:S(2)}) collective-permute-start(bf16[512,640]{1,0:T(8,128)(2,1)} %get-tuple-element.281), channel_id=1, source_target_pairs={{0,3},{1,0},{2,1},{3,2},{4,7},{5,4},{6,5},{7,6},{8,11},{9,8},{10,9... | collective-permute-start | bytes 1966088 | tf_op jit(solution)/shard_map/ppermute | solution.py:525
  288.0 34.8 %collective-permute-start.27 = (bf16[2,2,96,1664]{3,2,1,0:T(8,128)(2,1)}, bf16[2,2,96,1664]{3,2,1,0:T(8,128)(2,1)}, u32[]{:S(2)}, u32[]{:S(2)}) collective-permute-start(bf16[2,2,96,1664]{3,2,1,0:T(8,128)(2,1)} %dynamic-slice_bitcast_fusion), channel_id=1, source_target_pairs={{0,4},{4,0},{8,12},{12,8},{16,20},{20,16},{24,28},{28,24},{1,5},{5... | collective-permute-start | bytes 3833864 | tf_op jit(solution)/shard_map/ppermute | solution.py:529
  291.2 31.6 %collective-permute-start.23 = (bf16[4,144,768]{2,1,0:T(8,128)(2,1)}, bf16[4,144,768]{2,1,0:T(8,128)(2,1)}, u32[]{:S(2)}, u32[]{:S(2)}) collective-permute-start(bf16[4,144,768]{2,1,0:T(8,128)(2,1)} %get-tuple-element.274), channel_id=1, source_target_pairs={{0,16},{4,20},{8,24},{12,28},{16,0},{20,4},{24,8},{28,12},{1,17},{... | collective-permute-start | bytes 2654216 | tf_op jit(solution)/shard_map/ppermute | solution.py:529
  291.9 30.9 %collective-permute-start.26 = (bf16[512,640]{1,0:T(8,128)(2,1)}, bf16[512,640]{1,0:T(8,128)(2,1)}, u32[]{:S(2)}, u32[]{:S(2)}) collective-permute-start(bf16[512,640]{1,0:T(8,128)(2,1)} %get-tuple-element.280), channel_id=1, source_target_pairs={{0,2},{1,3},{2,0},{3,1},{4,6},{5,7},{6,4},{7,5},{8,10},{9,11},{10,... | collective-permute-start | bytes 1966088 | tf_op jit(solution)/shard_map/ppermute | solution.py:525
  295.8 27.0 %collective-permute-start.24 = (bf16[4,96,768]{2,1,0:T(8,128)(2,1)}, bf16[4,96,768]{2,1,0:T(8,128)(2,1)}, u32[]{:S(2)}, u32[]{:S(2)}) collective-permute-start(bf16[4,96,768]{2,1,0:T(8,128)(2,1)} %get-tuple-element.295), channel_id=1, source_target_pairs={{0,8},{4,12},{8,0},{12,4},{16,24},{20,28},{24,16},{28,20},{1,9},{5... | collective-permute-start | bytes 1769480 | tf_op jit(solution)/shard_map/ppermute | solution.py:529
  297.6 25.2 %collective-permute-start.25 = (f32[72,128]{1,0:T(8,128)}, f32[72,128]{1,0:T(8,128)}, u32[]{:S(2)}, u32[]{:S(2)}) collective-permute-start(f32[72,128]{1,0:T(8,128)} %add.268), channel_id=1, source_target_pairs={{0,16},{4,20},{8,24},{12,28},{16,0},{20,4},{24,8},{28,12},{1,17},{... | collective-permute-start | bytes 110600 | tf_op jit(solution)/shard_map/ppermute | solution.py:529
  299.1 25.7 %copy-start.22 = (bf16[4,96,768]{2,1,0:T(8,128)(2,1)S(1)}, bf16[4,96,768]{2,1,0:T(8,128)(2,1)}, u32[]{:S(2)}) copy-start(bf16[4,96,768]{2,1,0:T(8,128)(2,1)} %get-tuple-element.196) | copy-start | bytes 1769476
  324.4 16.4 %collective-permute-start.28 = (bf16[2,96,1664]{2,1,0:T(8,128)(2,1)S(1)}, bf16[2,96,1664]{2,1,0:T(8,128)(2,1)S(1)}, u32[]{:S(2)}, u32[]{:S(2)}) collective-permute-start(bf16[2,96,1664]{2,1,0:T(8,128)(2,1)S(1)} %fusion.12), channel_id=1, source_target_pairs={{0,8},{4,12},{8,0},{12,4},{16,24},{20,28},{24,16},{28,20},{1,9},{5... | collective-permute-start | bytes 1916936 | tf_op jit(solution)/shard_map/ppermute | solution.py:529
  328.5 25.5 %collective-permute-start.31 = (bf16[240,768]{1,0:T(8,128)(2,1)}, bf16[240,768]{1,0:T(8,128)(2,1)}, u32[]{:S(2)}, u32[]{:S(2)}) collective-permute-start(bf16[240,768]{1,0:T(8,128)(2,1)} %get-tuple-element.305), channel_id=1, source_target_pairs={{0,3},{1,0},{2,1},{3,2},{4,7},{5,4},{6,5},{7,6},{8,11},{9,8},{10,9... | collective-permute-start | bytes 1105928 | tf_op jit(solution)/shard_map/ppermute | solution.py:525
  329.1 31.5 %collective-permute-start.32 = (bf16[240,768]{1,0:T(8,128)(2,1)}, bf16[240,768]{1,0:T(8,128)(2,1)}, u32[]{:S(2)}, u32[]{:S(2)}) collective-permute-start(bf16[240,768]{1,0:T(8,128)(2,1)} %get-tuple-element.306), channel_id=1, source_target_pairs={{0,2},{1,3},{2,0},{3,1},{4,6},{5,7},{6,4},{7,5},{8,10},{9,11},{10,... | collective-permute-start | bytes 1105928 | tf_op jit(solution)/shard_map/ppermute | solution.py:525
  329.1 31.5 %collective-permute-start.33 = (bf16[240,768]{1,0:T(8,128)(2,1)}, bf16[240,768]{1,0:T(8,128)(2,1)}, u32[]{:S(2)}, u32[]{:S(2)}) collective-permute-start(bf16[240,768]{1,0:T(8,128)(2,1)} %get-tuple-element.303), channel_id=1, source_target_pairs={{0,1},{1,2},{2,3},{3,0},{4,5},{5,6},{6,7},{7,4},{8,9},{9,10},{10,1... | collective-permute-start | bytes 1105928 | tf_op jit(solution)/shard_map/ppermute | solution.py:525
  332.2 21.8 %collective-permute-start.30 = (f32[72,128]{1,0:T(8,128)}, f32[72,128]{1,0:T(8,128)}, u32[]{:S(2)}, u32[]{:S(2)}) collective-permute-start(f32[72,128]{1,0:T(8,128)} %add.273), channel_id=1, source_target_pairs={{0,1},{1,0},{2,3},{3,2},{4,5},{5,4},{6,7},{7,6},{8,9},{9,8},{10,11... | collective-permute-start | bytes 110600 | tf_op jit(solution)/shard_map/ppermute | solution.py:529
  343.8 9.0 %collective-permute-start.29 = (bf16[96,1664]{1,0:T(8,128)(2,1)}, bf16[96,1664]{1,0:T(8,128)(2,1)}, u32[]{:S(2)}, u32[]{:S(2)}) collective-permute-start(bf16[96,1664]{1,0:T(8,128)(2,1)} %dynamic-slice_bitcast_fusion.1), channel_id=1, source_target_pairs={{0,16},{4,20},{8,24},{12,28},{16,0},{20,4},{24,8},{28,12},{1,17},{... | collective-permute-start | bytes 958472 | tf_op jit(solution)/shard_map/ppermute | solution.py:529
  362.1 12.5 %collective-permute-start.39 = (bf16[240,768]{1,0:T(8,128)(2,1)S(1)}, bf16[240,768]{1,0:T(8,128)(2,1)S(1)}, u32[]{:S(2)}, u32[]{:S(2)}) collective-permute-start(bf16[240,768]{1,0:T(8,128)(2,1)S(1)} %add_convert_fusion.10), channel_id=1, source_target_pairs={{0,24},{4,28},{8,16},{12,20},{16,8},{20,12},{24,0},{28,4},{1,25},{... | collective-permute-start | bytes 1105928 | tf_op jit(solution)/shard_map/ppermute | solution.py:529
  364.6 17.9 %collective-permute-start.40 = (bf16[240,768]{1,0:T(8,128)(2,1)S(1)}, bf16[240,768]{1,0:T(8,128)(2,1)S(1)}, u32[]{:S(2)}, u32[]{:S(2)}) collective-permute-start(bf16[240,768]{1,0:T(8,128)(2,1)S(1)} %add_convert_fusion.10), channel_id=1, source_target_pairs={{0,16},{4,20},{8,24},{12,28},{16,0},{20,4},{24,8},{28,12},{1,17},{... | collective-permute-start | bytes 1105928 | tf_op jit(solution)/shard_map/ppermute | solution.py:529
  365.3 17.2 %collective-permute-start.41 = (bf16[240,768]{1,0:T(8,128)(2,1)S(1)}, bf16[240,768]{1,0:T(8,128)(2,1)S(1)}, u32[]{:S(2)}, u32[]{:S(2)}) collective-permute-start(bf16[240,768]{1,0:T(8,128)(2,1)S(1)} %add_convert_fusion.10), channel_id=1, source_target_pairs={{0,8},{4,12},{8,0},{12,4},{16,24},{20,28},{24,16},{28,20},{1,9},{5... | collective-permute-start | bytes 1105928 | tf_op jit(solution)/shard_map/ppermute | solution.py:529
  365.7 23.8 %collective-permute-start.35 = (bf16[96,1664]{1,0:T(8,128)(2,1)S(1)}, bf16[96,1664]{1,0:T(8,128)(2,1)}, u32[]{:S(2)}, u32[]{:S(2)}) collective-permute-start(bf16[96,1664]{1,0:T(8,128)(2,1)S(1)} %fusion.13), channel_id=1, source_target_pairs={{0,24},{4,28},{8,16},{12,20},{16,8},{20,12},{24,0},{28,4},{1,25},{... | collective-permute-start | bytes 958472 | tf_op jit(solution)/shard_map/ppermute | solution.py:529
  368.1 26.3 %collective-permute-start.36 = (bf16[96,1664]{1,0:T(8,128)(2,1)S(1)}, bf16[96,1664]{1,0:T(8,128)(2,1)}, u32[]{:S(2)}, u32[]{:S(2)}) collective-permute-start(bf16[96,1664]{1,0:T(8,128)(2,1)S(1)} %fusion.13), channel_id=1, source_target_pairs={{0,16},{4,20},{8,24},{12,28},{16,0},{20,4},{24,8},{28,12},{1,17},{... | collective-permute-start | bytes 958472 | tf_op jit(solution)/shard_map/ppermute | solution.py:529
  374.6 19.9 %collective-permute-start.37 = (bf16[96,1664]{1,0:T(8,128)(2,1)S(1)}, bf16[96,1664]{1,0:T(8,128)(2,1)S(1)}, u32[]{:S(2)}, u32[]{:S(2)}) collective-permute-start(bf16[96,1664]{1,0:T(8,128)(2,1)S(1)} %fusion.13), channel_id=1, source_target_pairs={{0,8},{4,12},{8,0},{12,4},{16,24},{20,28},{24,16},{28,20},{1,9},{5... | collective-permute-start | bytes 958472 | tf_op jit(solution)/shard_map/ppermute | solution.py:529
  384.7 30.0 %collective-permute-start.42 = (bf16[2,384,768]{2,1,0:T(8,128)(2,1)}, bf16[2,384,768]{2,1,0:T(8,128)(2,1)}, u32[]{:S(2)}, u32[]{:S(2)}) collective-permute-start(bf16[2,384,768]{2,1,0:T(8,128)(2,1)} %pad_maximum_fusion.7), channel_id=1, source_target_pairs={{0,4},{4,0},{8,12},{12,8},{16,20},{20,16},{24,28},{28,24},{1,5},{5... | collective-permute-start | bytes 3538952 | tf_op jit(solution)/shard_map/ppermute | solution.py:529
  396.9 22.9 %collective-permute-start.38 = (bf16[384,1664]{1,0:T(8,128)(2,1)}, bf16[384,1664]{1,0:T(8,128)(2,1)}, u32[]{:S(2)}, u32[]{:S(2)}) collective-permute-start(bf16[384,1664]{1,0:T(8,128)(2,1)} %pad_maximum_fusion.4), channel_id=1, source_target_pairs={{0,4},{4,0},{8,12},{12,8},{16,20},{20,16},{24,28},{28,24},{1,5},{5... | collective-permute-start | bytes 3833864 | tf_op jit(solution)/shard_map/ppermute | solution.py:529
  397.7 9.9 %collective-permute-start.34 = (f32[72,128]{1,0:T(8,128)S(1)}, f32[72,128]{1,0:T(8,128)S(1)}, u32[]{:S(2)}, u32[]{:S(2)}) collective-permute-start(f32[72,128]{1,0:T(8,128)S(1)} %add.276), channel_id=1, source_target_pairs={{0,2},{1,3},{2,0},{3,1},{4,6},{5,7},{6,4},{7,5},{8,10},{9,11},{10,... | collective-permute-start | bytes 110600 | tf_op jit(solution)/shard_map/ppermute | solution.py:529
  (40 other events, 218.5 us)
Sparse Core Ops, SparseCore 0:
  52.2 45.3 all-gather.8
  193.1 78.2 all-gather.4
  368.9 64.9 all-gather.6

commit v6 on v5

--- a/solution.py
+++ b/solution.py
@@ -225,10 +225,17 @@
         gq = jnp.transpose(jnp.concatenate(rows, axis=0))[:, :width]
         gkb = jnp.concatenate([gk[h, qcol, :] for h in range(heads)], axis=1) * scale
         gvb = jnp.concatenate([gv[h, qcol, :] for h in range(heads)], axis=1)
-        rows = [gq, gkb, gvb]
-        if gqkv.shape[1] > 3 * width:
-            rows.append(jnp.zeros((BLOCK, gqkv.shape[1] - 3 * width), F32))
-        gqkv[qcol, :] = jnp.concatenate(rows, axis=1).astype(BF16)
+        y = jnp.concatenate([gq, gkb, gvb], axis=1).astype(BF16)
+        pair = pl.ds(pl.multiple_of(qb // 2 * BLOCK, BLOCK), BLOCK)
+
+        @pl.when(lax.rem(qb, 2) == 0)
+        def _():
+            gqkv[pair, : 3 * width] = y
+
+        @pl.when(lax.rem(qb, 2) == 1)
+        def _():
+            gqkv[pair, 3 * width :] = y
+
         return 0
 
     lax.fori_loop(0, tokens // BLOCK, per_q, 0)
@@ -245,7 +252,7 @@
     return pl.pallas_call(
         functools.partial(attn_bwd_kernel, n_t),
         in_specs=[pl.BlockSpec(memory_space=pltpu.SMEM)] + [pl.BlockSpec(memory_space=pl.ANY)] * n_t + [vm] * 8,
-        out_shape=(sd((tokens, -(-3 * width // 128) * 128), BF16), sd(lmt.shape, F32)),
+        out_shape=(sd((tokens // 2, 6 * width), BF16), sd(lmt.shape, F32)),
         scratch_shapes=[
             pltpu.VMEM((heads, tokens, hd), F32),
             pltpu.VMEM((heads, tokens, hd), F32),
@@ -334,10 +341,13 @@
     acc[...] = jnp.zeros(acc.shape, F32)
 
     def add(i, total):
-        rows = pl.ds(pl.multiple_of(i * step, step), step)
-        y = gqkv[rows, :wide]
-        acc[...] += dot_tn(hid[rows, :], y)
-        return total + jnp.sum(y.astype(F32), axis=0, keepdims=True)
+        pair = pl.ds(pl.multiple_of(i * BLOCK, BLOCK), BLOCK)
+        for n in range(2):
+            rows = pl.ds(pl.multiple_of(i * step + n * BLOCK, BLOCK), BLOCK)
+            y = gqkv[pair, n * wide : (n + 1) * wide]
+            acc[...] += dot_tn(hid[rows, :], y)
+            total = total + jnp.sum(y.astype(F32), axis=0, keepdims=True)
+        return total
 
     total = lax.fori_loop(0, tokens // step, add, jnp.zeros((1, wide), F32))
     rows = [total[:, n * extra : (n + 1) * extra] for n in range(wide // extra)]
@@ -363,10 +373,15 @@
 def back_kernel(place, w, resid, *refs):
     pieces, out = refs[:-1], refs[-1]
     n_t, wide, _ = w.shape
-    total = resid[...]
-    for s in range(n_t):
-        total = total + dot(pieces[s][:, :wide], w[lax.rem(place[0] + n_t - s, n_t)])
-    out[...] = total.astype(BF16)
+    chunk = resid.shape[0]
+    for at in range(0, chunk, 2 * BLOCK):
+        for n in range(2):
+            rows = slice(at + n * BLOCK, at + (n + 1) * BLOCK)
+            total = resid[rows, :]
+            for s in range(n_t):
+                y = pieces[s][at // 2 : at // 2 + BLOCK, n * wide : (n + 1) * wide]
+                total = total + dot(y, w[lax.rem(place[0] + n_t - s, n_t)])
+            out[rows, :] = total.astype(BF16)
 
 
 def back_of(place, w, resid, pieces):
@@ -726,14 +741,17 @@
     gqkv, glm, keep, got, pack, pack_came = lax.optimization_barrier((gqkv, glm, keep, got, pack, pack_came))
     pack = pack + pack_came
     pack_came = dp_swap(pack, low_bits[0])
-    parts = [rows_of(gqkv, ti * chunk, chunk)] + [
-        shift(rows_of(gqkv, lax.rem(ti + s, n_t) * chunk, chunk), n_t, s) for s in range(1, n_t)
+    pairs = chunk // 2
+    parts = [rows_of(gqkv, ti * pairs, pairs)] + [
+        shift(rows_of(gqkv, lax.rem(ti + s, n_t) * pairs, pairs), n_t, s) for s in range(1, n_t)
     ]
+    tall = keep.shape[2]
+    mid = -(-tall // 32) * 16
     keep = keep.reshape(lead + keep.shape[1:])
     got = got.reshape(lead + got.shape[1:])
-    a_keep, a_send, bit = narrow_pair(keep, got, low_bits, 0, cut)
+    a_keep, a_send, bit = narrow_pair(keep, got, low_bits, 0, mid)
     a_came = dp_swap(a_send, bit)
-    b_keep, b_send, bit = narrow_pair(keep, got, high_bits, cut, slab)
+    b_keep, b_send, bit = narrow_pair(keep, got, high_bits, mid, tall - mid)
     b_came = dp_swap(b_send, bit)
     tail = tail_of(hidden, gqkv, glm, table, noise, 3 * local)
     w_all = jnp.concatenate([jnp.where(up, w_other, w_side), jnp.where(up, w_side, w_other)], axis=1)

time: 455 us -> 452 us (level)
  transfers between devices with their start and end apart: 46 -> 46, of which waited for: 18 -> 19; matrix products, arithmetic and copies ran while one was open for 21% -> 21% of each run, Pallas kernels for 33% -> 33%
where the time goes in v6:
time: 452 us; the launch traced here: 445 us
  Pallas kernels  149 us (33%)
  waiting for transfers between devices  104 us (23%)
  other arithmetic  74.3 us (16%)
  starting transfers between devices  59.1 us (13%)
  local copies, waits for them, and re-layouts  40.3 us (9%)
  between operations  18.3 us (4%)
    ppermute x15, waiting for transfers between devices, shift(): lax.ppermute(x, 'tensor', [(j, (j + amount) % size) for j in range(size)])  58.5 us
    pallas_call x1, Pallas kernels, attn_bwd(): pl.pallas_call(functools.partial(attn_bwd_kernel, n_t), in_specs=[pl.Bloc...  41.9 us
    ppermute x28, waiting for transfers between devices, swap(): return lax.ppermute(x, axis, [(j, j ^ bit) for j in range(size)])  41.3 us
    pallas_call x1, Pallas kernels, ffn(): pl.pallas_call(functools.partial(ffn_kernel, n_t, slab), in_specs=[sm] +...  34 us
    pallas_call x3, Pallas kernels, attn_fwd(): pl.pallas_call(functools.partial(attn_fwd_kernel, lo, len(prev)), grid=(h...  30.8 us
    ppermute x15, starting transfers between devices, shift(): lax.ppermute(x, 'tensor', [(j, (j + amount) % size) for j in range(size)])  30.4 us
    ppermute x28, starting transfers between devices, swap(): return lax.ppermute(x, axis, [(j, j ^ bit) for j in range(size)])  28.5 us
    reshape x6, other arithmetic, half(): return (part(x) + part(y)).astype(BF16).reshape(sizes[:ax] + sizes[ax + 1:])  17.8 us
  transfers between devices with their start and end apart: 46, of which 19 were waited for; matrix products, arithmetic and copies ran while one was open for 21% of the time, Pallas kernels for 33%

profile of v6, /device:TPU:0, one launch (start us, length us, event | category | flops | bytes accessed | tf_op | source)
XLA Modules:
  0.0 444.8 jit_solution(10854199188629480538)
XLA Ops:
  11.4 3.1 collective-permute-start
  14.5 2.6 collective-permute-start.1
  20.7 15.0 %attn_prep.1 = (bf16[3,2048,64]{2,1,0:T(8,128)(2,1)}, bf16[3,2048,64]{2,1,0:T(8,128)(2,1)}, bf16[3,2048,64]{2,1,0:T(8,128)(2,1)}, bf16[192,2048]{1,0:T(8,128)(2,...) custom-call(bf16[2048,768]{1,0:T(8,128)(2,1)} %hid.3, ...), custom_call_target="tpu_custom_call" | custom-call | flops 15000000512 | bytes 20971520 | tf_op jit(solution)/shard_map/attn_prep/pallas_call | solution.py:75
  36.5 9.5 %attn_fwd.3 = (bf16[2048,192]{1,0:T(8,128)(2,1)}, f32[192,2048]{1,0:T(8,128)}, f32[8,2048]{1,0:T(8,128)}) custom-call(bf16[192,2048]{1,0:T(8,128)(2,1)} %get-tuple-element.111.qt.refs_8_, bf16[3,2048,64]{2,1,0:T(8,128)(2,1)} %get-tuple-element.112.k3.refs_6_, bf16[192,2048]{1,0:T(8,128)(2,1)} %get-tuple-element.113.vt, ...), custom_call_target="tpu_custom_call" | custom-call | flops 3000000000 | bytes 8388608 | tf_op jit(solution)/shard_map/attn_fwd/pallas_call | solution.py:148
  52.0 9.6 %attn_fwd.4 = (bf16[2048,192]{1,0:T(8,128)(2,1)}, f32[192,2048]{1,0:T(8,128)}, f32[8,2048]{1,0:T(8,128)}) custom-call(bf16[192,2048]{1,0:T(8,128)(2,1)} %get-tuple-element.111.qt.refs_8_, bf16[3,2048,64]{2,1,0:T(8,128)(2,1)} %get-tuple-element.112.k3.refs_6_, ...), custom_call_target="tpu_custom_call", output_to_operand_aliasing={{0}: (4, {}), {1}: (5, {}), {2}: (6, {})} | custom-call | flops 3750000128 | bytes 8388608 | tf_op jit(solution)/shard_map/attn_fwd/pallas_call | solution.py:148
  61.6 2.1 collective-permute-done.3
  72.6 11.7 %attn_fwd.5 = (bf16[2048,192]{1,0:T(8,128)(2,1)}, f32[192,2048]{1,0:T(8,128)}, f32[8,2048]{1,0:T(8,128)}) custom-call(bf16[192,2048]{1,0:T(8,128)(2,1)} %get-tuple-element.111.qt.refs_8_, bf16[3,2048,64]{2,1,0:T(8,128)(2,1)} %get-tuple-element.112.k3.refs_6_, ...), custom_call_target="tpu_custom_call", output_to_operand_aliasing={{0}: (4, {}), {1}: (5, {}), {2}: (6, {})} | custom-call | flops 5249999872 | bytes 8388608 | tf_op jit(solution)/shard_map/attn_fwd/pallas_call | solution.py:148
  84.3 2.0 constant_dynamic-slice_fusion.9
  86.3 6.0 %collective-permute-start.5 = (bf16[512,192]{1,0:T(8,128)(2,1)S(1)}, bf16[512,192]{1,0:T(8,128)(2,1)S(1)}, u32[]{:S(2)}, u32[]{:S(2)}) collective-permute-start(bf16[512,192]{1,0:T(8,128)(2,1)S(1)} %get-tuple-element.315), channel_id=1, source_target_pairs={{0,1},{1,2},{2,3},{3,0},{4,5},{5,6},{6,7},{7,4},{8,9},{9,10},{10,1... | collective-permute-start | bytes 589832 | tf_op jit(solution)/shard_map/ppermute | solution.py:540
  99.6 2.0 collective-permute-done.5.refs_1_
  101.7 9.9 %collective-permute-done.6.refs_2_ = bf16[512,192]{1,0:T(8,128)(2,1)S(1)} collective-permute-done((bf16[512,192]{1,0:T(8,128)(2,1)S(1)}, bf16[512,192]{1,0:T(8,128)(2,1)S(1)}, u32[]{:S(2)}, u32[]{:S(2)}) %collective-permute-start.6) | collective-permute-done | bytes 196640 | tf_op jit(solution)/shard_map/ppermute | solution.py:540
  113.6 2.1 constant_dynamic-slice_fusion.8.refs_5_
  115.7 2.7 constant_dynamic-slice_fusion.7.refs_6_
  123.7 34.0 %ffn.1 = (f32[512,768]{1,0:T(8,128)}, bf16[512,768]{1,0:T(8,128)(2,1)}, bf16[512,3072]{1,0:T(8,128)(2,1)}, bf16[512,3072]{1,0:T(8,128)(2,1)}, bf16[512,768]{1,0:...) custom-call(s32[1]{0:T(128)} %bitcast.core, ...), custom_call_target="tpu_custom_call" | custom-call | flops 33999998976 | bytes 26214400 | tf_op jit(solution)/shard_map/ffn/pallas_call | solution.py:510
  161.2 6.4 %collective-permute-start.12 = (bf16[512,192]{1,0:T(8,128)(2,1)}, bf16[512,192]{1,0:T(8,128)(2,1)}, u32[]{:S(2)}, u32[]{:S(2)}) collective-permute-start(bf16[512,192]{1,0:T(8,128)(2,1)} %get-tuple-element.141), channel_id=1, source_target_pairs={{0,3},{1,0},{2,1},{3,2},{4,7},{5,4},{6,5},{7,6},{8,11},{9,8},{10,9... | collective-permute-start | bytes 589832 | tf_op jit(solution)/shard_map/ppermute | solution.py:540
  169.5 4.2 broadcast_select_fusion.1
  177.1 10.2 %wgrad.1 = (bf16[4,4,240,768]{3,2,1,0:T(8,128)(2,1)}, bf16[4,4,240,768]{3,2,1,0:T(8,128)(2,1)}) custom-call(bf16[512,3072]{1,0:T(8,128)(2,1)S(1)} %copy-done.10, bf16[512,768]{1,0:T(8,128)(2,1)S(1)} %copy-done.11, bf16[512,3072]{1,0:T(8,128)(2,1)S(1)} %copy-done.9, bf16[512,768]{1,0:T(8,128)(2,1)S(1)} %copy-done.12, bf16[512,768]{1,0:T(8,128)(2,1)S(1)} %copy-done.13, ...), custom_call_target="tpu_custom_call" | custom-call | flops 399999991808 | bytes 10485760 | tf_op jit(solution)/shard_map/wgrad/pallas_call | solution.py:312
  187.6 4.8 %collective-permute-done.13.refs_2_ = bf16[512,192]{1,0:T(8,128)(2,1)} collective-permute-done((bf16[512,192]{1,0:T(8,128)(2,1)}, bf16[512,192]{1,0:T(8,128)(2,1)}, u32[]{:S(2)}, u32[]{:S(2)}) %collective-permute-start.13) | collective-permute-done | bytes 196640 | tf_op jit(solution)/shard_map/ppermute | solution.py:540
  193.0 41.9 %attn_bwd.1 = (bf16[1024,1152]{1,0:T(8,128)(2,1)}, f32[3,512,512]{2,1,0:T(8,128)}) custom-call(s32[1]{0:T(128)} %bitcast.40.place, bf16[512,192]{1,0:T(8,128)(2,1)} %get-tuple-element.159.refs_0_, bf16[512,192]{1,0:T(8,128)(2,1)} %collective-permute-done.12.refs_1_, bf16[512,192]{1,0:T(8,128)(2,1)} %collective-permute-done.13.refs_2_, ...), custom_call_target="tpu_custom_call" | custom-call | flops 399999991808 | bytes 20971520 | tf_op jit(solution)/shard_map/attn_bwd/pallas_call | solution.py:252
  237.8 4.8 %fusion.3 = (bf16[2,4,112,768]{3,2,1,0:T(8,128)(2,1)}, bf16[2,4,112,768]{3,2,1,0:T(8,128)(2,1)}) fusion(bf16[2,2,4,240,768]{4,3,2,1,0:T(8,128)(2,1)} %bitcast.42, s32[]{:T(128)S(6)} %select_n.364, bf16[2,2,4,240,768]{4,3,2,1,0:T(8,128)(2,1)} %bitcast.163, s32[]{:T(128)S(6)} %select_n.363), kind=kLoop, calls=%fused_computation.29 | loop fusion | flops 5505024 | bytes 8257544 | tf_op jit(solution)/shard_map/reshape | solution.py:614
  244.0 3.4 fusion.1
  249.5 3.8 collective-permute-start.22
  253.3 11.7 %tail.1 = bf16[768,1664]{1,0:T(8,128)(2,1)} custom-call(bf16[2048,768]{1,0:T(8,128)(2,1)} %hid.3, bf16[1024,1152]{1,0:T(8,128)(2,1)} %get-tuple-element.173.gqkv, f32[3,512,512]{2,1,0:T(8,128)} %get-tuple-element.174.glm, f32[3,512,512]{2,1,0:T(8,128)} %table.3, f32[3,512,512]{2,1,0:T(8,128)} %noise.3), custom_call_target="tpu_custom_call" | custom-call | flops 399999991808 | bytes 20971520 | tf_op jit(solution)/shard_map/tail/pallas_call | solution.py:363
  265.0 2.4 fusion
  268.9 9.7 %collective-permute-done.22.refs_3_ = bf16[256,1152]{1,0:T(8,128)(2,1)} collective-permute-done((bf16[256,1152]{1,0:T(8,128)(2,1)}, bf16[256,1152]{1,0:T(8,128)(2,1)}, u32[]{:S(2)}, u32[]{:S(2)}) %collective-permute-start.22) | collective-permute-done | bytes 589856 | tf_op jit(solution)/shard_map/ppermute | solution.py:540
  278.6 4.9 %collective-permute-done.18 = bf16[2,4,128,768]{3,2,1,0:T(8,128)(2,1)} collective-permute-done((bf16[2,4,128,768]{3,2,1,0:T(8,128)(2,1)}, bf16[2,4,128,768]{3,2,1,0:T(8,128)(2,1)}, u32[]{:S(2)}, u32[]{:S(2)}) %collective-permute-start.18) | collective-permute-done | bytes 1572896 | tf_op jit(solution)/shard_map/ppermute | solution.py:544
  284.7 3.0 fusion.9
  288.4 2.7 fusion.12
  295.7 23.6 %collective-permute-done.26.refs_2_ = bf16[256,1152]{1,0:T(8,128)(2,1)} collective-permute-done((bf16[256,1152]{1,0:T(8,128)(2,1)}, bf16[256,1152]{1,0:T(8,128)(2,1)}, u32[]{:S(2)}, u32[]{:S(2)}) %collective-permute-start.26) | collective-permute-done | bytes 589856 | tf_op jit(solution)/shard_map/ppermute | solution.py:540
  326.8 1.7 collective-permute-start.33
  331.7 5.5 %collective-permute-done.28 = bf16[2,96,1664]{2,1,0:T(8,128)(2,1)S(1)} collective-permute-done((bf16[2,96,1664]{2,1,0:T(8,128)(2,1)S(1)}, bf16[2,96,1664]{2,1,0:T(8,128)(2,1)S(1)}, u32[]{:S(2)}, u32[]{:S(2)}) %collective-permute-start.28) | collective-permute-done | bytes 639008 | tf_op jit(solution)/shard_map/ppermute | solution.py:544
  341.8 4.9 %back.1 = bf16[512,768]{1,0:T(8,128)(2,1)} custom-call(s32[1]{0:T(128)} %bitcast.40.place, bf16[4,576,768]{2,1,0:T(8,128)(2,1)S(1)} %pad_maximum_fusion.w, f32[512,768]{1,0:T(8,128)S(1)} %copy-done.8, bf16[256,1152]{1,0:T(8,128)(2,1)S(1)} %copy-done, bf16[256,1152]{1,0:T(8,128)(2,1)} %collective-permute-done.21.refs_1_, ...), custom_call_target="tpu_custom_call" | custom-call | flops 5000000000 | bytes 10485760 | tf_op jit(solution)/shard_map/back/pallas_call | solution.py:389
  346.7 2.7 collective-permute-done.29
  351.6 7.0 %collective-permute-done.32 = bf16[240,768]{1,0:T(8,128)(2,1)} collective-permute-done((bf16[240,768]{1,0:T(8,128)(2,1)}, bf16[240,768]{1,0:T(8,128)(2,1)}, u32[]{:S(2)}, u32[]{:S(2)}) %collective-permute-start.32) | collective-permute-done | bytes 368672 | tf_op jit(solution)/shard_map/ppermute | solution.py:540
  365.5 7.0 %collective-permute-done.39 = bf16[240,768]{1,0:T(8,128)(2,1)S(1)} collective-permute-done((bf16[240,768]{1,0:T(8,128)(2,1)S(1)}, bf16[240,768]{1,0:T(8,128)(2,1)S(1)}, u32[]{:S(2)}, u32[]{:S(2)}) %collective-permute-start.39) | collective-permute-done | bytes 368672 | tf_op jit(solution)/shard_map/ppermute | solution.py:544
  372.9 7.6 %collective-permute-done.40 = bf16[240,768]{1,0:T(8,128)(2,1)S(1)} collective-permute-done((bf16[240,768]{1,0:T(8,128)(2,1)S(1)}, bf16[240,768]{1,0:T(8,128)(2,1)S(1)}, u32[]{:S(2)}, u32[]{:S(2)}) %collective-permute-start.40) | collective-permute-done | bytes 368672 | tf_op jit(solution)/shard_map/ppermute | solution.py:544
  382.7 4.8 %collective-permute-done.35 = bf16[96,1664]{1,0:T(8,128)(2,1)} collective-permute-done((bf16[96,1664]{1,0:T(8,128)(2,1)S(1)}, bf16[96,1664]{1,0:T(8,128)(2,1)}, u32[]{:S(2)}, u32[]{:S(2)}) %collective-permute-start.35) | collective-permute-done | bytes 319520 | tf_op jit(solution)/shard_map/ppermute | solution.py:544
  387.4 5.0 %collective-permute-done.36 = bf16[96,1664]{1,0:T(8,128)(2,1)} collective-permute-done((bf16[96,1664]{1,0:T(8,128)(2,1)S(1)}, bf16[96,1664]{1,0:T(8,128)(2,1)}, u32[]{:S(2)}, u32[]{:S(2)}) %collective-permute-start.36) | collective-permute-done | bytes 319520 | tf_op jit(solution)/shard_map/ppermute | solution.py:544
  395.6 4.3 collective-permute-start.34
  399.9 5.1 %convert_element_type.244 = f32[2048,768]{1,0:T(8,128)} convert(bf16[2048,768]{1,0:T(8,128)(2,1)} %all-gather.5.cloned.1.call-done) | non-fusion elementwise | flops 1572864 | bytes 9437184 | tf_op jit(solution)/shard_map/convert_element_type | solution.py:819
  413.9 1.8 multiply_bitcast_fusion
  415.6 1.9 copy.104
  417.6 1.8 broadcast_select_fusion.3
  419.8 1.8 convert_multiply_fusion.2
  421.6 2.9 copy.103
  424.7 2.1 convert_multiply_fusion.1
  427.3 4.4 all-gather.7.cloned.1.call-done
  431.7 5.0 %convert_multiply_fusion = f32[2048,768]{1,0:T(8,128)} fusion(bf16[2048,768]{1,0:T(8,128)(2,1)} %all-gather.7.cloned.1.call-done, f32[]{:T(128)} %bitcast.65), kind=kLoop, calls=%fused_computation.1 | loop fusion | flops 3145728 | bytes 9437188 | tf_op jit(solution)/shard_map/mul | solution.py:833
  (264 shorter events, 99.5 us)
Async XLA Ops:
  7.2 104.3 %all-gather.9.cloned.1.call-start = ((), (), s32[]{:S(2)}) async-start(), calls=%async_computation.2 | async-start | bytes 2211840 | tf_op jit(solution)/shard_map/all_gather | solution.py:678
  11.4 34.6 %collective-permute-start = (bf16[256,768]{1,0:T(8,128)(2,1)S(1)}, bf16[256,768]{1,0:T(8,128)(2,1)}, u32[]{:S(2)}, u32[]{:S(2)}) collective-permute-start(bf16[256,768]{1,0:T(8,128)(2,1)S(1)} %concatenate.53), channel_id=1, source_target_pairs={{0,1},{1,2},{2,3},{3,0},{4,5},{5,6},{6,7},{7,4},{8,9},{9,10},{10,1... | collective-permute-start | bytes 1179656 | tf_op jit(solution)/shard_map/ppermute | solution.py:540
  14.5 31.5 %collective-permute-start.1 = (bf16[256,768]{1,0:T(8,128)(2,1)S(1)}, bf16[256,768]{1,0:T(8,128)(2,1)S(1)}, u32[]{:S(2)}, u32[]{:S(2)}) collective-permute-start(bf16[256,768]{1,0:T(8,128)(2,1)S(1)} %concatenate.53), channel_id=1, source_target_pairs={{0,2},{1,3},{2,0},{3,1},{4,6},{5,7},{6,4},{7,5},{8,10},{9,11},{10,... | collective-permute-start | bytes 1179656 | tf_op jit(solution)/shard_map/ppermute | solution.py:540
  17.1 28.9 %collective-permute-start.2 = (bf16[256,768]{1,0:T(8,128)(2,1)S(1)}, bf16[256,768]{1,0:T(8,128)(2,1)S(1)}, u32[]{:S(2)}, u32[]{:S(2)}) collective-permute-start(bf16[256,768]{1,0:T(8,128)(2,1)S(1)} %concatenate.53), channel_id=1, source_target_pairs={{0,3},{1,0},{2,1},{3,2},{4,7},{5,4},{6,5},{7,6},{8,11},{9,8},{10,9... | collective-permute-start | bytes 1179656 | tf_op jit(solution)/shard_map/ppermute | solution.py:540
  47.8 15.9 %collective-permute-start.3 = (bf16[3,144,768]{2,1,0:T(8,128)(2,1)S(1)}, bf16[3,144,768]{2,1,0:T(8,128)(2,1)S(1)}, u32[]{:S(2)}, u32[]{:S(2)}) collective-permute-start(bf16[3,144,768]{2,1,0:T(8,128)(2,1)S(1)} %pad_maximum_fusion.10), channel_id=1, source_target_pairs={{0,8},{4,12},{8,0},{12,4},{16,24},{20,28},{24,16},{28,20},{1,9},{5... | collective-permute-start | bytes 1990664 | tf_op jit(solution)/shard_map/ppermute | solution.py:544
  50.4 11.3 %collective-permute-start.4 = (bf16[3,96,768]{2,1,0:T(8,128)(2,1)S(1)}, bf16[3,96,768]{2,1,0:T(8,128)(2,1)S(1)}, u32[]{:S(2)}, u32[]{:S(2)}) collective-permute-start(bf16[3,96,768]{2,1,0:T(8,128)(2,1)S(1)} %pad_maximum_fusion.11), channel_id=1, source_target_pairs={{0,16},{4,20},{8,24},{12,28},{16,0},{20,4},{24,8},{28,12},{1,17},{... | collective-permute-start | bytes 1327112 | tf_op jit(solution)/shard_map/ppermute | solution.py:544
  52.0 348.0 %all-gather.5.cloned.1.call-start = ((), (), s32[]{:S(2)}) async-start(), calls=%async_computation | async-start | bytes 3932160 | tf_op jit(solution)/shard_map/all_gather | solution.py:738
  65.8 29.0 %collective-permute-start.9 = (bf16[2,3,96,768]{3,2,1,0:T(8,128)(2,1)}, bf16[2,3,96,768]{3,2,1,0:T(8,128)(2,1)}, u32[]{:S(2)}, u32[]{:S(2)}) collective-permute-start(bf16[2,3,96,768]{3,2,1,0:T(8,128)(2,1)} %pad_maximum_fusion.8), channel_id=1, source_target_pairs={{0,8},{4,12},{8,0},{12,4},{16,24},{20,28},{24,16},{28,20},{1,9},{5... | collective-permute-start | bytes 2654216 | tf_op jit(solution)/shard_map/ppermute | solution.py:544
  68.6 29.2 %collective-permute-start.8 = (bf16[2,3,144,768]{3,2,1,0:T(8,128)(2,1)}, bf16[2,3,144,768]{3,2,1,0:T(8,128)(2,1)}, u32[]{:S(2)}, u32[]{:S(2)}) collective-permute-start(bf16[2,3,144,768]{3,2,1,0:T(8,128)(2,1)} %pad_maximum_fusion.3), channel_id=1, source_target_pairs={{0,16},{4,20},{8,24},{12,28},{16,0},{20,4},{24,8},{28,12},{1,17},{... | collective-permute-start | bytes 3981320 | tf_op jit(solution)/shard_map/ppermute | solution.py:544
  86.3 15.4 %collective-permute-start.5 = (bf16[512,192]{1,0:T(8,128)(2,1)S(1)}, bf16[512,192]{1,0:T(8,128)(2,1)S(1)}, u32[]{:S(2)}, u32[]{:S(2)}) collective-permute-start(bf16[512,192]{1,0:T(8,128)(2,1)S(1)} %get-tuple-element.315), channel_id=1, source_target_pairs={{0,1},{1,2},{2,3},{3,0},{4,5},{5,6},{6,7},{7,4},{8,9},{9,10},{10,1... | collective-permute-start | bytes 589832 | tf_op jit(solution)/shard_map/ppermute | solution.py:540
  92.2 19.3 %collective-permute-start.6 = (bf16[512,192]{1,0:T(8,128)(2,1)S(1)}, bf16[512,192]{1,0:T(8,128)(2,1)S(1)}, u32[]{:S(2)}, u32[]{:S(2)}) collective-permute-start(bf16[512,192]{1,0:T(8,128)(2,1)S(1)} %get-tuple-element.314), channel_id=1, source_target_pairs={{0,2},{1,3},{2,0},{3,1},{4,6},{5,7},{6,4},{7,5},{8,10},{9,11},{10,... | collective-permute-start | bytes 589832 | tf_op jit(solution)/shard_map/ppermute | solution.py:540
  93.4 18.1 %collective-permute-start.7 = (bf16[512,192]{1,0:T(8,128)(2,1)S(1)}, bf16[512,192]{1,0:T(8,128)(2,1)S(1)}, u32[]{:S(2)}, u32[]{:S(2)}) collective-permute-start(bf16[512,192]{1,0:T(8,128)(2,1)S(1)} %get-tuple-element.313), channel_id=1, source_target_pairs={{0,3},{1,0},{2,1},{3,2},{4,7},{5,4},{6,5},{7,6},{8,11},{9,8},{10,9... | collective-permute-start | bytes 589832 | tf_op jit(solution)/shard_map/ppermute | solution.py:540
  112.9 10.8 %collective-permute-start.10 = (bf16[1152,768]{1,0:T(8,128)(2,1)}, bf16[1152,768]{1,0:T(8,128)(2,1)}, u32[]{:S(2)}, u32[]{:S(2)}) collective-permute-start(bf16[1152,768]{1,0:T(8,128)(2,1)} %bitcast.31.refs_11_), channel_id=1, source_target_pairs={{0,4},{4,0},{8,12},{12,8},{16,20},{20,16},{24,28},{28,24},{1,5},{5... | collective-permute-start | bytes 5308424 | tf_op jit(solution)/shard_map/ppermute | solution.py:544
  113.0 10.7 %collective-permute-start.11 = (bf16[1152,768]{1,0:T(8,128)(2,1)}, bf16[1152,768]{1,0:T(8,128)(2,1)}, u32[]{:S(2)}, u32[]{:S(2)}) collective-permute-start(bf16[1152,768]{1,0:T(8,128)(2,1)} %bitcast.32.refs_14_), channel_id=1, source_target_pairs={{0,4},{4,0},{8,12},{12,8},{16,20},{20,16},{24,28},{28,24},{1,5},{5... | collective-permute-start | bytes 5308424 | tf_op jit(solution)/shard_map/ppermute | solution.py:544
  122.5 35.3 %collective-permute-start.15 = (bf16[4,288,768]{2,1,0:T(8,128)(2,1)S(1)}, bf16[4,288,768]{2,1,0:T(8,128)(2,1)S(1)}, u32[]{:S(2)}, u32[]{:S(2)}) collective-permute-start(bf16[4,288,768]{2,1,0:T(8,128)(2,1)S(1)} %bitcast.173), channel_id=1, source_target_pairs={{0,4},{4,0},{8,12},{12,8},{16,20},{20,16},{24,28},{28,24},{1,5},{5... | collective-permute-start | bytes 5308424 | tf_op jit(solution)/shard_map/ppermute | solution.py:544
  161.2 26.4 %collective-permute-start.12 = (bf16[512,192]{1,0:T(8,128)(2,1)}, bf16[512,192]{1,0:T(8,128)(2,1)}, u32[]{:S(2)}, u32[]{:S(2)}) collective-permute-start(bf16[512,192]{1,0:T(8,128)(2,1)} %get-tuple-element.141), channel_id=1, source_target_pairs={{0,3},{1,0},{2,1},{3,2},{4,7},{5,4},{6,5},{7,6},{8,11},{9,8},{10,9... | collective-permute-start | bytes 589832 | tf_op jit(solution)/shard_map/ppermute | solution.py:540
  167.6 24.8 %collective-permute-start.13 = (bf16[512,192]{1,0:T(8,128)(2,1)}, bf16[512,192]{1,0:T(8,128)(2,1)}, u32[]{:S(2)}, u32[]{:S(2)}) collective-permute-start(bf16[512,192]{1,0:T(8,128)(2,1)} %get-tuple-element.142), channel_id=1, source_target_pairs={{0,2},{1,3},{2,0},{3,1},{4,6},{5,7},{6,4},{7,5},{8,10},{9,11},{10,... | collective-permute-start | bytes 589832 | tf_op jit(solution)/shard_map/ppermute | solution.py:540
  168.6 23.8 %collective-permute-start.14 = (bf16[512,192]{1,0:T(8,128)(2,1)}, bf16[512,192]{1,0:T(8,128)(2,1)}, u32[]{:S(2)}, u32[]{:S(2)}) collective-permute-start(bf16[512,192]{1,0:T(8,128)(2,1)} %get-tuple-element.143), channel_id=1, source_target_pairs={{0,1},{1,2},{2,3},{3,0},{4,5},{5,6},{6,7},{7,4},{8,9},{9,10},{10,1... | collective-permute-start | bytes 589832 | tf_op jit(solution)/shard_map/ppermute | solution.py:540
  192.4 42.5 %collective-permute-start.16 = (bf16[4,4,240,768]{3,2,1,0:T(8,128)(2,1)}, bf16[4,4,240,768]{3,2,1,0:T(8,128)(2,1)}, u32[]{:S(2)}, u32[]{:S(2)}) collective-permute-start(bf16[4,4,240,768]{3,2,1,0:T(8,128)(2,1)} %get-tuple-element.171), channel_id=1, source_target_pairs={{0,4},{4,0},{8,12},{12,8},{16,20},{20,16},{24,28},{28,24},{1,5},{5... | collective-permute-start | bytes 17694728 | tf_op jit(solution)/shard_map/ppermute | solution.py:544
  192.4 42.5 %collective-permute-start.17 = (f32[72,128]{1,0:T(8,128)}, f32[72,128]{1,0:T(8,128)}, u32[]{:S(2)}, u32[]{:S(2)}) collective-permute-start(f32[72,128]{1,0:T(8,128)} %maximum_bitcast_fusion.6), channel_id=1, source_target_pairs={{0,4},{4,0},{8,12},{12,8},{16,20},{20,16},{24,28},{28,24},{1,5},{5... | collective-permute-start | bytes 110600 | tf_op jit(solution)/shard_map/ppermute | solution.py:544
  192.9 238.8 %all-gather.7.cloned.1.call-start = ((), (), s32[]{:S(2)}) async-start(), calls=%async_computation.1 | async-start | bytes 3932160 | tf_op jit(solution)/shard_map/all_gather | solution.py:794
  193.0 42.0 %copy-start.33 = (f32[72,128]{1,0:T(8,128)S(1)}, f32[72,128]{1,0:T(8,128)}, u32[]{:S(2)}) copy-start(f32[72,128]{1,0:T(8,128)} %maximum_bitcast_fusion.6) | copy-start | bytes 110596
  236.3 31.1 %collective-permute-start.20 = (f32[72,128]{1,0:T(8,128)}, f32[72,128]{1,0:T(8,128)}, u32[]{:S(2)}, u32[]{:S(2)}) collective-permute-start(f32[72,128]{1,0:T(8,128)} %add.271), channel_id=1, source_target_pairs={{0,8},{4,12},{8,0},{12,4},{16,24},{20,28},{24,16},{28,20},{1,9},{5... | collective-permute-start | bytes 110600 | tf_op jit(solution)/shard_map/ppermute | solution.py:544
  242.6 36.1 %collective-permute-start.19 = (bf16[2,4,112,768]{3,2,1,0:T(8,128)(2,1)}, bf16[2,4,112,768]{3,2,1,0:T(8,128)(2,1)}, u32[]{:S(2)}, u32[]{:S(2)}) collective-permute-start(bf16[2,4,112,768]{3,2,1,0:T(8,128)(2,1)} %get-tuple-element.272), channel_id=1, source_target_pairs={{0,16},{4,20},{8,24},{12,28},{16,0},{20,4},{24,8},{28,12},{1,17},{... | collective-permute-start | bytes 4128776 | tf_op jit(solution)/shard_map/ppermute | solution.py:544
  247.4 36.1 %collective-permute-start.18 = (bf16[2,4,128,768]{3,2,1,0:T(8,128)(2,1)}, bf16[2,4,128,768]{3,2,1,0:T(8,128)(2,1)}, u32[]{:S(2)}, u32[]{:S(2)}) collective-permute-start(bf16[2,4,128,768]{3,2,1,0:T(8,128)(2,1)} %fusion.1), channel_id=1, source_target_pairs={{0,8},{4,12},{8,0},{12,4},{16,24},{20,28},{24,16},{28,20},{1,9},{5... | collective-permute-start | bytes 4718600 | tf_op jit(solution)/shard_map/ppermute | solution.py:544
  249.5 19.4 %collective-permute-start.21 = (bf16[256,1152]{1,0:T(8,128)(2,1)}, bf16[256,1152]{1,0:T(8,128)(2,1)}, u32[]{:S(2)}, u32[]{:S(2)}) collective-permute-start(bf16[256,1152]{1,0:T(8,128)(2,1)} %get-tuple-element.295), channel_id=1, source_target_pairs={{0,1},{1,2},{2,3},{3,0},{4,5},{5,6},{6,7},{7,4},{8,9},{9,10},{10,1... | collective-permute-start | bytes 1769480 | tf_op jit(solution)/shard_map/ppermute | solution.py:540
  249.5 29.2 %collective-permute-start.22 = (bf16[256,1152]{1,0:T(8,128)(2,1)}, bf16[256,1152]{1,0:T(8,128)(2,1)}, u32[]{:S(2)}, u32[]{:S(2)}) collective-permute-start(bf16[256,1152]{1,0:T(8,128)(2,1)} %get-tuple-element.294), channel_id=1, source_target_pairs={{0,3},{1,0},{2,1},{3,2},{4,7},{5,4},{6,5},{7,6},{8,11},{9,8},{10,9... | collective-permute-start | bytes 1769480 | tf_op jit(solution)/shard_map/ppermute | solution.py:540
  284.7 34.7 %collective-permute-start.27 = (bf16[2,2,96,1664]{3,2,1,0:T(8,128)(2,1)}, bf16[2,2,96,1664]{3,2,1,0:T(8,128)(2,1)}, u32[]{:S(2)}, u32[]{:S(2)}) collective-permute-start(bf16[2,2,96,1664]{3,2,1,0:T(8,128)(2,1)} %dynamic-slice_bitcast_fusion), channel_id=1, source_target_pairs={{0,4},{4,0},{8,12},{12,8},{16,20},{20,16},{24,28},{28,24},{1,5},{5... | collective-permute-start | bytes 3833864 | tf_op jit(solution)/shard_map/ppermute | solution.py:544
  287.7 31.6 %collective-permute-start.23 = (bf16[4,128,768]{2,1,0:T(8,128)(2,1)}, bf16[4,128,768]{2,1,0:T(8,128)(2,1)}, u32[]{:S(2)}, u32[]{:S(2)}) collective-permute-start(bf16[4,128,768]{2,1,0:T(8,128)(2,1)} %get-tuple-element.276), channel_id=1, source_target_pairs={{0,16},{4,20},{8,24},{12,28},{16,0},{20,4},{24,8},{28,12},{1,17},{... | collective-permute-start | bytes 2359304 | tf_op jit(solution)/shard_map/ppermute | solution.py:544
  291.1 28.2 %collective-permute-start.24 = (bf16[4,112,768]{2,1,0:T(8,128)(2,1)}, bf16[4,112,768]{2,1,0:T(8,128)(2,1)}, u32[]{:S(2)}, u32[]{:S(2)}) collective-permute-start(bf16[4,112,768]{2,1,0:T(8,128)(2,1)} %get-tuple-element.278), channel_id=1, source_target_pairs={{0,8},{4,12},{8,0},{12,4},{16,24},{20,28},{24,16},{28,20},{1,9},{5... | collective-permute-start | bytes 2064392 | tf_op jit(solution)/shard_map/ppermute | solution.py:544
  291.6 27.7 %collective-permute-start.26 = (bf16[256,1152]{1,0:T(8,128)(2,1)}, bf16[256,1152]{1,0:T(8,128)(2,1)}, u32[]{:S(2)}, u32[]{:S(2)}) collective-permute-start(bf16[256,1152]{1,0:T(8,128)(2,1)} %get-tuple-element.293), channel_id=1, source_target_pairs={{0,2},{1,3},{2,0},{3,1},{4,6},{5,7},{6,4},{7,5},{8,10},{9,11},{10,... | collective-permute-start | bytes 1769480 | tf_op jit(solution)/shard_map/ppermute | solution.py:540
  294.2 25.1 %collective-permute-start.25 = (f32[72,128]{1,0:T(8,128)}, f32[72,128]{1,0:T(8,128)}, u32[]{:S(2)}, u32[]{:S(2)}) collective-permute-start(f32[72,128]{1,0:T(8,128)} %add.279), channel_id=1, source_target_pairs={{0,16},{4,20},{8,24},{12,28},{16,0},{20,4},{24,8},{28,12},{1,17},{... | collective-permute-start | bytes 110600 | tf_op jit(solution)/shard_map/ppermute | solution.py:544
  295.7 26.8 %copy-start.19 = (bf16[4,112,768]{2,1,0:T(8,128)(2,1)S(1)}, bf16[4,112,768]{2,1,0:T(8,128)(2,1)}, u32[]{:S(2)}) copy-start(bf16[4,112,768]{2,1,0:T(8,128)(2,1)} %get-tuple-element.196) | copy-start | bytes 2064388
  320.9 16.4 %collective-permute-start.28 = (bf16[2,96,1664]{2,1,0:T(8,128)(2,1)S(1)}, bf16[2,96,1664]{2,1,0:T(8,128)(2,1)S(1)}, u32[]{:S(2)}, u32[]{:S(2)}) collective-permute-start(bf16[2,96,1664]{2,1,0:T(8,128)(2,1)S(1)} %fusion.14), channel_id=1, source_target_pairs={{0,8},{4,12},{8,0},{12,4},{16,24},{20,28},{24,16},{28,20},{1,9},{5... | collective-permute-start | bytes 1916936 | tf_op jit(solution)/shard_map/ppermute | solution.py:544
  326.3 25.3 %collective-permute-start.31 = (bf16[240,768]{1,0:T(8,128)(2,1)}, bf16[240,768]{1,0:T(8,128)(2,1)}, u32[]{:S(2)}, u32[]{:S(2)}) collective-permute-start(bf16[240,768]{1,0:T(8,128)(2,1)} %get-tuple-element.305), channel_id=1, source_target_pairs={{0,3},{1,0},{2,1},{3,2},{4,7},{5,4},{6,5},{7,6},{8,11},{9,8},{10,9... | collective-permute-start | bytes 1105928 | tf_op jit(solution)/shard_map/ppermute | solution.py:540
  326.8 31.8 %collective-permute-start.32 = (bf16[240,768]{1,0:T(8,128)(2,1)}, bf16[240,768]{1,0:T(8,128)(2,1)}, u32[]{:S(2)}, u32[]{:S(2)}) collective-permute-start(bf16[240,768]{1,0:T(8,128)(2,1)} %get-tuple-element.306), channel_id=1, source_target_pairs={{0,2},{1,3},{2,0},{3,1},{4,6},{5,7},{6,4},{7,5},{8,10},{9,11},{10,... | collective-permute-start | bytes 1105928 | tf_op jit(solution)/shard_map/ppermute | solution.py:540
  326.8 31.8 %collective-permute-start.33 = (bf16[240,768]{1,0:T(8,128)(2,1)}, bf16[240,768]{1,0:T(8,128)(2,1)}, u32[]{:S(2)}, u32[]{:S(2)}) collective-permute-start(bf16[240,768]{1,0:T(8,128)(2,1)} %get-tuple-element.303), channel_id=1, source_target_pairs={{0,1},{1,2},{2,3},{3,0},{4,5},{5,6},{6,7},{7,4},{8,9},{9,10},{10,1... | collective-permute-start | bytes 1105928 | tf_op jit(solution)/shard_map/ppermute | solution.py:540
  330.0 21.6 %collective-permute-start.30 = (f32[72,128]{1,0:T(8,128)}, f32[72,128]{1,0:T(8,128)}, u32[]{:S(2)}, u32[]{:S(2)}) collective-permute-start(f32[72,128]{1,0:T(8,128)} %add.285), channel_id=1, source_target_pairs={{0,1},{1,0},{2,3},{3,2},{4,5},{5,4},{6,7},{7,6},{8,9},{9,8},{10,11... | collective-permute-start | bytes 110600 | tf_op jit(solution)/shard_map/ppermute | solution.py:544
  340.3 9.0 %collective-permute-start.29 = (bf16[96,1664]{1,0:T(8,128)(2,1)}, bf16[96,1664]{1,0:T(8,128)(2,1)}, u32[]{:S(2)}, u32[]{:S(2)}) collective-permute-start(bf16[96,1664]{1,0:T(8,128)(2,1)} %dynamic-slice_bitcast_fusion.1), channel_id=1, source_target_pairs={{0,16},{4,20},{8,24},{12,28},{16,0},{20,4},{24,8},{28,12},{1,17},{... | collective-permute-start | bytes 958472 | tf_op jit(solution)/shard_map/ppermute | solution.py:544
  360.1 12.4 %collective-permute-start.39 = (bf16[240,768]{1,0:T(8,128)(2,1)S(1)}, bf16[240,768]{1,0:T(8,128)(2,1)S(1)}, u32[]{:S(2)}, u32[]{:S(2)}) collective-permute-start(bf16[240,768]{1,0:T(8,128)(2,1)S(1)} %add_convert_fusion.10), channel_id=1, source_target_pairs={{0,24},{4,28},{8,16},{12,20},{16,8},{20,12},{24,0},{28,4},{1,25},{... | collective-permute-start | bytes 1105928 | tf_op jit(solution)/shard_map/ppermute | solution.py:544
  361.4 19.1 %collective-permute-start.40 = (bf16[240,768]{1,0:T(8,128)(2,1)S(1)}, bf16[240,768]{1,0:T(8,128)(2,1)S(1)}, u32[]{:S(2)}, u32[]{:S(2)}) collective-permute-start(bf16[240,768]{1,0:T(8,128)(2,1)S(1)} %add_convert_fusion.10), channel_id=1, source_target_pairs={{0,16},{4,20},{8,24},{12,28},{16,0},{20,4},{24,8},{28,12},{1,17},{... | collective-permute-start | bytes 1105928 | tf_op jit(solution)/shard_map/ppermute | solution.py:544
  362.0 18.5 %collective-permute-start.41 = (bf16[240,768]{1,0:T(8,128)(2,1)S(1)}, bf16[240,768]{1,0:T(8,128)(2,1)S(1)}, u32[]{:S(2)}, u32[]{:S(2)}) collective-permute-start(bf16[240,768]{1,0:T(8,128)(2,1)S(1)} %add_convert_fusion.10), channel_id=1, source_target_pairs={{0,8},{4,12},{8,0},{12,4},{16,24},{20,28},{24,16},{28,20},{1,9},{5... | collective-permute-start | bytes 1105928 | tf_op jit(solution)/shard_map/ppermute | solution.py:544
  363.6 23.8 %collective-permute-start.35 = (bf16[96,1664]{1,0:T(8,128)(2,1)S(1)}, bf16[96,1664]{1,0:T(8,128)(2,1)}, u32[]{:S(2)}, u32[]{:S(2)}) collective-permute-start(bf16[96,1664]{1,0:T(8,128)(2,1)S(1)} %fusion.15), channel_id=1, source_target_pairs={{0,24},{4,28},{8,16},{12,20},{16,8},{20,12},{24,0},{28,4},{1,25},{... | collective-permute-start | bytes 958472 | tf_op jit(solution)/shard_map/ppermute | solution.py:544
  364.9 27.5 %collective-permute-start.36 = (bf16[96,1664]{1,0:T(8,128)(2,1)S(1)}, bf16[96,1664]{1,0:T(8,128)(2,1)}, u32[]{:S(2)}, u32[]{:S(2)}) collective-permute-start(bf16[96,1664]{1,0:T(8,128)(2,1)S(1)} %fusion.15), channel_id=1, source_target_pairs={{0,16},{4,20},{8,24},{12,28},{16,0},{20,4},{24,8},{28,12},{1,17},{... | collective-permute-start | bytes 958472 | tf_op jit(solution)/shard_map/ppermute | solution.py:544
  372.5 19.9 %collective-permute-start.37 = (bf16[96,1664]{1,0:T(8,128)(2,1)S(1)}, bf16[96,1664]{1,0:T(8,128)(2,1)S(1)}, u32[]{:S(2)}, u32[]{:S(2)}) collective-permute-start(bf16[96,1664]{1,0:T(8,128)(2,1)S(1)} %fusion.15), channel_id=1, source_target_pairs={{0,8},{4,12},{8,0},{12,4},{16,24},{20,28},{24,16},{28,20},{1,9},{5... | collective-permute-start | bytes 958472 | tf_op jit(solution)/shard_map/ppermute | solution.py:544
  382.7 29.8 %collective-permute-start.42 = (bf16[2,384,768]{2,1,0:T(8,128)(2,1)}, bf16[2,384,768]{2,1,0:T(8,128)(2,1)}, u32[]{:S(2)}, u32[]{:S(2)}) collective-permute-start(bf16[2,384,768]{2,1,0:T(8,128)(2,1)} %pad_maximum_fusion.7), channel_id=1, source_target_pairs={{0,4},{4,0},{8,12},{12,8},{16,20},{20,16},{24,28},{28,24},{1,5},{5... | collective-permute-start | bytes 3538952 | tf_op jit(solution)/shard_map/ppermute | solution.py:544
  394.8 22.8 %collective-permute-start.38 = (bf16[384,1664]{1,0:T(8,128)(2,1)}, bf16[384,1664]{1,0:T(8,128)(2,1)}, u32[]{:S(2)}, u32[]{:S(2)}) collective-permute-start(bf16[384,1664]{1,0:T(8,128)(2,1)} %pad_maximum_fusion.4), channel_id=1, source_target_pairs={{0,4},{4,0},{8,12},{12,8},{16,20},{20,16},{24,28},{28,24},{1,5},{5... | collective-permute-start | bytes 3833864 | tf_op jit(solution)/shard_map/ppermute | solution.py:544
  395.6 9.7 %collective-permute-start.34 = (f32[72,128]{1,0:T(8,128)S(1)}, f32[72,128]{1,0:T(8,128)S(1)}, u32[]{:S(2)}, u32[]{:S(2)}) collective-permute-start(f32[72,128]{1,0:T(8,128)S(1)} %add.288), channel_id=1, source_target_pairs={{0,2},{1,3},{2,0},{3,1},{4,6},{5,7},{6,4},{7,5},{8,10},{9,11},{10,... | collective-permute-start | bytes 110600 | tf_op jit(solution)/shard_map/ppermute | solution.py:544
  (40 other events, 212.0 us)
Sparse Core Ops, SparseCore 0:
  52.1 45.3 all-gather.8
  193.0 76.6 all-gather.4
  365.6 66.0 all-gather.6

commit v7 on v6

--- a/solution.py
+++ b/solution.py
@@ -746,7 +746,7 @@
         shift(rows_of(gqkv, lax.rem(ti + s, n_t) * pairs, pairs), n_t, s) for s in range(1, n_t)
     ]
     tall = keep.shape[2]
-    mid = -(-tall // 32) * 16
+    mid = tall // 32 * 16
     keep = keep.reshape(lead + keep.shape[1:])
     got = got.reshape(lead + got.shape[1:])
     a_keep, a_send, bit = narrow_pair(keep, got, low_bits, 0, mid)

time: 452 us -> 449 us (level)
  waiting for transfers between devices: 104 us -> 97.1 us
    ppermute x28, waiting for transfers between devices: 41.3 us -> 34.2 us  [swap(): return lax.ppermute(x, axis, [(j, j ^ bit) for j in range(size)])]
  transfers between devices with their start and end apart: 46 -> 46, of which waited for: 19 -> 19; matrix products, arithmetic and copies ran while one was open for 21% -> 21% of each run, Pallas kernels for 33% -> 34%
where the time goes in v7:
time: 449 us; the launch traced here: 442 us
  Pallas kernels  149 us (33%)
  waiting for transfers between devices  97.1 us (22%)
  other arithmetic  74.5 us (17%)
  starting transfers between devices  63.2 us (14%)
  local copies, waits for them, and re-layouts  40.3 us (9%)
  between operations  18.3 us (4%)
    ppermute x15, waiting for transfers between devices, shift(): lax.ppermute(x, 'tensor', [(j, (j + amount) % size) for j in range(size)])  58.4 us
    pallas_call x1, Pallas kernels, attn_bwd(): pl.pallas_call(functools.partial(attn_bwd_kernel, n_t), in_specs=[pl.Bloc...  41.9 us
    ppermute x28, waiting for transfers between devices, swap(): return lax.ppermute(x, axis, [(j, j ^ bit) for j in range(size)])  34.2 us
    pallas_call x1, Pallas kernels, ffn(): pl.pallas_call(functools.partial(ffn_kernel, n_t, slab), in_specs=[sm] +...  34 us
    ppermute x15, starting transfers between devices, shift(): lax.ppermute(x, 'tensor', [(j, (j + amount) % size) for j in range(size)])  32.6 us
    pallas_call x3, Pallas kernels, attn_fwd(): pl.pallas_call(functools.partial(attn_fwd_kernel, lo, len(prev)), grid=(h...  30.8 us
    ppermute x28, starting transfers between devices, swap(): return lax.ppermute(x, axis, [(j, j ^ bit) for j in range(size)])  30.5 us
    reshape x6, other arithmetic, half(): return (part(x) + part(y)).astype(BF16).reshape(sizes[:ax] + sizes[ax + 1:])  18 us
  transfers between devices with their start and end apart: 46, of which 19 were waited for; matrix products, arithmetic and copies ran while one was open for 21% of the time, Pallas kernels for 34%

profile of v7, /device:TPU:0, one launch (start us, length us, event | category | flops | bytes accessed | tf_op | source)
XLA Modules:
  0.0 441.9 jit_solution(4507779655357528811)
XLA Ops:
  11.4 3.1 collective-permute-start
  14.5 2.6 collective-permute-start.1
  20.7 15.0 %attn_prep.1 = (bf16[3,2048,64]{2,1,0:T(8,128)(2,1)}, bf16[3,2048,64]{2,1,0:T(8,128)(2,1)}, bf16[3,2048,64]{2,1,0:T(8,128)(2,1)}, bf16[192,2048]{1,0:T(8,128)(2,...) custom-call(bf16[2048,768]{1,0:T(8,128)(2,1)} %hid.3, ...), custom_call_target="tpu_custom_call" | custom-call | flops 15000000512 | bytes 20971520 | tf_op jit(solution)/shard_map/attn_prep/pallas_call | solution.py:75
  36.5 9.5 %attn_fwd.3 = (bf16[2048,192]{1,0:T(8,128)(2,1)}, f32[192,2048]{1,0:T(8,128)}, f32[8,2048]{1,0:T(8,128)}) custom-call(bf16[192,2048]{1,0:T(8,128)(2,1)} %get-tuple-element.111.qt.refs_8_, bf16[3,2048,64]{2,1,0:T(8,128)(2,1)} %get-tuple-element.112.k3.refs_6_, bf16[192,2048]{1,0:T(8,128)(2,1)} %get-tuple-element.113.vt, ...), custom_call_target="tpu_custom_call" | custom-call | flops 3000000000 | bytes 8388608 | tf_op jit(solution)/shard_map/attn_fwd/pallas_call | solution.py:148
  52.0 9.6 %attn_fwd.4 = (bf16[2048,192]{1,0:T(8,128)(2,1)}, f32[192,2048]{1,0:T(8,128)}, f32[8,2048]{1,0:T(8,128)}) custom-call(bf16[192,2048]{1,0:T(8,128)(2,1)} %get-tuple-element.111.qt.refs_8_, bf16[3,2048,64]{2,1,0:T(8,128)(2,1)} %get-tuple-element.112.k3.refs_6_, ...), custom_call_target="tpu_custom_call", output_to_operand_aliasing={{0}: (4, {}), {1}: (5, {}), {2}: (6, {})} | custom-call | flops 3750000128 | bytes 8388608 | tf_op jit(solution)/shard_map/attn_fwd/pallas_call | solution.py:148
  61.6 2.1 collective-permute-done.3
  72.6 11.7 %attn_fwd.5 = (bf16[2048,192]{1,0:T(8,128)(2,1)}, f32[192,2048]{1,0:T(8,128)}, f32[8,2048]{1,0:T(8,128)}) custom-call(bf16[192,2048]{1,0:T(8,128)(2,1)} %get-tuple-element.111.qt.refs_8_, bf16[3,2048,64]{2,1,0:T(8,128)(2,1)} %get-tuple-element.112.k3.refs_6_, ...), custom_call_target="tpu_custom_call", output_to_operand_aliasing={{0}: (4, {}), {1}: (5, {}), {2}: (6, {})} | custom-call | flops 5249999872 | bytes 8388608 | tf_op jit(solution)/shard_map/attn_fwd/pallas_call | solution.py:148
  84.3 2.0 constant_dynamic-slice_fusion.9
  86.3 6.0 %collective-permute-start.5 = (bf16[512,192]{1,0:T(8,128)(2,1)S(1)}, bf16[512,192]{1,0:T(8,128)(2,1)S(1)}, u32[]{:S(2)}, u32[]{:S(2)}) collective-permute-start(bf16[512,192]{1,0:T(8,128)(2,1)S(1)} %get-tuple-element.315), channel_id=1, source_target_pairs={{0,1},{1,2},{2,3},{3,0},{4,5},{5,6},{6,7},{7,4},{8,9},{9,10},{10,1... | collective-permute-start | bytes 589832 | tf_op jit(solution)/shard_map/ppermute | solution.py:540
  99.6 2.0 collective-permute-done.5.refs_1_
  101.7 9.9 %collective-permute-done.6.refs_2_ = bf16[512,192]{1,0:T(8,128)(2,1)S(1)} collective-permute-done((bf16[512,192]{1,0:T(8,128)(2,1)S(1)}, bf16[512,192]{1,0:T(8,128)(2,1)S(1)}, u32[]{:S(2)}, u32[]{:S(2)}) %collective-permute-start.6) | collective-permute-done | bytes 196640 | tf_op jit(solution)/shard_map/ppermute | solution.py:540
  113.6 2.1 constant_dynamic-slice_fusion.8.refs_5_
  115.7 2.7 constant_dynamic-slice_fusion.7.refs_6_
  123.7 34.0 %ffn.1 = (f32[512,768]{1,0:T(8,128)}, bf16[512,768]{1,0:T(8,128)(2,1)}, bf16[512,3072]{1,0:T(8,128)(2,1)}, bf16[512,3072]{1,0:T(8,128)(2,1)}, bf16[512,768]{1,0:...) custom-call(s32[1]{0:T(128)} %bitcast.core, ...), custom_call_target="tpu_custom_call" | custom-call | flops 33999998976 | bytes 26214400 | tf_op jit(solution)/shard_map/ffn/pallas_call | solution.py:510
  161.2 6.4 %collective-permute-start.12 = (bf16[512,192]{1,0:T(8,128)(2,1)}, bf16[512,192]{1,0:T(8,128)(2,1)}, u32[]{:S(2)}, u32[]{:S(2)}) collective-permute-start(bf16[512,192]{1,0:T(8,128)(2,1)} %get-tuple-element.141), channel_id=1, source_target_pairs={{0,3},{1,0},{2,1},{3,2},{4,7},{5,4},{6,5},{7,6},{8,11},{9,8},{10,9... | collective-permute-start | bytes 589832 | tf_op jit(solution)/shard_map/ppermute | solution.py:540
  169.5 4.2 broadcast_select_fusion.1
  177.1 10.2 %wgrad.1 = (bf16[4,4,240,768]{3,2,1,0:T(8,128)(2,1)}, bf16[4,4,240,768]{3,2,1,0:T(8,128)(2,1)}) custom-call(bf16[512,3072]{1,0:T(8,128)(2,1)S(1)} %copy-done.10, bf16[512,768]{1,0:T(8,128)(2,1)S(1)} %copy-done.11, bf16[512,3072]{1,0:T(8,128)(2,1)S(1)} %copy-done.9, bf16[512,768]{1,0:T(8,128)(2,1)S(1)} %copy-done.12, bf16[512,768]{1,0:T(8,128)(2,1)S(1)} %copy-done.13, ...), custom_call_target="tpu_custom_call" | custom-call | flops 399999991808 | bytes 10485760 | tf_op jit(solution)/shard_map/wgrad/pallas_call | solution.py:312
  187.6 4.8 %collective-permute-done.13.refs_2_ = bf16[512,192]{1,0:T(8,128)(2,1)} collective-permute-done((bf16[512,192]{1,0:T(8,128)(2,1)}, bf16[512,192]{1,0:T(8,128)(2,1)}, u32[]{:S(2)}, u32[]{:S(2)}) %collective-permute-start.13) | collective-permute-done | bytes 196640 | tf_op jit(solution)/shard_map/ppermute | solution.py:540
  193.0 41.9 %attn_bwd.1 = (bf16[1024,1152]{1,0:T(8,128)(2,1)}, f32[3,512,512]{2,1,0:T(8,128)}) custom-call(s32[1]{0:T(128)} %bitcast.40.place, bf16[512,192]{1,0:T(8,128)(2,1)} %get-tuple-element.159.refs_0_, bf16[512,192]{1,0:T(8,128)(2,1)} %collective-permute-done.12.refs_1_, bf16[512,192]{1,0:T(8,128)(2,1)} %collective-permute-done.13.refs_2_, ...), custom_call_target="tpu_custom_call" | custom-call | flops 399999991808 | bytes 20971520 | tf_op jit(solution)/shard_map/attn_bwd/pallas_call | solution.py:252
  237.8 5.5 %fusion.1 = (bf16[2,4,128,768]{3,2,1,0:T(8,128)(2,1)}, bf16[2,4,128,768]{3,2,1,0:T(8,128)(2,1)}) fusion(bf16[2,2,4,240,768]{4,3,2,1,0:T(8,128)(2,1)} %bitcast.42, s32[]{:T(128)S(6)} %select_n.364, bf16[2,2,4,240,768]{4,3,2,1,0:T(8,128)(2,1)} %bitcast.163, s32[]{:T(128)S(6)} %select_n.363), kind=kLoop, calls=%fused_computation.24 | loop fusion | flops 6291456 | bytes 9437192 | tf_op jit(solution)/shard_map/reshape | solution.py:614
  244.7 3.2 fusion.3
  249.9 3.8 collective-permute-start.22
  253.7 11.7 %tail.1 = bf16[768,1664]{1,0:T(8,128)(2,1)} custom-call(bf16[2048,768]{1,0:T(8,128)(2,1)} %hid.3, bf16[1024,1152]{1,0:T(8,128)(2,1)} %get-tuple-element.173.gqkv, f32[3,512,512]{2,1,0:T(8,128)} %get-tuple-element.174.glm, f32[3,512,512]{2,1,0:T(8,128)} %table.3, f32[3,512,512]{2,1,0:T(8,128)} %noise.3), custom_call_target="tpu_custom_call" | custom-call | flops 399999991808 | bytes 20971520 | tf_op jit(solution)/shard_map/tail/pallas_call | solution.py:363
  265.4 2.2 fusion.2
  268.9 9.9 %collective-permute-done.22.refs_3_ = bf16[256,1152]{1,0:T(8,128)(2,1)} collective-permute-done((bf16[256,1152]{1,0:T(8,128)(2,1)}, bf16[256,1152]{1,0:T(8,128)(2,1)}, u32[]{:S(2)}, u32[]{:S(2)}) %collective-permute-start.22) | collective-permute-done | bytes 589856 | tf_op jit(solution)/shard_map/ppermute | solution.py:540
  280.9 2.9 fusion.9
  284.4 2.7 fusion.12
  288.4 2.9 collective-permute-start.26
  293.3 24.4 %collective-permute-done.26.refs_2_ = bf16[256,1152]{1,0:T(8,128)(2,1)} collective-permute-done((bf16[256,1152]{1,0:T(8,128)(2,1)}, bf16[256,1152]{1,0:T(8,128)(2,1)}, u32[]{:S(2)}, u32[]{:S(2)}) %collective-permute-start.26) | collective-permute-done | bytes 589856 | tf_op jit(solution)/shard_map/ppermute | solution.py:540
  324.3 2.1 collective-permute-start.31
  328.5 2.8 collective-permute-start.30
  331.3 3.6 collective-permute-done.28
  338.4 4.9 %back.1 = bf16[512,768]{1,0:T(8,128)(2,1)} custom-call(s32[1]{0:T(128)} %bitcast.40.place, bf16[4,576,768]{2,1,0:T(8,128)(2,1)S(1)} %pad_maximum_fusion.w, f32[512,768]{1,0:T(8,128)S(1)} %copy-done.8, bf16[256,1152]{1,0:T(8,128)(2,1)S(1)} %copy-done, bf16[256,1152]{1,0:T(8,128)(2,1)} %collective-permute-done.21.refs_1_, ...), custom_call_target="tpu_custom_call" | custom-call | flops 5000000000 | bytes 10485760 | tf_op jit(solution)/shard_map/back/pallas_call | solution.py:389
  343.3 3.1 collective-permute-done.29
  347.5 2.7 collective-permute-done.30
  350.2 6.1 %collective-permute-done.32 = bf16[240,768]{1,0:T(8,128)(2,1)} collective-permute-done((bf16[240,768]{1,0:T(8,128)(2,1)}, bf16[240,768]{1,0:T(8,128)(2,1)}, u32[]{:S(2)}, u32[]{:S(2)}) %collective-permute-start.32) | collective-permute-done | bytes 368672 | tf_op jit(solution)/shard_map/ppermute | solution.py:540
  364.4 5.9 %collective-permute-done.39 = bf16[240,768]{1,0:T(8,128)(2,1)S(1)} collective-permute-done((bf16[240,768]{1,0:T(8,128)(2,1)S(1)}, bf16[240,768]{1,0:T(8,128)(2,1)S(1)}, u32[]{:S(2)}, u32[]{:S(2)}) %collective-permute-start.39) | collective-permute-done | bytes 368672 | tf_op jit(solution)/shard_map/ppermute | solution.py:544
  371.8 6.5 %collective-permute-done.40 = bf16[240,768]{1,0:T(8,128)(2,1)S(1)} collective-permute-done((bf16[240,768]{1,0:T(8,128)(2,1)S(1)}, bf16[240,768]{1,0:T(8,128)(2,1)S(1)}, u32[]{:S(2)}, u32[]{:S(2)}) %collective-permute-start.40) | collective-permute-done | bytes 368672 | tf_op jit(solution)/shard_map/ppermute | solution.py:544
  380.4 4.7 %collective-permute-done.35 = bf16[96,1664]{1,0:T(8,128)(2,1)} collective-permute-done((bf16[96,1664]{1,0:T(8,128)(2,1)S(1)}, bf16[96,1664]{1,0:T(8,128)(2,1)}, u32[]{:S(2)}, u32[]{:S(2)}) %collective-permute-start.35) | collective-permute-done | bytes 319520 | tf_op jit(solution)/shard_map/ppermute | solution.py:544
  385.1 3.8 collective-permute-done.36
  392.2 4.8 %collective-permute-start.34 = (f32[72,128]{1,0:T(8,128)S(1)}, f32[72,128]{1,0:T(8,128)S(1)}, u32[]{:S(2)}, u32[]{:S(2)}) collective-permute-start(f32[72,128]{1,0:T(8,128)S(1)} %add.288), channel_id=1, source_target_pairs={{0,2},{1,3},{2,0},{3,1},{4,6},{5,7},{6,4},{7,5},{8,10},{9,11},{10,... | collective-permute-start | bytes 110600 | tf_op jit(solution)/shard_map/ppermute | solution.py:544
  397.0 5.1 %convert_element_type.244 = f32[2048,768]{1,0:T(8,128)} convert(bf16[2048,768]{1,0:T(8,128)(2,1)} %all-gather.5.cloned.1.call-done) | non-fusion elementwise | flops 1572864 | bytes 9437184 | tf_op jit(solution)/shard_map/convert_element_type | solution.py:819
  412.7 1.9 copy.104
  414.7 1.8 broadcast_select_fusion.3
  418.7 2.9 copy.103
  421.7 2.1 convert_multiply_fusion.1
  424.4 4.4 all-gather.7.cloned.1.call-done
  428.8 5.0 %convert_multiply_fusion = f32[2048,768]{1,0:T(8,128)} fusion(bf16[2048,768]{1,0:T(8,128)(2,1)} %all-gather.7.cloned.1.call-done, f32[]{:T(128)} %bitcast.65), kind=kLoop, calls=%fused_computation.1 | loop fusion | flops 3145728 | bytes 9437188 | tf_op jit(solution)/shard_map/mul | solution.py:833
  (264 shorter events, 100.3 us)
Async XLA Ops:
  7.2 104.3 %all-gather.9.cloned.1.call-start = ((), (), s32[]{:S(2)}) async-start(), calls=%async_computation.2 | async-start | bytes 2211840 | tf_op jit(solution)/shard_map/all_gather | solution.py:678
  11.4 34.6 %collective-permute-start = (bf16[256,768]{1,0:T(8,128)(2,1)S(1)}, bf16[256,768]{1,0:T(8,128)(2,1)}, u32[]{:S(2)}, u32[]{:S(2)}) collective-permute-start(bf16[256,768]{1,0:T(8,128)(2,1)S(1)} %concatenate.53), channel_id=1, source_target_pairs={{0,1},{1,2},{2,3},{3,0},{4,5},{5,6},{6,7},{7,4},{8,9},{9,10},{10,1... | collective-permute-start | bytes 1179656 | tf_op jit(solution)/shard_map/ppermute | solution.py:540
  14.5 31.5 %collective-permute-start.1 = (bf16[256,768]{1,0:T(8,128)(2,1)S(1)}, bf16[256,768]{1,0:T(8,128)(2,1)S(1)}, u32[]{:S(2)}, u32[]{:S(2)}) collective-permute-start(bf16[256,768]{1,0:T(8,128)(2,1)S(1)} %concatenate.53), channel_id=1, source_target_pairs={{0,2},{1,3},{2,0},{3,1},{4,6},{5,7},{6,4},{7,5},{8,10},{9,11},{10,... | collective-permute-start | bytes 1179656 | tf_op jit(solution)/shard_map/ppermute | solution.py:540
  17.1 28.9 %collective-permute-start.2 = (bf16[256,768]{1,0:T(8,128)(2,1)S(1)}, bf16[256,768]{1,0:T(8,128)(2,1)S(1)}, u32[]{:S(2)}, u32[]{:S(2)}) collective-permute-start(bf16[256,768]{1,0:T(8,128)(2,1)S(1)} %concatenate.53), channel_id=1, source_target_pairs={{0,3},{1,0},{2,1},{3,2},{4,7},{5,4},{6,5},{7,6},{8,11},{9,8},{10,9... | collective-permute-start | bytes 1179656 | tf_op jit(solution)/shard_map/ppermute | solution.py:540
  47.8 15.9 %collective-permute-start.3 = (bf16[3,144,768]{2,1,0:T(8,128)(2,1)S(1)}, bf16[3,144,768]{2,1,0:T(8,128)(2,1)S(1)}, u32[]{:S(2)}, u32[]{:S(2)}) collective-permute-start(bf16[3,144,768]{2,1,0:T(8,128)(2,1)S(1)} %pad_maximum_fusion.10), channel_id=1, source_target_pairs={{0,8},{4,12},{8,0},{12,4},{16,24},{20,28},{24,16},{28,20},{1,9},{5... | collective-permute-start | bytes 1990664 | tf_op jit(solution)/shard_map/ppermute | solution.py:544
  50.4 11.3 %collective-permute-start.4 = (bf16[3,96,768]{2,1,0:T(8,128)(2,1)S(1)}, bf16[3,96,768]{2,1,0:T(8,128)(2,1)S(1)}, u32[]{:S(2)}, u32[]{:S(2)}) collective-permute-start(bf16[3,96,768]{2,1,0:T(8,128)(2,1)S(1)} %pad_maximum_fusion.11), channel_id=1, source_target_pairs={{0,16},{4,20},{8,24},{12,28},{16,0},{20,4},{24,8},{28,12},{1,17},{... | collective-permute-start | bytes 1327112 | tf_op jit(solution)/shard_map/ppermute | solution.py:544
  52.0 345.0 %all-gather.5.cloned.1.call-start = ((), (), s32[]{:S(2)}) async-start(), calls=%async_computation | async-start | bytes 3932160 | tf_op jit(solution)/shard_map/all_gather | solution.py:738
  65.8 29.0 %collective-permute-start.9 = (bf16[2,3,96,768]{3,2,1,0:T(8,128)(2,1)}, bf16[2,3,96,768]{3,2,1,0:T(8,128)(2,1)}, u32[]{:S(2)}, u32[]{:S(2)}) collective-permute-start(bf16[2,3,96,768]{3,2,1,0:T(8,128)(2,1)} %pad_maximum_fusion.8), channel_id=1, source_target_pairs={{0,8},{4,12},{8,0},{12,4},{16,24},{20,28},{24,16},{28,20},{1,9},{5... | collective-permute-start | bytes 2654216 | tf_op jit(solution)/shard_map/ppermute | solution.py:544
  68.6 29.2 %collective-permute-start.8 = (bf16[2,3,144,768]{3,2,1,0:T(8,128)(2,1)}, bf16[2,3,144,768]{3,2,1,0:T(8,128)(2,1)}, u32[]{:S(2)}, u32[]{:S(2)}) collective-permute-start(bf16[2,3,144,768]{3,2,1,0:T(8,128)(2,1)} %pad_maximum_fusion.3), channel_id=1, source_target_pairs={{0,16},{4,20},{8,24},{12,28},{16,0},{20,4},{24,8},{28,12},{1,17},{... | collective-permute-start | bytes 3981320 | tf_op jit(solution)/shard_map/ppermute | solution.py:544
  86.3 15.4 %collective-permute-start.5 = (bf16[512,192]{1,0:T(8,128)(2,1)S(1)}, bf16[512,192]{1,0:T(8,128)(2,1)S(1)}, u32[]{:S(2)}, u32[]{:S(2)}) collective-permute-start(bf16[512,192]{1,0:T(8,128)(2,1)S(1)} %get-tuple-element.315), channel_id=1, source_target_pairs={{0,1},{1,2},{2,3},{3,0},{4,5},{5,6},{6,7},{7,4},{8,9},{9,10},{10,1... | collective-permute-start | bytes 589832 | tf_op jit(solution)/shard_map/ppermute | solution.py:540
  92.2 19.3 %collective-permute-start.6 = (bf16[512,192]{1,0:T(8,128)(2,1)S(1)}, bf16[512,192]{1,0:T(8,128)(2,1)S(1)}, u32[]{:S(2)}, u32[]{:S(2)}) collective-permute-start(bf16[512,192]{1,0:T(8,128)(2,1)S(1)} %get-tuple-element.314), channel_id=1, source_target_pairs={{0,2},{1,3},{2,0},{3,1},{4,6},{5,7},{6,4},{7,5},{8,10},{9,11},{10,... | collective-permute-start | bytes 589832 | tf_op jit(solution)/shard_map/ppermute | solution.py:540
  93.4 18.1 %collective-permute-start.7 = (bf16[512,192]{1,0:T(8,128)(2,1)S(1)}, bf16[512,192]{1,0:T(8,128)(2,1)S(1)}, u32[]{:S(2)}, u32[]{:S(2)}) collective-permute-start(bf16[512,192]{1,0:T(8,128)(2,1)S(1)} %get-tuple-element.313), channel_id=1, source_target_pairs={{0,3},{1,0},{2,1},{3,2},{4,7},{5,4},{6,5},{7,6},{8,11},{9,8},{10,9... | collective-permute-start | bytes 589832 | tf_op jit(solution)/shard_map/ppermute | solution.py:540
  112.9 10.8 %collective-permute-start.10 = (bf16[1152,768]{1,0:T(8,128)(2,1)}, bf16[1152,768]{1,0:T(8,128)(2,1)}, u32[]{:S(2)}, u32[]{:S(2)}) collective-permute-start(bf16[1152,768]{1,0:T(8,128)(2,1)} %bitcast.31.refs_11_), channel_id=1, source_target_pairs={{0,4},{4,0},{8,12},{12,8},{16,20},{20,16},{24,28},{28,24},{1,5},{5... | collective-permute-start | bytes 5308424 | tf_op jit(solution)/shard_map/ppermute | solution.py:544
  113.0 10.7 %collective-permute-start.11 = (bf16[1152,768]{1,0:T(8,128)(2,1)}, bf16[1152,768]{1,0:T(8,128)(2,1)}, u32[]{:S(2)}, u32[]{:S(2)}) collective-permute-start(bf16[1152,768]{1,0:T(8,128)(2,1)} %bitcast.32.refs_14_), channel_id=1, source_target_pairs={{0,4},{4,0},{8,12},{12,8},{16,20},{20,16},{24,28},{28,24},{1,5},{5... | collective-permute-start | bytes 5308424 | tf_op jit(solution)/shard_map/ppermute | solution.py:544
  122.5 35.3 %collective-permute-start.15 = (bf16[4,288,768]{2,1,0:T(8,128)(2,1)S(1)}, bf16[4,288,768]{2,1,0:T(8,128)(2,1)S(1)}, u32[]{:S(2)}, u32[]{:S(2)}) collective-permute-start(bf16[4,288,768]{2,1,0:T(8,128)(2,1)S(1)} %bitcast.173), channel_id=1, source_target_pairs={{0,4},{4,0},{8,12},{12,8},{16,20},{20,16},{24,28},{28,24},{1,5},{5... | collective-permute-start | bytes 5308424 | tf_op jit(solution)/shard_map/ppermute | solution.py:544
  161.2 26.4 %collective-permute-start.12 = (bf16[512,192]{1,0:T(8,128)(2,1)}, bf16[512,192]{1,0:T(8,128)(2,1)}, u32[]{:S(2)}, u32[]{:S(2)}) collective-permute-start(bf16[512,192]{1,0:T(8,128)(2,1)} %get-tuple-element.141), channel_id=1, source_target_pairs={{0,3},{1,0},{2,1},{3,2},{4,7},{5,4},{6,5},{7,6},{8,11},{9,8},{10,9... | collective-permute-start | bytes 589832 | tf_op jit(solution)/shard_map/ppermute | solution.py:540
  167.6 24.8 %collective-permute-start.13 = (bf16[512,192]{1,0:T(8,128)(2,1)}, bf16[512,192]{1,0:T(8,128)(2,1)}, u32[]{:S(2)}, u32[]{:S(2)}) collective-permute-start(bf16[512,192]{1,0:T(8,128)(2,1)} %get-tuple-element.142), channel_id=1, source_target_pairs={{0,2},{1,3},{2,0},{3,1},{4,6},{5,7},{6,4},{7,5},{8,10},{9,11},{10,... | collective-permute-start | bytes 589832 | tf_op jit(solution)/shard_map/ppermute | solution.py:540
  168.6 23.8 %collective-permute-start.14 = (bf16[512,192]{1,0:T(8,128)(2,1)}, bf16[512,192]{1,0:T(8,128)(2,1)}, u32[]{:S(2)}, u32[]{:S(2)}) collective-permute-start(bf16[512,192]{1,0:T(8,128)(2,1)} %get-tuple-element.143), channel_id=1, source_target_pairs={{0,1},{1,2},{2,3},{3,0},{4,5},{5,6},{6,7},{7,4},{8,9},{9,10},{10,1... | collective-permute-start | bytes 589832 | tf_op jit(solution)/shard_map/ppermute | solution.py:540
  192.4 42.5 %collective-permute-start.16 = (bf16[4,4,240,768]{3,2,1,0:T(8,128)(2,1)}, bf16[4,4,240,768]{3,2,1,0:T(8,128)(2,1)}, u32[]{:S(2)}, u32[]{:S(2)}) collective-permute-start(bf16[4,4,240,768]{3,2,1,0:T(8,128)(2,1)} %get-tuple-element.171), channel_id=1, source_target_pairs={{0,4},{4,0},{8,12},{12,8},{16,20},{20,16},{24,28},{28,24},{1,5},{5... | collective-permute-start | bytes 17694728 | tf_op jit(solution)/shard_map/ppermute | solution.py:544
  192.4 42.5 %collective-permute-start.17 = (f32[72,128]{1,0:T(8,128)}, f32[72,128]{1,0:T(8,128)}, u32[]{:S(2)}, u32[]{:S(2)}) collective-permute-start(f32[72,128]{1,0:T(8,128)} %maximum_bitcast_fusion.6), channel_id=1, source_target_pairs={{0,4},{4,0},{8,12},{12,8},{16,20},{20,16},{24,28},{28,24},{1,5},{5... | collective-permute-start | bytes 110600 | tf_op jit(solution)/shard_map/ppermute | solution.py:544
  192.9 235.9 %all-gather.7.cloned.1.call-start = ((), (), s32[]{:S(2)}) async-start(), calls=%async_computation.1 | async-start | bytes 3932160 | tf_op jit(solution)/shard_map/all_gather | solution.py:794
  193.0 42.0 %copy-start.33 = (f32[72,128]{1,0:T(8,128)S(1)}, f32[72,128]{1,0:T(8,128)}, u32[]{:S(2)}) copy-start(f32[72,128]{1,0:T(8,128)} %maximum_bitcast_fusion.6) | copy-start | bytes 110596
  236.3 31.3 %collective-permute-start.20 = (f32[72,128]{1,0:T(8,128)}, f32[72,128]{1,0:T(8,128)}, u32[]{:S(2)}, u32[]{:S(2)}) collective-permute-start(f32[72,128]{1,0:T(8,128)} %add.271), channel_id=1, source_target_pairs={{0,8},{4,12},{8,0},{12,4},{16,24},{20,28},{24,16},{28,20},{1,9},{5... | collective-permute-start | bytes 110600 | tf_op jit(solution)/shard_map/ppermute | solution.py:544
  243.3 36.5 %collective-permute-start.19 = (bf16[2,4,128,768]{3,2,1,0:T(8,128)(2,1)}, bf16[2,4,128,768]{3,2,1,0:T(8,128)(2,1)}, u32[]{:S(2)}, u32[]{:S(2)}) collective-permute-start(bf16[2,4,128,768]{3,2,1,0:T(8,128)(2,1)} %get-tuple-element.272), channel_id=1, source_target_pairs={{0,16},{4,20},{8,24},{12,28},{16,0},{20,4},{24,8},{28,12},{1,17},{... | collective-permute-start | bytes 4718600 | tf_op jit(solution)/shard_map/ppermute | solution.py:544
  247.9 31.9 %collective-permute-start.18 = (bf16[2,4,112,768]{3,2,1,0:T(8,128)(2,1)}, bf16[2,4,112,768]{3,2,1,0:T(8,128)(2,1)}, u32[]{:S(2)}, u32[]{:S(2)}) collective-permute-start(bf16[2,4,112,768]{3,2,1,0:T(8,128)(2,1)} %fusion.3), channel_id=1, source_target_pairs={{0,8},{4,12},{8,0},{12,4},{16,24},{20,28},{24,16},{28,20},{1,9},{5... | collective-permute-start | bytes 4128776 | tf_op jit(solution)/shard_map/ppermute | solution.py:544
  249.9 19.0 %collective-permute-start.21 = (bf16[256,1152]{1,0:T(8,128)(2,1)}, bf16[256,1152]{1,0:T(8,128)(2,1)}, u32[]{:S(2)}, u32[]{:S(2)}) collective-permute-start(bf16[256,1152]{1,0:T(8,128)(2,1)} %get-tuple-element.295), channel_id=1, source_target_pairs={{0,1},{1,2},{2,3},{3,0},{4,5},{5,6},{6,7},{7,4},{8,9},{9,10},{10,1... | collective-permute-start | bytes 1769480 | tf_op jit(solution)/shard_map/ppermute | solution.py:540
  249.9 28.9 %collective-permute-start.22 = (bf16[256,1152]{1,0:T(8,128)(2,1)}, bf16[256,1152]{1,0:T(8,128)(2,1)}, u32[]{:S(2)}, u32[]{:S(2)}) collective-permute-start(bf16[256,1152]{1,0:T(8,128)(2,1)} %get-tuple-element.294), channel_id=1, source_target_pairs={{0,3},{1,0},{2,1},{3,2},{4,7},{5,4},{6,5},{7,6},{8,11},{9,8},{10,9... | collective-permute-start | bytes 1769480 | tf_op jit(solution)/shard_map/ppermute | solution.py:540
  280.9 36.9 %collective-permute-start.27 = (bf16[2,2,96,1664]{3,2,1,0:T(8,128)(2,1)}, bf16[2,2,96,1664]{3,2,1,0:T(8,128)(2,1)}, u32[]{:S(2)}, u32[]{:S(2)}) collective-permute-start(bf16[2,2,96,1664]{3,2,1,0:T(8,128)(2,1)} %dynamic-slice_bitcast_fusion), channel_id=1, source_target_pairs={{0,4},{4,0},{8,12},{12,8},{16,20},{20,16},{24,28},{28,24},{1,5},{5... | collective-permute-start | bytes 3833864 | tf_op jit(solution)/shard_map/ppermute | solution.py:544
  283.8 33.9 %collective-permute-start.24 = (bf16[4,128,768]{2,1,0:T(8,128)(2,1)}, bf16[4,128,768]{2,1,0:T(8,128)(2,1)}, u32[]{:S(2)}, u32[]{:S(2)}) collective-permute-start(bf16[4,128,768]{2,1,0:T(8,128)(2,1)} %get-tuple-element.276), channel_id=1, source_target_pairs={{0,8},{4,12},{8,0},{12,4},{16,24},{20,28},{24,16},{28,20},{1,9},{5... | collective-permute-start | bytes 2359304 | tf_op jit(solution)/shard_map/ppermute | solution.py:544
  287.1 30.6 %collective-permute-start.23 = (bf16[4,112,768]{2,1,0:T(8,128)(2,1)}, bf16[4,112,768]{2,1,0:T(8,128)(2,1)}, u32[]{:S(2)}, u32[]{:S(2)}) collective-permute-start(bf16[4,112,768]{2,1,0:T(8,128)(2,1)} %get-tuple-element.278), channel_id=1, source_target_pairs={{0,16},{4,20},{8,24},{12,28},{16,0},{20,4},{24,8},{28,12},{1,17},{... | collective-permute-start | bytes 2064392 | tf_op jit(solution)/shard_map/ppermute | solution.py:544
  288.4 29.3 %collective-permute-start.26 = (bf16[256,1152]{1,0:T(8,128)(2,1)}, bf16[256,1152]{1,0:T(8,128)(2,1)}, u32[]{:S(2)}, u32[]{:S(2)}) collective-permute-start(bf16[256,1152]{1,0:T(8,128)(2,1)} %get-tuple-element.293), channel_id=1, source_target_pairs={{0,2},{1,3},{2,0},{3,1},{4,6},{5,7},{6,4},{7,5},{8,10},{9,11},{10,... | collective-permute-start | bytes 1769480 | tf_op jit(solution)/shard_map/ppermute | solution.py:540
  292.7 25.0 %collective-permute-start.25 = (f32[72,128]{1,0:T(8,128)}, f32[72,128]{1,0:T(8,128)}, u32[]{:S(2)}, u32[]{:S(2)}) collective-permute-start(f32[72,128]{1,0:T(8,128)} %add.279), channel_id=1, source_target_pairs={{0,16},{4,20},{8,24},{12,28},{16,0},{20,4},{24,8},{28,12},{1,17},{... | collective-permute-start | bytes 110600 | tf_op jit(solution)/shard_map/ppermute | solution.py:544
  293.3 27.3 %copy-start.19 = (bf16[4,112,768]{2,1,0:T(8,128)(2,1)S(1)}, bf16[4,112,768]{2,1,0:T(8,128)(2,1)}, u32[]{:S(2)}) copy-start(bf16[4,112,768]{2,1,0:T(8,128)(2,1)} %get-tuple-element.194) | copy-start | bytes 2064388
  319.3 15.7 %collective-permute-start.28 = (bf16[2,96,1664]{2,1,0:T(8,128)(2,1)S(1)}, bf16[2,96,1664]{2,1,0:T(8,128)(2,1)S(1)}, u32[]{:S(2)}, u32[]{:S(2)}) collective-permute-start(bf16[2,96,1664]{2,1,0:T(8,128)(2,1)S(1)} %fusion.14), channel_id=1, source_target_pairs={{0,8},{4,12},{8,0},{12,4},{16,24},{20,28},{24,16},{28,20},{1,9},{5... | collective-permute-start | bytes 1916936 | tf_op jit(solution)/shard_map/ppermute | solution.py:544
  324.3 26.0 %collective-permute-start.31 = (bf16[240,768]{1,0:T(8,128)(2,1)}, bf16[240,768]{1,0:T(8,128)(2,1)}, u32[]{:S(2)}, u32[]{:S(2)}) collective-permute-start(bf16[240,768]{1,0:T(8,128)(2,1)} %get-tuple-element.305), channel_id=1, source_target_pairs={{0,3},{1,0},{2,1},{3,2},{4,7},{5,4},{6,5},{7,6},{8,11},{9,8},{10,9... | collective-permute-start | bytes 1105928 | tf_op jit(solution)/shard_map/ppermute | solution.py:540
  326.4 29.9 %collective-permute-start.32 = (bf16[240,768]{1,0:T(8,128)(2,1)}, bf16[240,768]{1,0:T(8,128)(2,1)}, u32[]{:S(2)}, u32[]{:S(2)}) collective-permute-start(bf16[240,768]{1,0:T(8,128)(2,1)} %get-tuple-element.306), channel_id=1, source_target_pairs={{0,2},{1,3},{2,0},{3,1},{4,6},{5,7},{6,4},{7,5},{8,10},{9,11},{10,... | collective-permute-start | bytes 1105928 | tf_op jit(solution)/shard_map/ppermute | solution.py:540
  326.4 29.9 %collective-permute-start.33 = (bf16[240,768]{1,0:T(8,128)(2,1)}, bf16[240,768]{1,0:T(8,128)(2,1)}, u32[]{:S(2)}, u32[]{:S(2)}) collective-permute-start(bf16[240,768]{1,0:T(8,128)(2,1)} %get-tuple-element.303), channel_id=1, source_target_pairs={{0,1},{1,2},{2,3},{3,0},{4,5},{5,6},{6,7},{7,4},{8,9},{9,10},{10,1... | collective-permute-start | bytes 1105928 | tf_op jit(solution)/shard_map/ppermute | solution.py:540
  328.5 21.8 %collective-permute-start.30 = (f32[72,128]{1,0:T(8,128)}, f32[72,128]{1,0:T(8,128)}, u32[]{:S(2)}, u32[]{:S(2)}) collective-permute-start(f32[72,128]{1,0:T(8,128)} %add.285), channel_id=1, source_target_pairs={{0,1},{1,0},{2,3},{3,2},{4,5},{5,4},{6,7},{7,6},{8,9},{9,8},{10,11... | collective-permute-start | bytes 110600 | tf_op jit(solution)/shard_map/ppermute | solution.py:544
  338.0 8.3 %collective-permute-start.29 = (bf16[96,1664]{1,0:T(8,128)(2,1)}, bf16[96,1664]{1,0:T(8,128)(2,1)}, u32[]{:S(2)}, u32[]{:S(2)}) collective-permute-start(bf16[96,1664]{1,0:T(8,128)(2,1)} %dynamic-slice_bitcast_fusion.1), channel_id=1, source_target_pairs={{0,16},{4,20},{8,24},{12,28},{16,0},{20,4},{24,8},{28,12},{1,17},{... | collective-permute-start | bytes 958472 | tf_op jit(solution)/shard_map/ppermute | solution.py:544
  357.9 12.4 %collective-permute-start.39 = (bf16[240,768]{1,0:T(8,128)(2,1)S(1)}, bf16[240,768]{1,0:T(8,128)(2,1)S(1)}, u32[]{:S(2)}, u32[]{:S(2)}) collective-permute-start(bf16[240,768]{1,0:T(8,128)(2,1)S(1)} %add_convert_fusion.10), channel_id=1, source_target_pairs={{0,24},{4,28},{8,16},{12,20},{16,8},{20,12},{24,0},{28,4},{1,25},{... | collective-permute-start | bytes 1105928 | tf_op jit(solution)/shard_map/ppermute | solution.py:544
  359.4 18.9 %collective-permute-start.40 = (bf16[240,768]{1,0:T(8,128)(2,1)S(1)}, bf16[240,768]{1,0:T(8,128)(2,1)S(1)}, u32[]{:S(2)}, u32[]{:S(2)}) collective-permute-start(bf16[240,768]{1,0:T(8,128)(2,1)S(1)} %add_convert_fusion.10), channel_id=1, source_target_pairs={{0,16},{4,20},{8,24},{12,28},{16,0},{20,4},{24,8},{28,12},{1,17},{... | collective-permute-start | bytes 1105928 | tf_op jit(solution)/shard_map/ppermute | solution.py:544
  360.9 17.4 %collective-permute-start.41 = (bf16[240,768]{1,0:T(8,128)(2,1)S(1)}, bf16[240,768]{1,0:T(8,128)(2,1)S(1)}, u32[]{:S(2)}, u32[]{:S(2)}) collective-permute-start(bf16[240,768]{1,0:T(8,128)(2,1)S(1)} %add_convert_fusion.10), channel_id=1, source_target_pairs={{0,8},{4,12},{8,0},{12,4},{16,24},{20,28},{24,16},{28,20},{1,9},{5... | collective-permute-start | bytes 1105928 | tf_op jit(solution)/shard_map/ppermute | solution.py:544
  361.4 23.7 %collective-permute-start.35 = (bf16[96,1664]{1,0:T(8,128)(2,1)S(1)}, bf16[96,1664]{1,0:T(8,128)(2,1)}, u32[]{:S(2)}, u32[]{:S(2)}) collective-permute-start(bf16[96,1664]{1,0:T(8,128)(2,1)S(1)} %fusion.15), channel_id=1, source_target_pairs={{0,24},{4,28},{8,16},{12,20},{16,8},{20,12},{24,0},{28,4},{1,25},{... | collective-permute-start | bytes 958472 | tf_op jit(solution)/shard_map/ppermute | solution.py:544
  362.9 26.1 %collective-permute-start.36 = (bf16[96,1664]{1,0:T(8,128)(2,1)S(1)}, bf16[96,1664]{1,0:T(8,128)(2,1)}, u32[]{:S(2)}, u32[]{:S(2)}) collective-permute-start(bf16[96,1664]{1,0:T(8,128)(2,1)S(1)} %fusion.15), channel_id=1, source_target_pairs={{0,16},{4,20},{8,24},{12,28},{16,0},{20,4},{24,8},{28,12},{1,17},{... | collective-permute-start | bytes 958472 | tf_op jit(solution)/shard_map/ppermute | solution.py:544
  370.3 18.7 %collective-permute-start.37 = (bf16[96,1664]{1,0:T(8,128)(2,1)S(1)}, bf16[96,1664]{1,0:T(8,128)(2,1)S(1)}, u32[]{:S(2)}, u32[]{:S(2)}) collective-permute-start(bf16[96,1664]{1,0:T(8,128)(2,1)S(1)} %fusion.15), channel_id=1, source_target_pairs={{0,8},{4,12},{8,0},{12,4},{16,24},{20,28},{24,16},{28,20},{1,9},{5... | collective-permute-start | bytes 958472 | tf_op jit(solution)/shard_map/ppermute | solution.py:544
  380.4 29.1 %collective-permute-start.42 = (bf16[2,384,768]{2,1,0:T(8,128)(2,1)}, bf16[2,384,768]{2,1,0:T(8,128)(2,1)}, u32[]{:S(2)}, u32[]{:S(2)}) collective-permute-start(bf16[2,384,768]{2,1,0:T(8,128)(2,1)} %pad_maximum_fusion.7), channel_id=1, source_target_pairs={{0,4},{4,0},{8,12},{12,8},{16,20},{20,16},{24,28},{28,24},{1,5},{5... | collective-permute-start | bytes 3538952 | tf_op jit(solution)/shard_map/ppermute | solution.py:544
  391.4 23.3 %collective-permute-start.38 = (bf16[384,1664]{1,0:T(8,128)(2,1)}, bf16[384,1664]{1,0:T(8,128)(2,1)}, u32[]{:S(2)}, u32[]{:S(2)}) collective-permute-start(bf16[384,1664]{1,0:T(8,128)(2,1)} %pad_maximum_fusion.4), channel_id=1, source_target_pairs={{0,4},{4,0},{8,12},{12,8},{16,20},{20,16},{24,28},{28,24},{1,5},{5... | collective-permute-start | bytes 3833864 | tf_op jit(solution)/shard_map/ppermute | solution.py:544
  392.2 10.2 %collective-permute-start.34 = (f32[72,128]{1,0:T(8,128)S(1)}, f32[72,128]{1,0:T(8,128)S(1)}, u32[]{:S(2)}, u32[]{:S(2)}) collective-permute-start(f32[72,128]{1,0:T(8,128)S(1)} %add.288), channel_id=1, source_target_pairs={{0,2},{1,3},{2,0},{3,1},{4,6},{5,7},{6,4},{7,5},{8,10},{9,11},{10,... | collective-permute-start | bytes 110600 | tf_op jit(solution)/shard_map/ppermute | solution.py:544
  (40 other events, 213.3 us)
Sparse Core Ops, SparseCore 0:
  52.1 45.3 all-gather.8
  193.0 76.4 all-gather.4
  364.5 64.2 all-gather.6
